TPU v7x, 32 devices: a whole 2x2x4 slice. The times are simulated.
32 devices in a mesh: seq: 8 (over z, core), mlp: 4 (over y, x).
Axes of the slice: x: 2, y: 2, z: 4, core: 2. Of those that a mesh axis runs over, the one named last changes fastest.
Arguments:
- layer_input: bfloat16 [3072, 5120], P('seq')
- attention_gain: bfloat16 [5120], replicated, may hold values from 0.099609375 to 1.8984375
- feedforward_gain: bfloat16 [5120], replicated, may hold values from 0.099609375 to 1.8984375
- query_weight: bfloat16 [5120, 4096], P('seq', 'mlp'), may hold values from -0.078125 to 0.078125
- key_weight: bfloat16 [5120, 1024], P('seq'), may hold values from -0.078125 to 0.078125
- value_weight: bfloat16 [5120, 1024], P('seq'), may hold values from -0.078125 to 0.078125
- out_weight: bfloat16 [4096, 5120], P('mlp', 'seq'), may hold values from -0.09375 to 0.09375
- gate_weight: bfloat16 [5120, 6912], P('seq', 'mlp'), may hold values from -0.078125 to 0.078125
- up_weight: bfloat16 [5120, 6912], P('seq', 'mlp'), may hold values from -0.078125 to 0.078125
- down_weight: bfloat16 [6912, 5120], P('mlp', 'seq'), may hold values from -0.078125 to 0.078125
- query_bias: bfloat16 [4096], P('mlp'), may hold values from -5 to 5
- key_bias: bfloat16 [1024], replicated, may hold values from -250 to 250
- value_bias: bfloat16 [1024], replicated, may hold values from -5 to 5
- doc_lengths: int32 [4], replicated, may hold values from 1 to 1536, 3072 in all
- piece_order: int32 [16], replicated, may hold values from 0 to 15, each once
- cache_page: int32 [16], replicated, may hold values from 0 to 15, each once
Outputs:
- layer_output: bfloat16 [3072, 5120], P(('seq', 'mlp'))
- kv_cache: bfloat16 [3072, 2048], P('seq', 'mlp')
Inputs may be any that keep to these rules, and one draw needn't show every extreme that they name: `doc_lengths`: the lengths sum to 3072, the longest is exactly 1536. `piece_order`: each piece number appears once. `cache_page`: each page number appears once.
All inputs are finite; a program needn't handle non-finite values.
Results may differ from a plain program's by a relative error of at most 0.0096.
Values may be sent and summed in bfloat16 or wider, within the bound.
No kernel may reach another device: no remote copies, remote signals or barrier semaphores. Data moves between devices by JAX's collectives and lax.ppermute only.
A program may use at most 192 MiB of HBM per device.

v0:
```python
import math

import jax
import jax.numpy as jnp
from jax import lax
from jax.sharding import PartitionSpec as P

KVH = 8
HD = 128
PIECES_DEV = 2


rope_base = 1000000.0
norm_eps = 1e-06
far_below = -1e30


def rms_scale(values, gain_vec):
    mean_sq = jnp.mean(values * values, axis=-1, keepdims=True)
    return values * lax.rsqrt(mean_sq + norm_eps) * gain_vec.astype(jnp.float32)


def rope_tables(position, head_dim):
    half_dim = head_dim // 2
    inverse_freq = jnp.power(
        jnp.float32(rope_base), -2.0 * jnp.arange(half_dim, dtype=jnp.float32) / head_dim
    )
    angles = position.astype(jnp.float32)[:, None] * inverse_freq[None, :]
    return (jnp.cos(angles), jnp.sin(angles))


def rotate(values, cosine, sine_part, head_count):
    row_count = values.shape[0]
    halves = values.reshape(row_count, head_count, 2, -1)
    lower_half = halves[:, :, 0, :]
    upper_half = halves[:, :, 1, :]
    cos_wide = cosine[:, None, :]
    sin_wide = sine_part[:, None, :]
    new_lower = lower_half * cos_wide - upper_half * sin_wide
    new_upper = upper_half * cos_wide + lower_half * sin_wide
    return jnp.stack([new_lower, new_upper], axis=2).reshape(row_count, -1)


def lookup(small_table, indices):
    matches = indices[:, None] == jnp.arange(small_table.shape[0], dtype=jnp.int32)[None, :]
    return jnp.sum(jnp.where(matches, small_table[None, :], 0), axis=1)


def stream_segment(doc_lengths, piece_order, row_ids, piece_len):
    stream = lookup(piece_order, row_ids // piece_len) * piece_len + row_ids % piece_len
    doc_ends = jnp.cumsum(doc_lengths)
    segment = jnp.sum((stream[:, None] >= doc_ends[None, :]).astype(jnp.int32), axis=1)
    return (stream, segment)


def stream_layout(doc_lengths, piece_order, row_ids, piece_len):
    stream, segment = stream_segment(doc_lengths, piece_order, row_ids, piece_len)
    doc_ends = jnp.cumsum(doc_lengths)
    doc_first = lookup(doc_ends - doc_lengths, segment)
    return (stream, segment, stream - doc_first)


def shards(
    layer_input,
    attention_gain,
    feedforward_gain,
    query_weight,
    key_weight,
    value_weight,
    out_weight,
    gate_weight,
    up_weight,
    down_weight,
    query_bias,
    key_bias,
    value_bias,
    doc_lengths,
    piece_order,
    cache_page,
):
    mlp_count = lax.axis_size("mlp")
    seq_rank = lax.axis_index("seq")
    mlp_rank = lax.axis_index("mlp")
    row_count = layer_input.shape[0]
    piece_len = row_count // PIECES_DEV
    kv_cols = max(HD, KVH * HD // mlp_count)
    kv_first = mlp_rank * KVH // mlp_count * HD
    key_weight = lax.dynamic_slice_in_dim(key_weight, kv_first, kv_cols, 1)
    value_weight = lax.dynamic_slice_in_dim(value_weight, kv_first, kv_cols, 1)
    key_bias = lax.dynamic_slice_in_dim(key_bias, kv_first, kv_cols, 0)
    value_bias = lax.dynamic_slice_in_dim(value_bias, kv_first, kv_cols, 0)
    query_weight, key_weight, value_weight, out_weight, gate_weight, up_weight, down_weight = (
        lax.all_gather(query_weight, "seq", axis=0, tiled=True),
        lax.all_gather(key_weight, "seq", axis=0, tiled=True),
        lax.all_gather(value_weight, "seq", axis=0, tiled=True),
        lax.all_gather(out_weight, "seq", axis=1, tiled=True),
        lax.all_gather(gate_weight, "seq", axis=0, tiled=True),
        lax.all_gather(up_weight, "seq", axis=0, tiled=True),
        lax.all_gather(down_weight, "seq", axis=1, tiled=True),
    )
    row_ids = seq_rank * row_count + jnp.arange(row_count, dtype=jnp.int32)
    stream, segment, position = stream_layout(doc_lengths, piece_order, row_ids, piece_len)
    cosine, sine_part = rope_tables(position, HD)
    residual = layer_input.astype(jnp.float32)
    normed = rms_scale(residual, attention_gain).astype(jnp.bfloat16)
    query = jnp.dot(normed, query_weight, preferred_element_type=jnp.float32) + query_bias.astype(
        jnp.float32
    )
    key_full = jnp.dot(normed, key_weight, preferred_element_type=jnp.float32) + key_bias.astype(
        jnp.float32
    )
    value_full = jnp.dot(
        normed, value_weight, preferred_element_type=jnp.float32
    ) + value_bias.astype(jnp.float32)
    own_cols = KVH * HD // mlp_count
    kv_heads = key_full.shape[1] // HD
    query_heads = query.shape[1] // HD
    per_kv = query_heads // kv_heads
    query_rot = rotate(query, cosine, sine_part, query_heads).astype(jnp.bfloat16)
    key_rot = rotate(key_full, cosine, sine_part, kv_heads).astype(jnp.bfloat16)
    value_b = value_full.astype(jnp.bfloat16)
    cache_width = 2 * own_cols
    group_size = max(1, HD // own_cols)
    offset = mlp_rank % group_size * cache_width
    piece_total = piece_order.shape[0]
    pieces = jnp.arange(piece_total, dtype=jnp.int32)
    page_ids = seq_rank * PIECES_DEV + jnp.arange(PIECES_DEV, dtype=jnp.int32)
    stream_of_page = jnp.sum(
        jnp.where(cache_page[None, :] == page_ids[:, None], pieces[None, :], 0), axis=1
    )
    source_piece = jnp.sum(
        jnp.where(piece_order[None, :] == stream_of_page[:, None], pieces[None, :], 0), axis=1
    )
    source_rows = (
        source_piece[:, None] * piece_len + jnp.arange(piece_len, dtype=jnp.int32)[None, :]
    ).reshape(row_count)
    query_grouped = query_rot.reshape(row_count, kv_heads, per_kv, HD)
    key_rows = lax.all_gather(key_rot, "seq", axis=0, tiled=True)
    value_rows = lax.all_gather(value_b, "seq", axis=0, tiled=True)
    row_top = jnp.full((kv_heads, per_kv, row_count), far_below, jnp.float32)
    cache_rows = jnp.zeros((row_count, cache_width), jnp.bfloat16)
    key_count = key_rows.shape[0]
    key_ids = jnp.arange(key_count, dtype=jnp.int32)
    key_stream, key_segment = stream_segment(doc_lengths, piece_order, key_ids, piece_len)
    allowed = (segment[:, None] == key_segment[None, :]) & (key_stream[None, :] <= stream[:, None])
    old_top = row_top
    scores = jnp.einsum(
        "qgrd,kgd->grqk",
        query_grouped,
        key_rows.reshape(key_count, kv_heads, HD),
        preferred_element_type=jnp.float32,
    ) / math.sqrt(HD)
    masked = jnp.where(allowed[None, None], scores, far_below)
    new_top = jnp.maximum(old_top, jnp.max(masked, axis=3))
    weights = jnp.where(allowed[None, None], jnp.exp(scores - new_top[..., None]), 0.0)
    new_total = jnp.sum(weights, axis=3)
    new_out = jnp.einsum(
        "grqk,kgd->grqd",
        weights.astype(jnp.bfloat16),
        value_rows.reshape(key_count, kv_heads, HD),
        preferred_element_type=jnp.float32,
    )
    row_top = new_top
    row_total = new_total
    partial_out = new_out
    inside = (source_rows >= 0) & (source_rows < key_count)
    cache_key_count = key_rows.shape[0]
    joined = jnp.stack(
        [
            key_rows.reshape(cache_key_count, kv_heads, HD),
            value_rows.reshape(cache_key_count, kv_heads, HD),
        ],
        axis=2,
    ).reshape(cache_key_count, 2 * kv_heads * HD)
    picked = jnp.take(
        lax.dynamic_slice_in_dim(joined, offset, cache_width, 1),
        jnp.clip(source_rows, 0, key_count - 1),
        axis=0,
    )
    cache_rows = jnp.where(inside[:, None], picked, cache_rows)
    row_top, row_total, partial_out, kv_cache = (row_top, row_total, partial_out, cache_rows)
    mixed = (
        (partial_out / row_total[..., None])
        .transpose(2, 0, 1, 3)
        .reshape(row_count, query_heads * HD)
        .astype(jnp.bfloat16)
    )
    attn_sum = lax.psum(
        jnp.dot(mixed, out_weight, preferred_element_type=jnp.float32).astype(jnp.bfloat16), "mlp"
    ).astype(jnp.float32)
    residual = residual + attn_sum
    normed2 = rms_scale(residual, feedforward_gain).astype(jnp.bfloat16)
    gate_act = jnp.dot(normed2, gate_weight, preferred_element_type=jnp.float32)
    up_act = jnp.dot(normed2, up_weight, preferred_element_type=jnp.float32)
    hidden_units = (jax.nn.silu(gate_act) * up_act).astype(jnp.bfloat16)
    share_rows = row_count // mlp_count
    down_sum = lax.psum_scatter(
        jnp.dot(hidden_units, down_weight, preferred_element_type=jnp.float32).astype(jnp.bfloat16),
        "mlp",
        scatter_dimension=0,
        tiled=True,
    ).astype(jnp.float32)
    own_residual = lax.dynamic_slice_in_dim(residual, mlp_rank * share_rows, share_rows, 0)
    layer_output = (own_residual + down_sum).astype(jnp.bfloat16)
    return (layer_output, kv_cache)


def solution(mesh):
    placed = (
        P("seq", None),
        P(),
        P(),
        P("seq", "mlp"),
        P("seq", None),
        P("seq", None),
        P("mlp", "seq"),
        P("seq", "mlp"),
        P("seq", "mlp"),
        P("mlp", "seq"),
        P("mlp"),
        P(),
        P(),
        P(),
        P(),
        P(),
    )
    return jax.shard_map(
        shards,
        mesh=mesh,
        in_specs=placed,
        out_specs=(P(("seq", "mlp"), None), P("seq", "mlp")),
        check_vma=False,
    )
```

profile of v0, /device:TPU:0, one launch (start us, length us, event | category | flops | bytes accessed | tf_op | source)
XLA Modules:
  0.0 1007.2 jit_solution(9585072494029778548)
XLA Ops:
  12.6 3.0 fusion.8
  15.6 31.3 %all-gather.16.cloned.1.call-done = bf16[5120,256]{1,0:T(8,128)(2,1)} async-done(((bf16[640,256]{1,0:T(8,128)(2,1)}), bf16[5120,256]{1,0:T(8,128)(2,1)}) %all-gather.16.cloned.1.call-update) | async-done | bytes 2621456 | tf_op jit(solution)/shard_map/all_gather | solution.py:95
  46.8 4.8 fusion.15
  54.1 27.3 %all-gather.10.cloned.1.call-done = bf16[5120,256]{1,0:T(8,128)(2,1)} async-done(((bf16[640,256]{1,0:T(8,128)(2,1)}), bf16[5120,256]{1,0:T(8,128)(2,1)}) %all-gather.10.cloned.1.call-update) | async-done | bytes 2621456 | tf_op jit(solution)/shard_map/all_gather | solution.py:94
  81.4 4.7 convolution_add_fusion.2
  88.0 2.2 compare_and_fusion
  90.2 18.1 %all-gather.18.cloned.1.call-done = bf16[3072,256]{1,0:T(8,128)(2,1)} async-done(((bf16[384,256]{1,0:T(8,128)(2,1)}), bf16[3072,256]{1,0:T(8,128)(2,1)}) %all-gather.18.cloned.1.call-update) | async-done | bytes 1572880 | tf_op jit(solution)/shard_map/all_gather | solution.py:139
  108.3 2.6 copy.45
  110.9 97.9 %all-gather.14.cloned.1.call-done = bf16[5120,1024]{1,0:T(8,128)(2,1)} async-done(((bf16[640,1024]{1,0:T(8,128)(2,1)}), bf16[5120,1024]{1,0:T(8,128)(2,1)}) %all-gather.14.cloned.1.call-update) | async-done | bytes 10485776 | tf_op jit(solution)/shard_map/all_gather | solution.py:93
  208.8 10.6 %convolution_add_fusion = f32[384,1024]{1,0:T(8,128)} fusion(bf16[5120,1024]{1,0:T(8,128)(2,1)} %all-gather.14.cloned.1.call-done, f32[1024]{0:T(1024)S(1)} %convert_element_type.84, bf16[384,5120]{1,0:T(8,128)(2,1)} %param.16, f32[5120]{0:T(1024)S(1)} %convert_element_type.79, f32[384]{0:T(512)S(1)} %add_rsqrt_fusion.1), kind=kOutput, calls=%fused_computation.27 | convolution fusion | flops 4034789376 | bytes 16016896 | tf_op jit(solution)/shard_map/dot_general | solution.py:106
  219.4 1.9 copy.32
  221.6 12.9 %all-gather.12.cloned.1.call-done = bf16[3072,256]{0,1:T(8,128)(2,1)} async-done(((bf16[384,256]{0,1:T(8,128)(2,1)}), bf16[3072,256]{0,1:T(8,128)(2,1)}) %all-gather.12.cloned.1.call-update) | async-done | bytes 1572880 | tf_op jit(solution)/shard_map/all_gather | solution.py:138
  234.4 17.0 %fusion = (f32[2,4,384]{2,1,0:T(4,128)S(1)}, f32[2,3072,384,4]{2,1,3,0:T(8,128)}) fusion(pred[384,3072]{0,1:T(8,128)(4,1)S(1)} %compare_and_fusion, bf16[3072,2,128,1]{0,2,3,1:T(8,128)(2,1)} %bitcast.52, bf16[384,2,4,128]{0,3,2,1:T(8,128)(2,1)S(1)} %bitcast.55), kind=kOutput, calls=%fused_computation.3 | convolution fusion | flops 2444227584 | bytes 41299968 | tf_op jit(solution)/shard_map/qgrd,kgd->grqk/dot_general | solution.py:147
  251.5 16.4 %fusion.3 = f32[2,4,384]{2,1,0:T(4,128)S(1)} fusion(f32[2,3072,384,4]{2,1,3,0:T(8,128)} %get-tuple-element.11, f32[2,4,384]{2,1,0:T(4,128)S(1)} %broadcast_maximum_fusion, pred[384,3072]{0,1:T(8,128)(4,1)S(1)} %compare_and_fusion), kind=kLoop, calls=%fused_computation.6 | loop fusion | flops 37745664 | bytes 38952960 | tf_op jit(solution)/shard_map/reduce_sum | solution.py:156
  267.9 15.9 %fusion.12 = bf16[384,2,4,128]{0,3,2,1:T(8,128)(2,1)} fusion(bf16[3072,2,128,1]{0,2,3,1:T(8,128)(2,1)S(1)} %bitcast.54, f32[2,3072,384,4]{2,1,3,0:T(8,128)} %get-tuple-element.11, f32[2,4,384]{2,1,0:T(4,128)S(1)} %broadcast_maximum_fusion, pred[384,3072]{0,1:T(8,128)(4,1)S(1)} %compare_and_fusion, f32[384,2,4]{0,2,1:T(4,128)S(1)} %bitcast.59), kind=kOutput, calls=%fused_computation.26 | convolution fusion | flops 2454454272 | bytes 41312256 | tf_op jit(solution)/shard_map/grqk,kgd->grqd/dot_general | solution.py:157
  283.8 50.7 %all-gather.20.cloned.1.call-done = bf16[1024,5120]{1,0:T(8,128)(2,1)} async-done(((bf16[1024,640]{1,0:T(8,128)(2,1)}), bf16[1024,5120]{1,0:T(8,128)(2,1)}) %all-gather.20.cloned.1.call-update) | async-done | bytes 10485776 | tf_op jit(solution)/shard_map/all_gather | solution.py:96
  334.5 10.5 %convolution_convert_fusion.1 = bf16[384,5120]{1,0:T(8,128)(2,1)} fusion(bf16[384,1024]{0,1:T(8,128)(2,1)} %bitcast.57, bf16[1024,5120]{1,0:T(8,128)(2,1)} %all-gather.20.cloned.1.call-done), kind=kOutput, calls=%fused_computation.19 | convolution fusion | flops 4028497920 | bytes 15204352 | tf_op jit(solution)/shard_map/dot_general | solution.py:189
  347.1 96.7 %all-reduce.2.cloned.1.call-done = bf16[384,5120]{1,0:T(8,128)(2,1)} async-done(((bf16[384,5120]{1,0:T(8,128)(2,1)}), bf16[384,5120]{1,0:T(8,128)(2,1)}) %all-reduce.2.cloned.1.call-update) | async-done | bytes 3932176 | tf_op jit(solution)/shard_map/psum | solution.py:188
  443.9 7.7 convert_add_fusion
  451.6 152.5 %all-gather.22.cloned.1.call-done = bf16[5120,1728]{0,1:T(8,128)(2,1)} async-done(((bf16[640,1728]{0,1:T(8,128)(2,1)}), bf16[5120,1728]{0,1:T(8,128)(2,1)}) %all-gather.22.cloned.1.call-update) | async-done | bytes 17694736 | tf_op jit(solution)/shard_map/all_gather | solution.py:97
  604.1 16.5 %fusion.36 = f32[384,1728]{0,1:T(8,128)} fusion(bf16[5120,1728]{0,1:T(8,128)(2,1)} %all-gather.22.cloned.1.call-done, f32[5120]{0:T(1024)S(1)} %convert_element_type.93, f32[384]{0:T(512)S(1)} %add_rsqrt_fusion, bf16[384,5120]{1,0:T(8,128)(2,1)} %param.16, bf16[384,5120]{1,0:T(8,128)(2,1)} %all-reduce.2.cloned.1.call-done), kind=kOutput, calls=%fused_computation.96 | convolution fusion | flops 6806568960 | bytes 28235264 | tf_op jit(solution)/shard_map/dot_general | solution.py:193
  620.6 142.0 %all-gather.24.cloned.1.call-done = bf16[5120,1728]{0,1:T(8,128)(2,1)} async-done(((bf16[640,1728]{0,1:T(8,128)(2,1)}), bf16[5120,1728]{0,1:T(8,128)(2,1)}) %all-gather.24.cloned.1.call-update) | async-done | bytes 17694736 | tf_op jit(solution)/shard_map/all_gather | solution.py:98
  762.6 158.3 %all-gather.26.cloned.1.call-done = bf16[1728,5120]{1,0:T(8,128)(2,1)} async-done(((bf16[1728,640]{1,0:T(8,128)(2,1)}), bf16[1728,5120]{1,0:T(8,128)(2,1)}) %all-gather.26.cloned.1.call-update) | async-done | bytes 17694736 | tf_op jit(solution)/shard_map/all_gather | solution.py:99
  921.0 27.9 %convolution_convert_fusion = bf16[384,5120]{1,0:T(8,128)(2,1)} fusion(bf16[1728,5120]{1,0:T(8,128)(2,1)} %all-gather.26.cloned.1.call-done, bf16[5120,1728]{0,1:T(8,128)(2,1)} %all-gather.24.cloned.1.call-done, f32[384,1728]{0,1:T(8,128)} %fusion.36, f32[5120]{0:T(1024)S(1)} %convert_element_type.93, f32[384]{0:T(512)S(1)} %add_rsqrt_fusion, ...), kind=kOutput, calls=%fused_computation.18 | convolution fusion | flops 13607288832 | bytes 49862144 | tf_op jit(solution)/shard_map/dot_general | solution.py:198
  950.3 5.0 copy.37
  955.4 1.9 stack_reshape.7
  957.2 6.4 pad_maximum_fusion
  963.6 13.4 %copy.38 = bf16[3072,2,2,128]{3,2,1,0:T(2,128)(2,1)} copy(bf16[3072,2,2,128]{3,1,0,2:T(2,128)(2,1)S(1)} %pad_maximum_fusion) | data formatting | bytes 6291456 | tf_op jit(solution)/shard_map/stack | solution.py:168
  977.0 5.8 reshape.328
  982.8 5.0 gather_fusion
  988.7 9.0 reduce-scatter.2.cloned.1.call-done
  997.7 3.0 add_convert_fusion
  (81 shorter events, 14.3 us)
Async XLA Ops:
  7.2 1.3 copy-start
  7.2 39.7 %all-gather.16.cloned.1.call-start = ((), (), s32[]{:S(2)}) async-start(), calls=%async_computation.4 | async-start | bytes 2949120 | tf_op jit(solution)/shard_map/all_gather | solution.py:95
  9.3 72.1 %all-gather.10.cloned.1.call-start = ((), (), s32[]{:S(2)}) async-start(), calls=%async_computation.1 | async-start | bytes 2949120 | tf_op jit(solution)/shard_map/all_gather | solution.py:94
  11.1 97.2 %all-gather.18.cloned.1.call-start = ((), (), s32[]{:S(2)}) async-start(), calls=%async_computation.5 | async-start | bytes 1769472 | tf_op jit(solution)/shard_map/all_gather | solution.py:139
  15.6 36.8 %copy-start.7 = (s32[4]{0:T(128)S(1)}, s32[4]{0:T(128)}, u32[]{:S(2)}) copy-start(s32[4]{0:T(128)} %param.29) | copy-start | bytes 52
  15.6 37.7 %copy-start.6 = (s32[16]{0:T(128)S(1)}, s32[16]{0:T(128)}, u32[]{:S(2)}) copy-start(s32[16]{0:T(128)} %param.30) | copy-start | bytes 196
  51.7 157.1 %all-gather.14.cloned.1.call-start = ((), (), s32[]{:S(2)}) async-start(), calls=%async_computation.3 | async-start | bytes 11796480 | tf_op jit(solution)/shard_map/all_gather | solution.py:93
  52.3 182.2 %all-gather.12.cloned.1.call-start = ((), (), s32[]{:S(2)}) async-start(), calls=%async_computation.2 | async-start | bytes 1769472 | tf_op jit(solution)/shard_map/all_gather | solution.py:138
  54.1 33.7 %copy-start.5 = (bf16[1024]{0:T(1024)(128)(2,1)S(1)}, bf16[1024]{0:T(1024)(128)(2,1)}, u32[]{:S(2)}) copy-start(bf16[1024]{0:T(1024)(128)(2,1)} %param.26) | copy-start | bytes 6148
  86.9 247.6 %all-gather.20.cloned.1.call-start = ((), (), s32[]{:S(2)}) async-start(), calls=%async_computation.6 | async-start | bytes 11796480 | tf_op jit(solution)/shard_map/all_gather | solution.py:96
  87.5 356.4 %all-reduce.2.cloned.1.call-start = ((), (), s32[]{:S(2)}) async-start(), calls=%async_computation.7 | async-start | bytes 7864320 | tf_op jit(solution)/shard_map/psum | solution.py:188
  251.5 16.4 %copy-start.3 = (bf16[3072,256]{0,1:T(8,128)(2,1)S(1)}, bf16[3072,256]{0,1:T(8,128)(2,1)}, u32[]{:S(2)}) copy-start(bf16[3072,256]{0,1:T(8,128)(2,1)} %copy.45) | copy-start | bytes 4718596
  345.0 2.1 copy-start.4
  345.0 259.2 %all-gather.22.cloned.1.call-start = ((), (), s32[]{:S(2)}) async-start(), calls=%async_computation.8 | async-start | bytes 19906560 | tf_op jit(solution)/shard_map/all_gather | solution.py:97
  345.7 416.9 %all-gather.24.cloned.1.call-start = ((), (), s32[]{:S(2)}) async-start(), calls=%async_computation.9 | async-start | bytes 19906560 | tf_op jit(solution)/shard_map/all_gather | solution.py:98
  346.5 574.5 %all-gather.26.cloned.1.call-start = ((), (), s32[]{:S(2)}) async-start(), calls=%async_computation.10 | async-start | bytes 19906560 | tf_op jit(solution)/shard_map/all_gather | solution.py:99
  347.0 650.7 %reduce-scatter.2.cloned.1.call-start = ((), (), s32[]{:S(2)}) async-start(), calls=%async_computation.11 | async-start | bytes 4915200 | tf_op jit(solution)/shard_map/reduce_scatter | solution.py:197
  948.8 0.7 copy-start.8
  948.8 6.5 copy-start.2
  977.0 23.7 %copy-start.1 = (bf16[640,1024]{1,0:T(8,128)(2,1)S(1)}, bf16[640,1024]{1,0:T(8,128)(2,1)}, u32[]{:S(2)}) copy-start(bf16[640,1024]{1,0:T(8,128)(2,1)} %param.21) | copy-start | bytes 3932164
Sparse Core Ops, SparseCore 0:
  10.2 36.5 all-gather.15
  49.1 32.2 all-gather.9
  83.6 24.6 all-gather.17
  109.8 98.9 all-gather.13
  210.8 23.5 all-gather.11
  235.9 98.5 all-gather.19
  345.1 98.7 all-reduce.1
  445.6 158.5 all-gather.21
  605.8 156.7 all-gather.23
  764.2 156.7 all-gather.25
  949.0 48.7 reduce-scatter.1
where the time goes:
time: 1010 us
  waiting for transfers between devices  800 us (79%)
  matrix products  108 us (11%)
  other arithmetic  44.6 us (4%)
  local copies, waits for them, and re-layouts  40.1 us (4%)
  between operations  14.1 us (1%)
    all_gather x1, waiting for transfers between devices, shards(): lax.all_gather(down_weight, 'seq', axis=1, tiled=True)  158 us
    all_gather x1, waiting for transfers between devices, shards(): lax.all_gather(gate_weight, 'seq', axis=0, tiled=True)  153 us
    all_gather x1, waiting for transfers between devices, shards(): lax.all_gather(up_weight, 'seq', axis=0, tiled=True)  142 us
    all_gather x1, waiting for transfers between devices, shards(): lax.all_gather(query_weight, 'seq', axis=0, tiled=True)  97.9 us
    psum x1, waiting for transfers between devices, shards(): lax.psum(jnp.dot(mixed, out_weight, preferred_element_type=jnp.float32).a...  96.7 us
    all_gather x1, waiting for transfers between devices, shards(): lax.all_gather(out_weight, 'seq', axis=1, tiled=True)  50.7 us
    all_gather x1, waiting for transfers between devices, shards(): lax.all_gather(value_weight, 'seq', axis=0, tiled=True)  31.3 us
    dot_general x1, matrix products, shards(): jnp.dot(hidden_units, down_weight, preferred_element_type=jnp.float32)  27.9 us
  transfers between devices with their start and end apart: 11, of which 11 were waited for; matrix products, arithmetic and copies ran while one was open for 15% of the time, Pallas kernels for 0%

commit v1 on v0

v1 whole, which is shorter than its diff:
```python
import math

import jax
import jax.numpy as jnp
from jax import lax
from jax.experimental import pallas as pl
from jax.experimental.pallas import tpu as pltpu
from jax.sharding import PartitionSpec as P

KVH = 8
HD = 128
PIECES_DEV = 2
CORES = 2

rope_base = 1000000.0
norm_eps = 1e-06
far_below = -1e30
start_top = -1e29
F32 = jnp.float32
BF16 = jnp.bfloat16


def rope_tables(position, head_dim):
    half_dim = head_dim // 2
    inverse_freq = jnp.power(
        jnp.float32(rope_base), -2.0 * jnp.arange(half_dim, dtype=jnp.float32) / head_dim
    )
    angles = position.astype(jnp.float32)[:, None] * inverse_freq[None, :]
    return (jnp.cos(angles), jnp.sin(angles))


def rotate(values, cosine, sine_part, head_count):
    row_count = values.shape[0]
    halves = values.reshape(row_count, head_count, 2, -1)
    lower_half = halves[:, :, 0, :]
    upper_half = halves[:, :, 1, :]
    cos_wide = cosine[:, None, :]
    sin_wide = sine_part[:, None, :]
    new_lower = lower_half * cos_wide - upper_half * sin_wide
    new_upper = upper_half * cos_wide + lower_half * sin_wide
    return jnp.stack([new_lower, new_upper], axis=2).reshape(row_count, -1)


def lookup(small_table, indices):
    matches = indices[:, None] == jnp.arange(small_table.shape[0], dtype=jnp.int32)[None, :]
    return jnp.sum(jnp.where(matches, small_table[None, :], 0), axis=1)


def attend_kernel(count, active, piece_stream, q_ref, k_ref, v_ref, lo_ref, hi_ref, o_ref, acc_ref):
    chunk = pl.program_id(1)
    piece_len = k_ref.shape[0] // piece_stream.shape[0]
    rows = q_ref.shape[1]
    per_kv = q_ref.shape[2] // HD
    scale = 1.0 / math.sqrt(HD)
    q = jnp.concatenate([q_ref[0, :, i * HD : (i + 1) * HD] for i in range(per_kv)], axis=0)
    lo = lo_ref[0]
    hi = hi_ref[0]
    acc_ref[...] = jnp.zeros_like(acc_ref)

    def step(i, carry):
        top, total = carry
        piece = active[chunk, i]
        first = pl.multiple_of(piece * piece_len, piece_len)
        k = k_ref[pl.ds(first, piece_len), :]
        v = v_ref[pl.ds(first, piece_len), :]
        s = lax.dot_general(k, q, (((1,), (1,)), ((), ())), preferred_element_type=F32) * scale
        stream = piece_stream[piece] * piece_len + lax.broadcasted_iota(jnp.int32, s.shape, 0)
        s = jnp.where((stream >= lo) & (stream <= hi), s, far_below)
        new_top = jnp.maximum(top, jnp.max(s, axis=0, keepdims=True))
        w = jnp.exp(s - new_top)
        fade = jnp.exp(top - new_top)
        total = total * fade + jnp.sum(w, axis=0, keepdims=True)
        part = lax.dot_general(v, w.astype(BF16), (((0,), (0,)), ((), ())), preferred_element_type=F32)
        acc_ref[...] = acc_ref[...] * fade + part
        return (new_top, total)

    top = jnp.full((1, q.shape[0]), start_top, F32)
    total = jnp.zeros((1, q.shape[0]), F32)
    top, total = lax.fori_loop(0, count[chunk], step, (top, total))
    out = (acc_ref[...] / total).T.astype(BF16)
    for i in range(per_kv):
        o_ref[0, :, i * HD : (i + 1) * HD] = out[i * rows : (i + 1) * rows]


def attend(query, kv_rows, lo, hi, piece_stream, kv_heads):
    chunks, rows, width = query.shape
    per_kv = width // (kv_heads * HD)
    keys = kv_rows.shape[0]
    pieces = piece_stream.shape[0]
    piece_len = keys // pieces
    first = piece_stream[None, None, :] * piece_len
    touch = jnp.any(
        (lo[:, :, None] <= first + piece_len - 1) & (hi[:, :, None] >= first), axis=1
    ).astype(jnp.int32)
    place = jnp.cumsum(touch, axis=1) - 1
    ids = jnp.arange(pieces, dtype=jnp.int32)
    active = jnp.sum(
        jnp.where((touch[:, :, None] > 0) & (place[:, :, None] == ids), ids[None, :, None], 0), axis=1
    ).astype(jnp.int32)
    count = jnp.sum(touch, axis=1).astype(jnp.int32)
    lo_wide = jnp.tile(lo, (1, per_kv))[:, None, :]
    hi_wide = jnp.tile(hi, (1, per_kv))[:, None, :]
    return pl.pallas_call(
        attend_kernel,
        grid_spec=pltpu.PrefetchScalarGridSpec(
            num_scalar_prefetch=3,
            grid=(kv_heads, chunks),
            in_specs=[
                pl.BlockSpec((1, rows, per_kv * HD), lambda g, h, *_: (h, 0, g)),
                pl.BlockSpec((keys, HD), lambda g, h, *_: (0, 2 * g)),
                pl.BlockSpec((keys, HD), lambda g, h, *_: (0, 2 * g + 1)),
                pl.BlockSpec((1, 1, rows * per_kv), lambda g, h, *_: (h, 0, 0)),
                pl.BlockSpec((1, 1, rows * per_kv), lambda g, h, *_: (h, 0, 0)),
            ],
            out_specs=pl.BlockSpec((1, rows, per_kv * HD), lambda g, h, *_: (h, 0, g)),
            scratch_shapes=[pltpu.VMEM((HD, rows * per_kv), F32)],
        ),
        out_shape=jax.ShapeDtypeStruct(query.shape, BF16),
        compiler_params=pltpu.CompilerParams(vmem_limit_bytes=32 * 2**20),
    )(count, active, piece_stream, query, kv_rows, kv_rows, lo_wide, hi_wide)


def shards(
    layer_input,
    attention_gain,
    feedforward_gain,
    query_weight,
    key_weight,
    value_weight,
    out_weight,
    gate_weight,
    up_weight,
    down_weight,
    query_bias,
    key_bias,
    value_bias,
    doc_lengths,
    piece_order,
    cache_page,
):
    seq_count = lax.axis_size("seq")
    mlp_count = lax.axis_size("mlp")
    seq_rank = lax.axis_index("seq")
    mlp_rank = lax.axis_index("mlp")
    planes = seq_count // CORES
    plane = seq_rank // CORES
    core = seq_rank % CORES
    rows, width = layer_input.shape
    dz = width // planes
    ds = width // seq_count
    share = rows // mlp_count
    chunks = 2 if share % 32 == 0 else 1
    sub = share // chunks
    crows = mlp_count * sub
    piece_len = rows // PIECES_DEV

    def move(x, pairs):
        return lax.ppermute(
            x, "seq", [(a * CORES + e, b * CORES + e) for a, b in pairs for e in range(CORES)]
        )

    def sibling(x):
        return lax.ppermute(
            x, "seq", [(a * CORES + e, a * CORES + 1 - e) for a in range(planes) for e in range(CORES)]
        )

    def line_gather(x):
        ups, downs = [x], [x]
        for t in range(1, planes):
            ups.append(move(ups[-1], [(i, i + 1) for i in range(t - 1, planes - 1)]))
            downs.append(move(downs[-1], [(i, i - 1) for i in range(1, planes - t + 1)]))
        return [x] + [ups[k] + downs[planes - k] for k in range(1, planes)]

    def line_scatter(parts):
        up = down = None
        for t in range(1, planes):
            send_up, send_down = parts[t], parts[planes - t]
            if up is not None:
                send_up = (send_up.astype(F32) + up.astype(F32)).astype(BF16)
                send_down = (send_down.astype(F32) + down.astype(F32)).astype(BF16)
            up = move(send_up, [(i, i + 1) for i in range(0, min(t, planes - 1))])
            down = move(send_down, [(i, i - 1) for i in range(max(1, planes - t), planes)])
        return parts[0].astype(F32) + up.astype(F32) + down.astype(F32)

    def swap_halves(x):
        return jnp.where(core == 0, x, jnp.concatenate([x[..., ds:], x[..., :ds]], axis=-1))

    kv_cols = max(HD, KVH * HD // mlp_count)
    kv_first = mlp_rank * KVH // mlp_count * HD
    qkv_weight = jnp.concatenate(
        [
            lax.dynamic_slice_in_dim(key_weight, kv_first, kv_cols, 1),
            lax.dynamic_slice_in_dim(value_weight, kv_first, kv_cols, 1),
            query_weight,
        ],
        axis=1,
    )
    qkv_bias = jnp.concatenate(
        [
            lax.dynamic_slice_in_dim(key_bias, kv_first, kv_cols, 0),
            lax.dynamic_slice_in_dim(value_bias, kv_first, kv_cols, 0),
            query_bias,
        ]
    ).astype(F32)
    qkv_weight = lax.all_gather(qkv_weight, "seq", axis=0, tiled=True)

    units = gate_weight.shape[1]
    whole = units // HD * HD
    glu_own = jnp.concatenate(
        [gate_weight[:, :whole], up_weight[:, :whole], gate_weight[:, whole:], up_weight[:, whole:]],
        axis=1,
    )
    glu_weight = jnp.concatenate([glu_own, sibling(glu_own)], axis=0)
    out_wide = jnp.concatenate([out_weight, sibling(out_weight)], axis=1)
    down_wide = jnp.concatenate([down_weight, sibling(down_weight)], axis=1)

    def regroup(x):
        return jnp.swapaxes(x.reshape((mlp_count, chunks, sub) + x.shape[1:]), 0, 1).reshape(x.shape)

    def ungroup(x):
        return jnp.swapaxes(x.reshape((chunks, mlp_count, sub) + x.shape[1:]), 0, 1).reshape(x.shape)

    own_share = lax.dynamic_slice_in_dim(layer_input, mlp_rank * share, share, 0)
    lane_parts = []
    for k in range(planes):
        part = lax.dynamic_slice_in_dim(own_share, (plane + k) % planes * dz, dz, 1)
        if k:
            part = move(part, [(i, (i + k) % planes) for i in range(planes)])
        lane_parts.append(part)
    lane_input = swap_halves(jnp.stack(lane_parts, axis=0))
    lane_input = lane_input.reshape(planes, chunks, sub, dz)
    gain_lane = swap_halves(lax.dynamic_slice_in_dim(feedforward_gain, plane * dz, dz, 0)).astype(F32)

    row_ids = seq_rank * rows + regroup(jnp.arange(rows, dtype=jnp.int32))
    stream = lookup(piece_order, row_ids // piece_len) * piece_len + row_ids % piece_len
    doc_ends = jnp.cumsum(doc_lengths)
    segment = jnp.sum((stream[:, None] >= doc_ends[None, :]).astype(jnp.int32), axis=1)
    doc_first = lookup(doc_ends - doc_lengths, segment)
    cosine, sine_part = rope_tables(stream - doc_first, HD)

    x = regroup(layer_input).astype(F32)
    mean_sq = jnp.mean(x * x, axis=-1, keepdims=True)
    normed = (x * lax.rsqrt(mean_sq + norm_eps) * attention_gain.astype(F32)).astype(BF16)
    qkv = jnp.dot(normed, qkv_weight, preferred_element_type=F32) + qkv_bias
    kv_heads = kv_cols // HD
    query_heads = query_weight.shape[1] // HD
    key_rot = rotate(qkv[:, :kv_cols], cosine, sine_part, kv_heads).astype(BF16)
    value_b = qkv[:, kv_cols : 2 * kv_cols].astype(BF16)
    query_rot = rotate(qkv[:, 2 * kv_cols :], cosine, sine_part, query_heads).astype(BF16)
    joined = jnp.stack(
        [key_rot.reshape(rows, kv_heads, HD), value_b.reshape(rows, kv_heads, HD)], axis=2
    ).reshape(rows, 2 * kv_cols)
    kv_rows = lax.all_gather(ungroup(joined), "seq", axis=0, tiled=True)

    own_cols = KVH * HD // mlp_count
    cache_width = 2 * own_cols
    offset = mlp_rank % max(1, HD // own_cols) * cache_width
    pieces = jnp.arange(piece_order.shape[0], dtype=jnp.int32)
    pages = []
    for p in range(PIECES_DEV):
        stream_piece = jnp.sum(jnp.where(cache_page == seq_rank * PIECES_DEV + p, pieces, 0))
        source = jnp.sum(jnp.where(piece_order == stream_piece, pieces, 0))
        pages.append(lax.dynamic_slice(kv_rows, (source * piece_len, offset), (piece_len, cache_width)))
    kv_cache = jnp.concatenate(pages, axis=0)

    mixed = attend(
        query_rot.reshape(chunks, crows, query_heads * HD),
        kv_rows,
        doc_first.reshape(chunks, crows),
        stream.reshape(chunks, crows),
        piece_order,
        kv_heads,
    )

    def by_share(slots):
        return jnp.stack([v.reshape(mlp_count, sub, -1) for v in slots], axis=1).reshape(
            mlp_count * planes * sub, -1
        )

    finals = []
    for h in range(chunks):
        heads = by_share(line_gather(mixed[h]))
        attn = jnp.dot(heads, out_wide, preferred_element_type=F32).astype(BF16)
        attn = lax.psum_scatter(attn, "mlp", scatter_dimension=0, tiled=True)
        residual = lane_input[:, h].astype(F32).reshape(planes * sub, dz) + attn.astype(F32)
        square = jnp.sum(residual * residual, axis=-1).reshape(planes, sub)
        lane = lax.all_gather((residual * gain_lane).astype(BF16), "mlp", axis=0, tiled=True)
        square = sum(
            [square[0]]
            + [move(square[k], [(i, (i - k) % planes) for i in range(planes)]) for k in range(1, planes)]
        )
        square = lax.all_gather(square, "mlp", axis=0, tiled=True)
        scale = lax.rsqrt(square / width + norm_eps)[:, None]
        part = jnp.dot(lane, glu_weight, preferred_element_type=F32).astype(BF16)
        part = part.reshape(mlp_count, planes, sub, 2 * units)
        act = line_scatter([part[:, k].reshape(crows, 2 * units) for k in range(planes)]) * scale
        hidden = jax.nn.silu(act[:, :whole]) * act[:, whole : 2 * whole]
        if units > whole:
            last = act[:, 2 * whole :]
            edge = units - whole
            hidden = jnp.concatenate(
                [hidden, jax.nn.silu(last[:, :edge]) * last[:, edge:]], axis=1
            )
        hidden = by_share(line_gather(hidden.astype(BF16)))
        down = jnp.dot(hidden, down_wide, preferred_element_type=F32).astype(BF16)
        down = lax.psum_scatter(down, "mlp", scatter_dimension=0, tiled=True)
        final = (residual + down.astype(F32)).astype(BF16).reshape(planes, sub, dz)
        finals.append(
            jnp.stack(
                [final[0]]
                + [move(final[k], [(i, (i - k) % planes) for i in range(planes)]) for k in range(1, planes)]
            )
        )
    final = swap_halves(jnp.concatenate(finals, axis=1))
    final = lax.dynamic_slice_in_dim(
        jnp.concatenate([final, final], axis=0), (planes - plane) % planes, planes, 0
    )
    layer_output = jnp.swapaxes(final, 0, 1).reshape(share, width)
    return (layer_output, kv_cache)


def solution(mesh):
    placed = (
        P("seq", None),
        P(),
        P(),
        P("seq", "mlp"),
        P("seq", None),
        P("seq", None),
        P("mlp", "seq"),
        P("seq", "mlp"),
        P("seq", "mlp"),
        P("mlp", "seq"),
        P("mlp"),
        P(),
        P(),
        P(),
        P(),
        P(),
    )
    return jax.shard_map(
        shards,
        mesh=mesh,
        in_specs=placed,
        out_specs=(P(("seq", "mlp"), None), P("seq", "mlp")),
        check_vma=False,
    )
```

time: 1010 us -> 828 us (0.82)
  waiting for transfers between devices: 800 us -> 435 us
  starting transfers between devices: 0.62 us -> 135 us
  Pallas kernels: 0 us -> 32 us
  other arithmetic: 44.6 us -> 58.7 us
  matrix products: 108 us -> 96.4 us
    all_gather x9 -> x4, waiting for transfers between devices: 691 us -> 184 us  [the longest x1 127 us: shards(): qkv_weight = lax.all_gather(qkv_weight, 'seq', axis=0, tiled=True)]
    ppermute x0 -> x54, waiting for transfers between devices: none -> 216 us  [the longest x51 216 us: move(): lax.ppermute(x, 'seq', [(a * CORES + e, b * CORES + e) for a, b in pairs...]
    ppermute x0 -> x54, starting transfers between devices: none -> 135 us  [the longest x51 135 us: move(): lax.ppermute(x, 'seq', [(a * CORES + e, b * CORES + e) for a, b in pairs...]
    psum x1 -> x0, waiting for transfers between devices: 96.7 us -> none  [shards(): lax.psum(jnp.dot(mixed, out_weight, preferred_element_type=jnp.float32).a...]
    pallas_call x0 -> x1, Pallas kernels: none -> 32 us  [attend(): pl.pallas_call(attend_kernel, grid_spec=pltpu.PrefetchScalarGridSpec(num_...]
    reduce_scatter x1 -> x4, waiting for transfers between devices: 9 us -> 35 us  [the longest x2 26 us: shards(): down = lax.psum_scatter(down, 'mlp', scatter_dimension=0, tiled=True)]
    convert_element_type x6 -> x13, other arithmetic: 5.21 us -> 25.7 us  [the longest x1 7.71 us: shards(): (x * lax.rsqrt(mean_sq + norm_eps) * attention_gain.astype(F32)).astype(B...]
    another operation x3 -> x7, local copies, waits for them, and re-layouts: 20.3 us -> 1.12 us  [the longest x2 0.78 us: shards(): jnp.stack([key_rot.reshape(rows, kv_heads, HD), value_b.reshape(rows, kv_...]
  transfers between devices with their start and end apart: 11 -> 62, of which waited for: 11 -> 26; matrix products, arithmetic and copies ran while one was open for 15% -> 20% of each run, Pallas kernels for 0% -> 4%
where the time goes in v1:
time: 828 us; the launch traced here: 826 us
  waiting for transfers between devices  435 us (53%)
  starting transfers between devices  135 us (16%)
  matrix products  96.4 us (12%)
  other arithmetic  58.7 us (7%)
  local copies, waits for them, and re-layouts  41.3 us (5%)
  Pallas kernels  32 us (4%)
  between operations  17.6 us (2%)
  blocking collectives  8.9 us (1%)
    ppermute x51, waiting for transfers between devices, move(): lax.ppermute(x, 'seq', [(a * CORES + e, b * CORES + e) for a, b in pairs...  216 us
    ppermute x51, starting transfers between devices, move(): lax.ppermute(x, 'seq', [(a * CORES + e, b * CORES + e) for a, b in pairs...  135 us
    all_gather x1, waiting for transfers between devices, shards(): qkv_weight = lax.all_gather(qkv_weight, 'seq', axis=0, tiled=True)  127 us
    dot_general x2, matrix products, shards(): part = jnp.dot(lane, glu_weight, preferred_element_type=F32).astype(BF16)  69.1 us
    pallas_call x1, Pallas kernels, attend(): pl.pallas_call(attend_kernel, grid_spec=pltpu.PrefetchScalarGridSpec(num_...  32 us
    all_gather x2, waiting for transfers between devices, shards(): lax.all_gather((residual * gain_lane).astype(BF16), 'mlp', axis=0, tiled=...  29 us
    all_gather x1, waiting for transfers between devices, shards(): kv_rows = lax.all_gather(ungroup(joined), 'seq', axis=0, tiled=True)  28.7 us
    reduce_scatter x2, waiting for transfers between devices, shards(): down = lax.psum_scatter(down, 'mlp', scatter_dimension=0, tiled=True)  26 us
  transfers between devices with their start and end apart: 62, of which 26 were waited for; matrix products, arithmetic and copies ran while one was open for 20% of the time, Pallas kernels for 4%

profile of v1, /device:TPU:0, one launch (start us, length us, event | category | flops | bytes accessed | tf_op | source)
XLA Modules:
  0.0 825.7 jit_solution(8380527207259575005)
XLA Ops:
  21.2 7.7 fusion.1
  28.9 126.7 %all-gather.5.cloned.1.call-done = bf16[5120,1536]{1,0:T(8,128)(2,1)} async-done(((bf16[640,1536]{1,0:T(8,128)(2,1)}), bf16[5120,1536]{1,0:T(8,128)(2,1)}) %all-gather.5.cloned.1.call-update) | async-done | bytes 15728656 | tf_op jit(solution)/shard_map/all_gather | solution.py:205
  155.6 10.6 %convolution_add_fusion = f32[384,1536]{1,0:T(8,128)S(1)} fusion(bf16[384,5120]{1,0:T(8,128)(2,1)} %fusion.1, bf16[5120,1536]{1,0:T(8,128)(2,1)} %all-gather.5.cloned.1.call-done, f32[1536]{0:T(1024)S(1)} %maximum_convert_fusion), kind=kOutput, calls=%fused_computation.16 | convolution fusion | flops 6040387584 | bytes 22026240 | tf_op jit(solution)/shard_map/dot_general | solution.py:244
  177.8 28.7 %all-gather.7.cloned.1.call-done.k_ref.v_ref = bf16[3072,512]{1,0:T(8,128)(2,1)} async-done(((bf16[384,512]{1,0:T(8,128)(2,1)}), bf16[3072,512]{1,0:T(8,128)(2,1)}) %all-gather.7.cloned.1.call-update) | async-done | bytes 3145744 | tf_op jit(solution)/shard_map/all_gather | solution.py:253
  208.3 32.0 %shard_map.167 = bf16[2,192,1024]{2,1,0:T(8,128)(2,1)S(1)} custom-call(s32[2]{0:T(128)S(1)} %convert_reduce_fusion.1.count, s32[2,16]{1,0:T(2,128)S(1)} %select_reduce_fusion.1.active, s32[16]{0:T(128)S(1)} %copy-done.1, bf16[2,192,1024]{2,1,0:T(8,128)(2,1)S(1)} %copy.77.q_ref, bf16[3072,512]{1,0:T(8,128)(2,1)S(1)} %copy-done, ...), custom_call_target="tpu_custom_call" | custom-call | tf_op jit(solution)/shard_map/pallas_call | solution.py:103
  247.8 6.9 collective-permute-done.31
  256.8 11.7 %collective-permute-done.32 = bf16[192,1024]{1,0:T(8,128)(2,1)S(1)} collective-permute-done((bf16[192,1024]{1,0:T(8,128)(2,1)S(1)}, bf16[192,1024]{1,0:T(8,128)(2,1)S(1)}, u32[]{:S(2)}, u32[]{:S(2)}) %collective-permute-start.32) | collective-permute-done | bytes 393248 | tf_op jit(solution)/shard_map/ppermute | solution.py:158
  289.5 5.6 collective-permute-done.4
  297.1 8.7 %collective-permute-done.5 = bf16[192,1024]{1,0:T(8,128)(2,1)S(1)} collective-permute-done((bf16[192,1024]{1,0:T(8,128)(2,1)S(1)}, bf16[192,1024]{1,0:T(8,128)(2,1)S(1)}, u32[]{:S(2)}, u32[]{:S(2)}) %collective-permute-start.5) | collective-permute-done | bytes 393248 | tf_op jit(solution)/shard_map/ppermute | solution.py:158
  307.4 16.0 %collective-permute-done.6 = bf16[192,1024]{1,0:T(8,128)(2,1)S(1)} collective-permute-done((bf16[192,1024]{1,0:T(8,128)(2,1)S(1)}, bf16[192,1024]{1,0:T(8,128)(2,1)S(1)}, u32[]{:S(2)}, u32[]{:S(2)}) %collective-permute-start.6) | collective-permute-done | bytes 393248 | tf_op jit(solution)/shard_map/ppermute | solution.py:158
  335.3 14.5 %pad_maximum_fusion.1 = bf16[640,3456]{0,1:T(8,128)(2,1)} fusion(bf16[640,64]{0,1:T(8,128)(2,1)S(1)} %slice.202, bf16[640,64]{0,1:T(8,128)(2,1)S(1)} %slice.201, bf16[640,1664]{0,1:T(8,128)(2,1)S(1)} %slice.200, bf16[640,1664]{0,1:T(8,128)(2,1)S(1)} %slice.199), kind=kLoop, calls=%fused_computation.7 | loop fusion | flops 17694720 | bytes 8847360 | tf_op jit(solution)/shard_map/concatenate | solution.py:209
  350.7 9.0 %reduce-scatter.5.cloned.1.call-done = bf16[192,1280]{1,0:T(8,128)(2,1)} async-done(((bf16[768,1280]{1,0:T(8,128)(2,1)}), bf16[192,1280]{1,0:T(8,128)(2,1)}) %reduce-scatter.5.cloned.1.call-update) | async-done | bytes 491536 | tf_op jit(solution)/shard_map/reduce_scatter | solution.py:284
  367.7 29.0 %all-gather.11.cloned.1.call-done = bf16[768,1280]{1,0:T(8,128)(2,1)} async-done(((bf16[192,1280]{1,0:T(8,128)(2,1)}), bf16[768,1280]{1,0:T(8,128)(2,1)}) %all-gather.11.cloned.1.call-update) | async-done | bytes 1966096 | tf_op jit(solution)/shard_map/all_gather | solution.py:287
  396.7 34.4 %convolution_convert_fusion = bf16[768,3456]{1,0:T(8,128)(2,1)} fusion(bf16[768,1280]{1,0:T(8,128)(2,1)} %all-gather.11.cloned.1.call-done, bf16[640,3456]{0,1:T(8,128)(2,1)} %collective-permute-done.10, bf16[640,64]{0,1:T(8,128)(2,1)S(1)} %slice.202, bf16[640,64]{0,1:T(8,128)(2,1)S(1)} %slice.201, bf16[640,1664]{0,1:T(8,128)(2,1)S(1)} %slice.200, ...), kind=kOutput, calls=%fused_computation.5 | convolution fusion | flops 6841663488 | bytes 16121856 | tf_op jit(solution)/shard_map/dot_general | solution.py:294
  431.1 5.0 fusion.27
  442.3 34.7 %convolution_convert_fusion.1 = bf16[768,3456]{1,0:T(8,128)(2,1)} fusion(bf16[768,1280]{1,0:T(8,128)(2,1)} %all-gather.9.cloned.1.call-done, bf16[640,3456]{0,1:T(8,128)(2,1)} %collective-permute-done.10, bf16[640,64]{0,1:T(8,128)(2,1)S(1)} %slice.202, bf16[640,64]{0,1:T(8,128)(2,1)S(1)} %slice.201, bf16[640,1664]{0,1:T(8,128)(2,1)S(1)} %slice.200, ...), kind=kOutput, calls=%fused_computation.6 | convolution fusion | flops 6841663488 | bytes 16121856 | tf_op jit(solution)/shard_map/dot_general | solution.py:294
  489.4 21.4 %collective-permute-done.42 = f32[48]{0:T(128)S(1)} collective-permute-done((f32[48]{0:T(128)S(1)}, f32[48]{0:T(128)S(1)}, u32[]{:S(2)}, u32[]{:S(2)}) %collective-permute-start.42) | collective-permute-done | bytes 224 | tf_op jit(solution)/shard_map/ppermute | solution.py:158
  510.8 5.8 collective-permute-start.19
  516.7 26.8 %collective-permute-start.18 = (f32[48]{0:T(128)S(1)}, f32[48]{0:T(128)S(1)}, u32[]{:S(2)}, u32[]{:S(2)}) collective-permute-start(f32[48]{0:T(128)S(1)} %get-tuple-element.62), channel_id=1, source_target_pairs={{0,16},{4,20},{8,24},{12,28},{16,0},{20,4},{24,8},{28,12},{1,17},{... | collective-permute-start | bytes 584 | tf_op jit(solution)/shard_map/ppermute | solution.py:158
  552.1 21.1 %collective-permute-done.37 = bf16[192,3456]{1,0:T(8,128)(2,1)S(1)} collective-permute-done((bf16[192,3456]{1,0:T(8,128)(2,1)S(1)}, bf16[192,3456]{1,0:T(8,128)(2,1)S(1)}, u32[]{:S(2)}, u32[]{:S(2)}) %collective-permute-start.37) | collective-permute-done | bytes 1327136 | tf_op jit(solution)/shard_map/ppermute | solution.py:158
  579.1 5.7 collective-permute-start.38
  585.0 8.9 %all-reduce.2 = (f32[192]{0:T(256)S(1)}, f32[192]{0:T(256)S(1)}) all-reduce(f32[192]{0:T(256)S(1)} %add_dynamic-update-slice_fusion, f32[192]{0:T(256)S(1)} %add_dynamic-update-slice_fusion.1), channel_id=1, replica_groups=mesh['seq'=8,'mlp'=4] {'mlp'}, use_global_device_ids=true, to_apply=%add.1 | all-reduce | flops 384 | bytes 3072
  600.7 9.1 %collective-permute-done.41 = bf16[192,3456]{1,0:T(8,128)(2,1)} collective-permute-done((bf16[192,3456]{1,0:T(8,128)(2,1)}, bf16[192,3456]{1,0:T(8,128)(2,1)}, u32[]{:S(2)}, u32[]{:S(2)}) %collective-permute-start.41) | collective-permute-done | bytes 1327136 | tf_op jit(solution)/shard_map/ppermute | solution.py:158
  616.4 26.8 %collective-permute-start.45 = (bf16[192,1728]{1,0:T(8,128)(2,1)S(1)}, bf16[192,1728]{1,0:T(8,128)(2,1)S(1)}, u32[]{:S(2)}, u32[]{:S(2)}) collective-permute-start(bf16[192,1728]{1,0:T(8,128)(2,1)S(1)} %pad_maximum_fusion.11), channel_id=1, source_target_pairs={{0,8},{4,12},{8,16},{12,20},{16,24},{20,28},{1,9},{5,13},{9,17},{1... | collective-permute-start | bytes 1990664 | tf_op jit(solution)/shard_map/ppermute | solution.py:158
  649.6 9.4 %collective-permute-done.45 = bf16[192,1728]{1,0:T(8,128)(2,1)S(1)} collective-permute-done((bf16[192,1728]{1,0:T(8,128)(2,1)S(1)}, bf16[192,1728]{1,0:T(8,128)(2,1)S(1)}, u32[]{:S(2)}, u32[]{:S(2)}) %collective-permute-start.45) | collective-permute-done | bytes 663584 | tf_op jit(solution)/shard_map/ppermute | solution.py:158
  665.7 26.8 %collective-permute-done.47 = bf16[192,1728]{1,0:T(8,128)(2,1)S(1)} collective-permute-done((bf16[192,1728]{1,0:T(8,128)(2,1)S(1)}, bf16[192,1728]{1,0:T(8,128)(2,1)S(1)}, u32[]{:S(2)}, u32[]{:S(2)}) %collective-permute-start.47) | collective-permute-done | bytes 663584 | tf_op jit(solution)/shard_map/ppermute | solution.py:158
  694.9 18.1 %collective-permute-done.48 = bf16[192,1728]{1,0:T(8,128)(2,1)S(1)} collective-permute-done((bf16[192,1728]{1,0:T(8,128)(2,1)S(1)}, bf16[192,1728]{1,0:T(8,128)(2,1)S(1)}, u32[]{:S(2)}, u32[]{:S(2)}) %collective-permute-start.48) | collective-permute-done | bytes 663584 | tf_op jit(solution)/shard_map/ppermute | solution.py:158
  721.9 9.3 %collective-permute-done.20 = bf16[192,1728]{1,0:T(8,128)(2,1)S(1)} collective-permute-done((bf16[192,1728]{1,0:T(8,128)(2,1)S(1)}, bf16[192,1728]{1,0:T(8,128)(2,1)S(1)}, u32[]{:S(2)}, u32[]{:S(2)}) %collective-permute-start.20) | collective-permute-done | bytes 663584 | tf_op jit(solution)/shard_map/ppermute | solution.py:158
  737.6 14.4 %collective-permute-done.22 = bf16[192,1728]{1,0:T(8,128)(2,1)S(1)} collective-permute-done((bf16[192,1728]{1,0:T(8,128)(2,1)S(1)}, bf16[192,1728]{1,0:T(8,128)(2,1)S(1)}, u32[]{:S(2)}, u32[]{:S(2)}) %collective-permute-start.22) | collective-permute-done | bytes 663584 | tf_op jit(solution)/shard_map/ppermute | solution.py:158
  753.7 11.7 %collective-permute-done.23 = bf16[192,1728]{1,0:T(8,128)(2,1)S(1)} collective-permute-done((bf16[192,1728]{1,0:T(8,128)(2,1)S(1)}, bf16[192,1728]{1,0:T(8,128)(2,1)S(1)}, u32[]{:S(2)}, u32[]{:S(2)}) %collective-permute-start.23) | collective-permute-done | bytes 663584 | tf_op jit(solution)/shard_map/ppermute | solution.py:158
  765.9 4.9 convolution_convert_fusion.4
  777.3 26.0 %reduce-scatter.7.cloned.1.call-done = bf16[192,1280]{1,0:T(8,128)(2,1)} async-done(((bf16[768,1280]{1,0:T(8,128)(2,1)}), bf16[192,1280]{1,0:T(8,128)(2,1)}) %reduce-scatter.7.cloned.1.call-update) | async-done | bytes 491536 | tf_op jit(solution)/shard_map/reduce_scatter | solution.py:306
  (293 shorter events, 180.4 us)
Async XLA Ops:
  7.2 148.5 %all-gather.5.cloned.1.call-start = ((), (), s32[]{:S(2)}) async-start(), calls=%async_computation.4 | async-start | bytes 17694720 | tf_op jit(solution)/shard_map/all_gather | solution.py:205
  10.3 196.2 %all-gather.7.cloned.1.call-start = ((), (), s32[]{:S(2)}) async-start(), calls=%async_computation.5 | async-start | bytes 3538944 | tf_op jit(solution)/shard_map/all_gather | solution.py:253
  169.8 180.9 %reduce-scatter.9.cloned.1.call-start = ((), (), s32[]{:S(2)}) async-start(), calls=%async_computation.9 | async-start | bytes 2457600 | tf_op jit(solution)/shard_map/reduce_scatter | solution.py:284
  169.8 101.6 %collective-permute-start.9 = (bf16[1024,640]{1,0:T(8,128)(2,1)}, bf16[1024,640]{1,0:T(8,128)(2,1)}, u32[]{:S(2)}, u32[]{:S(2)}) collective-permute-start(bf16[1024,640]{1,0:T(8,128)(2,1)} %param.22), channel_id=1, source_target_pairs={{0,4},{4,0},{8,12},{12,8},{16,20},{20,16},{24,28},{28,24},{1,5},{5... | collective-permute-start | bytes 3932168 | tf_op jit(solution)/shard_map/ppermute | solution.py:163
  282.0 77.6 %reduce-scatter.5.cloned.1.call-start = ((), (), s32[]{:S(2)}) async-start(), calls=%async_computation.6 | async-start | bytes 2457600 | tf_op jit(solution)/shard_map/reduce_scatter | solution.py:284
  327.3 69.4 %all-gather.11.cloned.1.call-start = ((), (), s32[]{:S(2)}) async-start(), calls=%async_computation.10 | async-start | bytes 2457600 | tf_op jit(solution)/shard_map/all_gather | solution.py:287
  362.4 79.9 %all-gather.9.cloned.1.call-start = ((), (), s32[]{:S(2)}) async-start(), calls=%async_computation.7 | async-start | bytes 2457600 | tf_op jit(solution)/shard_map/all_gather | solution.py:287
  363.7 122.6 %collective-permute-start.44 = (f32[48]{0:T(128)S(1)}, f32[48]{0:T(128)S(1)}, u32[]{:S(2)}, u32[]{:S(2)}) collective-permute-start(f32[48]{0:T(128)S(1)} %get-tuple-element.64), channel_id=1, source_target_pairs={{0,8},{4,12},{8,16},{12,20},{16,24},{20,28},{24,0},{28,4},{1,9},{5... | collective-permute-start | bytes 584 | tf_op jit(solution)/shard_map/ppermute | solution.py:158
  365.2 124.1 %collective-permute-start.43 = (f32[48]{0:T(128)S(1)}, f32[48]{0:T(128)S(1)}, u32[]{:S(2)}, u32[]{:S(2)}) collective-permute-start(f32[48]{0:T(128)S(1)} %get-tuple-element.65), channel_id=1, source_target_pairs={{0,16},{4,20},{8,24},{12,28},{16,0},{20,4},{24,8},{28,12},{1,17},{... | collective-permute-start | bytes 584 | tf_op jit(solution)/shard_map/ppermute | solution.py:158
  367.7 404.5 %reduce-scatter.11.cloned.1.call-start = ((), (), s32[]{:S(2)}) async-start(), calls=%async_computation.11 | async-start | bytes 2457600 | tf_op jit(solution)/shard_map/reduce_scatter | solution.py:306
  436.0 46.4 %collective-permute-start.36 = (bf16[192,3456]{1,0:T(8,128)(2,1)}, bf16[192,3456]{1,0:T(8,128)(2,1)}, u32[]{:S(2)}, u32[]{:S(2)}) collective-permute-start(bf16[192,3456]{1,0:T(8,128)(2,1)} %bitcast.68), channel_id=1, source_target_pairs={{0,8},{4,12},{1,9},{5,13},{2,10},{6,14},{3,11},{7,15}} | collective-permute-start | bytes 3981320 | tf_op jit(solution)/shard_map/ppermute | solution.py:158
  440.5 42.7 %collective-permute-start.39 = (bf16[192,3456]{1,0:T(8,128)(2,1)}, bf16[192,3456]{1,0:T(8,128)(2,1)}, u32[]{:S(2)}, u32[]{:S(2)}) collective-permute-start(bf16[192,3456]{1,0:T(8,128)(2,1)} %bitcast.66), channel_id=1, source_target_pairs={{24,16},{28,20},{25,17},{29,21},{26,18},{30,22},{27,19},{31,23}} | collective-permute-start | bytes 3981320 | tf_op jit(solution)/shard_map/ppermute | solution.py:158
  481.1 35.6 %collective-permute-start.11 = (bf16[192,3456]{1,0:T(8,128)(2,1)S(1)}, bf16[192,3456]{1,0:T(8,128)(2,1)S(1)}, u32[]{:S(2)}, u32[]{:S(2)}) collective-permute-start(bf16[192,3456]{1,0:T(8,128)(2,1)S(1)} %bitcast.149), channel_id=1, source_target_pairs={{0,8},{4,12},{1,9},{5,13},{2,10},{6,14},{3,11},{7,15}} | collective-permute-start | bytes 3981320 | tf_op jit(solution)/shard_map/ppermute | solution.py:158
  482.4 61.1 %collective-permute-start.14 = (bf16[192,3456]{1,0:T(8,128)(2,1)S(1)}, bf16[192,3456]{1,0:T(8,128)(2,1)S(1)}, u32[]{:S(2)}, u32[]{:S(2)}) collective-permute-start(bf16[192,3456]{1,0:T(8,128)(2,1)S(1)} %bitcast.148), channel_id=1, source_target_pairs={{24,16},{28,20},{25,17},{29,21},{26,18},{30,22},{27,19},{31,23}} | collective-permute-start | bytes 3981320 | tf_op jit(solution)/shard_map/ppermute | solution.py:158
  485.5 62.8 %collective-permute-start.40 = (bf16[192,3456]{1,0:T(8,128)(2,1)S(1)}, bf16[192,3456]{1,0:T(8,128)(2,1)S(1)}, u32[]{:S(2)}, u32[]{:S(2)}) collective-permute-start(bf16[192,3456]{1,0:T(8,128)(2,1)S(1)} %get-tuple-element.27), channel_id=1, source_target_pairs={{16,8},{20,12},{24,16},{28,20},{17,9},{21,13},{25,17},{29,21},{18,... | collective-permute-start | bytes 3981320 | tf_op jit(solution)/shard_map/ppermute | solution.py:158
  489.4 173.5 %collective-permute-start.26 = (bf16[1728,640]{1,0:T(8,128)(2,1)}, bf16[1728,640]{1,0:T(8,128)(2,1)}, u32[]{:S(2)}, u32[]{:S(2)}) collective-permute-start(bf16[1728,640]{1,0:T(8,128)(2,1)} %param.25), channel_id=1, source_target_pairs={{0,4},{4,0},{8,12},{12,8},{16,20},{20,16},{24,28},{28,24},{1,5},{5... | collective-permute-start | bytes 6635528 | tf_op jit(solution)/shard_map/ppermute | solution.py:163
  510.8 66.9 %collective-permute-start.19 = (f32[48]{0:T(128)S(1)}, f32[48]{0:T(128)S(1)}, u32[]{:S(2)}, u32[]{:S(2)}) collective-permute-start(f32[48]{0:T(128)S(1)} %get-tuple-element.61), channel_id=1, source_target_pairs={{0,8},{4,12},{8,16},{12,20},{16,24},{20,28},{24,0},{28,4},{1,9},{5... | collective-permute-start | bytes 584 | tf_op jit(solution)/shard_map/ppermute | solution.py:158
  516.7 62.4 %collective-permute-start.18 = (f32[48]{0:T(128)S(1)}, f32[48]{0:T(128)S(1)}, u32[]{:S(2)}, u32[]{:S(2)}) collective-permute-start(f32[48]{0:T(128)S(1)} %get-tuple-element.62), channel_id=1, source_target_pairs={{0,16},{4,20},{8,24},{12,28},{16,0},{20,4},{24,8},{28,12},{1,17},{... | collective-permute-start | bytes 584 | tf_op jit(solution)/shard_map/ppermute | solution.py:158
  543.6 29.7 %collective-permute-start.37 = (bf16[192,3456]{1,0:T(8,128)(2,1)S(1)}, bf16[192,3456]{1,0:T(8,128)(2,1)S(1)}, u32[]{:S(2)}, u32[]{:S(2)}) collective-permute-start(bf16[192,3456]{1,0:T(8,128)(2,1)S(1)} %get-tuple-element.26), channel_id=1, source_target_pairs={{0,8},{4,12},{8,16},{12,20},{1,9},{5,13},{9,17},{13,21},{2,10},{6,... | collective-permute-start | bytes 3981320 | tf_op jit(solution)/shard_map/ppermute | solution.py:158
  548.3 36.6 %collective-permute-start.17 = (f32[48]{0:T(128)S(1)}, f32[48]{0:T(128)S(1)}, u32[]{:S(2)}, u32[]{:S(2)}) collective-permute-start(f32[48]{0:T(128)S(1)} %get-tuple-element.60), channel_id=1, source_target_pairs={{0,24},{4,28},{8,0},{12,4},{16,8},{20,12},{24,16},{28,20},{1,25},{... | collective-permute-start | bytes 584 | tf_op jit(solution)/shard_map/ppermute | solution.py:158
  577.7 32.1 %collective-permute-start.41 = (bf16[192,3456]{1,0:T(8,128)(2,1)}, bf16[192,3456]{1,0:T(8,128)(2,1)}, u32[]{:S(2)}, u32[]{:S(2)}) collective-permute-start(bf16[192,3456]{1,0:T(8,128)(2,1)} %add_convert_fusion), channel_id=1, source_target_pairs={{8,0},{12,4},{16,8},{20,12},{24,16},{28,20},{9,1},{13,5},{17,9},{2... | collective-permute-start | bytes 3981320 | tf_op jit(solution)/shard_map/ppermute | solution.py:158
  579.1 34.5 %collective-permute-start.38 = (bf16[192,3456]{1,0:T(8,128)(2,1)}, bf16[192,3456]{1,0:T(8,128)(2,1)}, u32[]{:S(2)}, u32[]{:S(2)}) collective-permute-start(bf16[192,3456]{1,0:T(8,128)(2,1)} %add_convert_fusion.1), channel_id=1, source_target_pairs={{0,8},{4,12},{8,16},{12,20},{16,24},{20,28},{1,9},{5,13},{9,17},{1... | collective-permute-start | bytes 3981320 | tf_op jit(solution)/shard_map/ppermute | solution.py:158
  593.9 50.6 %collective-permute-start.12 = (bf16[192,3456]{1,0:T(8,128)(2,1)}, bf16[192,3456]{1,0:T(8,128)(2,1)S(1)}, u32[]{:S(2)}, u32[]{:S(2)}) collective-permute-start(bf16[192,3456]{1,0:T(8,128)(2,1)} %get-tuple-element.24), channel_id=1, source_target_pairs={{0,8},{4,12},{8,16},{12,20},{1,9},{5,13},{9,17},{13,21},{2,10},{6,... | collective-permute-start | bytes 3981320 | tf_op jit(solution)/shard_map/ppermute | solution.py:158
  599.4 94.3 %collective-permute-start.16 = (bf16[192,3456]{1,0:T(8,128)(2,1)S(1)}, bf16[192,3456]{1,0:T(8,128)(2,1)S(1)}, u32[]{:S(2)}, u32[]{:S(2)}) collective-permute-start(bf16[192,3456]{1,0:T(8,128)(2,1)S(1)} %add_convert_fusion.2), channel_id=1, source_target_pairs={{8,0},{12,4},{16,8},{20,12},{24,16},{28,20},{9,1},{13,5},{17,9},{2... | collective-permute-start | bytes 3981320 | tf_op jit(solution)/shard_map/ppermute | solution.py:158
  616.4 42.6 %collective-permute-start.45 = (bf16[192,1728]{1,0:T(8,128)(2,1)S(1)}, bf16[192,1728]{1,0:T(8,128)(2,1)S(1)}, u32[]{:S(2)}, u32[]{:S(2)}) collective-permute-start(bf16[192,1728]{1,0:T(8,128)(2,1)S(1)} %pad_maximum_fusion.11), channel_id=1, source_target_pairs={{0,8},{4,12},{8,16},{12,20},{16,24},{20,28},{1,9},{5,13},{9,17},{1... | collective-permute-start | bytes 1990664 | tf_op jit(solution)/shard_map/ppermute | solution.py:158
  645.0 48.8 %collective-permute-start.13 = (bf16[192,3456]{1,0:T(8,128)(2,1)S(1)}, bf16[192,3456]{1,0:T(8,128)(2,1)S(1)}, u32[]{:S(2)}, u32[]{:S(2)}) collective-permute-start(bf16[192,3456]{1,0:T(8,128)(2,1)S(1)} %add_convert_fusion.3), channel_id=1, source_target_pairs={{0,8},{4,12},{8,16},{12,20},{16,24},{20,28},{1,9},{5,13},{9,17},{1... | collective-permute-start | bytes 3981320 | tf_op jit(solution)/shard_map/ppermute | solution.py:158
  659.7 32.8 %collective-permute-start.47 = (bf16[192,1728]{1,0:T(8,128)(2,1)S(1)}, bf16[192,1728]{1,0:T(8,128)(2,1)S(1)}, u32[]{:S(2)}, u32[]{:S(2)}) collective-permute-start(bf16[192,1728]{1,0:T(8,128)(2,1)S(1)} %collective-permute-done.46), channel_id=1, source_target_pairs={{8,0},{12,4},{16,8},{20,12},{9,1},{13,5},{17,9},{21,13},{10,2},{14... | collective-permute-start | bytes 1990664 | tf_op jit(solution)/shard_map/ppermute | solution.py:158
  665.0 29.8 %collective-permute-start.50 = (bf16[192,1728]{1,0:T(8,128)(2,1)S(1)}, bf16[192,1728]{1,0:T(8,128)(2,1)S(1)}, u32[]{:S(2)}, u32[]{:S(2)}) collective-permute-start(bf16[192,1728]{1,0:T(8,128)(2,1)S(1)} %collective-permute-done.49), channel_id=1, source_target_pairs={{16,24},{20,28},{17,25},{21,29},{18,26},{22,30},{19,27},{23,31}} | collective-permute-start | bytes 1990664 | tf_op jit(solution)/shard_map/ppermute | solution.py:158
  718.4 84.9 %reduce-scatter.7.cloned.1.call-start = ((), (), s32[]{:S(2)}) async-start(), calls=%async_computation.8 | async-start | bytes 2457600 | tf_op jit(solution)/shard_map/reduce_scatter | solution.py:306
  773.4 35.1 %collective-permute-start.53 = (bf16[48,1280]{1,0:T(8,128)(2,1)S(1)}, bf16[48,1280]{1,0:T(8,128)(2,1)S(1)}, u32[]{:S(2)}, u32[]{:S(2)}) collective-permute-start(bf16[48,1280]{1,0:T(8,128)(2,1)S(1)} %get-tuple-element.47), channel_id=1, source_target_pairs={{0,8},{4,12},{8,16},{12,20},{16,24},{20,28},{24,0},{28,4},{1,9},{5... | collective-permute-start | bytes 368648 | tf_op jit(solution)/shard_map/ppermute | solution.py:158
  773.5 38.2 %collective-permute-start.52 = (bf16[48,1280]{1,0:T(8,128)(2,1)S(1)}, bf16[48,1280]{1,0:T(8,128)(2,1)S(1)}, u32[]{:S(2)}, u32[]{:S(2)}) collective-permute-start(bf16[48,1280]{1,0:T(8,128)(2,1)S(1)} %get-tuple-element.48), channel_id=1, source_target_pairs={{0,16},{4,20},{8,24},{12,28},{16,0},{20,4},{24,8},{28,12},{1,17},{... | collective-permute-start | bytes 368648 | tf_op jit(solution)/shard_map/ppermute | solution.py:158
  775.6 36.2 %collective-permute-start.51 = (bf16[48,1280]{1,0:T(8,128)(2,1)S(1)}, bf16[48,1280]{1,0:T(8,128)(2,1)S(1)}, u32[]{:S(2)}, u32[]{:S(2)}) collective-permute-start(bf16[48,1280]{1,0:T(8,128)(2,1)S(1)} %get-tuple-element.49), channel_id=1, source_target_pairs={{0,24},{4,28},{8,0},{12,4},{16,8},{20,12},{24,16},{28,20},{1,25},{... | collective-permute-start | bytes 368648 | tf_op jit(solution)/shard_map/ppermute | solution.py:158
  (54 other events, 665.6 us)
Sparse Core Ops, SparseCore 0:
  10.4 145.2 all-gather.4
  169.9 36.5 all-gather.6
  282.1 32.2 reduce-scatter.8
  327.4 32.2 reduce-scatter.4
  362.5 34.1 all-gather.10
  398.4 34.2 all-gather.8
  718.5 33.5 reduce-scatter.10
  770.9 32.2 reduce-scatter.6

commit v2 on v1

--- a/solution.py
+++ b/solution.py
@@ -153,6 +153,7 @@
     sub = share // chunks
     crows = mlp_count * sub
     piece_len = rows // PIECES_DEV
+    bits = mlp_count.bit_length() - 1
 
     def move(x, pairs):
         return lax.ppermute(
@@ -164,45 +165,120 @@
             x, "seq", [(a * CORES + e, a * CORES + 1 - e) for a in range(planes) for e in range(CORES)]
         )
 
+    def partner(x, bit):
+        return lax.ppermute(x, "mlp", [(a, a ^ bit) for a in range(mlp_count)])
+
+    def after(x, dep):
+        return lax.optimization_barrier((x, dep))
+
+    def add(a, b):
+        return (a.astype(F32) + b.astype(F32)).astype(BF16)
+
+    def gather_step(state, t):
+        ups, downs = state
+        ups.append(move(ups[-1], [(i, i + 1) for i in range(t - 1, planes - 1)]))
+        downs.append(move(downs[-1], [(i, i - 1) for i in range(1, planes - t + 1)]))
+
+    def gather_slots(state):
+        ups, downs = state
+        return [ups[0]] + [ups[k] + downs[planes - k] for k in range(1, planes)]
+
     def line_gather(x):
-        ups, downs = [x], [x]
+        state = ([x], [x])
         for t in range(1, planes):
-            ups.append(move(ups[-1], [(i, i + 1) for i in range(t - 1, planes - 1)]))
-            downs.append(move(downs[-1], [(i, i - 1) for i in range(1, planes - t + 1)]))
-        return [x] + [ups[k] + downs[planes - k] for k in range(1, planes)]
-
-    def line_scatter(parts):
-        up = down = None
-        for t in range(1, planes):
-            send_up, send_down = parts[t], parts[planes - t]
-            if up is not None:
-                send_up = (send_up.astype(F32) + up.astype(F32)).astype(BF16)
-                send_down = (send_down.astype(F32) + down.astype(F32)).astype(BF16)
-            up = move(send_up, [(i, i + 1) for i in range(0, min(t, planes - 1))])
-            down = move(send_down, [(i, i - 1) for i in range(max(1, planes - t), planes)])
-        return parts[0].astype(F32) + up.astype(F32) + down.astype(F32)
+            gather_step(state, t)
+        return gather_slots(state)
+
+    def scatter_step(parts, carried, t):
+        send_up, send_down = parts[t], parts[planes - t]
+        if carried is not None:
+            send_up, send_down = add(send_up, carried[0]), add(send_down, carried[1])
+        up = move(send_up, [(i, i + 1) for i in range(0, min(t, planes - 1))])
+        down = move(send_down, [(i, i - 1) for i in range(max(1, planes - t), planes)])
+        return (up, down)
+
+    half = max(1, planes // 2)
+    orders = [list(range(bits)), [(b + bits // 2) % bits for b in range(bits)]]
+
+    def mlp_scatter(x):
+        out = []
+        for part, order in zip((x[:half], x[half:]), orders):
+            slots = {j: part[:, j] for j in range(mlp_count)}
+            for b in order:
+                bit = 1 << b
+                sent = [j for j in sorted(slots) if j & bit]
+                got = partner(jnp.stack([slots[j].astype(BF16) for j in sent], axis=0), bit)
+                slots = {
+                    j ^ bit: slots[j ^ bit].astype(F32) + got[i].astype(F32)
+                    for i, j in enumerate(sent)
+                }
+            out.append(slots[0])
+        return jnp.concatenate(out, axis=0)
+
+    def mlp_gather(x):
+        out = []
+        for part, order in zip((x[:half], x[half:]), orders):
+            slots = {0: part}
+            for b in reversed(order):
+                bit = 1 << b
+                have = sorted(slots)
+                got = partner(jnp.stack([slots[j] for j in have], axis=0), bit)
+                for i, j in enumerate(have):
+                    slots[j | bit] = got[i]
+            out.append(jnp.stack([slots[j] for j in range(mlp_count)], axis=1))
+        return jnp.concatenate(out, axis=0)
 
     def swap_halves(x):
         return jnp.where(core == 0, x, jnp.concatenate([x[..., ds:], x[..., :ds]], axis=-1))
 
     kv_cols = max(HD, KVH * HD // mlp_count)
     kv_first = mlp_rank * KVH // mlp_count * HD
-    qkv_weight = jnp.concatenate(
+    kv_weight = jnp.concatenate(
         [
             lax.dynamic_slice_in_dim(key_weight, kv_first, kv_cols, 1),
             lax.dynamic_slice_in_dim(value_weight, kv_first, kv_cols, 1),
-            query_weight,
         ],
         axis=1,
     )
-    qkv_bias = jnp.concatenate(
+    kv_bias = jnp.concatenate(
         [
             lax.dynamic_slice_in_dim(key_bias, kv_first, kv_cols, 0),
             lax.dynamic_slice_in_dim(value_bias, kv_first, kv_cols, 0),
-            query_bias,
         ]
     ).astype(F32)
-    qkv_weight = lax.all_gather(qkv_weight, "seq", axis=0, tiled=True)
+    kv_state = ([kv_weight], [kv_weight])
+    for t in range(1, planes - 1):
+        gather_step(kv_state, t)
+    query_weight, (kv_state[0][-1], kv_state[1][-1]) = after(
+        query_weight, (kv_state[0][-1], kv_state[1][-1])
+    )
+    gather_step(kv_state, planes - 1)
+    q_state = ([query_weight], [query_weight])
+    for t in range(1, planes):
+        gather_step(q_state, t)
+
+    relative = [mlp_rank ^ j for j in range(mlp_count)]
+
+    def regroup(x):
+        parts = x.reshape((mlp_count, share) + x.shape[1:])
+        parts = jnp.stack([lax.dynamic_index_in_dim(parts, r, 0, False) for r in relative], axis=0)
+        parts = parts.reshape((mlp_count, chunks, sub) + x.shape[1:])
+        return jnp.swapaxes(parts, 0, 1).reshape(x.shape)
+
+    def ungroup(x):
+        parts = jnp.swapaxes(x.reshape((chunks, mlp_count, sub) + x.shape[1:]), 0, 1)
+        parts = jnp.stack([lax.dynamic_index_in_dim(parts, r, 0, False) for r in relative], axis=0)
+        return parts.reshape(x.shape)
+
+    x = regroup(layer_input).astype(F32)
+    mean_sq = jnp.mean(x * x, axis=-1, keepdims=True)
+    normed = (x * lax.rsqrt(mean_sq + norm_eps) * attention_gain.astype(F32)).astype(BF16)
+    even = jnp.concatenate([normed[:, CORES * z * ds : (CORES * z + 1) * ds] for z in range(planes)], axis=1)
+    odd = jnp.concatenate([normed[:, (CORES * z + 1) * ds : CORES * (z + 1) * ds] for z in range(planes)], axis=1)
+    mine = jnp.where(core == 0, even, odd)
+    theirs = sibling(jnp.where(core == 0, odd, even))
+    both = jnp.concatenate([mine, theirs], axis=0)
+    lanes = [lax.dynamic_slice_in_dim(both, (plane - k) % planes * ds, ds, 1) for k in range(planes)]
 
     units = gate_weight.shape[1]
     whole = units // HD * HD
@@ -210,15 +286,10 @@
         [gate_weight[:, :whole], up_weight[:, :whole], gate_weight[:, whole:], up_weight[:, whole:]],
         axis=1,
     )
+    glu_own = lax.optimization_barrier(glu_own)
     glu_weight = jnp.concatenate([glu_own, sibling(glu_own)], axis=0)
     out_wide = jnp.concatenate([out_weight, sibling(out_weight)], axis=1)
     down_wide = jnp.concatenate([down_weight, sibling(down_weight)], axis=1)
-
-    def regroup(x):
-        return jnp.swapaxes(x.reshape((mlp_count, chunks, sub) + x.shape[1:]), 0, 1).reshape(x.shape)
-
-    def ungroup(x):
-        return jnp.swapaxes(x.reshape((chunks, mlp_count, sub) + x.shape[1:]), 0, 1).reshape(x.shape)
 
     own_share = lax.dynamic_slice_in_dim(layer_input, mlp_rank * share, share, 0)
     lane_parts = []
@@ -230,6 +301,9 @@
     lane_input = swap_halves(jnp.stack(lane_parts, axis=0))
     lane_input = lane_input.reshape(planes, chunks, sub, dz)
     gain_lane = swap_halves(lax.dynamic_slice_in_dim(feedforward_gain, plane * dz, dz, 0)).astype(F32)
+    lanes, glu_weight, out_wide, down_wide, lane_input = lax.optimization_barrier(
+        (lanes, glu_weight, out_wide, down_wide, lane_input)
+    )
 
     row_ids = seq_rank * rows + regroup(jnp.arange(rows, dtype=jnp.int32))
     stream = lookup(piece_order, row_ids // piece_len) * piece_len + row_ids % piece_len
@@ -238,19 +312,27 @@
     doc_first = lookup(doc_ends - doc_lengths, segment)
     cosine, sine_part = rope_tables(stream - doc_first, HD)
 
-    x = regroup(layer_input).astype(F32)
-    mean_sq = jnp.mean(x * x, axis=-1, keepdims=True)
-    normed = (x * lax.rsqrt(mean_sq + norm_eps) * attention_gain.astype(F32)).astype(BF16)
-    qkv = jnp.dot(normed, qkv_weight, preferred_element_type=F32) + qkv_bias
+    def project(state, bias):
+        total = None
+        for lane, weight in zip(lanes, gather_slots(state)):
+            part = jnp.dot(lane, lax.optimization_barrier(weight), preferred_element_type=F32)
+            total = part if total is None else total + part
+        return total[:rows] + sibling(total[rows:]) + bias
+
     kv_heads = kv_cols // HD
     query_heads = query_weight.shape[1] // HD
-    key_rot = rotate(qkv[:, :kv_cols], cosine, sine_part, kv_heads).astype(BF16)
-    value_b = qkv[:, kv_cols : 2 * kv_cols].astype(BF16)
-    query_rot = rotate(qkv[:, 2 * kv_cols :], cosine, sine_part, query_heads).astype(BF16)
+    kv = project(kv_state, kv_bias)
+    key_rot = rotate(kv[:, :kv_cols], cosine, sine_part, kv_heads).astype(BF16)
+    value_b = kv[:, kv_cols:].astype(BF16)
     joined = jnp.stack(
         [key_rot.reshape(rows, kv_heads, HD), value_b.reshape(rows, kv_heads, HD)], axis=2
     ).reshape(rows, 2 * kv_cols)
-    kv_rows = lax.all_gather(ungroup(joined), "seq", axis=0, tiled=True)
+    core_rows = jnp.concatenate(line_gather(ungroup(joined)), axis=0)
+    kv_rows = jnp.concatenate([core_rows, sibling(core_rows)], axis=0)
+    offsets = (plane - jnp.arange(planes, dtype=jnp.int32)) % planes
+    slots = jnp.concatenate([offsets * CORES + core, offsets * CORES + 1 - core])
+    slots = (slots[:, None] * PIECES_DEV + jnp.arange(PIECES_DEV, dtype=jnp.int32)).reshape(-1)
+    piece_stream = lookup(piece_order, slots)
 
     own_cols = KVH * HD // mlp_count
     cache_width = 2 * own_cols
@@ -259,41 +341,72 @@
     pages = []
     for p in range(PIECES_DEV):
         stream_piece = jnp.sum(jnp.where(cache_page == seq_rank * PIECES_DEV + p, pieces, 0))
-        source = jnp.sum(jnp.where(piece_order == stream_piece, pieces, 0))
+        source = jnp.sum(jnp.where(piece_stream == stream_piece, pieces, 0))
         pages.append(lax.dynamic_slice(kv_rows, (source * piece_len, offset), (piece_len, cache_width)))
     kv_cache = jnp.concatenate(pages, axis=0)
 
+    query = project(q_state, query_bias.astype(F32))
+    query_rot = rotate(query, cosine, sine_part, query_heads).astype(BF16)
     mixed = attend(
         query_rot.reshape(chunks, crows, query_heads * HD),
         kv_rows,
         doc_first.reshape(chunks, crows),
         stream.reshape(chunks, crows),
-        piece_order,
+        piece_stream,
         kv_heads,
     )
 
-    def by_share(slots):
-        return jnp.stack([v.reshape(mlp_count, sub, -1) for v in slots], axis=1).reshape(
-            mlp_count * planes * sub, -1
-        )
-
-    finals = []
+    mixed_states = []
+    dep = None
     for h in range(chunks):
-        heads = by_share(line_gather(mixed[h]))
+        first = mixed[h]
+        if dep is not None:
+            first, dep = after(first, dep)
+            mixed_states[-1][0][-1], mixed_states[-1][1][-1] = dep
+            gather_step(mixed_states[-1], planes - 1)
+        state = ([first], [first])
+        for t in range(1, planes - 1):
+            gather_step(state, t)
+        dep = (state[0][-1], state[1][-1])
+        mixed_states.append(state)
+    gather_step(mixed_states[-1], planes - 1)
+
+    residuals, scales, parts = [], [], []
+    for h in range(chunks):
+        heads = jnp.concatenate(gather_slots(mixed_states[h]), axis=0)
         attn = jnp.dot(heads, out_wide, preferred_element_type=F32).astype(BF16)
-        attn = lax.psum_scatter(attn, "mlp", scatter_dimension=0, tiled=True)
-        residual = lane_input[:, h].astype(F32).reshape(planes * sub, dz) + attn.astype(F32)
-        square = jnp.sum(residual * residual, axis=-1).reshape(planes, sub)
-        lane = lax.all_gather((residual * gain_lane).astype(BF16), "mlp", axis=0, tiled=True)
+        attn = mlp_scatter(attn.reshape(planes, mlp_count, sub, dz))
+        residual = lane_input[:, h].astype(F32) + attn
+        square = jnp.sum(residual * residual, axis=-1)
+        lane = mlp_gather((residual * gain_lane).astype(BF16))
         square = sum(
             [square[0]]
             + [move(square[k], [(i, (i - k) % planes) for i in range(planes)]) for k in range(1, planes)]
         )
-        square = lax.all_gather(square, "mlp", axis=0, tiled=True)
-        scale = lax.rsqrt(square / width + norm_eps)[:, None]
-        part = jnp.dot(lane, glu_weight, preferred_element_type=F32).astype(BF16)
-        part = part.reshape(mlp_count, planes, sub, 2 * units)
-        act = line_scatter([part[:, k].reshape(crows, 2 * units) for k in range(planes)]) * scale
+        found = {0: square}
+        for b in range(bits):
+            bit = 1 << b
+            have = sorted(found)
+            got = partner(jnp.stack([found[j] for j in have], axis=0), bit)
+            for i, j in enumerate(have):
+                found[j | bit] = got[i]
+        square = jnp.stack([found[j] for j in range(mlp_count)], axis=0).reshape(crows, 1)
+        scales.append(lax.rsqrt(square / width + norm_eps))
+        part = jnp.dot(lane.reshape(planes * crows, dz), glu_weight, preferred_element_type=F32)
+        parts.append(part.astype(BF16).reshape(planes, crows, 2 * units))
+        residuals.append(residual)
+
+    carried = [None] * chunks
+    for h in range(chunks):
+        for t in range(1, planes):
+            if t == planes - 1 and h + 1 < chunks:
+                parts[h + 1], carried[h] = after(parts[h + 1], carried[h])
+            carried[h] = scatter_step(parts[h], carried[h], t)
+
+    finals = []
+    for h in range(chunks):
+        act = parts[h][0].astype(F32) + carried[h][0].astype(F32) + carried[h][1].astype(F32)
+        act = act * scales[h]
         hidden = jax.nn.silu(act[:, :whole]) * act[:, whole : 2 * whole]
         if units > whole:
             last = act[:, 2 * whole :]
@@ -301,10 +414,10 @@
             hidden = jnp.concatenate(
                 [hidden, jax.nn.silu(last[:, :edge]) * last[:, edge:]], axis=1
             )
-        hidden = by_share(line_gather(hidden.astype(BF16)))
+        hidden = jnp.concatenate(line_gather(hidden.astype(BF16)), axis=0)
         down = jnp.dot(hidden, down_wide, preferred_element_type=F32).astype(BF16)
-        down = lax.psum_scatter(down, "mlp", scatter_dimension=0, tiled=True)
-        final = (residual + down.astype(F32)).astype(BF16).reshape(planes, sub, dz)
+        down = mlp_scatter(down.reshape(planes, mlp_count, sub, dz))
+        final = (residuals[h] + down).astype(BF16)
         finals.append(
             jnp.stack(
                 [final[0]]

time: 828 us -> 753 us (0.909)
  waiting for transfers between devices: 435 us -> 310 us
  starting transfers between devices: 135 us -> 209 us
  other arithmetic: 58.7 us -> 120 us
  matrix products: 96.4 us -> 46.2 us
  Pallas kernels: 32 us -> 10.7 us
  between operations: 17.6 us -> 4.43 us
  blocking collectives: 8.9 us -> 0 us
    all_gather x4 -> x0, waiting for transfers between devices: 184 us -> none  [the longest x1 127 us: shards(): qkv_weight = lax.all_gather(qkv_weight, 'seq', axis=0, tiled=True)]
    dot_general x3 -> x10, matrix products: 79.7 us -> 29.9 us  [the longest x2 19.3 us: shards(): jnp.dot(lane.reshape(planes * crows, dz), glu_weight, preferred_element_t...]
    ppermute x0 -> x28, waiting for transfers between devices: none -> 49.8 us  [partner(): return lax.ppermute(x, 'mlp', [(a, a ^ bit) for a in range(mlp_count)])]
    ppermute x51 -> x69, waiting for transfers between devices: 216 us -> 260 us  [move(): lax.ppermute(x, 'seq', [(a * CORES + e, b * CORES + e) for a, b in pairs...]
    ppermute x0 -> x28, starting transfers between devices: none -> 36.8 us  [partner(): return lax.ppermute(x, 'mlp', [(a, a ^ bit) for a in range(mlp_count)])]
    ppermute x51 -> x69, starting transfers between devices: 135 us -> 171 us  [move(): lax.ppermute(x, 'seq', [(a * CORES + e, b * CORES + e) for a, b in pairs...]
    reduce_scatter x4 -> x0, waiting for transfers between devices: 35 us -> none  [the longest x2 26 us: shards(): down = lax.psum_scatter(down, 'mlp', scatter_dimension=0, tiled=True)]
    add x12 -> x29, other arithmetic: 1.8 us -> 31.2 us  [the longest x18 24.6 us: gather_slots(): return [ups[0]] + [ups[k] + downs[planes - k] for k in range(1, planes)]]
  transfers between devices with their start and end apart: 62 -> 104, of which waited for: 26 -> 47; matrix products, arithmetic and copies ran while one was open for 20% -> 26% of each run, Pallas kernels for 4% -> 0%
where the time goes in v2:
time: 753 us; the launch traced here: 747 us
  waiting for transfers between devices  310 us (41%)
  starting transfers between devices  209 us (28%)
  other arithmetic  120 us (16%)
  local copies, waits for them, and re-layouts  47.4 us (6%)
  matrix products  46.2 us (6%)
  Pallas kernels  10.7 us (1%)
    ppermute x69, waiting for transfers between devices, move(): lax.ppermute(x, 'seq', [(a * CORES + e, b * CORES + e) for a, b in pairs...  260 us
    ppermute x69, starting transfers between devices, move(): lax.ppermute(x, 'seq', [(a * CORES + e, b * CORES + e) for a, b in pairs...  171 us
    ppermute x28, waiting for transfers between devices, partner(): return lax.ppermute(x, 'mlp', [(a, a ^ bit) for a in range(mlp_count)])  49.8 us
    ppermute x28, starting transfers between devices, partner(): return lax.ppermute(x, 'mlp', [(a, a ^ bit) for a in range(mlp_count)])  36.8 us
    add x18, other arithmetic, gather_slots(): return [ups[0]] + [ups[k] + downs[planes - k] for k in range(1, planes)]  24.6 us
    dot_general x2, matrix products, shards(): jnp.dot(lane.reshape(planes * crows, dz), glu_weight, preferred_element_t...  19.3 us
  transfers between devices with their start and end apart: 104, of which 47 were waited for; matrix products, arithmetic and copies ran while one was open for 26% of the time, Pallas kernels for 0%

profile of v2, /device:TPU:0, one launch (start us, length us, event | category | flops | bytes accessed | tf_op | source)
XLA Modules:
  0.0 746.9 jit_solution(7937465253294643007)
XLA Ops:
  3.1 6.4 collective-permute-start.7
  15.8 14.5 %pad_maximum_fusion.1 = bf16[640,3456]{0,1:T(8,128)(2,1)} fusion(bf16[640,64]{0,1:T(8,128)(2,1)S(1)} %slice-done.6, bf16[640,64]{0,1:T(8,128)(2,1)S(1)} %slice-done.4, bf16[640,1664]{0,1:T(8,128)(2,1)S(1)} %slice-done.5, bf16[640,1664]{0,1:T(8,128)(2,1)S(1)} %slice-done.3), kind=kLoop, calls=%fused_computation.15 | loop fusion | flops 17694720 | bytes 8847360 | tf_op jit(solution)/shard_map/concatenate | solution.py:285
  37.6 7.2 copy.144
  63.0 23.5 %collective-permute-done.5 = bf16[96,1280]{1,0:T(8,128)(2,1)S(1)} collective-permute-done((bf16[96,1280]{1,0:T(8,128)(2,1)}, bf16[96,1280]{1,0:T(8,128)(2,1)S(1)}, u32[]{:S(2)}, u32[]{:S(2)}) %collective-permute-start.5) | collective-permute-done | bytes 245792 | tf_op jit(solution)/shard_map/ppermute | solution.py:159
  90.6 5.9 collective-permute-done.6
  101.2 13.3 %collective-permute-done.18 = bf16[640,512]{1,0:T(8,128)(2,1)} collective-permute-done((bf16[640,512]{1,0:T(8,128)(2,1)}, bf16[640,512]{1,0:T(8,128)(2,1)}, u32[]{:S(2)}, u32[]{:S(2)}) %collective-permute-start.18) | collective-permute-done | bytes 655392 | tf_op jit(solution)/shard_map/ppermute | solution.py:159
  148.5 7.6 %pad_maximum_fusion = bf16[1280,3456]{0,1:T(8,128)(2,1)} fusion(bf16[640,3456]{0,1:T(8,128)(2,1)} %collective-permute-done.1, bf16[640,3456]{0,1:T(8,128)(2,1)} %pad_maximum_fusion.1), kind=kLoop, calls=%fused_computation | loop fusion | flops 17694720 | bytes 17694720 | tf_op jit(solution)/shard_map/concatenate | solution.py:290
  162.6 13.0 %collective-permute-done.13 = bf16[640,1024]{1,0:T(8,128)(2,1)} collective-permute-done((bf16[640,1024]{1,0:T(8,128)(2,1)}, bf16[640,1024]{1,0:T(8,128)(2,1)}, u32[]{:S(2)}, u32[]{:S(2)}) %collective-permute-start.13) | collective-permute-done | bytes 1310752 | tf_op jit(solution)/shard_map/ppermute | solution.py:159
  186.5 6.2 collective-permute-start.21
  192.8 22.7 %collective-permute-done.22 = bf16[384,512]{1,0:T(8,128)(2,1)S(1)} collective-permute-done((bf16[384,512]{1,0:T(8,128)(2,1)S(1)}, bf16[384,512]{1,0:T(8,128)(2,1)S(1)}, u32[]{:S(2)}, u32[]{:S(2)}) %collective-permute-start.22) | collective-permute-done | bytes 393248 | tf_op jit(solution)/shard_map/ppermute | solution.py:159
  257.8 10.7 %shard_map.167 = bf16[2,192,1024]{2,1,0:T(8,128)(2,1)S(1)} custom-call(s32[2]{0:T(128)S(1)} %convert_reduce_fusion.1.count, s32[2,16]{1,0:T(2,128)S(1)} %select_reduce_fusion.1.active, s32[16]{0:T(128)S(1)} %select_reduce_fusion.2.piece_stream, bf16[2,192,1024]{2,1,0:T(8,128)(2,1)S(1)} %copy-done, ...), custom_call_target="tpu_custom_call" | custom-call | tf_op jit(solution)/shard_map/pallas_call | solution.py:103
  278.8 8.3 %collective-permute-done.30 = bf16[192,1024]{1,0:T(8,128)(2,1)S(1)} collective-permute-done((bf16[192,1024]{1,0:T(8,128)(2,1)S(1)}, bf16[192,1024]{1,0:T(8,128)(2,1)S(1)}, u32[]{:S(2)}, u32[]{:S(2)}) %collective-permute-start.30) | collective-permute-done | bytes 393248 | tf_op jit(solution)/shard_map/ppermute | solution.py:159
  289.2 12.5 %collective-permute-done.31 = bf16[192,1024]{1,0:T(8,128)(2,1)} collective-permute-done((bf16[192,1024]{1,0:T(8,128)(2,1)S(1)}, bf16[192,1024]{1,0:T(8,128)(2,1)}, u32[]{:S(2)}, u32[]{:S(2)}) %collective-permute-start.31) | collective-permute-done | bytes 393248 | tf_op jit(solution)/shard_map/ppermute | solution.py:159
  307.1 6.0 collective-permute-start.42
  325.6 7.8 %collective-permute-done.44 = bf16[192,1024]{1,0:T(8,128)(2,1)S(1)} collective-permute-done((bf16[192,1024]{1,0:T(8,128)(2,1)S(1)}, bf16[192,1024]{1,0:T(8,128)(2,1)S(1)}, u32[]{:S(2)}, u32[]{:S(2)}) %collective-permute-start.44) | collective-permute-done | bytes 393248 | tf_op jit(solution)/shard_map/ppermute | solution.py:159
  359.9 7.3 collective-permute-done.48
  369.8 8.0 %collective-permute-done.39 = bf16[2,2,48,1280]{3,2,1,0:T(8,128)(2,1)S(1)} collective-permute-done((bf16[2,2,48,1280]{3,2,1,0:T(8,128)(2,1)S(1)}, bf16[2,2,48,1280]{3,2,1,0:T(8,128)(2,1)S(1)}, u32[]{:S(2)}, u32[]{:S(2)}) %collective-permute-start.39) | collective-permute-done | bytes 491552 | tf_op jit(solution)/shard_map/ppermute | solution.py:169
  388.2 8.7 %convolution_convert_fusion.1 = bf16[768,3456]{1,0:T(8,128)(2,1)S(1)} fusion(bf16[768,1280]{1,0:T(8,128)(2,1)} %bitcast.489, bf16[1280,3456]{0,1:T(8,128)(2,1)S(1)} %bitcast.454), kind=kOutput, calls=%fused_computation.6 | convolution fusion | flops 6797426688 | bytes 16121856 | tf_op jit(solution)/shard_map/dot_general | solution.py:395
  416.7 16.8 %collective-permute-done.56 = bf16[192,3456]{1,0:T(8,128)(2,1)S(1)} collective-permute-done((bf16[192,3456]{1,0:T(8,128)(2,1)S(1)}, bf16[192,3456]{1,0:T(8,128)(2,1)S(1)}, u32[]{:S(2)}, u32[]{:S(2)}) %collective-permute-start.56) | collective-permute-done | bytes 1327136 | tf_op jit(solution)/shard_map/ppermute | solution.py:159
  443.1 10.6 %convolution_convert_fusion = bf16[768,3456]{1,0:T(8,128)(2,1)} fusion(bf16[768,1280]{1,0:T(8,128)(2,1)} %bitcast.490, bf16[1280,3456]{0,1:T(8,128)(2,1)S(1)} %bitcast.454), kind=kOutput, calls=%fused_computation.5 | convolution fusion | flops 6797426688 | bytes 16121856 | tf_op jit(solution)/shard_map/dot_general | solution.py:395
  453.7 13.7 %collective-permute-done.57 = bf16[192,3456]{1,0:T(8,128)(2,1)} collective-permute-done((bf16[192,3456]{1,0:T(8,128)(2,1)}, bf16[192,3456]{1,0:T(8,128)(2,1)}, u32[]{:S(2)}, u32[]{:S(2)}) %collective-permute-start.57) | collective-permute-done | bytes 1327136 | tf_op jit(solution)/shard_map/ppermute | solution.py:159
  471.4 15.1 %collective-permute-start.60 = (bf16[192,3456]{1,0:T(8,128)(2,1)}, bf16[192,3456]{1,0:T(8,128)(2,1)}, u32[]{:S(2)}, u32[]{:S(2)}) collective-permute-start(bf16[192,3456]{1,0:T(8,128)(2,1)} %get-tuple-element.46), channel_id=1, source_target_pairs={{0,8},{4,12},{8,16},{12,20},{16,24},{20,28},{1,9},{5,13},{9,17},{1... | collective-permute-start | bytes 3981320 | tf_op jit(solution)/shard_map/ppermute | solution.py:159
  503.8 11.2 %collective-permute-done.60 = bf16[192,3456]{1,0:T(8,128)(2,1)} collective-permute-done((bf16[192,3456]{1,0:T(8,128)(2,1)}, bf16[192,3456]{1,0:T(8,128)(2,1)}, u32[]{:S(2)}, u32[]{:S(2)}) %collective-permute-start.60) | collective-permute-done | bytes 1327136 | tf_op jit(solution)/shard_map/ppermute | solution.py:159
  531.3 11.9 %collective-permute-done.80 = bf16[192,3456]{1,0:T(8,128)(2,1)S(1)} collective-permute-done((bf16[192,3456]{1,0:T(8,128)(2,1)S(1)}, bf16[192,3456]{1,0:T(8,128)(2,1)S(1)}, u32[]{:S(2)}, u32[]{:S(2)}) %collective-permute-start.80) | collective-permute-done | bytes 1327136 | tf_op jit(solution)/shard_map/ppermute | solution.py:159
  562.9 23.6 %collective-permute-done.86 = f32[48]{0:T(128)S(1)} collective-permute-done((f32[48]{0:T(128)S(1)}, f32[48]{0:T(128)S(1)}, u32[]{:S(2)}, u32[]{:S(2)}) %collective-permute-start.86) | collective-permute-done | bytes 224 | tf_op jit(solution)/shard_map/ppermute | solution.py:159
  586.5 13.3 %collective-permute-start.87 = (f32[48]{0:T(128)S(1)}, f32[48]{0:T(128)S(1)}, u32[]{:S(2)}, u32[]{:S(2)}) collective-permute-start(f32[48]{0:T(128)S(1)} %get-tuple-element.157), channel_id=1, source_target_pairs={{0,16},{4,20},{8,24},{12,28},{16,0},{20,4},{24,8},{28,12},{1,17},{... | collective-permute-start | bytes 584 | tf_op jit(solution)/shard_map/ppermute | solution.py:159
  627.8 7.2 collective-permute-done.70
  637.6 6.0 convolution_convert_fusion.3
  648.0 9.9 %collective-permute-done.85 = bf16[192,3456]{1,0:T(8,128)(2,1)S(1)} collective-permute-done((bf16[192,3456]{1,0:T(8,128)(2,1)S(1)}, bf16[192,3456]{1,0:T(8,128)(2,1)S(1)}, u32[]{:S(2)}, u32[]{:S(2)}) %collective-permute-start.85) | collective-permute-done | bytes 1327136 | tf_op jit(solution)/shard_map/ppermute | solution.py:159
  683.3 10.1 %collective-permute-done.93 = bf16[192,1728]{1,0:T(8,128)(2,1)S(1)} collective-permute-done((bf16[192,1728]{1,0:T(8,128)(2,1)}, bf16[192,1728]{1,0:T(8,128)(2,1)S(1)}, u32[]{:S(2)}, u32[]{:S(2)}) %collective-permute-start.93) | collective-permute-done | bytes 663584 | tf_op jit(solution)/shard_map/ppermute | solution.py:159
  696.8 9.3 %collective-permute-done.94 = bf16[192,1728]{1,0:T(8,128)(2,1)S(1)} collective-permute-done((bf16[192,1728]{1,0:T(8,128)(2,1)S(1)}, bf16[192,1728]{1,0:T(8,128)(2,1)S(1)}, u32[]{:S(2)}, u32[]{:S(2)}) %collective-permute-start.94) | collective-permute-done | bytes 663584 | tf_op jit(solution)/shard_map/ppermute | solution.py:159
  708.7 6.0 convolution_convert_fusion.2
  (505 shorter events, 388.1 us)
Async XLA Ops:
  1.8 53.6 %collective-permute-start.9 = (bf16[640,512]{1,0:T(8,128)(2,1)S(1)}, bf16[640,512]{1,0:T(8,128)(2,1)}, u32[]{:S(2)}, u32[]{:S(2)}) collective-permute-start(bf16[640,512]{1,0:T(8,128)(2,1)S(1)} %pad_maximum_fusion.11), channel_id=1, source_target_pairs={{8,0},{12,4},{16,8},{20,12},{24,16},{28,20},{9,1},{13,5},{17,9},{2... | collective-permute-start | bytes 1966088 | tf_op jit(solution)/shard_map/ppermute | solution.py:159
  3.1 59.2 %collective-permute-start.7 = (bf16[640,512]{1,0:T(8,128)(2,1)S(1)}, bf16[640,512]{1,0:T(8,128)(2,1)}, u32[]{:S(2)}, u32[]{:S(2)}) collective-permute-start(bf16[640,512]{1,0:T(8,128)(2,1)S(1)} %pad_maximum_fusion.11), channel_id=1, source_target_pairs={{0,8},{4,12},{8,16},{12,20},{16,24},{20,28},{1,9},{5,13},{9,17},{1... | collective-permute-start | bytes 1966088 | tf_op jit(solution)/shard_map/ppermute | solution.py:159
  12.2 44.7 %collective-permute-start.4 = (bf16[96,1280]{1,0:T(8,128)(2,1)}, bf16[96,1280]{1,0:T(8,128)(2,1)}, u32[]{:S(2)}, u32[]{:S(2)}) collective-permute-start(bf16[96,1280]{1,0:T(8,128)(2,1)} %get-tuple-element.59), channel_id=1, source_target_pairs={{0,8},{4,12},{8,16},{12,20},{16,24},{20,28},{24,0},{28,4},{1,9},{5... | collective-permute-start | bytes 737288 | tf_op jit(solution)/shard_map/ppermute | solution.py:159
  30.3 118.3 %collective-permute-start.1 = (bf16[640,3456]{0,1:T(8,128)(2,1)}, bf16[640,3456]{0,1:T(8,128)(2,1)}, u32[]{:S(2)}, u32[]{:S(2)}) collective-permute-start(bf16[640,3456]{0,1:T(8,128)(2,1)} %pad_maximum_fusion.1), channel_id=1, source_target_pairs={{0,4},{4,0},{8,12},{12,8},{16,20},{20,16},{24,28},{28,24},{1,5},{5... | collective-permute-start | bytes 13271048 | tf_op jit(solution)/shard_map/ppermute | solution.py:164
  30.3 67.5 %collective-permute-start.2 = (bf16[1024,640]{1,0:T(8,128)(2,1)}, bf16[1024,640]{1,0:T(8,128)(2,1)}, u32[]{:S(2)}, u32[]{:S(2)}) collective-permute-start(bf16[1024,640]{1,0:T(8,128)(2,1)} %param.22), channel_id=1, source_target_pairs={{0,4},{4,0},{8,12},{12,8},{16,20},{20,16},{24,28},{28,24},{1,5},{5... | collective-permute-start | bytes 3932168 | tf_op jit(solution)/shard_map/ppermute | solution.py:164
  55.4 31.1 %collective-permute-start.10 = (bf16[640,512]{1,0:T(8,128)(2,1)}, bf16[640,512]{1,0:T(8,128)(2,1)}, u32[]{:S(2)}, u32[]{:S(2)}) collective-permute-start(bf16[640,512]{1,0:T(8,128)(2,1)} %collective-permute-done.9), channel_id=1, source_target_pairs={{8,0},{12,4},{16,8},{20,12},{9,1},{13,5},{17,9},{21,13},{10,2},{14... | collective-permute-start | bytes 1966088 | tf_op jit(solution)/shard_map/ppermute | solution.py:159
  56.8 29.7 %collective-permute-start.5 = (bf16[96,1280]{1,0:T(8,128)(2,1)}, bf16[96,1280]{1,0:T(8,128)(2,1)S(1)}, u32[]{:S(2)}, u32[]{:S(2)}) collective-permute-start(bf16[96,1280]{1,0:T(8,128)(2,1)} %get-tuple-element.61), channel_id=1, source_target_pairs={{0,16},{4,20},{8,24},{12,28},{16,0},{20,4},{24,8},{28,12},{1,17},{... | collective-permute-start | bytes 737288 | tf_op jit(solution)/shard_map/ppermute | solution.py:159
  86.5 47.3 %collective-permute-start = (bf16[384,2560]{1,0:T(8,128)(2,1)}, bf16[384,2560]{1,0:T(8,128)(2,1)}, u32[]{:S(2)}, u32[]{:S(2)}) collective-permute-start(bf16[384,2560]{1,0:T(8,128)(2,1)} %get-tuple-element.66), channel_id=1, source_target_pairs={{0,4},{4,0},{8,12},{12,8},{16,20},{20,16},{24,28},{28,24},{1,5},{5... | collective-permute-start | bytes 5898248 | tf_op jit(solution)/shard_map/ppermute | solution.py:164
  86.5 50.7 %collective-permute-start.3 = (bf16[1728,640]{1,0:T(8,128)(2,1)}, bf16[1728,640]{1,0:T(8,128)(2,1)}, u32[]{:S(2)}, u32[]{:S(2)}) collective-permute-start(bf16[1728,640]{1,0:T(8,128)(2,1)} %param.25), channel_id=1, source_target_pairs={{0,4},{4,0},{8,12},{12,8},{16,20},{20,16},{24,28},{28,24},{1,5},{5... | collective-permute-start | bytes 6635528 | tf_op jit(solution)/shard_map/ppermute | solution.py:164
  114.5 30.9 %collective-permute-start.12 = (bf16[640,1024]{1,0:T(8,128)(2,1)S(1)}, bf16[640,1024]{1,0:T(8,128)(2,1)}, u32[]{:S(2)}, u32[]{:S(2)}) collective-permute-start(bf16[640,1024]{1,0:T(8,128)(2,1)S(1)} %copy-done.45), channel_id=1, source_target_pairs={{8,0},{12,4},{16,8},{20,12},{24,16},{28,20},{9,1},{13,5},{17,9},{2... | collective-permute-start | bytes 3932168 | tf_op jit(solution)/shard_map/ppermute | solution.py:159
  115.8 30.9 %collective-permute-start.11 = (bf16[640,1024]{1,0:T(8,128)(2,1)S(1)}, bf16[640,1024]{1,0:T(8,128)(2,1)}, u32[]{:S(2)}, u32[]{:S(2)}) collective-permute-start(bf16[640,1024]{1,0:T(8,128)(2,1)S(1)} %copy-done.45), channel_id=1, source_target_pairs={{0,8},{4,12},{8,16},{12,20},{16,24},{20,28},{1,9},{5,13},{9,17},{1... | collective-permute-start | bytes 3932168 | tf_op jit(solution)/shard_map/ppermute | solution.py:159
  145.4 30.2 %collective-permute-start.13 = (bf16[640,1024]{1,0:T(8,128)(2,1)}, bf16[640,1024]{1,0:T(8,128)(2,1)}, u32[]{:S(2)}, u32[]{:S(2)}) collective-permute-start(bf16[640,1024]{1,0:T(8,128)(2,1)} %collective-permute-done.12), channel_id=1, source_target_pairs={{8,0},{12,4},{16,8},{20,12},{9,1},{13,5},{17,9},{21,13},{10,2},{14... | collective-permute-start | bytes 3932168 | tf_op jit(solution)/shard_map/ppermute | solution.py:159
  177.9 39.3 %collective-permute-start.14 = (bf16[640,1024]{1,0:T(8,128)(2,1)}, bf16[640,1024]{1,0:T(8,128)(2,1)}, u32[]{:S(2)}, u32[]{:S(2)}) collective-permute-start(bf16[640,1024]{1,0:T(8,128)(2,1)} %collective-permute-done.13), channel_id=1, source_target_pairs={{8,0},{12,4},{9,1},{13,5},{10,2},{14,6},{11,3},{15,7}} | collective-permute-start | bytes 3932168 | tf_op jit(solution)/shard_map/ppermute | solution.py:159
  179.2 40.3 %collective-permute-start.16 = (bf16[640,1024]{1,0:T(8,128)(2,1)}, bf16[640,1024]{1,0:T(8,128)(2,1)}, u32[]{:S(2)}, u32[]{:S(2)}) collective-permute-start(bf16[640,1024]{1,0:T(8,128)(2,1)} %collective-permute-done.15), channel_id=1, source_target_pairs={{16,24},{20,28},{17,25},{21,29},{18,26},{22,30},{19,27},{23,31}} | collective-permute-start | bytes 3932168 | tf_op jit(solution)/shard_map/ppermute | solution.py:159
  182.3 33.2 %collective-permute-start.22 = (bf16[384,512]{1,0:T(8,128)(2,1)S(1)}, bf16[384,512]{1,0:T(8,128)(2,1)S(1)}, u32[]{:S(2)}, u32[]{:S(2)}) collective-permute-start(bf16[384,512]{1,0:T(8,128)(2,1)S(1)} %bitcast.481), channel_id=1, source_target_pairs={{8,0},{12,4},{16,8},{20,12},{24,16},{28,20},{9,1},{13,5},{17,9},{2... | collective-permute-start | bytes 1179656 | tf_op jit(solution)/shard_map/ppermute | solution.py:159
  186.5 36.7 %collective-permute-start.21 = (bf16[384,512]{1,0:T(8,128)(2,1)S(1)}, bf16[384,512]{1,0:T(8,128)(2,1)S(1)}, u32[]{:S(2)}, u32[]{:S(2)}) collective-permute-start(bf16[384,512]{1,0:T(8,128)(2,1)S(1)} %bitcast.482), channel_id=1, source_target_pairs={{0,8},{4,12},{8,16},{12,20},{16,24},{20,28},{1,9},{5,13},{9,17},{1... | collective-permute-start | bytes 1179656 | tf_op jit(solution)/shard_map/ppermute | solution.py:159
  345.2 142.5 %collective-permute-start.62 = (f32[48]{0:T(128)S(1)}, f32[48]{0:T(128)S(1)}, u32[]{:S(2)}, u32[]{:S(2)}) collective-permute-start(f32[48]{0:T(128)S(1)} %get-tuple-element.152), channel_id=1, source_target_pairs={{0,24},{4,28},{8,0},{12,4},{16,8},{20,12},{24,16},{28,20},{1,25},{... | collective-permute-start | bytes 584 | tf_op jit(solution)/shard_map/ppermute | solution.py:159
  349.1 138.6 %collective-permute-start.63 = (f32[48]{0:T(128)S(1)}, f32[48]{0:T(128)S(1)}, u32[]{:S(2)}, u32[]{:S(2)}) collective-permute-start(f32[48]{0:T(128)S(1)} %get-tuple-element.154), channel_id=1, source_target_pairs={{0,16},{4,20},{8,24},{12,28},{16,0},{20,4},{24,8},{28,12},{1,17},{... | collective-permute-start | bytes 584 | tf_op jit(solution)/shard_map/ppermute | solution.py:159
  403.8 29.8 %collective-permute-start.56 = (bf16[192,3456]{1,0:T(8,128)(2,1)S(1)}, bf16[192,3456]{1,0:T(8,128)(2,1)S(1)}, u32[]{:S(2)}, u32[]{:S(2)}) collective-permute-start(bf16[192,3456]{1,0:T(8,128)(2,1)S(1)} %get-tuple-element.57), channel_id=1, source_target_pairs={{0,8},{4,12},{1,9},{5,13},{2,10},{6,14},{3,11},{7,15}} | collective-permute-start | bytes 3981320 | tf_op jit(solution)/shard_map/ppermute | solution.py:159
  411.4 76.4 %collective-permute-start.64 = (f32[48]{0:T(128)S(1)}, f32[48]{0:T(128)S(1)}, u32[]{:S(2)}, u32[]{:S(2)}) collective-permute-start(f32[48]{0:T(128)S(1)} %get-tuple-element.153), channel_id=1, source_target_pairs={{0,8},{4,12},{8,16},{12,20},{16,24},{20,28},{24,0},{28,4},{1,9},{5... | collective-permute-start | bytes 584 | tf_op jit(solution)/shard_map/ppermute | solution.py:159
  435.7 31.7 %collective-permute-start.57 = (bf16[192,3456]{1,0:T(8,128)(2,1)}, bf16[192,3456]{1,0:T(8,128)(2,1)}, u32[]{:S(2)}, u32[]{:S(2)}) collective-permute-start(bf16[192,3456]{1,0:T(8,128)(2,1)} %get-tuple-element.55), channel_id=1, source_target_pairs={{0,8},{4,12},{8,16},{12,20},{1,9},{5,13},{9,17},{13,21},{2,10},{6,... | collective-permute-start | bytes 3981320 | tf_op jit(solution)/shard_map/ppermute | solution.py:159
  471.4 43.5 %collective-permute-start.60 = (bf16[192,3456]{1,0:T(8,128)(2,1)}, bf16[192,3456]{1,0:T(8,128)(2,1)}, u32[]{:S(2)}, u32[]{:S(2)}) collective-permute-start(bf16[192,3456]{1,0:T(8,128)(2,1)} %get-tuple-element.46), channel_id=1, source_target_pairs={{0,8},{4,12},{8,16},{12,20},{16,24},{20,28},{1,9},{5,13},{9,17},{1... | collective-permute-start | bytes 3981320 | tf_op jit(solution)/shard_map/ppermute | solution.py:159
  486.5 34.1 %collective-permute-start.61 = (bf16[192,3456]{1,0:T(8,128)(2,1)}, bf16[192,3456]{1,0:T(8,128)(2,1)}, u32[]{:S(2)}, u32[]{:S(2)}) collective-permute-start(bf16[192,3456]{1,0:T(8,128)(2,1)} %get-tuple-element.47), channel_id=1, source_target_pairs={{8,0},{12,4},{16,8},{20,12},{24,16},{28,20},{9,1},{13,5},{17,9},{2... | collective-permute-start | bytes 3981320 | tf_op jit(solution)/shard_map/ppermute | solution.py:159
  498.4 44.9 %collective-permute-start.80 = (bf16[192,3456]{1,0:T(8,128)(2,1)S(1)}, bf16[192,3456]{1,0:T(8,128)(2,1)S(1)}, u32[]{:S(2)}, u32[]{:S(2)}) collective-permute-start(bf16[192,3456]{1,0:T(8,128)(2,1)S(1)} %get-tuple-element.52), channel_id=1, source_target_pairs={{0,8},{4,12},{1,9},{5,13},{2,10},{6,14},{3,11},{7,15}} | collective-permute-start | bytes 3981320 | tf_op jit(solution)/shard_map/ppermute | solution.py:159
  503.0 40.2 %collective-permute-start.83 = (bf16[192,3456]{1,0:T(8,128)(2,1)S(1)}, bf16[192,3456]{1,0:T(8,128)(2,1)S(1)}, u32[]{:S(2)}, u32[]{:S(2)}) collective-permute-start(bf16[192,3456]{1,0:T(8,128)(2,1)S(1)} %get-tuple-element.53), channel_id=1, source_target_pairs={{24,16},{28,20},{25,17},{29,21},{26,18},{30,22},{27,19},{31,23}} | collective-permute-start | bytes 3981320 | tf_op jit(solution)/shard_map/ppermute | solution.py:159
  524.6 29.2 %collective-permute-start.68 = (bf16[192,1728]{1,0:T(8,128)(2,1)S(1)}, bf16[192,1728]{1,0:T(8,128)(2,1)}, u32[]{:S(2)}, u32[]{:S(2)}) collective-permute-start(bf16[192,1728]{1,0:T(8,128)(2,1)S(1)} %pad_maximum_fusion.9), channel_id=1, source_target_pairs={{8,0},{12,4},{16,8},{20,12},{24,16},{28,20},{9,1},{13,5},{17,9},{2... | collective-permute-start | bytes 1990664 | tf_op jit(solution)/shard_map/ppermute | solution.py:159
  525.9 32.1 %collective-permute-start.67 = (bf16[192,1728]{1,0:T(8,128)(2,1)S(1)}, bf16[192,1728]{1,0:T(8,128)(2,1)}, u32[]{:S(2)}, u32[]{:S(2)}) collective-permute-start(bf16[192,1728]{1,0:T(8,128)(2,1)S(1)} %pad_maximum_fusion.9), channel_id=1, source_target_pairs={{0,8},{4,12},{8,16},{12,20},{16,24},{20,28},{1,9},{5,13},{9,17},{1... | collective-permute-start | bytes 1990664 | tf_op jit(solution)/shard_map/ppermute | solution.py:159
  546.6 70.4 %collective-permute-start.81 = (bf16[192,3456]{1,0:T(8,128)(2,1)}, bf16[192,3456]{1,0:T(8,128)(2,1)}, u32[]{:S(2)}, u32[]{:S(2)}) collective-permute-start(bf16[192,3456]{1,0:T(8,128)(2,1)} %get-tuple-element.50), channel_id=1, source_target_pairs={{0,8},{4,12},{8,16},{12,20},{1,9},{5,13},{9,17},{13,21},{2,10},{6,... | collective-permute-start | bytes 3981320 | tf_op jit(solution)/shard_map/ppermute | solution.py:159
  552.1 64.9 %collective-permute-start.84 = (bf16[192,3456]{1,0:T(8,128)(2,1)}, bf16[192,3456]{1,0:T(8,128)(2,1)}, u32[]{:S(2)}, u32[]{:S(2)}) collective-permute-start(bf16[192,3456]{1,0:T(8,128)(2,1)} %get-tuple-element.51), channel_id=1, source_target_pairs={{16,8},{20,12},{24,16},{28,20},{17,9},{21,13},{25,17},{29,21},{18,... | collective-permute-start | bytes 3981320 | tf_op jit(solution)/shard_map/ppermute | solution.py:159
  553.8 61.1 %collective-permute-start.69 = (bf16[192,1728]{1,0:T(8,128)(2,1)}, bf16[192,1728]{1,0:T(8,128)(2,1)}, u32[]{:S(2)}, u32[]{:S(2)}) collective-permute-start(bf16[192,1728]{1,0:T(8,128)(2,1)} %collective-permute-done.68), channel_id=1, source_target_pairs={{8,0},{12,4},{16,8},{20,12},{9,1},{13,5},{17,9},{21,13},{10,2},{14... | collective-permute-start | bytes 1990664 | tf_op jit(solution)/shard_map/ppermute | solution.py:159
  558.0 58.2 %collective-permute-start.71 = (bf16[192,1728]{1,0:T(8,128)(2,1)}, bf16[192,1728]{1,0:T(8,128)(2,1)}, u32[]{:S(2)}, u32[]{:S(2)}) collective-permute-start(bf16[192,1728]{1,0:T(8,128)(2,1)} %collective-permute-done.67), channel_id=1, source_target_pairs={{8,16},{12,20},{16,24},{20,28},{9,17},{13,21},{17,25},{21,29},{10,... | collective-permute-start | bytes 1990664 | tf_op jit(solution)/shard_map/ppermute | solution.py:159
  624.8 33.1 %collective-permute-start.85 = (bf16[192,3456]{1,0:T(8,128)(2,1)S(1)}, bf16[192,3456]{1,0:T(8,128)(2,1)S(1)}, u32[]{:S(2)}, u32[]{:S(2)}) collective-permute-start(bf16[192,3456]{1,0:T(8,128)(2,1)S(1)} %get-tuple-element.49), channel_id=1, source_target_pairs={{8,0},{12,4},{16,8},{20,12},{24,16},{28,20},{9,1},{13,5},{17,9},{2... | collective-permute-start | bytes 3981320 | tf_op jit(solution)/shard_map/ppermute | solution.py:159
  (127 other events, 1595.1 us)

commit v3 on v2

--- a/solution.py
+++ b/solution.py
@@ -228,6 +228,11 @@
             out.append(jnp.stack([slots[j] for j in range(mlp_count)], axis=1))
         return jnp.concatenate(out, axis=0)
 
+    lines = [[z * CORES + e for z in range(planes)] for e in range(CORES)]
+
+    def line_collect(x):
+        return lax.all_gather(x, "seq", axis=0, tiled=True, axis_index_groups=lines)
+
     def swap_halves(x):
         return jnp.where(core == 0, x, jnp.concatenate([x[..., ds:], x[..., :ds]], axis=-1))
 
@@ -246,16 +251,8 @@
             lax.dynamic_slice_in_dim(value_bias, kv_first, kv_cols, 0),
         ]
     ).astype(F32)
-    kv_state = ([kv_weight], [kv_weight])
-    for t in range(1, planes - 1):
-        gather_step(kv_state, t)
-    query_weight, (kv_state[0][-1], kv_state[1][-1]) = after(
-        query_weight, (kv_state[0][-1], kv_state[1][-1])
-    )
-    gather_step(kv_state, planes - 1)
-    q_state = ([query_weight], [query_weight])
-    for t in range(1, planes):
-        gather_step(q_state, t)
+    kv_weight = line_collect(kv_weight)
+    q_weight = line_collect(query_weight)
 
     relative = [mlp_rank ^ j for j in range(mlp_count)]
 
@@ -278,7 +275,6 @@
     mine = jnp.where(core == 0, even, odd)
     theirs = sibling(jnp.where(core == 0, odd, even))
     both = jnp.concatenate([mine, theirs], axis=0)
-    lanes = [lax.dynamic_slice_in_dim(both, (plane - k) % planes * ds, ds, 1) for k in range(planes)]
 
     units = gate_weight.shape[1]
     whole = units // HD * HD
@@ -287,10 +283,41 @@
         axis=1,
     )
     glu_own = lax.optimization_barrier(glu_own)
-    glu_weight = jnp.concatenate([glu_own, sibling(glu_own)], axis=0)
+    glu_weight = jnp.concatenate(
+        [
+            jnp.pad(jnp.concatenate([glu_own, sibling(glu_own)], axis=0), ((0, 0), (0, HD))),
+            jnp.pad(jnp.eye(HD, dtype=BF16), ((0, 0), (2 * units, 0))),
+        ],
+        axis=0,
+    )
     out_wide = jnp.concatenate([out_weight, sibling(out_weight)], axis=1)
     down_wide = jnp.concatenate([down_weight, sibling(down_weight)], axis=1)
 
+    both, glu_weight, out_wide, down_wide = lax.optimization_barrier(
+        (both, glu_weight, out_wide, down_wide)
+    )
+
+    row_ids = seq_rank * rows + regroup(jnp.arange(rows, dtype=jnp.int32))
+    stream = lookup(piece_order, row_ids // piece_len) * piece_len + row_ids % piece_len
+    doc_ends = jnp.cumsum(doc_lengths)
+    segment = jnp.sum((stream[:, None] >= doc_ends[None, :]).astype(jnp.int32), axis=1)
+    doc_first = lookup(doc_ends - doc_lengths, segment)
+    cosine, sine_part = rope_tables(stream - doc_first, HD)
+
+    def project(weight, bias):
+        total = jnp.dot(both, weight, preferred_element_type=F32)
+        return total[:rows] + sibling(total[rows:]) + bias
+
+    kv_heads = kv_cols // HD
+    query_heads = query_weight.shape[1] // HD
+    kv = project(kv_weight, kv_bias)
+    key_rot = rotate(kv[:, :kv_cols], cosine, sine_part, kv_heads).astype(BF16)
+    value_b = kv[:, kv_cols:].astype(BF16)
+    joined = jnp.stack(
+        [key_rot.reshape(rows, kv_heads, HD), value_b.reshape(rows, kv_heads, HD)], axis=2
+    ).reshape(rows, 2 * kv_cols)
+    core_rows = jnp.concatenate(line_gather(ungroup(joined)), axis=0)
+    layer_input, core_rows = after(layer_input, core_rows)
     own_share = lax.dynamic_slice_in_dim(layer_input, mlp_rank * share, share, 0)
     lane_parts = []
     for k in range(planes):
@@ -301,33 +328,6 @@
     lane_input = swap_halves(jnp.stack(lane_parts, axis=0))
     lane_input = lane_input.reshape(planes, chunks, sub, dz)
     gain_lane = swap_halves(lax.dynamic_slice_in_dim(feedforward_gain, plane * dz, dz, 0)).astype(F32)
-    lanes, glu_weight, out_wide, down_wide, lane_input = lax.optimization_barrier(
-        (lanes, glu_weight, out_wide, down_wide, lane_input)
-    )
-
-    row_ids = seq_rank * rows + regroup(jnp.arange(rows, dtype=jnp.int32))
-    stream = lookup(piece_order, row_ids // piece_len) * piece_len + row_ids % piece_len
-    doc_ends = jnp.cumsum(doc_lengths)
-    segment = jnp.sum((stream[:, None] >= doc_ends[None, :]).astype(jnp.int32), axis=1)
-    doc_first = lookup(doc_ends - doc_lengths, segment)
-    cosine, sine_part = rope_tables(stream - doc_first, HD)
-
-    def project(state, bias):
-        total = None
-        for lane, weight in zip(lanes, gather_slots(state)):
-            part = jnp.dot(lane, lax.optimization_barrier(weight), preferred_element_type=F32)
-            total = part if total is None else total + part
-        return total[:rows] + sibling(total[rows:]) + bias
-
-    kv_heads = kv_cols // HD
-    query_heads = query_weight.shape[1] // HD
-    kv = project(kv_state, kv_bias)
-    key_rot = rotate(kv[:, :kv_cols], cosine, sine_part, kv_heads).astype(BF16)
-    value_b = kv[:, kv_cols:].astype(BF16)
-    joined = jnp.stack(
-        [key_rot.reshape(rows, kv_heads, HD), value_b.reshape(rows, kv_heads, HD)], axis=2
-    ).reshape(rows, 2 * kv_cols)
-    core_rows = jnp.concatenate(line_gather(ungroup(joined)), axis=0)
     kv_rows = jnp.concatenate([core_rows, sibling(core_rows)], axis=0)
     offsets = (plane - jnp.arange(planes, dtype=jnp.int32)) % planes
     slots = jnp.concatenate([offsets * CORES + core, offsets * CORES + 1 - core])
@@ -345,7 +345,7 @@
         pages.append(lax.dynamic_slice(kv_rows, (source * piece_len, offset), (piece_len, cache_width)))
     kv_cache = jnp.concatenate(pages, axis=0)
 
-    query = project(q_state, query_bias.astype(F32))
+    query = project(q_weight, query_bias.astype(F32))
     query_rot = rotate(query, cosine, sine_part, query_heads).astype(BF16)
     mixed = attend(
         query_rot.reshape(chunks, crows, query_heads * HD),
@@ -356,44 +356,25 @@
         kv_heads,
     )
 
-    mixed_states = []
-    dep = None
+    collected = [line_collect(mixed[h]) for h in range(chunks)]
+    residuals, parts = [], []
     for h in range(chunks):
-        first = mixed[h]
-        if dep is not None:
-            first, dep = after(first, dep)
-            mixed_states[-1][0][-1], mixed_states[-1][1][-1] = dep
-            gather_step(mixed_states[-1], planes - 1)
-        state = ([first], [first])
-        for t in range(1, planes - 1):
-            gather_step(state, t)
-        dep = (state[0][-1], state[1][-1])
-        mixed_states.append(state)
-    gather_step(mixed_states[-1], planes - 1)
-
-    residuals, scales, parts = [], [], []
-    for h in range(chunks):
-        heads = jnp.concatenate(gather_slots(mixed_states[h]), axis=0)
+        heads = jnp.concatenate(
+            [
+                lax.dynamic_slice_in_dim(collected[h], (plane - k) % planes * crows, crows, 0)
+                for k in range(planes)
+            ],
+            axis=0,
+        )
         attn = jnp.dot(heads, out_wide, preferred_element_type=F32).astype(BF16)
         attn = mlp_scatter(attn.reshape(planes, mlp_count, sub, dz))
         residual = lane_input[:, h].astype(F32) + attn
-        square = jnp.sum(residual * residual, axis=-1)
-        lane = mlp_gather((residual * gain_lane).astype(BF16))
-        square = sum(
-            [square[0]]
-            + [move(square[k], [(i, (i - k) % planes) for i in range(planes)]) for k in range(1, planes)]
-        )
-        found = {0: square}
-        for b in range(bits):
-            bit = 1 << b
-            have = sorted(found)
-            got = partner(jnp.stack([found[j] for j in have], axis=0), bit)
-            for i, j in enumerate(have):
-                found[j | bit] = got[i]
-        square = jnp.stack([found[j] for j in range(mlp_count)], axis=0).reshape(crows, 1)
-        scales.append(lax.rsqrt(square / width + norm_eps))
-        part = jnp.dot(lane.reshape(planes * crows, dz), glu_weight, preferred_element_type=F32)
-        parts.append(part.astype(BF16).reshape(planes, crows, 2 * units))
+        square = residual * residual
+        square = sum(square[..., i : i + HD] for i in range(0, dz, HD))
+        lane = jnp.concatenate([(residual * gain_lane).astype(BF16), square.astype(BF16)], axis=-1)
+        lane = mlp_gather(lane).reshape(planes * crows, dz + HD)
+        part = jnp.dot(lane, glu_weight, preferred_element_type=F32)
+        parts.append(part.astype(BF16).reshape(planes, crows, 2 * units + HD))
         residuals.append(residual)
 
     carried = [None] * chunks
@@ -406,10 +387,11 @@
     finals = []
     for h in range(chunks):
         act = parts[h][0].astype(F32) + carried[h][0].astype(F32) + carried[h][1].astype(F32)
-        act = act * scales[h]
+        square = jnp.sum(act[:, 2 * units :], axis=1, keepdims=True)
+        act = act * lax.rsqrt(square / width + norm_eps)
         hidden = jax.nn.silu(act[:, :whole]) * act[:, whole : 2 * whole]
         if units > whole:
-            last = act[:, 2 * whole :]
+            last = act[:, 2 * whole : 2 * units]
             edge = units - whole
             hidden = jnp.concatenate(
                 [hidden, jax.nn.silu(last[:, :edge]) * last[:, edge:]], axis=1

time: 753 us -> 758 us (level)
  waiting for transfers between devices: 310 us -> 420 us
  starting transfers between devices: 209 us -> 103 us
  other arithmetic: 120 us -> 98.5 us
  between operations: 4.43 us -> 17.2 us
    ppermute x69 -> x39, starting transfers between devices: 171 us -> 75.5 us  [move(): lax.ppermute(x, 'seq', [(a * CORES + e, b * CORES + e) for a, b in pairs...]
    ppermute x69 -> x39, waiting for transfers between devices: 260 us -> 323 us  [move(): lax.ppermute(x, 'seq', [(a * CORES + e, b * CORES + e) for a, b in pairs...]
    all_gather x0 -> x4, waiting for transfers between devices: none -> 45.6 us  [line_collect(): return lax.all_gather(x, 'seq', axis=0, tiled=True, axis_index_groups=lines)]
    add x18 -> x9, other arithmetic: 24.6 us -> 4.86 us  [gather_slots(): return [ups[0]] + [ups[k] + downs[planes - k] for k in range(1, planes)]]
    ppermute x28 -> x24, starting transfers between devices: 36.8 us -> 25.2 us  [partner(): return lax.ppermute(x, 'mlp', [(a, a ^ bit) for a in range(mlp_count)])]
    concatenate x1 -> x2, other arithmetic: 7.64 us -> 18.6 us  [the longest x1 10.5 us: shards(): jnp.concatenate([glu_own, sibling(glu_own)], axis=0)]
    convert_element_type x4, other arithmetic: 12.6 us -> 2.49 us  [add(): return (a.astype(F32) + b.astype(F32)).astype(BF16)]
    dot_general x10 -> x4, matrix products: 29.9 us -> 35.3 us  [the longest x2 22.8 us: shards(): part = jnp.dot(lane, glu_weight, preferred_element_type=F32)]
  transfers between devices with their start and end apart: 104 -> 74, of which waited for: 47 -> 40; matrix products, arithmetic and copies ran while one was open for 26% -> 20% of each run, Pallas kernels for 0% -> 0%
where the time goes in v3:
time: 758 us; the launch traced here: 749 us
  waiting for transfers between devices  420 us (55%)
  starting transfers between devices  103 us (14%)
  other arithmetic  98.5 us (13%)
  matrix products  49.4 us (7%)
  local copies, waits for them, and re-layouts  43.5 us (6%)
  between operations  17.2 us (2%)
  Pallas kernels  17.1 us (2%)
    ppermute x39, waiting for transfers between devices, move(): lax.ppermute(x, 'seq', [(a * CORES + e, b * CORES + e) for a, b in pairs...  323 us
    ppermute x39, starting transfers between devices, move(): lax.ppermute(x, 'seq', [(a * CORES + e, b * CORES + e) for a, b in pairs...  75.5 us
    ppermute x24, waiting for transfers between devices, partner(): return lax.ppermute(x, 'mlp', [(a, a ^ bit) for a in range(mlp_count)])  47.8 us
    all_gather x4, waiting for transfers between devices, line_collect(): return lax.all_gather(x, 'seq', axis=0, tiled=True, axis_index_groups=lines)  45.6 us
    ppermute x24, starting transfers between devices, partner(): return lax.ppermute(x, 'mlp', [(a, a ^ bit) for a in range(mlp_count)])  25.2 us
    dot_general x2, matrix products, shards(): part = jnp.dot(lane, glu_weight, preferred_element_type=F32)  22.8 us
    pallas_call x1, Pallas kernels, attend(): pl.pallas_call(attend_kernel, grid_spec=pltpu.PrefetchScalarGridSpec(num_...  17.1 us
  transfers between devices with their start and end apart: 74, of which 40 were waited for; matrix products, arithmetic and copies ran while one was open for 20% of the time, Pallas kernels for 0%

profile of v3, /device:TPU:0, one launch (start us, length us, event | category | flops | bytes accessed | tf_op | source)
XLA Modules:
  0.0 749.0 jit_solution(13041452954261584512)
XLA Ops:
  9.5 14.5 %pad_maximum_fusion.1 = bf16[640,3456]{0,1:T(8,128)(2,1)} fusion(bf16[640,64]{0,1:T(8,128)(2,1)S(1)} %slice-done, bf16[640,64]{0,1:T(8,128)(2,1)S(1)} %slice-done.2, bf16[640,1664]{0,1:T(8,128)(2,1)S(1)} %slice-done.1, bf16[640,1664]{0,1:T(8,128)(2,1)S(1)} %slice-done.3), kind=kLoop, calls=%fused_computation.11 | loop fusion | flops 17694720 | bytes 8847360 | tf_op jit(solution)/shard_map/concatenate | solution.py:281
  34.5 6.9 fusion.4
  63.7 10.5 %fusion.2 = bf16[1280,3584]{0,1:T(8,128)(2,1)} fusion(bf16[640,3456]{0,1:T(8,128)(2,1)} %collective-permute-done.1, bf16[640,3456]{0,1:T(8,128)(2,1)} %pad_maximum_fusion.1), kind=kLoop, calls=%fused_computation.4 | loop fusion | flops 32112640 | bytes 18022400 | tf_op jit(solution)/shard_map/concatenate | solution.py:288
  74.2 8.1 %pad_maximum_fusion = bf16[1408,3584]{0,1:T(8,128)(2,1)} fusion(bf16[128,3584]{0,1:T(8,128)(2,1)S(1)} %pad_convert_fusion, bf16[1280,3584]{0,1:T(8,128)(2,1)} %fusion.2), kind=kLoop, calls=%fused_computation.3 | loop fusion | flops 20185088 | bytes 20185088 | tf_op jit(solution)/shard_map/concatenate | solution.py:286
  97.2 16.3 %collective-permute-done.5 = bf16[384,512]{1,0:T(8,128)(2,1)S(1)} collective-permute-done((bf16[384,512]{1,0:T(8,128)(2,1)S(1)}, bf16[384,512]{1,0:T(8,128)(2,1)S(1)}, u32[]{:S(2)}, u32[]{:S(2)}) %collective-permute-start.5) | collective-permute-done | bytes 393248 | tf_op jit(solution)/shard_map/ppermute | solution.py:159
  114.2 14.1 %collective-permute-done.6 = bf16[384,512]{1,0:T(8,128)(2,1)S(1)} collective-permute-done((bf16[384,512]{1,0:T(8,128)(2,1)S(1)}, bf16[384,512]{1,0:T(8,128)(2,1)S(1)}, u32[]{:S(2)}, u32[]{:S(2)}) %collective-permute-start.6) | collective-permute-done | bytes 393248 | tf_op jit(solution)/shard_map/ppermute | solution.py:159
  130.4 25.6 %collective-permute-done.7 = bf16[384,512]{1,0:T(8,128)(2,1)S(1)} collective-permute-done((bf16[384,512]{1,0:T(8,128)(2,1)S(1)}, bf16[384,512]{1,0:T(8,128)(2,1)S(1)}, u32[]{:S(2)}, u32[]{:S(2)}) %collective-permute-start.7) | collective-permute-done | bytes 393248 | tf_op jit(solution)/shard_map/ppermute | solution.py:159
  158.5 46.6 %collective-permute-done.8 = bf16[384,512]{1,0:T(8,128)(2,1)S(1)} collective-permute-done((bf16[384,512]{1,0:T(8,128)(2,1)S(1)}, bf16[384,512]{1,0:T(8,128)(2,1)S(1)}, u32[]{:S(2)}, u32[]{:S(2)}) %collective-permute-start.8) | collective-permute-done | bytes 393248 | tf_op jit(solution)/shard_map/ppermute | solution.py:159
  206.5 7.3 fusion.102
  239.2 17.1 %shard_map.167 = bf16[2,192,1024]{2,1,0:T(8,128)(2,1)S(1)} custom-call(s32[2]{0:T(128)S(1)} %convert_reduce_fusion.1.count, s32[2,16]{1,0:T(2,128)S(1)} %select_reduce_fusion.1.active, s32[16]{0:T(128)S(1)} %select_reduce_fusion.2.piece_stream, bf16[2,192,1024]{2,1,0:T(8,128)(2,1)S(1)} %copy-done, ...), custom_call_target="tpu_custom_call" | custom-call | tf_op jit(solution)/shard_map/pallas_call | solution.py:103
  260.1 9.5 %collective-permute-start.13 = (bf16[96,1280]{1,0:T(8,128)(2,1)}, bf16[96,1280]{1,0:T(8,128)(2,1)}, u32[]{:S(2)}, u32[]{:S(2)}) collective-permute-start(bf16[96,1280]{1,0:T(8,128)(2,1)} %get-tuple-element.37), channel_id=1, source_target_pairs={{0,24},{4,28},{8,0},{12,4},{16,8},{20,12},{24,16},{28,20},{1,25},{... | collective-permute-start | bytes 737288 | tf_op jit(solution)/shard_map/ppermute | solution.py:159
  270.5 8.6 %collective-permute-done.13 = bf16[96,1280]{1,0:T(8,128)(2,1)} collective-permute-done((bf16[96,1280]{1,0:T(8,128)(2,1)}, bf16[96,1280]{1,0:T(8,128)(2,1)}, u32[]{:S(2)}, u32[]{:S(2)}) %collective-permute-start.13) | collective-permute-done | bytes 245792 | tf_op jit(solution)/shard_map/ppermute | solution.py:159
  279.1 13.8 %collective-permute-done.12 = bf16[96,1280]{1,0:T(8,128)(2,1)} collective-permute-done((bf16[96,1280]{1,0:T(8,128)(2,1)}, bf16[96,1280]{1,0:T(8,128)(2,1)}, u32[]{:S(2)}, u32[]{:S(2)}) %collective-permute-start.12) | collective-permute-done | bytes 245792 | tf_op jit(solution)/shard_map/ppermute | solution.py:159
  298.8 10.0 %all-gather.11.cloned.1.call-done = bf16[1,768,1024]{2,1,0:T(8,128)(2,1)} async-done(((bf16[1,192,1024]{2,1,0:T(8,128)(2,1)}), bf16[1,768,1024]{2,1,0:T(8,128)(2,1)}) %all-gather.11.cloned.1.call-update) | async-done | bytes 1572880 | tf_op jit(solution)/shard_map/all_gather | solution.py:234
  318.2 34.0 %all-gather.13.cloned.1.call-done = bf16[1,768,1024]{2,1,0:T(8,128)(2,1)} async-done(((bf16[1,192,1024]{2,1,0:T(8,128)(2,1)}), bf16[1,768,1024]{2,1,0:T(8,128)(2,1)}) %all-gather.13.cloned.1.call-update) | async-done | bytes 1572880 | tf_op jit(solution)/shard_map/all_gather | solution.py:234
  363.3 7.8 %collective-permute-done.26 = bf16[2,2,48,1280]{3,2,1,0:T(8,128)(2,1)S(1)} collective-permute-done((bf16[2,2,48,1280]{3,2,1,0:T(8,128)(2,1)S(1)}, bf16[2,2,48,1280]{3,2,1,0:T(8,128)(2,1)S(1)}, u32[]{:S(2)}, u32[]{:S(2)}) %collective-permute-start.26) | collective-permute-done | bytes 491552 | tf_op jit(solution)/shard_map/ppermute | solution.py:169
  402.7 9.3 %collective-permute-done.23 = bf16[2,2,48,1408]{3,2,1,0:T(8,128)(2,1)S(1)} collective-permute-done((bf16[2,2,48,1408]{3,2,1,0:T(8,128)(2,1)S(1)}, bf16[2,2,48,1408]{3,2,1,0:T(8,128)(2,1)S(1)}, u32[]{:S(2)}, u32[]{:S(2)}) %collective-permute-start.23) | collective-permute-done | bytes 540704 | tf_op jit(solution)/shard_map/ppermute | solution.py:169
  415.1 11.4 %convolution_convert_fusion.1 = bf16[768,3584]{1,0:T(8,128)(2,1)S(1)} fusion(bf16[768,1408]{1,0:T(8,128)(2,1)S(1)} %bitcast.456, bf16[1408,3584]{0,1:T(8,128)(2,1)} %pad_maximum_fusion), kind=kOutput, calls=%fused_computation.10 | convolution fusion | flops 7753826304 | bytes 17760256 | tf_op jit(solution)/shard_map/dot_general | solution.py:376
  430.5 24.3 %collective-permute-done.32 = bf16[192,3584]{1,0:T(8,128)(2,1)S(1)} collective-permute-done((bf16[192,3584]{1,0:T(8,128)(2,1)S(1)}, bf16[192,3584]{1,0:T(8,128)(2,1)S(1)}, u32[]{:S(2)}, u32[]{:S(2)}) %collective-permute-start.32) | collective-permute-done | bytes 1376288 | tf_op jit(solution)/shard_map/ppermute | solution.py:159
  460.7 11.4 %convolution_convert_fusion = bf16[768,3584]{1,0:T(8,128)(2,1)S(1)} fusion(bf16[768,1408]{1,0:T(8,128)(2,1)S(1)} %bitcast.455, bf16[1408,3584]{0,1:T(8,128)(2,1)} %pad_maximum_fusion), kind=kOutput, calls=%fused_computation.9 | convolution fusion | flops 7753826304 | bytes 17760256 | tf_op jit(solution)/shard_map/dot_general | solution.py:376
  472.1 11.1 %collective-permute-done.33 = bf16[192,3584]{1,0:T(8,128)(2,1)S(1)} collective-permute-done((bf16[192,3584]{1,0:T(8,128)(2,1)S(1)}, bf16[192,3584]{1,0:T(8,128)(2,1)S(1)}, u32[]{:S(2)}, u32[]{:S(2)}) %collective-permute-start.33) | collective-permute-done | bytes 1376288 | tf_op jit(solution)/shard_map/ppermute | solution.py:159
  496.4 9.0 %collective-permute-done.37 = bf16[192,3584]{1,0:T(8,128)(2,1)S(1)} collective-permute-done((bf16[192,3584]{1,0:T(8,128)(2,1)S(1)}, bf16[192,3584]{1,0:T(8,128)(2,1)S(1)}, u32[]{:S(2)}, u32[]{:S(2)}) %collective-permute-start.37) | collective-permute-done | bytes 1376288 | tf_op jit(solution)/shard_map/ppermute | solution.py:159
  505.3 15.5 %collective-permute-done.36 = bf16[192,3584]{1,0:T(8,128)(2,1)S(1)} collective-permute-done((bf16[192,3584]{1,0:T(8,128)(2,1)S(1)}, bf16[192,3584]{1,0:T(8,128)(2,1)S(1)}, u32[]{:S(2)}, u32[]{:S(2)}) %collective-permute-start.36) | collective-permute-done | bytes 1376288 | tf_op jit(solution)/shard_map/ppermute | solution.py:159
  522.2 22.8 %collective-permute-done.51 = bf16[192,3584]{1,0:T(8,128)(2,1)S(1)} collective-permute-done((bf16[192,3584]{1,0:T(8,128)(2,1)S(1)}, bf16[192,3584]{1,0:T(8,128)(2,1)S(1)}, u32[]{:S(2)}, u32[]{:S(2)}) %collective-permute-start.51) | collective-permute-done | bytes 1376288 | tf_op jit(solution)/shard_map/ppermute | solution.py:159
  554.7 28.7 %collective-permute-done.38 = bf16[192,1728]{1,0:T(8,128)(2,1)S(1)} collective-permute-done((bf16[192,1728]{1,0:T(8,128)(2,1)S(1)}, bf16[192,1728]{1,0:T(8,128)(2,1)S(1)}, u32[]{:S(2)}, u32[]{:S(2)}) %collective-permute-start.38) | collective-permute-done | bytes 663584 | tf_op jit(solution)/shard_map/ppermute | solution.py:159
  586.1 17.3 %collective-permute-done.40 = bf16[192,1728]{1,0:T(8,128)(2,1)S(1)} collective-permute-done((bf16[192,1728]{1,0:T(8,128)(2,1)S(1)}, bf16[192,1728]{1,0:T(8,128)(2,1)S(1)}, u32[]{:S(2)}, u32[]{:S(2)}) %collective-permute-start.40) | collective-permute-done | bytes 663584 | tf_op jit(solution)/shard_map/ppermute | solution.py:159
  612.9 11.2 %collective-permute-done.41 = bf16[192,1728]{1,0:T(8,128)(2,1)S(1)} collective-permute-done((bf16[192,1728]{1,0:T(8,128)(2,1)S(1)}, bf16[192,1728]{1,0:T(8,128)(2,1)S(1)}, u32[]{:S(2)}, u32[]{:S(2)}) %collective-permute-start.41) | collective-permute-done | bytes 663584 | tf_op jit(solution)/shard_map/ppermute | solution.py:159
  628.2 17.0 %collective-permute-done.56 = bf16[192,3584]{1,0:T(8,128)(2,1)S(1)} collective-permute-done((bf16[192,3584]{1,0:T(8,128)(2,1)S(1)}, bf16[192,3584]{1,0:T(8,128)(2,1)S(1)}, u32[]{:S(2)}, u32[]{:S(2)}) %collective-permute-start.56) | collective-permute-done | bytes 1376288 | tf_op jit(solution)/shard_map/ppermute | solution.py:159
  658.2 10.9 %collective-permute-done.58 = bf16[192,1728]{1,0:T(8,128)(2,1)} collective-permute-done((bf16[192,1728]{1,0:T(8,128)(2,1)S(1)}, bf16[192,1728]{1,0:T(8,128)(2,1)}, u32[]{:S(2)}, u32[]{:S(2)}) %collective-permute-start.58) | collective-permute-done | bytes 663584 | tf_op jit(solution)/shard_map/ppermute | solution.py:159
  676.5 11.9 %collective-permute-done.59 = bf16[192,1728]{1,0:T(8,128)(2,1)} collective-permute-done((bf16[192,1728]{1,0:T(8,128)(2,1)}, bf16[192,1728]{1,0:T(8,128)(2,1)}, u32[]{:S(2)}, u32[]{:S(2)}) %collective-permute-start.59) | collective-permute-done | bytes 663584 | tf_op jit(solution)/shard_map/ppermute | solution.py:159
  695.2 6.3 collective-permute-done.60
  702.8 6.0 convolution_convert_fusion.2
  (392 shorter events, 257.0 us)
Async XLA Ops:
  7.2 76.8 %all-gather.7.cloned.1.call-start = ((), (), s32[]{:S(2)}) async-start(), calls=%async_computation | async-start | bytes 3276800 | tf_op jit(solution)/shard_map/all_gather | solution.py:234
  24.1 39.6 %collective-permute-start.1 = (bf16[640,3456]{0,1:T(8,128)(2,1)}, bf16[640,3456]{0,1:T(8,128)(2,1)}, u32[]{:S(2)}, u32[]{:S(2)}) collective-permute-start(bf16[640,3456]{0,1:T(8,128)(2,1)} %pad_maximum_fusion.1), channel_id=1, source_target_pairs={{0,4},{4,0},{8,12},{12,8},{16,20},{20,16},{24,28},{28,24},{1,5},{5... | collective-permute-start | bytes 13271048 | tf_op jit(solution)/shard_map/ppermute | solution.py:164
  26.6 179.9 %all-gather.9.cloned.1.call-start = ((), (), s32[]{:S(2)}) async-start(), calls=%async_computation.1 | async-start | bytes 6553600 | tf_op jit(solution)/shard_map/all_gather | solution.py:234
  46.1 262.7 %all-gather.11.cloned.1.call-start = ((), (), s32[]{:S(2)}) async-start(), calls=%async_computation.2 | async-start | bytes 1966080 | tf_op jit(solution)/shard_map/all_gather | solution.py:234
  92.8 20.7 %collective-permute-start.5 = (bf16[384,512]{1,0:T(8,128)(2,1)S(1)}, bf16[384,512]{1,0:T(8,128)(2,1)S(1)}, u32[]{:S(2)}, u32[]{:S(2)}) collective-permute-start(bf16[384,512]{1,0:T(8,128)(2,1)S(1)} %bitcast.459), channel_id=1, source_target_pairs={{0,8},{4,12},{8,16},{12,20},{16,24},{20,28},{1,9},{5,13},{9,17},{1... | collective-permute-start | bytes 1179656 | tf_op jit(solution)/shard_map/ppermute | solution.py:159
  95.9 32.4 %collective-permute-start.6 = (bf16[384,512]{1,0:T(8,128)(2,1)S(1)}, bf16[384,512]{1,0:T(8,128)(2,1)S(1)}, u32[]{:S(2)}, u32[]{:S(2)}) collective-permute-start(bf16[384,512]{1,0:T(8,128)(2,1)S(1)} %bitcast.460), channel_id=1, source_target_pairs={{8,0},{12,4},{16,8},{20,12},{24,16},{28,20},{9,1},{13,5},{17,9},{2... | collective-permute-start | bytes 1179656 | tf_op jit(solution)/shard_map/ppermute | solution.py:159
  128.3 27.7 %collective-permute-start.7 = (bf16[384,512]{1,0:T(8,128)(2,1)S(1)}, bf16[384,512]{1,0:T(8,128)(2,1)S(1)}, u32[]{:S(2)}, u32[]{:S(2)}) collective-permute-start(bf16[384,512]{1,0:T(8,128)(2,1)S(1)} %collective-permute-done.6), channel_id=1, source_target_pairs={{8,0},{12,4},{16,8},{20,12},{9,1},{13,5},{17,9},{21,13},{10,2},{14... | collective-permute-start | bytes 1179656 | tf_op jit(solution)/shard_map/ppermute | solution.py:159
  129.7 28.6 %collective-permute-start.10 = (bf16[384,512]{1,0:T(8,128)(2,1)S(1)}, bf16[384,512]{1,0:T(8,128)(2,1)S(1)}, u32[]{:S(2)}, u32[]{:S(2)}) collective-permute-start(bf16[384,512]{1,0:T(8,128)(2,1)S(1)} %collective-permute-done.9), channel_id=1, source_target_pairs={{16,24},{20,28},{17,25},{21,29},{18,26},{22,30},{19,27},{23,31}} | collective-permute-start | bytes 1179656 | tf_op jit(solution)/shard_map/ppermute | solution.py:159
  156.0 49.1 %collective-permute-start.8 = (bf16[384,512]{1,0:T(8,128)(2,1)S(1)}, bf16[384,512]{1,0:T(8,128)(2,1)S(1)}, u32[]{:S(2)}, u32[]{:S(2)}) collective-permute-start(bf16[384,512]{1,0:T(8,128)(2,1)S(1)} %collective-permute-done.7), channel_id=1, source_target_pairs={{8,0},{12,4},{9,1},{13,5},{10,2},{14,6},{11,3},{15,7}} | collective-permute-start | bytes 1179656 | tf_op jit(solution)/shard_map/ppermute | solution.py:159
  257.3 94.8 %all-gather.13.cloned.1.call-start = ((), (), s32[]{:S(2)}) async-start(), calls=%async_computation.3 | async-start | bytes 1966080 | tf_op jit(solution)/shard_map/all_gather | solution.py:234
  269.6 23.3 %collective-permute-start.12 = (bf16[96,1280]{1,0:T(8,128)(2,1)}, bf16[96,1280]{1,0:T(8,128)(2,1)}, u32[]{:S(2)}, u32[]{:S(2)}) collective-permute-start(bf16[96,1280]{1,0:T(8,128)(2,1)} %get-tuple-element.38), channel_id=1, source_target_pairs={{0,16},{4,20},{8,24},{12,28},{16,0},{20,4},{24,8},{28,12},{1,17},{... | collective-permute-start | bytes 737288 | tf_op jit(solution)/shard_map/ppermute | solution.py:159
  269.6 25.3 %collective-permute-start.11 = (bf16[96,1280]{1,0:T(8,128)(2,1)}, bf16[96,1280]{1,0:T(8,128)(2,1)}, u32[]{:S(2)}, u32[]{:S(2)}) collective-permute-start(bf16[96,1280]{1,0:T(8,128)(2,1)} %get-tuple-element.39), channel_id=1, source_target_pairs={{0,8},{4,12},{8,16},{12,20},{16,24},{20,28},{24,0},{28,4},{1,9},{5... | collective-permute-start | bytes 737288 | tf_op jit(solution)/shard_map/ppermute | solution.py:159
  314.3 45.7 %collective-permute-start.18 = (bf16[2,2,48,1280]{3,2,1,0:T(8,128)(2,1)}, bf16[2,2,48,1280]{3,2,1,0:T(8,128)(2,1)}, u32[]{:S(2)}, u32[]{:S(2)}) collective-permute-start(bf16[2,2,48,1280]{3,2,1,0:T(8,128)(2,1)} %pad_maximum_fusion.18), channel_id=1, source_target_pairs={{0,2},{1,3},{2,0},{3,1},{4,6},{5,7},{6,4},{7,5},{8,10},{9,11},{10,... | collective-permute-start | bytes 1474568 | tf_op jit(solution)/shard_map/ppermute | solution.py:169
  316.7 44.9 %collective-permute-start.16 = (bf16[2,2,48,1280]{3,2,1,0:T(8,128)(2,1)}, bf16[2,2,48,1280]{3,2,1,0:T(8,128)(2,1)}, u32[]{:S(2)}, u32[]{:S(2)}) collective-permute-start(bf16[2,2,48,1280]{3,2,1,0:T(8,128)(2,1)} %pad_maximum_fusion.17), channel_id=1, source_target_pairs={{0,1},{1,0},{2,3},{3,2},{4,5},{5,4},{6,7},{7,6},{8,9},{9,8},{10,11... | collective-permute-start | bytes 1474568 | tf_op jit(solution)/shard_map/ppermute | solution.py:169
  395.8 34.0 %collective-permute-start.31 = (bf16[2,2,48,1408]{3,2,1,0:T(8,128)(2,1)S(1)}, bf16[2,2,48,1408]{3,2,1,0:T(8,128)(2,1)S(1)}, u32[]{:S(2)}, u32[]{:S(2)}) collective-permute-start(bf16[2,2,48,1408]{3,2,1,0:T(8,128)(2,1)S(1)} %pad_maximum_fusion.16), channel_id=1, source_target_pairs={{0,2},{1,3},{2,0},{3,1},{4,6},{5,7},{6,4},{7,5},{8,10},{9,11},{10,... | collective-permute-start | bytes 1622024 | tf_op jit(solution)/shard_map/ppermute | solution.py:169
  402.0 27.8 %collective-permute-start.29 = (bf16[2,2,48,1408]{3,2,1,0:T(8,128)(2,1)S(1)}, bf16[2,2,48,1408]{3,2,1,0:T(8,128)(2,1)S(1)}, u32[]{:S(2)}, u32[]{:S(2)}) collective-permute-start(bf16[2,2,48,1408]{3,2,1,0:T(8,128)(2,1)S(1)} %pad_maximum_fusion.15), channel_id=1, source_target_pairs={{0,1},{1,0},{2,3},{3,2},{4,5},{5,4},{6,7},{7,6},{8,9},{9,8},{10,11... | collective-permute-start | bytes 1622024 | tf_op jit(solution)/shard_map/ppermute | solution.py:169
  427.5 27.4 %collective-permute-start.32 = (bf16[192,3584]{1,0:T(8,128)(2,1)S(1)}, bf16[192,3584]{1,0:T(8,128)(2,1)S(1)}, u32[]{:S(2)}, u32[]{:S(2)}) collective-permute-start(bf16[192,3584]{1,0:T(8,128)(2,1)S(1)} %get-tuple-element.35), channel_id=1, source_target_pairs={{0,8},{4,12},{1,9},{5,13},{2,10},{6,14},{3,11},{7,15}} | collective-permute-start | bytes 4128776 | tf_op jit(solution)/shard_map/ppermute | solution.py:159
  455.4 27.7 %collective-permute-start.33 = (bf16[192,3584]{1,0:T(8,128)(2,1)S(1)}, bf16[192,3584]{1,0:T(8,128)(2,1)S(1)}, u32[]{:S(2)}, u32[]{:S(2)}) collective-permute-start(bf16[192,3584]{1,0:T(8,128)(2,1)S(1)} %get-tuple-element.33), channel_id=1, source_target_pairs={{0,8},{4,12},{8,16},{12,20},{1,9},{5,13},{9,17},{13,21},{2,10},{6,... | collective-permute-start | bytes 4128776 | tf_op jit(solution)/shard_map/ppermute | solution.py:159
  459.9 23.2 %collective-permute-start.35 = (bf16[192,3584]{1,0:T(8,128)(2,1)S(1)}, bf16[192,3584]{1,0:T(8,128)(2,1)S(1)}, u32[]{:S(2)}, u32[]{:S(2)}) collective-permute-start(bf16[192,3584]{1,0:T(8,128)(2,1)S(1)} %get-tuple-element.32), channel_id=1, source_target_pairs={{16,8},{20,12},{24,16},{28,20},{17,9},{21,13},{25,17},{29,21},{18,... | collective-permute-start | bytes 4128776 | tf_op jit(solution)/shard_map/ppermute | solution.py:159
  483.9 21.5 %collective-permute-start.37 = (bf16[192,3584]{1,0:T(8,128)(2,1)S(1)}, bf16[192,3584]{1,0:T(8,128)(2,1)S(1)}, u32[]{:S(2)}, u32[]{:S(2)}) collective-permute-start(bf16[192,3584]{1,0:T(8,128)(2,1)S(1)} %get-tuple-element.25), channel_id=1, source_target_pairs={{8,0},{12,4},{16,8},{20,12},{24,16},{28,20},{9,1},{13,5},{17,9},{2... | collective-permute-start | bytes 4128776 | tf_op jit(solution)/shard_map/ppermute | solution.py:159
  485.2 35.6 %collective-permute-start.36 = (bf16[192,3584]{1,0:T(8,128)(2,1)S(1)}, bf16[192,3584]{1,0:T(8,128)(2,1)S(1)}, u32[]{:S(2)}, u32[]{:S(2)}) collective-permute-start(bf16[192,3584]{1,0:T(8,128)(2,1)S(1)} %get-tuple-element.24), channel_id=1, source_target_pairs={{0,8},{4,12},{8,16},{12,20},{16,24},{20,28},{1,9},{5,13},{9,17},{1... | collective-permute-start | bytes 4128776 | tf_op jit(solution)/shard_map/ppermute | solution.py:159
  490.5 54.6 %collective-permute-start.51 = (bf16[192,3584]{1,0:T(8,128)(2,1)S(1)}, bf16[192,3584]{1,0:T(8,128)(2,1)S(1)}, u32[]{:S(2)}, u32[]{:S(2)}) collective-permute-start(bf16[192,3584]{1,0:T(8,128)(2,1)S(1)} %get-tuple-element.30), channel_id=1, source_target_pairs={{0,8},{4,12},{1,9},{5,13},{2,10},{6,14},{3,11},{7,15}} | collective-permute-start | bytes 4128776 | tf_op jit(solution)/shard_map/ppermute | solution.py:159
  495.6 49.4 %collective-permute-start.54 = (bf16[192,3584]{1,0:T(8,128)(2,1)S(1)}, bf16[192,3584]{1,0:T(8,128)(2,1)S(1)}, u32[]{:S(2)}, u32[]{:S(2)}) collective-permute-start(bf16[192,3584]{1,0:T(8,128)(2,1)S(1)} %get-tuple-element.31), channel_id=1, source_target_pairs={{24,16},{28,20},{25,17},{29,21},{26,18},{30,22},{27,19},{31,23}} | collective-permute-start | bytes 4128776 | tf_op jit(solution)/shard_map/ppermute | solution.py:159
  545.6 59.5 %collective-permute-start.52 = (bf16[192,3584]{1,0:T(8,128)(2,1)S(1)}, bf16[192,3584]{1,0:T(8,128)(2,1)S(1)}, u32[]{:S(2)}, u32[]{:S(2)}) collective-permute-start(bf16[192,3584]{1,0:T(8,128)(2,1)S(1)} %get-tuple-element.28), channel_id=1, source_target_pairs={{0,8},{4,12},{8,16},{12,20},{1,9},{5,13},{9,17},{13,21},{2,10},{6,... | collective-permute-start | bytes 4128776 | tf_op jit(solution)/shard_map/ppermute | solution.py:159
  550.1 55.1 %collective-permute-start.55 = (bf16[192,3584]{1,0:T(8,128)(2,1)S(1)}, bf16[192,3584]{1,0:T(8,128)(2,1)S(1)}, u32[]{:S(2)}, u32[]{:S(2)}) collective-permute-start(bf16[192,3584]{1,0:T(8,128)(2,1)S(1)} %get-tuple-element.29), channel_id=1, source_target_pairs={{16,8},{20,12},{24,16},{28,20},{17,9},{21,13},{25,17},{29,21},{18,... | collective-permute-start | bytes 4128776 | tf_op jit(solution)/shard_map/ppermute | solution.py:159
  550.9 32.4 %collective-permute-start.38 = (bf16[192,1728]{1,0:T(8,128)(2,1)S(1)}, bf16[192,1728]{1,0:T(8,128)(2,1)S(1)}, u32[]{:S(2)}, u32[]{:S(2)}) collective-permute-start(bf16[192,1728]{1,0:T(8,128)(2,1)S(1)} %pad_maximum_fusion.10), channel_id=1, source_target_pairs={{0,8},{4,12},{8,16},{12,20},{16,24},{20,28},{1,9},{5,13},{9,17},{1... | collective-permute-start | bytes 1990664 | tf_op jit(solution)/shard_map/ppermute | solution.py:159
  553.4 30.7 %collective-permute-start.39 = (bf16[192,1728]{1,0:T(8,128)(2,1)S(1)}, bf16[192,1728]{1,0:T(8,128)(2,1)S(1)}, u32[]{:S(2)}, u32[]{:S(2)}) collective-permute-start(bf16[192,1728]{1,0:T(8,128)(2,1)S(1)} %pad_maximum_fusion.10), channel_id=1, source_target_pairs={{8,0},{12,4},{16,8},{20,12},{24,16},{28,20},{9,1},{13,5},{17,9},{2... | collective-permute-start | bytes 1990664 | tf_op jit(solution)/shard_map/ppermute | solution.py:159
  585.4 27.4 %collective-permute-start.43 = (bf16[192,1728]{1,0:T(8,128)(2,1)S(1)}, bf16[192,1728]{1,0:T(8,128)(2,1)S(1)}, u32[]{:S(2)}, u32[]{:S(2)}) collective-permute-start(bf16[192,1728]{1,0:T(8,128)(2,1)S(1)} %collective-permute-done.42), channel_id=1, source_target_pairs={{16,24},{20,28},{17,25},{21,29},{18,26},{22,30},{19,27},{23,31}} | collective-permute-start | bytes 1990664 | tf_op jit(solution)/shard_map/ppermute | solution.py:159
  603.6 20.5 %collective-permute-start.41 = (bf16[192,1728]{1,0:T(8,128)(2,1)S(1)}, bf16[192,1728]{1,0:T(8,128)(2,1)S(1)}, u32[]{:S(2)}, u32[]{:S(2)}) collective-permute-start(bf16[192,1728]{1,0:T(8,128)(2,1)S(1)} %collective-permute-done.40), channel_id=1, source_target_pairs={{8,0},{12,4},{9,1},{13,5},{10,2},{14,6},{11,3},{15,7}} | collective-permute-start | bytes 1990664 | tf_op jit(solution)/shard_map/ppermute | solution.py:159
  605.9 39.4 %collective-permute-start.56 = (bf16[192,3584]{1,0:T(8,128)(2,1)S(1)}, bf16[192,3584]{1,0:T(8,128)(2,1)S(1)}, u32[]{:S(2)}, u32[]{:S(2)}) collective-permute-start(bf16[192,3584]{1,0:T(8,128)(2,1)S(1)} %get-tuple-element.27), channel_id=1, source_target_pairs={{8,0},{12,4},{16,8},{20,12},{24,16},{28,20},{9,1},{13,5},{17,9},{2... | collective-permute-start | bytes 4128776 | tf_op jit(solution)/shard_map/ppermute | solution.py:159
  607.2 38.1 %collective-permute-start.53 = (bf16[192,3584]{1,0:T(8,128)(2,1)S(1)}, bf16[192,3584]{1,0:T(8,128)(2,1)S(1)}, u32[]{:S(2)}, u32[]{:S(2)}) collective-permute-start(bf16[192,3584]{1,0:T(8,128)(2,1)S(1)} %get-tuple-element.26), channel_id=1, source_target_pairs={{0,8},{4,12},{8,16},{12,20},{16,24},{20,28},{1,9},{5,13},{9,17},{1... | collective-permute-start | bytes 4128776 | tf_op jit(solution)/shard_map/ppermute | solution.py:159
  651.2 22.8 %collective-permute-start.46 = (bf16[2,2,48,1280]{3,2,1,0:T(8,128)(2,1)}, bf16[2,2,48,1280]{3,2,1,0:T(8,128)(2,1)}, u32[]{:S(2)}, u32[]{:S(2)}) collective-permute-start(bf16[2,2,48,1280]{3,2,1,0:T(8,128)(2,1)} %pad_maximum_fusion.22), channel_id=1, source_target_pairs={{0,2},{1,3},{2,0},{3,1},{4,6},{5,7},{6,4},{7,5},{8,10},{9,11},{10,... | collective-permute-start | bytes 1474568 | tf_op jit(solution)/shard_map/ppermute | solution.py:169
  (77 other events, 842.1 us)
Sparse Core Ops, SparseCore 0:
  26.7 57.2 all-gather.6
  85.5 119.6 all-gather.8
  257.5 51.2 all-gather.10
  310.2 41.9 all-gather.12

commit v4 on v3

--- a/solution.py
+++ b/solution.py
@@ -26,19 +26,12 @@
         jnp.float32(rope_base), -2.0 * jnp.arange(half_dim, dtype=jnp.float32) / head_dim
     )
     angles = position.astype(jnp.float32)[:, None] * inverse_freq[None, :]
-    return (jnp.cos(angles), jnp.sin(angles))
-
-
-def rotate(values, cosine, sine_part, head_count):
-    row_count = values.shape[0]
-    halves = values.reshape(row_count, head_count, 2, -1)
-    lower_half = halves[:, :, 0, :]
-    upper_half = halves[:, :, 1, :]
-    cos_wide = cosine[:, None, :]
-    sin_wide = sine_part[:, None, :]
-    new_lower = lower_half * cos_wide - upper_half * sin_wide
-    new_upper = upper_half * cos_wide + lower_half * sin_wide
-    return jnp.stack([new_lower, new_upper], axis=2).reshape(row_count, -1)
+    cosine, sine = jnp.cos(angles), jnp.sin(angles)
+    return (jnp.concatenate([cosine, cosine], axis=1), jnp.concatenate([-sine, sine], axis=1))
+
+
+def rotate_wide(values, cosine, sine):
+    return values * cosine + pltpu.roll(values, HD // 2, 1) * sine
 
 
 def lookup(small_table, indices):
@@ -46,20 +39,30 @@
     return jnp.sum(jnp.where(matches, small_table[None, :], 0), axis=1)
 
 
-def attend_kernel(count, active, piece_stream, q_ref, k_ref, v_ref, lo_ref, hi_ref, o_ref, acc_ref):
-    chunk = pl.program_id(1)
+def attend_kernel(
+    count, active, piece_stream, own_ref, sib_ref, bias_ref, cos_ref, sin_ref, k_ref, v_ref, lo_ref, hi_ref, o_ref, acc_ref
+):
+    slot = pl.program_id(1)
     piece_len = k_ref.shape[0] // piece_stream.shape[0]
-    rows = q_ref.shape[1]
-    per_kv = q_ref.shape[2] // HD
+    rows, wide = own_ref.shape
+    per_kv = wide // HD
     scale = 1.0 / math.sqrt(HD)
-    q = jnp.concatenate([q_ref[0, :, i * HD : (i + 1) * HD] for i in range(per_kv)], axis=0)
+    cosine, sine = cos_ref[...], sin_ref[...]
+    query = own_ref[...] + sib_ref[...] + bias_ref[...]
+    q = jnp.concatenate(
+        [
+            rotate_wide(query[:, i * HD : (i + 1) * HD], cosine, sine).astype(BF16)
+            for i in range(per_kv)
+        ],
+        axis=0,
+    )
     lo = lo_ref[0]
     hi = hi_ref[0]
     acc_ref[...] = jnp.zeros_like(acc_ref)
 
     def step(i, carry):
         top, total = carry
-        piece = active[chunk, i]
+        piece = active[slot, i]
         first = pl.multiple_of(piece * piece_len, piece_len)
         k = k_ref[pl.ds(first, piece_len), :]
         v = v_ref[pl.ds(first, piece_len), :]
@@ -76,14 +79,16 @@
 
     top = jnp.full((1, q.shape[0]), start_top, F32)
     total = jnp.zeros((1, q.shape[0]), F32)
-    top, total = lax.fori_loop(0, count[chunk], step, (top, total))
+    top, total = lax.fori_loop(0, count[slot], step, (top, total))
     out = (acc_ref[...] / total).T.astype(BF16)
     for i in range(per_kv):
-        o_ref[0, :, i * HD : (i + 1) * HD] = out[i * rows : (i + 1) * rows]
-
-
-def attend(query, kv_rows, lo, hi, piece_stream, kv_heads):
-    chunks, rows, width = query.shape
+        o_ref[:, i * HD : (i + 1) * HD] = out[i * rows : (i + 1) * rows]
+
+
+def attend(query, query_sib, bias, cosine, sine, kv_rows, lo, hi, piece_stream, kv_heads):
+    rows, width = query_sib.shape
+    slots = PIECES_DEV
+    lo, hi = lo.reshape(slots, -1), hi.reshape(slots, -1)
     per_kv = width // (kv_heads * HD)
     keys = kv_rows.shape[0]
     pieces = piece_stream.shape[0]
@@ -100,24 +105,41 @@
     count = jnp.sum(touch, axis=1).astype(jnp.int32)
     lo_wide = jnp.tile(lo, (1, per_kv))[:, None, :]
     hi_wide = jnp.tile(hi, (1, per_kv))[:, None, :]
+    tile = (piece_len, per_kv * HD)
     return pl.pallas_call(
         attend_kernel,
         grid_spec=pltpu.PrefetchScalarGridSpec(
             num_scalar_prefetch=3,
-            grid=(kv_heads, chunks),
+            grid=(kv_heads, slots),
             in_specs=[
-                pl.BlockSpec((1, rows, per_kv * HD), lambda g, h, *_: (h, 0, g)),
+                pl.BlockSpec(tile, lambda g, h, *_: (h, g)),
+                pl.BlockSpec(tile, lambda g, h, *_: (h, g)),
+                pl.BlockSpec((1, per_kv * HD), lambda g, h, *_: (0, g)),
+                pl.BlockSpec((piece_len, HD), lambda g, h, *_: (h, 0)),
+                pl.BlockSpec((piece_len, HD), lambda g, h, *_: (h, 0)),
                 pl.BlockSpec((keys, HD), lambda g, h, *_: (0, 2 * g)),
                 pl.BlockSpec((keys, HD), lambda g, h, *_: (0, 2 * g + 1)),
-                pl.BlockSpec((1, 1, rows * per_kv), lambda g, h, *_: (h, 0, 0)),
-                pl.BlockSpec((1, 1, rows * per_kv), lambda g, h, *_: (h, 0, 0)),
+                pl.BlockSpec((1, 1, piece_len * per_kv), lambda g, h, *_: (h, 0, 0)),
+                pl.BlockSpec((1, 1, piece_len * per_kv), lambda g, h, *_: (h, 0, 0)),
             ],
-            out_specs=pl.BlockSpec((1, rows, per_kv * HD), lambda g, h, *_: (h, 0, g)),
-            scratch_shapes=[pltpu.VMEM((HD, rows * per_kv), F32)],
+            out_specs=pl.BlockSpec(tile, lambda g, h, *_: (h, g)),
+            scratch_shapes=[pltpu.VMEM((HD, piece_len * per_kv), F32)],
         ),
-        out_shape=jax.ShapeDtypeStruct(query.shape, BF16),
+        out_shape=jax.ShapeDtypeStruct((rows, width), BF16),
         compiler_params=pltpu.CompilerParams(vmem_limit_bytes=32 * 2**20),
-    )(count, active, piece_stream, query, kv_rows, kv_rows, lo_wide, hi_wide)
+    )(count, active, piece_stream, query, query_sib, bias, cosine, sine, kv_rows, kv_rows, lo_wide, hi_wide)
+
+
+def join_kernel(own_ref, sib_ref, bias_ref, cos_ref, sin_ref, o_ref):
+    rows, wide = o_ref.shape
+    heads = wide // (2 * HD)
+    cosine, sine = cos_ref[...], sin_ref[...]
+    kv = own_ref[:rows, :] + sib_ref[...] + bias_ref[...]
+    for g in range(heads):
+        key = rotate_wide(kv[:, g * HD : (g + 1) * HD], cosine, sine)
+        o_ref[:, 2 * g * HD : (2 * g + 1) * HD] = key.astype(BF16)
+        value = kv[:, (heads + g) * HD : (heads + g + 1) * HD]
+        o_ref[:, (2 * g + 1) * HD : (2 * g + 2) * HD] = value.astype(BF16)
 
 
 def shards(
@@ -251,23 +273,13 @@
             lax.dynamic_slice_in_dim(value_bias, kv_first, kv_cols, 0),
         ]
     ).astype(F32)
+    kv_weight, (gate_weight, up_weight, out_weight, down_weight, layer_input) = after(
+        kv_weight, (gate_weight, up_weight, out_weight, down_weight, layer_input)
+    )
     kv_weight = line_collect(kv_weight)
     q_weight = line_collect(query_weight)
 
-    relative = [mlp_rank ^ j for j in range(mlp_count)]
-
-    def regroup(x):
-        parts = x.reshape((mlp_count, share) + x.shape[1:])
-        parts = jnp.stack([lax.dynamic_index_in_dim(parts, r, 0, False) for r in relative], axis=0)
-        parts = parts.reshape((mlp_count, chunks, sub) + x.shape[1:])
-        return jnp.swapaxes(parts, 0, 1).reshape(x.shape)
-
-    def ungroup(x):
-        parts = jnp.swapaxes(x.reshape((chunks, mlp_count, sub) + x.shape[1:]), 0, 1)
-        parts = jnp.stack([lax.dynamic_index_in_dim(parts, r, 0, False) for r in relative], axis=0)
-        return parts.reshape(x.shape)
-
-    x = regroup(layer_input).astype(F32)
+    x = layer_input.astype(F32)
     mean_sq = jnp.mean(x * x, axis=-1, keepdims=True)
     normed = (x * lax.rsqrt(mean_sq + norm_eps) * attention_gain.astype(F32)).astype(BF16)
     even = jnp.concatenate([normed[:, CORES * z * ds : (CORES * z + 1) * ds] for z in range(planes)], axis=1)
@@ -297,27 +309,37 @@
         (both, glu_weight, out_wide, down_wide)
     )
 
-    row_ids = seq_rank * rows + regroup(jnp.arange(rows, dtype=jnp.int32))
+    row_ids = seq_rank * rows + jnp.arange(rows, dtype=jnp.int32)
     stream = lookup(piece_order, row_ids // piece_len) * piece_len + row_ids % piece_len
     doc_ends = jnp.cumsum(doc_lengths)
     segment = jnp.sum((stream[:, None] >= doc_ends[None, :]).astype(jnp.int32), axis=1)
     doc_first = lookup(doc_ends - doc_lengths, segment)
-    cosine, sine_part = rope_tables(stream - doc_first, HD)
-
-    def project(weight, bias):
-        total = jnp.dot(both, weight, preferred_element_type=F32)
-        return total[:rows] + sibling(total[rows:]) + bias
+    cosine, sine = rope_tables(stream - doc_first, HD)
 
     kv_heads = kv_cols // HD
-    query_heads = query_weight.shape[1] // HD
-    kv = project(kv_weight, kv_bias)
-    key_rot = rotate(kv[:, :kv_cols], cosine, sine_part, kv_heads).astype(BF16)
-    value_b = kv[:, kv_cols:].astype(BF16)
-    joined = jnp.stack(
-        [key_rot.reshape(rows, kv_heads, HD), value_b.reshape(rows, kv_heads, HD)], axis=2
-    ).reshape(rows, 2 * kv_cols)
-    core_rows = jnp.concatenate(line_gather(ungroup(joined)), axis=0)
-    layer_input, core_rows = after(layer_input, core_rows)
+    kv = jnp.dot(both, kv_weight, preferred_element_type=F32)
+    joined = pl.pallas_call(
+        join_kernel, out_shape=jax.ShapeDtypeStruct((rows, 2 * kv_cols), BF16)
+    )(kv, sibling(kv[rows:]), kv_bias[None, :], cosine, sine)
+    core_rows = jnp.concatenate(line_gather(joined), axis=0)
+    kv_rows = jnp.concatenate([core_rows, sibling(core_rows)], axis=0)
+    offsets = (plane - jnp.arange(planes, dtype=jnp.int32)) % planes
+    slots = jnp.concatenate([offsets * CORES + core, offsets * CORES + 1 - core])
+    slots = (slots[:, None] * PIECES_DEV + jnp.arange(PIECES_DEV, dtype=jnp.int32)).reshape(-1)
+    piece_stream = lookup(piece_order, slots)
+
+    own_cols = KVH * HD // mlp_count
+    cache_width = 2 * own_cols
+    offset = mlp_rank % max(1, HD // own_cols) * cache_width
+    pieces = jnp.arange(piece_order.shape[0], dtype=jnp.int32)
+    pages = []
+    for p in range(PIECES_DEV):
+        stream_piece = jnp.sum(jnp.where(cache_page == seq_rank * PIECES_DEV + p, pieces, 0))
+        source = jnp.sum(jnp.where(piece_stream == stream_piece, pieces, 0))
+        pages.append(lax.dynamic_slice(kv_rows, (source * piece_len, offset), (piece_len, cache_width)))
+    kv_cache = jnp.concatenate(pages, axis=0)
+
+    layer_input, q_weight = after(layer_input, q_weight)
     own_share = lax.dynamic_slice_in_dim(layer_input, mlp_rank * share, share, 0)
     lane_parts = []
     for k in range(planes):
@@ -328,37 +350,25 @@
     lane_input = swap_halves(jnp.stack(lane_parts, axis=0))
     lane_input = lane_input.reshape(planes, chunks, sub, dz)
     gain_lane = swap_halves(lax.dynamic_slice_in_dim(feedforward_gain, plane * dz, dz, 0)).astype(F32)
-    kv_rows = jnp.concatenate([core_rows, sibling(core_rows)], axis=0)
-    offsets = (plane - jnp.arange(planes, dtype=jnp.int32)) % planes
-    slots = jnp.concatenate([offsets * CORES + core, offsets * CORES + 1 - core])
-    slots = (slots[:, None] * PIECES_DEV + jnp.arange(PIECES_DEV, dtype=jnp.int32)).reshape(-1)
-    piece_stream = lookup(piece_order, slots)
-
-    own_cols = KVH * HD // mlp_count
-    cache_width = 2 * own_cols
-    offset = mlp_rank % max(1, HD // own_cols) * cache_width
-    pieces = jnp.arange(piece_order.shape[0], dtype=jnp.int32)
-    pages = []
-    for p in range(PIECES_DEV):
-        stream_piece = jnp.sum(jnp.where(cache_page == seq_rank * PIECES_DEV + p, pieces, 0))
-        source = jnp.sum(jnp.where(piece_stream == stream_piece, pieces, 0))
-        pages.append(lax.dynamic_slice(kv_rows, (source * piece_len, offset), (piece_len, cache_width)))
-    kv_cache = jnp.concatenate(pages, axis=0)
-
-    query = project(q_weight, query_bias.astype(F32))
-    query_rot = rotate(query, cosine, sine_part, query_heads).astype(BF16)
+    query = jnp.dot(both, q_weight, preferred_element_type=F32)
+    query_sib, lane_input = after(sibling(query[rows:]), lane_input)
     mixed = attend(
-        query_rot.reshape(chunks, crows, query_heads * HD),
-        kv_rows,
-        doc_first.reshape(chunks, crows),
-        stream.reshape(chunks, crows),
-        piece_stream,
-        kv_heads,
-    )
-
-    collected = [line_collect(mixed[h]) for h in range(chunks)]
-    residuals, parts = [], []
-    for h in range(chunks):
+        query, query_sib, query_bias.astype(F32)[None, :], cosine, sine, kv_rows, doc_first, stream, piece_stream, kv_heads
+    )
+    chunked = [
+        jnp.concatenate(
+            [
+                lax.dynamic_slice_in_dim(mixed, (mlp_rank ^ j) * share + h * sub, sub, 0)
+                for j in range(mlp_count)
+            ],
+            axis=0,
+        )
+        for h in range(chunks)
+    ]
+
+    collected = [line_collect(v) for v in chunked]
+
+    def attn_sum(h):
         heads = jnp.concatenate(
             [
                 lax.dynamic_slice_in_dim(collected[h], (plane - k) % planes * crows, crows, 0)
@@ -368,25 +378,18 @@
         )
         attn = jnp.dot(heads, out_wide, preferred_element_type=F32).astype(BF16)
         attn = mlp_scatter(attn.reshape(planes, mlp_count, sub, dz))
-        residual = lane_input[:, h].astype(F32) + attn
+        return lane_input[:, h].astype(F32) + attn
+
+    def contract(residual):
         square = residual * residual
         square = sum(square[..., i : i + HD] for i in range(0, dz, HD))
         lane = jnp.concatenate([(residual * gain_lane).astype(BF16), square.astype(BF16)], axis=-1)
         lane = mlp_gather(lane).reshape(planes * crows, dz + HD)
         part = jnp.dot(lane, glu_weight, preferred_element_type=F32)
-        parts.append(part.astype(BF16).reshape(planes, crows, 2 * units + HD))
-        residuals.append(residual)
-
-    carried = [None] * chunks
-    for h in range(chunks):
-        for t in range(1, planes):
-            if t == planes - 1 and h + 1 < chunks:
-                parts[h + 1], carried[h] = after(parts[h + 1], carried[h])
-            carried[h] = scatter_step(parts[h], carried[h], t)
-
-    finals = []
-    for h in range(chunks):
-        act = parts[h][0].astype(F32) + carried[h][0].astype(F32) + carried[h][1].astype(F32)
+        return part.astype(BF16).reshape(planes, crows, 2 * units + HD)
+
+    def activate(part, carried):
+        act = part[0].astype(F32) + carried[0].astype(F32) + carried[1].astype(F32)
         square = jnp.sum(act[:, 2 * units :], axis=1, keepdims=True)
         act = act * lax.rsqrt(square / width + norm_eps)
         hidden = jax.nn.silu(act[:, :whole]) * act[:, whole : 2 * whole]
@@ -396,7 +399,55 @@
             hidden = jnp.concatenate(
                 [hidden, jax.nn.silu(last[:, :edge]) * last[:, edge:]], axis=1
             )
-        hidden = jnp.concatenate(line_gather(hidden.astype(BF16)), axis=0)
+        return hidden.astype(BF16)
+
+    steps = planes - 1
+    delay = max(1, steps - 1)
+    residuals, parts = [None] * chunks, [None] * chunks
+    carried, states = [None] * chunks, [None] * chunks
+    residuals[0] = attn_sum(0)
+    parts[0] = contract(residuals[0])
+    if chunks > 1:
+        parts[0], collected[1] = after(parts[0], collected[1])
+    for g in range(1, 2 * steps + (chunks - 1) * delay + 1):
+        for h in range(chunks):
+            t = g - h * delay
+            if 1 <= t <= steps:
+                carried[h] = scatter_step(parts[h], carried[h], t)
+            elif steps < t <= 2 * steps:
+                if t == steps + 1:
+                    hidden = activate(parts[h], carried[h])
+                    states[h] = ([hidden], [hidden])
+                gather_step(states[h], t - steps)
+        if chunks > 1:
+            flight = []
+            for h in range(chunks):
+                t = g - h * delay
+                if 1 <= t <= steps:
+                    flight.append(carried[h])
+                elif steps < t <= 2 * steps:
+                    flight.append((states[h][0][-1], states[h][1][-1]))
+            if g == 1:
+                residuals[1] = attn_sum(1)
+                flight.append(residuals[1])
+            if g == delay:
+                parts[1] = contract(residuals[1])
+                flight.append(parts[1])
+            flight = list(lax.optimization_barrier(tuple(flight)))
+            if g == delay:
+                parts[1] = flight.pop()
+            if g == 1:
+                residuals[1] = flight.pop()
+            for h in range(chunks):
+                t = g - h * delay
+                if 1 <= t <= steps:
+                    carried[h] = flight.pop(0)
+                elif steps < t <= 2 * steps:
+                    states[h][0][-1], states[h][1][-1] = flight.pop(0)
+
+    finals = []
+    for h in range(chunks):
+        hidden = jnp.concatenate(gather_slots(states[h]), axis=0)
         down = jnp.dot(hidden, down_wide, preferred_element_type=F32).astype(BF16)
         down = mlp_scatter(down.reshape(planes, mlp_count, sub, dz))
         final = (residuals[h] + down).astype(BF16)

time: 758 us -> 721 us (0.951)
  waiting for transfers between devices: 420 us -> 392 us
  starting transfers between devices: 103 us -> 118 us
  local copies, waits for them, and re-layouts: 43.5 us -> 29.7 us
  other arithmetic: 98.5 us -> 88.4 us
    ppermute x39, waiting for transfers between devices: 323 us -> 286 us  [move(): lax.ppermute(x, 'seq', [(a * CORES + e, b * CORES + e) for a, b in pairs...]
    convert_element_type x3 -> x0, local copies, waits for them, and re-layouts: 11 us -> none  [the longest x2 7.41 us: shards(): query_rot = rotate(query, cosine, sine_part, query_heads).astype(BF16)]
    ppermute x24, starting transfers between devices: 25.2 us -> 34.9 us  [partner(): return lax.ppermute(x, 'mlp', [(a, a ^ bit) for a in range(mlp_count)])]
    ppermute x24, waiting for transfers between devices: 47.8 us -> 56.2 us  [partner(): return lax.ppermute(x, 'mlp', [(a, a ^ bit) for a in range(mlp_count)])]
  transfers between devices with their start and end apart: 74 -> 74, of which waited for: 40 -> 36; matrix products, arithmetic and copies ran while one was open for 20% -> 18% of each run, Pallas kernels for 0% -> 0%
where the time goes in v4:
time: 721 us; the launch traced here: 709 us
  waiting for transfers between devices  392 us (54%)
  starting transfers between devices  118 us (16%)
  other arithmetic  88.4 us (12%)
  matrix products  50.1 us (7%)
  local copies, waits for them, and re-layouts  29.7 us (4%)
  between operations  17.1 us (2%)
  Pallas kernels  13.7 us (2%)
    ppermute x39, waiting for transfers between devices, move(): lax.ppermute(x, 'seq', [(a * CORES + e, b * CORES + e) for a, b in pairs...  286 us
    ppermute x39, starting transfers between devices, move(): lax.ppermute(x, 'seq', [(a * CORES + e, b * CORES + e) for a, b in pairs...  81 us
    ppermute x24, waiting for transfers between devices, partner(): return lax.ppermute(x, 'mlp', [(a, a ^ bit) for a in range(mlp_count)])  56.2 us
    all_gather x4, waiting for transfers between devices, line_collect(): return lax.all_gather(x, 'seq', axis=0, tiled=True, axis_index_groups=lines)  46.8 us
    ppermute x24, starting transfers between devices, partner(): return lax.ppermute(x, 'mlp', [(a, a ^ bit) for a in range(mlp_count)])  34.9 us
    dot_general x2, matrix products, contract(): part = jnp.dot(lane, glu_weight, preferred_element_type=F32)  25.7 us
    concatenate x1, other arithmetic, shards(): jnp.concatenate([gate_weight[:, :whole], up_weight[:, :whole], gate_weigh...  14.5 us
  transfers between devices with their start and end apart: 74, of which 36 were waited for; matrix products, arithmetic and copies ran while one was open for 18% of the time, Pallas kernels for 0%

profile of v4, /device:TPU:0, one launch (start us, length us, event | category | flops | bytes accessed | tf_op | source)
XLA Modules:
  0.0 709.0 jit_solution(5723853510266647431)
XLA Ops:
  11.6 14.5 %pad_maximum_fusion.1 = bf16[640,3456]{0,1:T(8,128)(2,1)} fusion(bf16[640,64]{0,1:T(8,128)(2,1)S(1)} %slice-done.2, bf16[640,64]{0,1:T(8,128)(2,1)S(1)} %slice-done.4, bf16[640,1664]{0,1:T(8,128)(2,1)S(1)} %slice-done.3, bf16[640,1664]{0,1:T(8,128)(2,1)S(1)} %slice-done.5), kind=kLoop, calls=%fused_computation.12 | loop fusion | flops 17694720 | bytes 8847360 | tf_op jit(solution)/shard_map/concatenate | solution.py:293
  53.0 10.4 %fusion.2 = bf16[1280,3584]{0,1:T(8,128)(2,1)} fusion(bf16[640,3456]{0,1:T(8,128)(2,1)} %collective-permute-done.1, bf16[640,3456]{0,1:T(8,128)(2,1)} %pad_maximum_fusion.1), kind=kLoop, calls=%fused_computation.6 | loop fusion | flops 32112640 | bytes 18022400 | tf_op jit(solution)/shard_map/concatenate | solution.py:300
  63.5 8.2 %pad_maximum_fusion = bf16[1408,3584]{0,1:T(8,128)(2,1)} fusion(bf16[128,3584]{0,1:T(8,128)(2,1)S(1)} %pad_convert_fusion, bf16[1280,3584]{0,1:T(8,128)(2,1)} %fusion.2), kind=kLoop, calls=%fused_computation.3 | loop fusion | flops 20185088 | bytes 20185088 | tf_op jit(solution)/shard_map/concatenate | solution.py:298
  71.7 5.2 fusion.105.own_ref
  87.4 6.5 collective-permute-start.9
  93.8 21.6 %collective-permute-done.10 = bf16[384,512]{1,0:T(8,128)(2,1)S(1)} collective-permute-done((bf16[384,512]{1,0:T(8,128)(2,1)}, bf16[384,512]{1,0:T(8,128)(2,1)S(1)}, u32[]{:S(2)}, u32[]{:S(2)}) %collective-permute-start.10) | collective-permute-done | bytes 393248 | tf_op jit(solution)/shard_map/ppermute | solution.py:181
  120.2 22.4 %collective-permute-done.11 = bf16[384,512]{1,0:T(8,128)(2,1)} collective-permute-done((bf16[384,512]{1,0:T(8,128)(2,1)S(1)}, bf16[384,512]{1,0:T(8,128)(2,1)}, u32[]{:S(2)}, u32[]{:S(2)}) %collective-permute-start.11) | collective-permute-done | bytes 393248 | tf_op jit(solution)/shard_map/ppermute | solution.py:181
  146.7 42.3 %collective-permute-done.12 = bf16[384,512]{1,0:T(8,128)(2,1)} collective-permute-done((bf16[384,512]{1,0:T(8,128)(2,1)}, bf16[384,512]{1,0:T(8,128)(2,1)}, u32[]{:S(2)}, u32[]{:S(2)}) %collective-permute-start.12) | collective-permute-done | bytes 393248 | tf_op jit(solution)/shard_map/ppermute | solution.py:181
  192.8 7.3 %fusion.104.own_ref = f32[768,1024]{1,0:T(8,128)S(1)} fusion(bf16[768,2560]{1,0:T(8,128)(2,1)} %pad_maximum_fusion.3, bf16[2560,1024]{1,0:T(8,128)(2,1)} %all-gather.5.cloned.1.call-done), kind=kOutput, calls=%fused_computation.351 | convolution fusion | flops 4026531840 | bytes 12320768 | tf_op jit(solution)/shard_map/dot_general | solution.py:353
  213.9 14.7 %collective-permute-done.6 = bf16[96,1280]{1,0:T(8,128)(2,1)S(1)} collective-permute-done((bf16[96,1280]{1,0:T(8,128)(2,1)S(1)}, bf16[96,1280]{1,0:T(8,128)(2,1)S(1)}, u32[]{:S(2)}, u32[]{:S(2)}) %collective-permute-start.6) | collective-permute-done | bytes 245792 | tf_op jit(solution)/shard_map/ppermute | solution.py:181
  231.0 11.0 %shard_map.168 = bf16[384,1024]{1,0:T(8,128)(2,1)S(1)} custom-call(s32[2]{0:T(128)S(1)} %convert_reduce_fusion.1.count, s32[2,16]{1,0:T(2,128)S(1)} %select_reduce_fusion.1.active, s32[16]{0:T(128)S(1)} %select_reduce_fusion.2.piece_stream, f32[768,1024]{1,0:T(8,128)S(1)} %copy-done.1, f32[384,1024]{1,0:T(8,128)} %collective-permute-done.4.sib_ref, ...), custom_call_target="tpu_custom_call" | custom-call | tf_op jit(solution)/shard_map/pallas_call | solution.py:109
  244.0 37.4 %all-gather.9.cloned.1.call-done = bf16[768,1024]{1,0:T(8,128)(2,1)} async-done(((bf16[192,1024]{1,0:T(8,128)(2,1)}), bf16[768,1024]{1,0:T(8,128)(2,1)}) %all-gather.9.cloned.1.call-update) | async-done | bytes 1572880 | tf_op jit(solution)/shard_map/all_gather | solution.py:256
  289.3 9.7 %collective-permute-done.18 = bf16[2,2,48,1280]{3,2,1,0:T(8,128)(2,1)S(1)} collective-permute-done((bf16[2,2,48,1280]{3,2,1,0:T(8,128)(2,1)S(1)}, bf16[2,2,48,1280]{3,2,1,0:T(8,128)(2,1)S(1)}, u32[]{:S(2)}, u32[]{:S(2)}) %collective-permute-start.18) | collective-permute-done | bytes 491552 | tf_op jit(solution)/shard_map/ppermute | solution.py:191
  320.7 6.9 collective-permute-done.23
  332.8 14.3 %convolution_convert_fusion.1 = bf16[768,3584]{1,0:T(8,128)(2,1)} fusion(bf16[768,1408]{1,0:T(8,128)(2,1)S(1)} %bitcast.422, bf16[1408,3584]{0,1:T(8,128)(2,1)} %pad_maximum_fusion), kind=kOutput, calls=%fused_computation.11 | convolution fusion | flops 7753826304 | bytes 17760256 | tf_op jit(solution)/shard_map/dot_general | solution.py:388
  347.1 9.4 %all-gather.11.cloned.1.call-done = bf16[768,1024]{1,0:T(8,128)(2,1)} async-done(((bf16[192,1024]{1,0:T(8,128)(2,1)}), bf16[768,1024]{1,0:T(8,128)(2,1)}) %all-gather.11.cloned.1.call-update) | async-done | bytes 1572880 | tf_op jit(solution)/shard_map/all_gather | solution.py:256
  367.9 6.2 collective-permute-done.28
  382.4 13.3 %collective-permute-done.24 = bf16[192,3584]{1,0:T(8,128)(2,1)S(1)} collective-permute-done((bf16[192,3584]{1,0:T(8,128)(2,1)S(1)}, bf16[192,3584]{1,0:T(8,128)(2,1)S(1)}, u32[]{:S(2)}, u32[]{:S(2)}) %collective-permute-start.24) | collective-permute-done | bytes 1376288 | tf_op jit(solution)/shard_map/ppermute | solution.py:181
  397.1 5.4 collective-permute-done.34
  415.3 11.4 %convolution_convert_fusion = bf16[768,3584]{1,0:T(8,128)(2,1)S(1)} fusion(bf16[768,1408]{1,0:T(8,128)(2,1)S(1)} %bitcast.421, bf16[1408,3584]{0,1:T(8,128)(2,1)} %pad_maximum_fusion), kind=kOutput, calls=%fused_computation.10 | convolution fusion | flops 7753826304 | bytes 17760256 | tf_op jit(solution)/shard_map/dot_general | solution.py:388
  426.7 9.1 %collective-permute-done.30 = bf16[192,3584]{1,0:T(8,128)(2,1)S(1)} collective-permute-done((bf16[192,3584]{1,0:T(8,128)(2,1)S(1)}, bf16[192,3584]{1,0:T(8,128)(2,1)S(1)}, u32[]{:S(2)}, u32[]{:S(2)}) %collective-permute-start.30) | collective-permute-done | bytes 1376288 | tf_op jit(solution)/shard_map/ppermute | solution.py:181
  436.5 8.7 %collective-permute-start.36 = (bf16[192,3584]{1,0:T(8,128)(2,1)S(1)}, bf16[192,3584]{1,0:T(8,128)(2,1)S(1)}, u32[]{:S(2)}, u32[]{:S(2)}) collective-permute-start(bf16[192,3584]{1,0:T(8,128)(2,1)S(1)} %get-tuple-element.103), channel_id=1, source_target_pairs={{0,8},{4,12},{8,16},{12,20},{16,24},{20,28},{1,9},{5,13},{9,17},{1... | collective-permute-start | bytes 4128776 | tf_op jit(solution)/shard_map/ppermute | solution.py:181
  452.1 23.6 %collective-permute-done.36 = bf16[192,3584]{1,0:T(8,128)(2,1)S(1)} collective-permute-done((bf16[192,3584]{1,0:T(8,128)(2,1)S(1)}, bf16[192,3584]{1,0:T(8,128)(2,1)S(1)}, u32[]{:S(2)}, u32[]{:S(2)}) %collective-permute-start.36) | collective-permute-done | bytes 1376288 | tf_op jit(solution)/shard_map/ppermute | solution.py:181
  475.8 23.2 %collective-permute-done.38 = bf16[192,3584]{1,0:T(8,128)(2,1)S(1)} collective-permute-done((bf16[192,3584]{1,0:T(8,128)(2,1)S(1)}, bf16[192,3584]{1,0:T(8,128)(2,1)S(1)}, u32[]{:S(2)}, u32[]{:S(2)}) %collective-permute-start.38) | collective-permute-done | bytes 1376288 | tf_op jit(solution)/shard_map/ppermute | solution.py:181
  512.0 31.3 %collective-permute-done.40 = bf16[192,1728]{1,0:T(8,128)(2,1)S(1)} collective-permute-done((bf16[192,1728]{1,0:T(8,128)(2,1)S(1)}, bf16[192,1728]{1,0:T(8,128)(2,1)S(1)}, u32[]{:S(2)}, u32[]{:S(2)}) %collective-permute-start.40) | collective-permute-done | bytes 663584 | tf_op jit(solution)/shard_map/ppermute | solution.py:181
  544.0 8.3 %collective-permute-start.46 = (bf16[192,3584]{1,0:T(8,128)(2,1)S(1)}, bf16[192,3584]{1,0:T(8,128)(2,1)S(1)}, u32[]{:S(2)}, u32[]{:S(2)}) collective-permute-start(bf16[192,3584]{1,0:T(8,128)(2,1)S(1)} %get-tuple-element.97), channel_id=1, source_target_pairs={{0,8},{4,12},{8,16},{12,20},{16,24},{20,28},{1,9},{5,13},{9,17},{1... | collective-permute-start | bytes 4128776 | tf_op jit(solution)/shard_map/ppermute | solution.py:181
  555.6 39.3 %collective-permute-done.45 = bf16[192,1728]{1,0:T(8,128)(2,1)S(1)} collective-permute-done((bf16[192,1728]{1,0:T(8,128)(2,1)S(1)}, bf16[192,1728]{1,0:T(8,128)(2,1)S(1)}, u32[]{:S(2)}, u32[]{:S(2)}) %collective-permute-start.45) | collective-permute-done | bytes 663584 | tf_op jit(solution)/shard_map/ppermute | solution.py:181
  605.1 10.7 %collective-permute-done.49 = bf16[192,1728]{1,0:T(8,128)(2,1)S(1)} collective-permute-done((bf16[192,1728]{1,0:T(8,128)(2,1)S(1)}, bf16[192,1728]{1,0:T(8,128)(2,1)S(1)}, u32[]{:S(2)}, u32[]{:S(2)}) %collective-permute-start.49) | collective-permute-done | bytes 663584 | tf_op jit(solution)/shard_map/ppermute | solution.py:181
  615.8 7.4 %collective-permute-done.51 = bf16[192,1728]{1,0:T(8,128)(2,1)S(1)} collective-permute-done((bf16[192,1728]{1,0:T(8,128)(2,1)S(1)}, bf16[192,1728]{1,0:T(8,128)(2,1)S(1)}, u32[]{:S(2)}, u32[]{:S(2)}) %collective-permute-start.51) | collective-permute-done | bytes 663584 | tf_op jit(solution)/shard_map/ppermute | solution.py:181
  640.3 5.3 collective-permute-start.55
  648.3 5.8 collective-permute-done.60
  659.0 12.7 %collective-permute-done.62 = bf16[192,1728]{1,0:T(8,128)(2,1)S(1)} collective-permute-done((bf16[192,1728]{1,0:T(8,128)(2,1)S(1)}, bf16[192,1728]{1,0:T(8,128)(2,1)S(1)}, u32[]{:S(2)}, u32[]{:S(2)}) %collective-permute-start.62) | collective-permute-done | bytes 663584 | tf_op jit(solution)/shard_map/ppermute | solution.py:181
  (399 shorter events, 228.4 us)
Async XLA Ops:
  7.2 64.5 %all-gather.7.cloned.1.call-start = ((), (), s32[]{:S(2)}) async-start(), calls=%async_computation.1 | async-start | bytes 3276800 | tf_op jit(solution)/shard_map/all_gather | solution.py:256
  9.3 183.5 %all-gather.5.cloned.1.call-start = ((), (), s32[]{:S(2)}) async-start(), calls=%async_computation | async-start | bytes 6553600 | tf_op jit(solution)/shard_map/all_gather | solution.py:256
  26.1 26.9 %collective-permute-start.1 = (bf16[640,3456]{0,1:T(8,128)(2,1)}, bf16[640,3456]{0,1:T(8,128)(2,1)}, u32[]{:S(2)}, u32[]{:S(2)}) collective-permute-start(bf16[640,3456]{0,1:T(8,128)(2,1)} %pad_maximum_fusion.1), channel_id=1, source_target_pairs={{0,4},{4,0},{8,12},{12,8},{16,20},{20,16},{24,28},{28,24},{1,5},{5... | collective-permute-start | bytes 13271048 | tf_op jit(solution)/shard_map/ppermute | solution.py:186
  35.6 245.8 %all-gather.9.cloned.1.call-start = ((), (), s32[]{:S(2)}) async-start(), calls=%async_computation.2 | async-start | bytes 1966080 | tf_op jit(solution)/shard_map/all_gather | solution.py:256
  83.7 31.7 %collective-permute-start.10 = (bf16[384,512]{1,0:T(8,128)(2,1)}, bf16[384,512]{1,0:T(8,128)(2,1)S(1)}, u32[]{:S(2)}, u32[]{:S(2)}) collective-permute-start(bf16[384,512]{1,0:T(8,128)(2,1)} %shard_map.167), channel_id=1, source_target_pairs={{8,0},{12,4},{16,8},{20,12},{24,16},{28,20},{9,1},{13,5},{17,9},{2... | collective-permute-start | bytes 1179656 | tf_op jit(solution)/shard_map/ppermute | solution.py:181
  87.4 31.4 %collective-permute-start.9 = (bf16[384,512]{1,0:T(8,128)(2,1)}, bf16[384,512]{1,0:T(8,128)(2,1)}, u32[]{:S(2)}, u32[]{:S(2)}) collective-permute-start(bf16[384,512]{1,0:T(8,128)(2,1)} %shard_map.167), channel_id=1, source_target_pairs={{0,8},{4,12},{8,16},{12,20},{16,24},{20,28},{1,9},{5,13},{9,17},{1... | collective-permute-start | bytes 1179656 | tf_op jit(solution)/shard_map/ppermute | solution.py:181
  115.5 27.2 %collective-permute-start.11 = (bf16[384,512]{1,0:T(8,128)(2,1)S(1)}, bf16[384,512]{1,0:T(8,128)(2,1)}, u32[]{:S(2)}, u32[]{:S(2)}) collective-permute-start(bf16[384,512]{1,0:T(8,128)(2,1)S(1)} %collective-permute-done.10), channel_id=1, source_target_pairs={{8,0},{12,4},{16,8},{20,12},{9,1},{13,5},{17,9},{21,13},{10,2},{14... | collective-permute-start | bytes 1179656 | tf_op jit(solution)/shard_map/ppermute | solution.py:181
  118.7 27.3 %collective-permute-start.13 = (bf16[384,512]{1,0:T(8,128)(2,1)}, bf16[384,512]{1,0:T(8,128)(2,1)}, u32[]{:S(2)}, u32[]{:S(2)}) collective-permute-start(bf16[384,512]{1,0:T(8,128)(2,1)} %collective-permute-done.9), channel_id=1, source_target_pairs={{8,16},{12,20},{16,24},{20,28},{9,17},{13,21},{17,25},{21,29},{10,... | collective-permute-start | bytes 1179656 | tf_op jit(solution)/shard_map/ppermute | solution.py:181
  142.6 46.4 %collective-permute-start.12 = (bf16[384,512]{1,0:T(8,128)(2,1)}, bf16[384,512]{1,0:T(8,128)(2,1)}, u32[]{:S(2)}, u32[]{:S(2)}) collective-permute-start(bf16[384,512]{1,0:T(8,128)(2,1)} %collective-permute-done.11), channel_id=1, source_target_pairs={{8,0},{12,4},{9,1},{13,5},{10,2},{14,6},{11,3},{15,7}} | collective-permute-start | bytes 1179656 | tf_op jit(solution)/shard_map/ppermute | solution.py:181
  146.0 45.4 %collective-permute-start.14 = (bf16[384,512]{1,0:T(8,128)(2,1)}, bf16[384,512]{1,0:T(8,128)(2,1)S(1)}, u32[]{:S(2)}, u32[]{:S(2)}) collective-permute-start(bf16[384,512]{1,0:T(8,128)(2,1)} %collective-permute-done.13), channel_id=1, source_target_pairs={{16,24},{20,28},{17,25},{21,29},{18,26},{22,30},{19,27},{23,31}} | collective-permute-start | bytes 1179656 | tf_op jit(solution)/shard_map/ppermute | solution.py:181
  203.2 26.9 %collective-permute-start.4 = (f32[384,1024]{1,0:T(8,128)}, f32[384,1024]{1,0:T(8,128)}, u32[]{:S(2)}, u32[]{:S(2)}) collective-permute-start(f32[384,1024]{1,0:T(8,128)} %slice.596), channel_id=1, source_target_pairs={{0,4},{4,0},{8,12},{12,8},{16,20},{20,16},{24,28},{28,24},{1,5},{5... | collective-permute-start | bytes 4718600 | tf_op jit(solution)/shard_map/ppermute | solution.py:186
  206.0 22.6 %collective-permute-start.6 = (bf16[96,1280]{1,0:T(8,128)(2,1)S(1)}, bf16[96,1280]{1,0:T(8,128)(2,1)S(1)}, u32[]{:S(2)}, u32[]{:S(2)}) collective-permute-start(bf16[96,1280]{1,0:T(8,128)(2,1)S(1)} %get-tuple-element.110), channel_id=1, source_target_pairs={{0,16},{4,20},{8,24},{12,28},{16,0},{20,4},{24,8},{28,12},{1,17},{... | collective-permute-start | bytes 737288 | tf_op jit(solution)/shard_map/ppermute | solution.py:181
  207.0 21.7 %collective-permute-start.5 = (bf16[96,1280]{1,0:T(8,128)(2,1)S(1)}, bf16[96,1280]{1,0:T(8,128)(2,1)S(1)}, u32[]{:S(2)}, u32[]{:S(2)}) collective-permute-start(bf16[96,1280]{1,0:T(8,128)(2,1)S(1)} %get-tuple-element.111), channel_id=1, source_target_pairs={{0,8},{4,12},{8,16},{12,20},{16,24},{20,28},{24,0},{28,4},{1,9},{5... | collective-permute-start | bytes 737288 | tf_op jit(solution)/shard_map/ppermute | solution.py:181
  243.6 112.9 %all-gather.11.cloned.1.call-start = ((), (), s32[]{:S(2)}) async-start(), calls=%async_computation.3 | async-start | bytes 1966080 | tf_op jit(solution)/shard_map/all_gather | solution.py:256
  364.5 31.1 %collective-permute-start.24 = (bf16[192,3584]{1,0:T(8,128)(2,1)S(1)}, bf16[192,3584]{1,0:T(8,128)(2,1)S(1)}, u32[]{:S(2)}, u32[]{:S(2)}) collective-permute-start(bf16[192,3584]{1,0:T(8,128)(2,1)S(1)} %get-tuple-element.107), channel_id=1, source_target_pairs={{0,8},{4,12},{1,9},{5,13},{2,10},{6,14},{3,11},{7,15}} | collective-permute-start | bytes 4128776 | tf_op jit(solution)/shard_map/ppermute | solution.py:181
  367.1 28.6 %collective-permute-start.25 = (bf16[192,3584]{1,0:T(8,128)(2,1)S(1)}, bf16[192,3584]{1,0:T(8,128)(2,1)S(1)}, u32[]{:S(2)}, u32[]{:S(2)}) collective-permute-start(bf16[192,3584]{1,0:T(8,128)(2,1)S(1)} %get-tuple-element.106), channel_id=1, source_target_pairs={{24,16},{28,20},{25,17},{29,21},{26,18},{30,22},{27,19},{31,23}} | collective-permute-start | bytes 4128776 | tf_op jit(solution)/shard_map/ppermute | solution.py:181
  406.9 29.0 %collective-permute-start.30 = (bf16[192,3584]{1,0:T(8,128)(2,1)S(1)}, bf16[192,3584]{1,0:T(8,128)(2,1)S(1)}, u32[]{:S(2)}, u32[]{:S(2)}) collective-permute-start(bf16[192,3584]{1,0:T(8,128)(2,1)S(1)} %get-tuple-element.105), channel_id=1, source_target_pairs={{0,8},{4,12},{8,16},{12,20},{1,9},{5,13},{9,17},{13,21},{2,10},{6,... | collective-permute-start | bytes 4128776 | tf_op jit(solution)/shard_map/ppermute | solution.py:181
  411.4 24.5 %collective-permute-start.31 = (bf16[192,3584]{1,0:T(8,128)(2,1)S(1)}, bf16[192,3584]{1,0:T(8,128)(2,1)S(1)}, u32[]{:S(2)}, u32[]{:S(2)}) collective-permute-start(bf16[192,3584]{1,0:T(8,128)(2,1)S(1)} %get-tuple-element.104), channel_id=1, source_target_pairs={{16,8},{20,12},{24,16},{28,20},{17,9},{21,13},{25,17},{29,21},{18,... | collective-permute-start | bytes 4128776 | tf_op jit(solution)/shard_map/ppermute | solution.py:181
  436.5 39.2 %collective-permute-start.36 = (bf16[192,3584]{1,0:T(8,128)(2,1)S(1)}, bf16[192,3584]{1,0:T(8,128)(2,1)S(1)}, u32[]{:S(2)}, u32[]{:S(2)}) collective-permute-start(bf16[192,3584]{1,0:T(8,128)(2,1)S(1)} %get-tuple-element.103), channel_id=1, source_target_pairs={{0,8},{4,12},{8,16},{12,20},{16,24},{20,28},{1,9},{5,13},{9,17},{1... | collective-permute-start | bytes 4128776 | tf_op jit(solution)/shard_map/ppermute | solution.py:181
  445.2 30.5 %collective-permute-start.37 = (bf16[192,3584]{1,0:T(8,128)(2,1)S(1)}, bf16[192,3584]{1,0:T(8,128)(2,1)S(1)}, u32[]{:S(2)}, u32[]{:S(2)}) collective-permute-start(bf16[192,3584]{1,0:T(8,128)(2,1)S(1)} %get-tuple-element.102), channel_id=1, source_target_pairs={{8,0},{12,4},{16,8},{20,12},{24,16},{28,20},{9,1},{13,5},{17,9},{2... | collective-permute-start | bytes 4128776 | tf_op jit(solution)/shard_map/ppermute | solution.py:181
  446.7 52.3 %collective-permute-start.38 = (bf16[192,3584]{1,0:T(8,128)(2,1)S(1)}, bf16[192,3584]{1,0:T(8,128)(2,1)S(1)}, u32[]{:S(2)}, u32[]{:S(2)}) collective-permute-start(bf16[192,3584]{1,0:T(8,128)(2,1)S(1)} %get-tuple-element.101), channel_id=1, source_target_pairs={{0,8},{4,12},{1,9},{5,13},{2,10},{6,14},{3,11},{7,15}} | collective-permute-start | bytes 4128776 | tf_op jit(solution)/shard_map/ppermute | solution.py:181
  451.4 47.6 %collective-permute-start.39 = (bf16[192,3584]{1,0:T(8,128)(2,1)S(1)}, bf16[192,3584]{1,0:T(8,128)(2,1)S(1)}, u32[]{:S(2)}, u32[]{:S(2)}) collective-permute-start(bf16[192,3584]{1,0:T(8,128)(2,1)S(1)} %get-tuple-element.100), channel_id=1, source_target_pairs={{24,16},{28,20},{25,17},{29,21},{26,18},{30,22},{27,19},{31,23}} | collective-permute-start | bytes 4128776 | tf_op jit(solution)/shard_map/ppermute | solution.py:181
  500.7 42.6 %collective-permute-start.42 = (bf16[192,3584]{1,0:T(8,128)(2,1)S(1)}, bf16[192,3584]{1,0:T(8,128)(2,1)S(1)}, u32[]{:S(2)}, u32[]{:S(2)}) collective-permute-start(bf16[192,3584]{1,0:T(8,128)(2,1)S(1)} %get-tuple-element.99), channel_id=1, source_target_pairs={{0,8},{4,12},{8,16},{12,20},{1,9},{5,13},{9,17},{13,21},{2,10},{6,... | collective-permute-start | bytes 4128776 | tf_op jit(solution)/shard_map/ppermute | solution.py:181
  505.2 38.1 %collective-permute-start.43 = (bf16[192,3584]{1,0:T(8,128)(2,1)S(1)}, bf16[192,3584]{1,0:T(8,128)(2,1)S(1)}, u32[]{:S(2)}, u32[]{:S(2)}) collective-permute-start(bf16[192,3584]{1,0:T(8,128)(2,1)S(1)} %get-tuple-element.98), channel_id=1, source_target_pairs={{16,8},{20,12},{24,16},{28,20},{17,9},{21,13},{25,17},{29,21},{18,... | collective-permute-start | bytes 4128776 | tf_op jit(solution)/shard_map/ppermute | solution.py:181
  506.4 36.9 %collective-permute-start.40 = (bf16[192,1728]{1,0:T(8,128)(2,1)S(1)}, bf16[192,1728]{1,0:T(8,128)(2,1)S(1)}, u32[]{:S(2)}, u32[]{:S(2)}) collective-permute-start(bf16[192,1728]{1,0:T(8,128)(2,1)S(1)} %pad_maximum_fusion.9), channel_id=1, source_target_pairs={{0,8},{4,12},{8,16},{12,20},{16,24},{20,28},{1,9},{5,13},{9,17},{1... | collective-permute-start | bytes 1990664 | tf_op jit(solution)/shard_map/ppermute | solution.py:181
  510.7 32.6 %collective-permute-start.41 = (bf16[192,1728]{1,0:T(8,128)(2,1)S(1)}, bf16[192,1728]{1,0:T(8,128)(2,1)S(1)}, u32[]{:S(2)}, u32[]{:S(2)}) collective-permute-start(bf16[192,1728]{1,0:T(8,128)(2,1)S(1)} %pad_maximum_fusion.9), channel_id=1, source_target_pairs={{8,0},{12,4},{16,8},{20,12},{24,16},{28,20},{9,1},{13,5},{17,9},{2... | collective-permute-start | bytes 1990664 | tf_op jit(solution)/shard_map/ppermute | solution.py:181
  544.0 50.9 %collective-permute-start.46 = (bf16[192,3584]{1,0:T(8,128)(2,1)S(1)}, bf16[192,3584]{1,0:T(8,128)(2,1)S(1)}, u32[]{:S(2)}, u32[]{:S(2)}) collective-permute-start(bf16[192,3584]{1,0:T(8,128)(2,1)S(1)} %get-tuple-element.97), channel_id=1, source_target_pairs={{0,8},{4,12},{8,16},{12,20},{16,24},{20,28},{1,9},{5,13},{9,17},{1... | collective-permute-start | bytes 4128776 | tf_op jit(solution)/shard_map/ppermute | solution.py:181
  552.3 42.7 %collective-permute-start.47 = (bf16[192,3584]{1,0:T(8,128)(2,1)S(1)}, bf16[192,3584]{1,0:T(8,128)(2,1)S(1)}, u32[]{:S(2)}, u32[]{:S(2)}) collective-permute-start(bf16[192,3584]{1,0:T(8,128)(2,1)S(1)} %get-tuple-element.96), channel_id=1, source_target_pairs={{8,0},{12,4},{16,8},{20,12},{24,16},{28,20},{9,1},{13,5},{17,9},{2... | collective-permute-start | bytes 4128776 | tf_op jit(solution)/shard_map/ppermute | solution.py:181
  554.3 40.7 %collective-permute-start.45 = (bf16[192,1728]{1,0:T(8,128)(2,1)S(1)}, bf16[192,1728]{1,0:T(8,128)(2,1)S(1)}, u32[]{:S(2)}, u32[]{:S(2)}) collective-permute-start(bf16[192,1728]{1,0:T(8,128)(2,1)S(1)} %collective-permute-done.41), channel_id=1, source_target_pairs={{8,0},{12,4},{16,8},{20,12},{9,1},{13,5},{17,9},{21,13},{10,2},{14... | collective-permute-start | bytes 1990664 | tf_op jit(solution)/shard_map/ppermute | solution.py:181
  603.3 19.8 %collective-permute-start.51 = (bf16[192,1728]{1,0:T(8,128)(2,1)S(1)}, bf16[192,1728]{1,0:T(8,128)(2,1)S(1)}, u32[]{:S(2)}, u32[]{:S(2)}) collective-permute-start(bf16[192,1728]{1,0:T(8,128)(2,1)S(1)} %pad_maximum_fusion.10), channel_id=1, source_target_pairs={{8,0},{12,4},{16,8},{20,12},{24,16},{28,20},{9,1},{13,5},{17,9},{2... | collective-permute-start | bytes 1990664 | tf_op jit(solution)/shard_map/ppermute | solution.py:181
  676.4 20.0 %collective-permute-start.57 = (bf16[48,1280]{1,0:T(8,128)(2,1)S(1)}, bf16[48,1280]{1,0:T(8,128)(2,1)S(1)}, u32[]{:S(2)}, u32[]{:S(2)}) collective-permute-start(bf16[48,1280]{1,0:T(8,128)(2,1)S(1)} %get-tuple-element.190), channel_id=1, source_target_pairs={{0,16},{4,20},{8,24},{12,28},{16,0},{20,4},{24,8},{28,12},{1,17},{... | collective-permute-start | bytes 368648 | tf_op jit(solution)/shard_map/ppermute | solution.py:181
  676.5 19.9 %collective-permute-start.56 = (bf16[48,1280]{1,0:T(8,128)(2,1)S(1)}, bf16[48,1280]{1,0:T(8,128)(2,1)S(1)}, u32[]{:S(2)}, u32[]{:S(2)}) collective-permute-start(bf16[48,1280]{1,0:T(8,128)(2,1)S(1)} %get-tuple-element.191), channel_id=1, source_target_pairs={{0,24},{4,28},{8,0},{12,4},{16,8},{20,12},{24,16},{28,20},{1,25},{... | collective-permute-start | bytes 368648 | tf_op jit(solution)/shard_map/ppermute | solution.py:181
  (93 other events, 941.1 us)
Sparse Core Ops, SparseCore 0:
  10.1 57.4 all-gather.6
  69.2 118.2 all-gather.4
  243.7 37.6 all-gather.8
  320.8 35.6 all-gather.10

commit v5 on v4

--- a/solution.py
+++ b/solution.py
@@ -130,6 +130,28 @@
     )(count, active, piece_stream, query, query_sib, bias, cosine, sine, kv_rows, kv_rows, lo_wide, hi_wide)
 
 
+def product_kernel(x_ref, w_ref, o_ref):
+    o_ref[...] = jnp.dot(x_ref[...], w_ref[...], preferred_element_type=F32).astype(o_ref.dtype)
+
+
+def product(x, w, out_type):
+    rows, inner = x.shape
+    cols = w.shape[1]
+    tile = next((t for t in (512, 384, 256) if cols % t == 0), cols)
+    return pl.pallas_call(
+        product_kernel,
+        grid=(cols // tile,),
+        in_specs=[
+            pl.BlockSpec((rows, inner), lambda n: (0, 0)),
+            pl.BlockSpec((inner, tile), lambda n: (0, n)),
+        ],
+        out_specs=pl.BlockSpec((rows, tile), lambda n: (0, n)),
+        out_shape=jax.ShapeDtypeStruct((rows, cols), out_type),
+        cost_estimate=pl.CostEstimate(flops=0, transcendentals=0, bytes_accessed=0),
+        compiler_params=pltpu.CompilerParams(vmem_limit_bytes=48 * 2**20),
+    )(x, w)
+
+
 def join_kernel(own_ref, sib_ref, bias_ref, cos_ref, sin_ref, o_ref):
     rows, wide = o_ref.shape
     heads = wide // (2 * HD)
@@ -211,13 +233,14 @@
             gather_step(state, t)
         return gather_slots(state)
 
-    def scatter_step(parts, carried, t):
+    def scatter_step(parts, carried, t, held=()):
         send_up, send_down = parts[t], parts[planes - t]
         if carried is not None:
             send_up, send_down = add(send_up, carried[0]), add(send_down, carried[1])
+        send_up, send_down, held = lax.optimization_barrier((send_up, send_down, held))
         up = move(send_up, [(i, i + 1) for i in range(0, min(t, planes - 1))])
         down = move(send_down, [(i, i - 1) for i in range(max(1, planes - t), planes)])
-        return (up, down)
+        return (up, down), held
 
     half = max(1, planes // 2)
     orders = [list(range(bits)), [(b + bits // 2) % bits for b in range(bits)]]
@@ -248,7 +271,7 @@
                 for i, j in enumerate(have):
                     slots[j | bit] = got[i]
             out.append(jnp.stack([slots[j] for j in range(mlp_count)], axis=1))
-        return jnp.concatenate(out, axis=0)
+        return out
 
     lines = [[z * CORES + e for z in range(planes)] for e in range(CORES)]
 
@@ -257,6 +280,18 @@
 
     def swap_halves(x):
         return jnp.where(core == 0, x, jnp.concatenate([x[..., ds:], x[..., :ds]], axis=-1))
+
+    order = []
+    for k in range(1, planes // 2 + 1):
+        order += [k] if 2 * k == planes else [k, planes - k]
+    order.append(0)
+    own_share = lax.dynamic_slice_in_dim(layer_input, mlp_rank * share, share, 0)
+    lane_parts = []
+    for k in order:
+        part = lax.dynamic_slice_in_dim(own_share, (plane + k) % planes * dz, dz, 1)
+        if k:
+            part = move(part, [(i, (i + k) % planes) for i in range(planes)])
+        lane_parts.append(part)
 
     kv_cols = max(HD, KVH * HD // mlp_count)
     kv_first = mlp_rank * KVH // mlp_count * HD
@@ -305,8 +340,10 @@
     out_wide = jnp.concatenate([out_weight, sibling(out_weight)], axis=1)
     down_wide = jnp.concatenate([down_weight, sibling(down_weight)], axis=1)
 
-    both, glu_weight, out_wide, down_wide = lax.optimization_barrier(
-        (both, glu_weight, out_wide, down_wide)
+    lane_input = swap_halves(jnp.stack(lane_parts, axis=0)).reshape(planes, chunks, sub, dz)
+    gain_lane = swap_halves(lax.dynamic_slice_in_dim(feedforward_gain, plane * dz, dz, 0)).astype(F32)
+    both, glu_weight, out_wide, down_wide, lane_input = lax.optimization_barrier(
+        (both, glu_weight, out_wide, down_wide, lane_input)
     )
 
     row_ids = seq_rank * rows + jnp.arange(rows, dtype=jnp.int32)
@@ -317,7 +354,7 @@
     cosine, sine = rope_tables(stream - doc_first, HD)
 
     kv_heads = kv_cols // HD
-    kv = jnp.dot(both, kv_weight, preferred_element_type=F32)
+    kv = product(both, kv_weight, F32)
     joined = pl.pallas_call(
         join_kernel, out_shape=jax.ShapeDtypeStruct((rows, 2 * kv_cols), BF16)
     )(kv, sibling(kv[rows:]), kv_bias[None, :], cosine, sine)
@@ -339,19 +376,8 @@
         pages.append(lax.dynamic_slice(kv_rows, (source * piece_len, offset), (piece_len, cache_width)))
     kv_cache = jnp.concatenate(pages, axis=0)
 
-    layer_input, q_weight = after(layer_input, q_weight)
-    own_share = lax.dynamic_slice_in_dim(layer_input, mlp_rank * share, share, 0)
-    lane_parts = []
-    for k in range(planes):
-        part = lax.dynamic_slice_in_dim(own_share, (plane + k) % planes * dz, dz, 1)
-        if k:
-            part = move(part, [(i, (i + k) % planes) for i in range(planes)])
-        lane_parts.append(part)
-    lane_input = swap_halves(jnp.stack(lane_parts, axis=0))
-    lane_input = lane_input.reshape(planes, chunks, sub, dz)
-    gain_lane = swap_halves(lax.dynamic_slice_in_dim(feedforward_gain, plane * dz, dz, 0)).astype(F32)
-    query = jnp.dot(both, q_weight, preferred_element_type=F32)
-    query_sib, lane_input = after(sibling(query[rows:]), lane_input)
+    query = product(both, q_weight, F32)
+    query_sib = sibling(query[rows:])
     mixed = attend(
         query, query_sib, query_bias.astype(F32)[None, :], cosine, sine, kv_rows, doc_first, stream, piece_stream, kv_heads
     )
@@ -372,21 +398,28 @@
         heads = jnp.concatenate(
             [
                 lax.dynamic_slice_in_dim(collected[h], (plane - k) % planes * crows, crows, 0)
-                for k in range(planes)
+                for k in order
             ],
             axis=0,
         )
-        attn = jnp.dot(heads, out_wide, preferred_element_type=F32).astype(BF16)
+        attn = product(heads, out_wide, BF16)
         attn = mlp_scatter(attn.reshape(planes, mlp_count, sub, dz))
         return lane_input[:, h].astype(F32) + attn
 
-    def contract(residual):
+    def spread(residual):
         square = residual * residual
         square = sum(square[..., i : i + HD] for i in range(0, dz, HD))
         lane = jnp.concatenate([(residual * gain_lane).astype(BF16), square.astype(BF16)], axis=-1)
-        lane = mlp_gather(lane).reshape(planes * crows, dz + HD)
-        part = jnp.dot(lane, glu_weight, preferred_element_type=F32)
-        return part.astype(BF16).reshape(planes, crows, 2 * units + HD)
+        return mlp_gather(lane)
+
+    def contract_half(lane):
+        part = product(lane.reshape(-1, dz + HD), glu_weight, BF16).reshape(-1, crows, 2 * units + HD)
+        return [part[i] for i in range(part.shape[0])]
+
+    def contract(lanes):
+        first = contract_half(lanes[0])
+        last, first[0] = after(lanes[1], first[0])
+        return dict(zip(order, first + contract_half(last)))
 
     def activate(part, carried):
         act = part[0].astype(F32) + carried[0].astype(F32) + carried[1].astype(F32)
@@ -401,62 +434,64 @@
             )
         return hidden.astype(BF16)
 
+    def deliver(h, down):
+        final = (residuals[h] + down).astype(BF16)
+        found = {
+            k: move(final[i], [(p, (p - k) % planes) for p in range(planes)]) if k else final[i]
+            for i, k in enumerate(order)
+        }
+        return jnp.stack([found[k] for k in range(planes)])
+
+    def project_down(state):
+        slots = gather_slots(state)
+        hidden = jnp.concatenate([slots[k] for k in order], axis=0)
+        down = product(hidden, down_wide, BF16)
+        return mlp_scatter(down.reshape(planes, mlp_count, sub, dz))
+
     steps = planes - 1
-    delay = max(1, steps - 1)
-    residuals, parts = [None] * chunks, [None] * chunks
-    carried, states = [None] * chunks, [None] * chunks
-    residuals[0] = attn_sum(0)
-    parts[0] = contract(residuals[0])
-    if chunks > 1:
-        parts[0], collected[1] = after(parts[0], collected[1])
-    for g in range(1, 2 * steps + (chunks - 1) * delay + 1):
-        for h in range(chunks):
-            t = g - h * delay
-            if 1 <= t <= steps:
-                carried[h] = scatter_step(parts[h], carried[h], t)
-            elif steps < t <= 2 * steps:
-                if t == steps + 1:
-                    hidden = activate(parts[h], carried[h])
-                    states[h] = ([hidden], [hidden])
-                gather_step(states[h], t - steps)
+    residuals = [attn_sum(0)]
+    lanes = spread(residuals[0])
+    first = contract_half(lanes[0])
+    carried, last = scatter_step(dict(zip(order, first)), None, 1, lanes[1])
+    parts = dict(zip(order, first + contract_half(last)))
+    queued = None
+    for t in range(1, steps + 1):
+        if t > 1:
+            carried, queued = scatter_step(parts, carried, t, queued)
         if chunks > 1:
-            flight = []
-            for h in range(chunks):
-                t = g - h * delay
-                if 1 <= t <= steps:
-                    flight.append(carried[h])
-                elif steps < t <= 2 * steps:
-                    flight.append((states[h][0][-1], states[h][1][-1]))
-            if g == 1:
-                residuals[1] = attn_sum(1)
-                flight.append(residuals[1])
-            if g == delay:
-                parts[1] = contract(residuals[1])
-                flight.append(parts[1])
-            flight = list(lax.optimization_barrier(tuple(flight)))
-            if g == delay:
-                parts[1] = flight.pop()
-            if g == 1:
-                residuals[1] = flight.pop()
-            for h in range(chunks):
-                t = g - h * delay
-                if 1 <= t <= steps:
-                    carried[h] = flight.pop(0)
-                elif steps < t <= 2 * steps:
-                    states[h][0][-1], states[h][1][-1] = flight.pop(0)
-
+            if t == 1:
+                collected[1], carried = after(collected[1], carried)
+            if t == min(2, steps):
+                residuals.append(attn_sum(1))
+                queued, carried = after(residuals[1], carried)
+            if t == steps:
+                queued = contract(spread(queued))
     finals = []
     for h in range(chunks):
-        hidden = jnp.concatenate(gather_slots(states[h]), axis=0)
-        down = jnp.dot(hidden, down_wide, preferred_element_type=F32).astype(BF16)
-        down = mlp_scatter(down.reshape(planes, mlp_count, sub, dz))
-        final = (residuals[h] + down).astype(BF16)
-        finals.append(
-            jnp.stack(
-                [final[0]]
-                + [move(final[k], [(i, (i - k) % planes) for i in range(planes)]) for k in range(1, planes)]
+        following = queued if h + 1 < chunks else None
+        ahead = None
+        if following is not None:
+            ahead, carried = scatter_step(following, None, 1, carried)
+        hidden = activate(parts, carried)
+        state = ([hidden], [hidden])
+        if following is None:
+            for t in range(1, steps + 1):
+                gather_step(state, t)
+            finals.append(deliver(h, project_down(state)))
+            continue
+        gather_step(state, 1)
+        gather_step(state, 2)
+        for t in range(2, steps + 1):
+            ahead, (state[0][-1], state[1][-1]) = after(ahead, (state[0][-1], state[1][-1]))
+            ahead, (state[0][-1], state[1][-1]) = scatter_step(
+                following, ahead, t, (state[0][-1], state[1][-1])
             )
-        )
+            if t < steps:
+                gather_step(state, t + 1)
+        down = project_down(state)
+        down, carried = after(down, ahead)
+        parts = following
+        finals.append(deliver(h, down))
     final = swap_halves(jnp.concatenate(finals, axis=1))
     final = lax.dynamic_slice_in_dim(
         jnp.concatenate([final, final], axis=0), (planes - plane) % planes, planes, 0

time: 721 us -> 712 us (0.988)
  Pallas kernels: 13.7 us -> 77.4 us
  matrix products: 50.1 us -> 0 us
  local copies, waits for them, and re-layouts: 29.7 us -> 52.1 us
  waiting for transfers between devices: 392 us -> 374 us
  other arithmetic: 88.4 us -> 70.9 us
    pallas_call x0 -> x10, Pallas kernels: none -> 65.5 us  [product(): pl.pallas_call(product_kernel, grid=(cols // tile,), in_specs=[pl.BlockSp...]
    dot_general x8 -> x0, matrix products: 50.1 us -> none  [the longest x2 25.7 us: contract(): part = jnp.dot(lane, glu_weight, preferred_element_type=F32)]
    ppermute x39, waiting for transfers between devices: 286 us -> 268 us  [move(): lax.ppermute(x, 'seq', [(a * CORES + e, b * CORES + e) for a, b in pairs...]
    concatenate x3 -> x5, other arithmetic: 16.4 us -> 6.41 us  [the longest x2 5.11 us: project_down(): hidden = jnp.concatenate([slots[k] for k in order], axis=0)]
    unnamed x95 -> x101, local copies, waits for them, and re-layouts: 8.01 us -> 15.5 us
    optimization_barrier x0 -> x4, local copies, waits for them, and re-layouts: none -> 7.47 us  [the longest x3 7.39 us: after(): return lax.optimization_barrier((x, dep))]
  transfers between devices with their start and end apart: 74 -> 74, of which waited for: 36 -> 41; matrix products, arithmetic and copies ran while one was open for 18% -> 12% of each run, Pallas kernels for 0% -> 7%
where the time goes in v5:
time: 712 us; the launch traced here: 703 us
  waiting for transfers between devices  374 us (53%)
  starting transfers between devices  112 us (16%)
  Pallas kernels  77.4 us (11%)
  other arithmetic  70.9 us (10%)
  local copies, waits for them, and re-layouts  52.1 us (7%)
  between operations  17.1 us (2%)
    ppermute x39, waiting for transfers between devices, move(): lax.ppermute(x, 'seq', [(a * CORES + e, b * CORES + e) for a, b in pairs...  268 us
    ppermute x39, starting transfers between devices, move(): lax.ppermute(x, 'seq', [(a * CORES + e, b * CORES + e) for a, b in pairs...  80.9 us
    pallas_call x10, Pallas kernels, product(): pl.pallas_call(product_kernel, grid=(cols // tile,), in_specs=[pl.BlockSp...  65.5 us
    ppermute x24, waiting for transfers between devices, partner(): return lax.ppermute(x, 'mlp', [(a, a ^ bit) for a in range(mlp_count)])  60 us
    all_gather x4, waiting for transfers between devices, line_collect(): return lax.all_gather(x, 'seq', axis=0, tiled=True, axis_index_groups=lines)  45.1 us
    ppermute x24, starting transfers between devices, partner(): return lax.ppermute(x, 'mlp', [(a, a ^ bit) for a in range(mlp_count)])  28.9 us
    unnamed x101, local copies, waits for them, and re-layouts  15.5 us
  transfers between devices with their start and end apart: 74, of which 41 were waited for; matrix products, arithmetic and copies ran while one was open for 12% of the time, Pallas kernels for 7%

profile of v5, /device:TPU:0, one launch (start us, length us, event | category | flops | bytes accessed | tf_op | source)
XLA Modules:
  0.0 702.8 jit_solution(4780092782762916104)
XLA Ops:
  21.5 7.0 concatenate.133
  43.1 26.0 %collective-permute-done.6 = bf16[96,1280]{1,0:T(8,128)(2,1)S(1)} collective-permute-done((bf16[96,1280]{1,0:T(8,128)(2,1)S(1)}, bf16[96,1280]{1,0:T(8,128)(2,1)S(1)}, u32[]{:S(2)}, u32[]{:S(2)}) %collective-permute-start.6) | collective-permute-done | bytes 245792 | tf_op jit(solution)/shard_map/ppermute | solution.py:203
  74.4 7.9 %collective-permute-done.5 = bf16[96,1280]{1,0:T(8,128)(2,1)S(1)} collective-permute-done((bf16[96,1280]{1,0:T(8,128)(2,1)S(1)}, bf16[96,1280]{1,0:T(8,128)(2,1)S(1)}, u32[]{:S(2)}, u32[]{:S(2)}) %collective-permute-start.5) | collective-permute-done | bytes 245792 | tf_op jit(solution)/shard_map/ppermute | solution.py:203
  84.0 8.0 %collective-permute-done.4 = bf16[96,1280]{1,0:T(8,128)(2,1)S(1)} collective-permute-done((bf16[96,1280]{1,0:T(8,128)(2,1)S(1)}, bf16[96,1280]{1,0:T(8,128)(2,1)S(1)}, u32[]{:S(2)}, u32[]{:S(2)}) %collective-permute-start.4) | collective-permute-done | bytes 245792 | tf_op jit(solution)/shard_map/ppermute | solution.py:203
  110.3 7.3 %pad_maximum_fusion.w_ref = bf16[1408,3584]{1,0:T(8,128)(2,1)} fusion(bf16[128,3584]{1,0:T(8,128)(2,1)S(1)} %pad_convert_fusion, bf16[1280,3584]{1,0:T(8,128)(2,1)S(1)} %fusion.2), kind=kLoop, calls=%fused_computation.3 | loop fusion | flops 20185088 | bytes 20185088 | tf_op jit(solution)/shard_map/concatenate | solution.py:333
  136.7 26.3 %collective-permute-done.10 = bf16[384,512]{1,0:T(8,128)(2,1)S(1)} collective-permute-done((bf16[384,512]{1,0:T(8,128)(2,1)}, bf16[384,512]{1,0:T(8,128)(2,1)S(1)}, u32[]{:S(2)}, u32[]{:S(2)}) %collective-permute-start.10) | collective-permute-done | bytes 393248 | tf_op jit(solution)/shard_map/ppermute | solution.py:203
  165.1 24.9 %collective-permute-done.11 = bf16[384,512]{1,0:T(8,128)(2,1)S(1)} collective-permute-done((bf16[384,512]{1,0:T(8,128)(2,1)S(1)}, bf16[384,512]{1,0:T(8,128)(2,1)S(1)}, u32[]{:S(2)}, u32[]{:S(2)}) %collective-permute-start.11) | collective-permute-done | bytes 393248 | tf_op jit(solution)/shard_map/ppermute | solution.py:203
  193.9 11.8 %collective-permute-done.12 = bf16[384,512]{1,0:T(8,128)(2,1)S(1)} collective-permute-done((bf16[384,512]{1,0:T(8,128)(2,1)S(1)}, bf16[384,512]{1,0:T(8,128)(2,1)S(1)}, u32[]{:S(2)}, u32[]{:S(2)}) %collective-permute-start.12) | collective-permute-done | bytes 393248 | tf_op jit(solution)/shard_map/ppermute | solution.py:203
  209.9 7.5 %shard_map.167.own_ref = f32[768,1024]{1,0:T(8,128)S(1)} custom-call(bf16[768,2560]{1,0:T(8,128)(2,1)} %pad_maximum_fusion.2.x_ref, bf16[2560,1024]{1,0:T(8,128)(2,1)} %all-gather.5.cloned.1.call-done.w_ref), custom_call_target="tpu_custom_call" | custom-call | tf_op jit(solution)/shard_map/pallas_call | solution.py:141
  227.6 9.2 %shard_map.170 = bf16[384,1024]{1,0:T(8,128)(2,1)S(1)} custom-call(s32[2]{0:T(128)S(1)} %convert_reduce_fusion.1.count, s32[2,16]{1,0:T(2,128)S(1)} %select_reduce_fusion.1.active, s32[16]{0:T(128)S(1)} %select_reduce_fusion.2.piece_stream, f32[768,1024]{1,0:T(8,128)S(1)} %copy-done.3, f32[384,1024]{1,0:T(8,128)} %collective-permute-done.7.sib_ref, ...), custom_call_target="tpu_custom_call" | custom-call | tf_op jit(solution)/shard_map/pallas_call | solution.py:109
  238.5 45.1 %all-gather.9.cloned.1.call-done = bf16[768,1024]{1,0:T(8,128)(2,1)} async-done(((bf16[192,1024]{1,0:T(8,128)(2,1)}), bf16[768,1024]{1,0:T(8,128)(2,1)}) %all-gather.9.cloned.1.call-update) | async-done | bytes 1572880 | tf_op jit(solution)/shard_map/all_gather | solution.py:279
  291.9 9.7 %collective-permute-done.18 = bf16[2,2,48,1280]{3,2,1,0:T(8,128)(2,1)S(1)} collective-permute-done((bf16[2,2,48,1280]{3,2,1,0:T(8,128)(2,1)S(1)}, bf16[2,2,48,1280]{3,2,1,0:T(8,128)(2,1)S(1)}, u32[]{:S(2)}, u32[]{:S(2)}) %collective-permute-start.18) | collective-permute-done | bytes 491552 | tf_op jit(solution)/shard_map/ppermute | solution.py:213
  320.2 13.6 %collective-permute-done.22 = bf16[1,2,48,1408]{3,2,1,0:T(8,128)(2,1)S(1)} collective-permute-done((bf16[1,2,48,1408]{3,2,1,0:T(8,128)(2,1)S(1)}, bf16[1,2,48,1408]{3,2,1,0:T(8,128)(2,1)S(1)}, u32[]{:S(2)}, u32[]{:S(2)}) %collective-permute-start.22) | collective-permute-done | bytes 270368 | tf_op jit(solution)/shard_map/ppermute | solution.py:213
  335.7 8.8 %shard_map.172 = bf16[384,3584]{1,0:T(8,128)(2,1)S(1)} custom-call(bf16[384,1408]{1,0:T(8,128)(2,1)S(1)} %bitcast.341, bf16[1408,3584]{1,0:T(8,128)(2,1)} %pad_maximum_fusion.w_ref), custom_call_target="tpu_custom_call" | custom-call | tf_op jit(solution)/shard_map/pallas_call | solution.py:141
  351.4 8.7 %shard_map.173 = bf16[384,3584]{1,0:T(8,128)(2,1)S(1)} custom-call(bf16[384,1408]{1,0:T(8,128)(2,1)S(1)} %bitcast.342, bf16[1408,3584]{1,0:T(8,128)(2,1)} %pad_maximum_fusion.w_ref), custom_call_target="tpu_custom_call" | custom-call | tf_op jit(solution)/shard_map/pallas_call | solution.py:141
  361.7 20.3 %collective-permute-done.24 = bf16[192,3584]{1,0:T(8,128)(2,1)} collective-permute-done((bf16[192,3584]{1,0:T(8,128)(2,1)}, bf16[192,3584]{1,0:T(8,128)(2,1)}, u32[]{:S(2)}, u32[]{:S(2)}) %collective-permute-start.24) | collective-permute-done | bytes 1376288 | tf_op jit(solution)/shard_map/ppermute | solution.py:203
  409.5 16.4 %collective-permute-done.30 = bf16[192,3584]{1,0:T(8,128)(2,1)S(1)} collective-permute-done((bf16[192,3584]{1,0:T(8,128)(2,1)S(1)}, bf16[192,3584]{1,0:T(8,128)(2,1)S(1)}, u32[]{:S(2)}, u32[]{:S(2)}) %collective-permute-start.30) | collective-permute-done | bytes 1376288 | tf_op jit(solution)/shard_map/ppermute | solution.py:203
  430.4 5.5 collective-permute-done.32
  439.9 8.6 %collective-permute-start.36 = (bf16[192,3584]{1,0:T(8,128)(2,1)}, bf16[192,3584]{1,0:T(8,128)(2,1)S(1)}, u32[]{:S(2)}, u32[]{:S(2)}) collective-permute-start(bf16[192,3584]{1,0:T(8,128)(2,1)} %get-tuple-element.75), channel_id=1, source_target_pairs={{0,8},{4,12},{8,16},{12,20},{16,24},{20,28},{1,9},{5,13},{9,17},{1... | collective-permute-start | bytes 4128776 | tf_op jit(solution)/shard_map/ppermute | solution.py:203
  450.2 8.7 %shard_map.175 = bf16[384,3584]{1,0:T(8,128)(2,1)S(1)} custom-call(bf16[384,1408]{1,0:T(8,128)(2,1)S(1)} %bitcast.343, bf16[1408,3584]{1,0:T(8,128)(2,1)} %pad_maximum_fusion.w_ref), custom_call_target="tpu_custom_call" | custom-call | tf_op jit(solution)/shard_map/pallas_call | solution.py:141
  459.3 12.1 %collective-permute-done.36 = bf16[192,3584]{1,0:T(8,128)(2,1)S(1)} collective-permute-done((bf16[192,3584]{1,0:T(8,128)(2,1)}, bf16[192,3584]{1,0:T(8,128)(2,1)S(1)}, u32[]{:S(2)}, u32[]{:S(2)}) %collective-permute-start.36) | collective-permute-done | bytes 1376288 | tf_op jit(solution)/shard_map/ppermute | solution.py:203
  482.1 32.9 %collective-permute-done.38 = bf16[192,1728]{1,0:T(8,128)(2,1)S(1)} collective-permute-done((bf16[192,1728]{1,0:T(8,128)(2,1)S(1)}, bf16[192,1728]{1,0:T(8,128)(2,1)S(1)}, u32[]{:S(2)}, u32[]{:S(2)}) %collective-permute-start.38) | collective-permute-done | bytes 663584 | tf_op jit(solution)/shard_map/ppermute | solution.py:203
  517.2 8.7 %shard_map.176 = bf16[384,3584]{1,0:T(8,128)(2,1)S(1)} custom-call(bf16[384,1408]{1,0:T(8,128)(2,1)S(1)} %bitcast.340, bf16[1408,3584]{1,0:T(8,128)(2,1)} %pad_maximum_fusion.w_ref), custom_call_target="tpu_custom_call" | custom-call | tf_op jit(solution)/shard_map/pallas_call | solution.py:141
  539.1 10.5 %collective-permute-done.47 = bf16[192,1728]{1,0:T(8,128)(2,1)S(1)} collective-permute-done((bf16[192,1728]{1,0:T(8,128)(2,1)}, bf16[192,1728]{1,0:T(8,128)(2,1)S(1)}, u32[]{:S(2)}, u32[]{:S(2)}) %collective-permute-start.47) | collective-permute-done | bytes 663584 | tf_op jit(solution)/shard_map/ppermute | solution.py:203
  558.3 6.2 shard_map.177
  567.2 9.2 %collective-permute-start.52 = (bf16[192,3584]{1,0:T(8,128)(2,1)S(1)}, bf16[192,3584]{1,0:T(8,128)(2,1)S(1)}, u32[]{:S(2)}, u32[]{:S(2)}) collective-permute-start(bf16[192,3584]{1,0:T(8,128)(2,1)S(1)} %add_convert_fusion.1), channel_id=1, source_target_pairs={{0,8},{4,12},{8,16},{12,20},{16,24},{20,28},{1,9},{5,13},{9,17},{1... | collective-permute-start | bytes 4128776 | tf_op jit(solution)/shard_map/ppermute | solution.py:203
  585.9 12.9 %collective-permute-done.52 = bf16[192,3584]{1,0:T(8,128)(2,1)S(1)} collective-permute-done((bf16[192,3584]{1,0:T(8,128)(2,1)S(1)}, bf16[192,3584]{1,0:T(8,128)(2,1)S(1)}, u32[]{:S(2)}, u32[]{:S(2)}) %collective-permute-start.52) | collective-permute-done | bytes 1376288 | tf_op jit(solution)/shard_map/ppermute | solution.py:203
  608.0 7.1 %collective-permute-done.57 = bf16[192,1728]{1,0:T(8,128)(2,1)S(1)} collective-permute-done((bf16[192,1728]{1,0:T(8,128)(2,1)S(1)}, bf16[192,1728]{1,0:T(8,128)(2,1)S(1)}, u32[]{:S(2)}, u32[]{:S(2)}) %collective-permute-start.57) | collective-permute-done | bytes 663584 | tf_op jit(solution)/shard_map/ppermute | solution.py:203
  617.5 9.1 %collective-permute-done.58 = bf16[192,1728]{1,0:T(8,128)(2,1)S(1)} collective-permute-done((bf16[192,1728]{1,0:T(8,128)(2,1)S(1)}, bf16[192,1728]{1,0:T(8,128)(2,1)S(1)}, u32[]{:S(2)}, u32[]{:S(2)}) %collective-permute-start.58) | collective-permute-done | bytes 663584 | tf_op jit(solution)/shard_map/ppermute | solution.py:203
  629.4 16.5 %collective-permute-done.59 = bf16[192,1728]{1,0:T(8,128)(2,1)} collective-permute-done((bf16[192,1728]{1,0:T(8,128)(2,1)S(1)}, bf16[192,1728]{1,0:T(8,128)(2,1)}, u32[]{:S(2)}, u32[]{:S(2)}) %collective-permute-start.59) | collective-permute-done | bytes 663584 | tf_op jit(solution)/shard_map/ppermute | solution.py:203
  652.7 6.4 collective-permute-done.60
  662.9 6.2 shard_map.178
  (416 shorter events, 266.5 us)
Async XLA Ops:
  7.2 110.4 %all-gather.7.cloned.1.call-start = ((), (), s32[]{:S(2)}) async-start(), calls=%async_computation.1 | async-start | bytes 3276800 | tf_op jit(solution)/shard_map/all_gather | solution.py:279
  9.3 200.6 %all-gather.5.cloned.1.call-start = ((), (), s32[]{:S(2)}) async-start(), calls=%async_computation | async-start | bytes 6553600 | tf_op jit(solution)/shard_map/all_gather | solution.py:279
  28.5 77.0 %collective-permute-start.1 = (bf16[640,3456]{1,0:T(8,128)(2,1)}, bf16[640,3456]{1,0:T(8,128)(2,1)}, u32[]{:S(2)}, u32[]{:S(2)}) collective-permute-start(bf16[640,3456]{1,0:T(8,128)(2,1)} %concatenate.133), channel_id=1, source_target_pairs={{0,4},{4,0},{8,12},{12,8},{16,20},{20,16},{24,28},{28,24},{1,5},{5... | collective-permute-start | bytes 13271048 | tf_op jit(solution)/shard_map/ppermute | solution.py:208
  36.3 59.8 %collective-permute-start = (bf16[384,2560]{1,0:T(8,128)(2,1)}, bf16[384,2560]{1,0:T(8,128)(2,1)}, u32[]{:S(2)}, u32[]{:S(2)}) collective-permute-start(bf16[384,2560]{1,0:T(8,128)(2,1)} %get-tuple-element.117), channel_id=1, source_target_pairs={{0,4},{4,0},{8,12},{12,8},{16,20},{20,16},{24,28},{28,24},{1,5},{5... | collective-permute-start | bytes 5898248 | tf_op jit(solution)/shard_map/ppermute | solution.py:208
  36.3 58.1 %collective-permute-start.2 = (bf16[1024,640]{1,0:T(8,128)(2,1)S(1)}, bf16[1024,640]{1,0:T(8,128)(2,1)}, u32[]{:S(2)}, u32[]{:S(2)}) collective-permute-start(bf16[1024,640]{1,0:T(8,128)(2,1)S(1)} %copy-done.21), channel_id=1, source_target_pairs={{0,4},{4,0},{8,12},{12,8},{16,20},{20,16},{24,28},{28,24},{1,5},{5... | collective-permute-start | bytes 3932168 | tf_op jit(solution)/shard_map/ppermute | solution.py:208
  36.8 64.0 %collective-permute-start.3 = (bf16[1728,640]{1,0:T(8,128)(2,1)}, bf16[1728,640]{1,0:T(8,128)(2,1)}, u32[]{:S(2)}, u32[]{:S(2)}) collective-permute-start(bf16[1728,640]{1,0:T(8,128)(2,1)} %param.25), channel_id=1, source_target_pairs={{0,4},{4,0},{8,12},{12,8},{16,20},{20,16},{24,28},{28,24},{1,5},{5... | collective-permute-start | bytes 6635528 | tf_op jit(solution)/shard_map/ppermute | solution.py:208
  38.7 30.4 %collective-permute-start.6 = (bf16[96,1280]{1,0:T(8,128)(2,1)S(1)}, bf16[96,1280]{1,0:T(8,128)(2,1)S(1)}, u32[]{:S(2)}, u32[]{:S(2)}) collective-permute-start(bf16[96,1280]{1,0:T(8,128)(2,1)S(1)} %get-tuple-element.115), channel_id=1, source_target_pairs={{0,16},{4,20},{8,24},{12,28},{16,0},{20,4},{24,8},{28,12},{1,17},{... | collective-permute-start | bytes 737288 | tf_op jit(solution)/shard_map/ppermute | solution.py:203
  42.8 240.8 %all-gather.9.cloned.1.call-start = ((), (), s32[]{:S(2)}) async-start(), calls=%async_computation.2 | async-start | bytes 1966080 | tf_op jit(solution)/shard_map/all_gather | solution.py:279
  130.8 32.1 %collective-permute-start.10 = (bf16[384,512]{1,0:T(8,128)(2,1)}, bf16[384,512]{1,0:T(8,128)(2,1)S(1)}, u32[]{:S(2)}, u32[]{:S(2)}) collective-permute-start(bf16[384,512]{1,0:T(8,128)(2,1)} %shard_map.169), channel_id=1, source_target_pairs={{8,0},{12,4},{16,8},{20,12},{24,16},{28,20},{9,1},{13,5},{17,9},{2... | collective-permute-start | bytes 1179656 | tf_op jit(solution)/shard_map/ppermute | solution.py:203
  132.1 32.3 %collective-permute-start.9 = (bf16[384,512]{1,0:T(8,128)(2,1)}, bf16[384,512]{1,0:T(8,128)(2,1)S(1)}, u32[]{:S(2)}, u32[]{:S(2)}) collective-permute-start(bf16[384,512]{1,0:T(8,128)(2,1)} %shard_map.169), channel_id=1, source_target_pairs={{0,8},{4,12},{8,16},{12,20},{16,24},{20,28},{1,9},{5,13},{9,17},{1... | collective-permute-start | bytes 1179656 | tf_op jit(solution)/shard_map/ppermute | solution.py:203
  163.0 27.1 %collective-permute-start.11 = (bf16[384,512]{1,0:T(8,128)(2,1)S(1)}, bf16[384,512]{1,0:T(8,128)(2,1)S(1)}, u32[]{:S(2)}, u32[]{:S(2)}) collective-permute-start(bf16[384,512]{1,0:T(8,128)(2,1)S(1)} %collective-permute-done.10), channel_id=1, source_target_pairs={{8,0},{12,4},{16,8},{20,12},{9,1},{13,5},{17,9},{21,13},{10,2},{14... | collective-permute-start | bytes 1179656 | tf_op jit(solution)/shard_map/ppermute | solution.py:203
  164.4 28.8 %collective-permute-start.13 = (bf16[384,512]{1,0:T(8,128)(2,1)S(1)}, bf16[384,512]{1,0:T(8,128)(2,1)S(1)}, u32[]{:S(2)}, u32[]{:S(2)}) collective-permute-start(bf16[384,512]{1,0:T(8,128)(2,1)S(1)} %collective-permute-done.9), channel_id=1, source_target_pairs={{8,16},{12,20},{16,24},{20,28},{9,17},{13,21},{17,25},{21,29},{10,... | collective-permute-start | bytes 1179656 | tf_op jit(solution)/shard_map/ppermute | solution.py:203
  238.3 123.4 %all-gather.11.cloned.1.call-start = ((), (), s32[]{:S(2)}) async-start(), calls=%async_computation.3 | async-start | bytes 1966080 | tf_op jit(solution)/shard_map/all_gather | solution.py:279
  346.4 35.5 %collective-permute-start.24 = (bf16[192,3584]{1,0:T(8,128)(2,1)}, bf16[192,3584]{1,0:T(8,128)(2,1)}, u32[]{:S(2)}, u32[]{:S(2)}) collective-permute-start(bf16[192,3584]{1,0:T(8,128)(2,1)} %get-tuple-element.63), channel_id=1, source_target_pairs={{0,8},{4,12},{1,9},{5,13},{2,10},{6,14},{3,11},{7,15}} | collective-permute-start | bytes 4128776 | tf_op jit(solution)/shard_map/ppermute | solution.py:203
  349.6 32.4 %collective-permute-start.25 = (bf16[192,3584]{1,0:T(8,128)(2,1)}, bf16[192,3584]{1,0:T(8,128)(2,1)}, u32[]{:S(2)}, u32[]{:S(2)}) collective-permute-start(bf16[192,3584]{1,0:T(8,128)(2,1)} %get-tuple-element.64), channel_id=1, source_target_pairs={{24,16},{28,20},{25,17},{29,21},{26,18},{30,22},{27,19},{31,23}} | collective-permute-start | bytes 4128776 | tf_op jit(solution)/shard_map/ppermute | solution.py:203
  394.2 31.7 %collective-permute-start.30 = (bf16[192,3584]{1,0:T(8,128)(2,1)S(1)}, bf16[192,3584]{1,0:T(8,128)(2,1)S(1)}, u32[]{:S(2)}, u32[]{:S(2)}) collective-permute-start(bf16[192,3584]{1,0:T(8,128)(2,1)S(1)} %get-tuple-element.68), channel_id=1, source_target_pairs={{0,8},{4,12},{8,16},{12,20},{1,9},{5,13},{9,17},{13,21},{2,10},{6,... | collective-permute-start | bytes 4128776 | tf_op jit(solution)/shard_map/ppermute | solution.py:203
  398.8 27.1 %collective-permute-start.31 = (bf16[192,3584]{1,0:T(8,128)(2,1)S(1)}, bf16[192,3584]{1,0:T(8,128)(2,1)S(1)}, u32[]{:S(2)}, u32[]{:S(2)}) collective-permute-start(bf16[192,3584]{1,0:T(8,128)(2,1)S(1)} %get-tuple-element.69), channel_id=1, source_target_pairs={{16,8},{20,12},{24,16},{28,20},{17,9},{21,13},{25,17},{29,21},{18,... | collective-permute-start | bytes 4128776 | tf_op jit(solution)/shard_map/ppermute | solution.py:203
  439.9 31.4 %collective-permute-start.36 = (bf16[192,3584]{1,0:T(8,128)(2,1)}, bf16[192,3584]{1,0:T(8,128)(2,1)S(1)}, u32[]{:S(2)}, u32[]{:S(2)}) collective-permute-start(bf16[192,3584]{1,0:T(8,128)(2,1)} %get-tuple-element.75), channel_id=1, source_target_pairs={{0,8},{4,12},{8,16},{12,20},{16,24},{20,28},{1,9},{5,13},{9,17},{1... | collective-permute-start | bytes 4128776 | tf_op jit(solution)/shard_map/ppermute | solution.py:203
  448.5 26.5 %collective-permute-start.37 = (bf16[192,3584]{1,0:T(8,128)(2,1)}, bf16[192,3584]{1,0:T(8,128)(2,1)S(1)}, u32[]{:S(2)}, u32[]{:S(2)}) collective-permute-start(bf16[192,3584]{1,0:T(8,128)(2,1)} %get-tuple-element.76), channel_id=1, source_target_pairs={{8,0},{12,4},{16,8},{20,12},{24,16},{28,20},{9,1},{13,5},{17,9},{2... | collective-permute-start | bytes 4128776 | tf_op jit(solution)/shard_map/ppermute | solution.py:203
  476.4 53.4 %collective-permute-start.39 = (bf16[192,3584]{1,0:T(8,128)(2,1)S(1)}, bf16[192,3584]{1,0:T(8,128)(2,1)S(1)}, u32[]{:S(2)}, u32[]{:S(2)}) collective-permute-start(bf16[192,3584]{1,0:T(8,128)(2,1)S(1)} %get-tuple-element.80), channel_id=1, source_target_pairs={{0,8},{4,12},{1,9},{5,13},{2,10},{6,14},{3,11},{7,15}} | collective-permute-start | bytes 4128776 | tf_op jit(solution)/shard_map/ppermute | solution.py:203
  478.6 51.2 %collective-permute-start.40 = (bf16[192,3584]{1,0:T(8,128)(2,1)S(1)}, bf16[192,3584]{1,0:T(8,128)(2,1)S(1)}, u32[]{:S(2)}, u32[]{:S(2)}) collective-permute-start(bf16[192,3584]{1,0:T(8,128)(2,1)S(1)} %get-tuple-element.81), channel_id=1, source_target_pairs={{24,16},{28,20},{25,17},{29,21},{26,18},{30,22},{27,19},{31,23}} | collective-permute-start | bytes 4128776 | tf_op jit(solution)/shard_map/ppermute | solution.py:203
  479.5 35.6 %collective-permute-start.38 = (bf16[192,1728]{1,0:T(8,128)(2,1)S(1)}, bf16[192,1728]{1,0:T(8,128)(2,1)S(1)}, u32[]{:S(2)}, u32[]{:S(2)}) collective-permute-start(bf16[192,1728]{1,0:T(8,128)(2,1)S(1)} %pad_maximum_fusion.16), channel_id=1, source_target_pairs={{0,8},{4,12},{8,16},{12,20},{16,24},{20,28},{1,9},{5,13},{9,17},{1... | collective-permute-start | bytes 1990664 | tf_op jit(solution)/shard_map/ppermute | solution.py:203
  480.8 34.9 %collective-permute-start.42 = (bf16[192,1728]{1,0:T(8,128)(2,1)S(1)}, bf16[192,1728]{1,0:T(8,128)(2,1)S(1)}, u32[]{:S(2)}, u32[]{:S(2)}) collective-permute-start(bf16[192,1728]{1,0:T(8,128)(2,1)S(1)} %pad_maximum_fusion.16), channel_id=1, source_target_pairs={{8,0},{12,4},{16,8},{20,12},{24,16},{28,20},{9,1},{13,5},{17,9},{2... | collective-permute-start | bytes 1990664 | tf_op jit(solution)/shard_map/ppermute | solution.py:203
  530.4 23.6 %collective-permute-start.44 = (bf16[192,3584]{1,0:T(8,128)(2,1)S(1)}, bf16[192,3584]{1,0:T(8,128)(2,1)S(1)}, u32[]{:S(2)}, u32[]{:S(2)}) collective-permute-start(bf16[192,3584]{1,0:T(8,128)(2,1)S(1)} %get-tuple-element.86), channel_id=1, source_target_pairs={{0,8},{4,12},{8,16},{12,20},{1,9},{5,13},{9,17},{13,21},{2,10},{6,... | collective-permute-start | bytes 4128776 | tf_op jit(solution)/shard_map/ppermute | solution.py:203
  535.0 18.9 %collective-permute-start.45 = (bf16[192,3584]{1,0:T(8,128)(2,1)S(1)}, bf16[192,3584]{1,0:T(8,128)(2,1)S(1)}, u32[]{:S(2)}, u32[]{:S(2)}) collective-permute-start(bf16[192,3584]{1,0:T(8,128)(2,1)S(1)} %get-tuple-element.87), channel_id=1, source_target_pairs={{16,8},{20,12},{24,16},{28,20},{17,9},{21,13},{25,17},{29,21},{18,... | collective-permute-start | bytes 4128776 | tf_op jit(solution)/shard_map/ppermute | solution.py:203
  567.2 31.6 %collective-permute-start.52 = (bf16[192,3584]{1,0:T(8,128)(2,1)S(1)}, bf16[192,3584]{1,0:T(8,128)(2,1)S(1)}, u32[]{:S(2)}, u32[]{:S(2)}) collective-permute-start(bf16[192,3584]{1,0:T(8,128)(2,1)S(1)} %add_convert_fusion.1), channel_id=1, source_target_pairs={{0,8},{4,12},{8,16},{12,20},{16,24},{20,28},{1,9},{5,13},{9,17},{1... | collective-permute-start | bytes 4128776 | tf_op jit(solution)/shard_map/ppermute | solution.py:203
  576.4 26.7 %collective-permute-start.53 = (bf16[192,3584]{1,0:T(8,128)(2,1)S(1)}, bf16[192,3584]{1,0:T(8,128)(2,1)S(1)}, u32[]{:S(2)}, u32[]{:S(2)}) collective-permute-start(bf16[192,3584]{1,0:T(8,128)(2,1)S(1)} %add_convert_fusion), channel_id=1, source_target_pairs={{8,0},{12,4},{16,8},{20,12},{24,16},{28,20},{9,1},{13,5},{17,9},{2... | collective-permute-start | bytes 4128776 | tf_op jit(solution)/shard_map/ppermute | solution.py:203
  606.7 19.9 %collective-permute-start.58 = (bf16[192,1728]{1,0:T(8,128)(2,1)S(1)}, bf16[192,1728]{1,0:T(8,128)(2,1)S(1)}, u32[]{:S(2)}, u32[]{:S(2)}) collective-permute-start(bf16[192,1728]{1,0:T(8,128)(2,1)S(1)} %pad_maximum_fusion.17), channel_id=1, source_target_pairs={{8,0},{12,4},{16,8},{20,12},{24,16},{28,20},{9,1},{13,5},{17,9},{2... | collective-permute-start | bytes 1990664 | tf_op jit(solution)/shard_map/ppermute | solution.py:203
  626.6 19.3 %collective-permute-start.59 = (bf16[192,1728]{1,0:T(8,128)(2,1)S(1)}, bf16[192,1728]{1,0:T(8,128)(2,1)}, u32[]{:S(2)}, u32[]{:S(2)}) collective-permute-start(bf16[192,1728]{1,0:T(8,128)(2,1)S(1)} %collective-permute-done.58), channel_id=1, source_target_pairs={{8,0},{12,4},{16,8},{20,12},{9,1},{13,5},{17,9},{21,13},{10,2},{14... | collective-permute-start | bytes 1990664 | tf_op jit(solution)/shard_map/ppermute | solution.py:203
  627.9 23.5 %collective-permute-start.62 = (bf16[192,1728]{1,0:T(8,128)(2,1)}, bf16[192,1728]{1,0:T(8,128)(2,1)}, u32[]{:S(2)}, u32[]{:S(2)}) collective-permute-start(bf16[192,1728]{1,0:T(8,128)(2,1)} %collective-permute-done.61), channel_id=1, source_target_pairs={{16,24},{20,28},{17,25},{21,29},{18,26},{22,30},{19,27},{23,31}} | collective-permute-start | bytes 1990664 | tf_op jit(solution)/shard_map/ppermute | solution.py:203
  671.6 19.6 %collective-permute-start.55 = (bf16[48,1280]{1,0:T(8,128)(2,1)S(1)}, bf16[48,1280]{1,0:T(8,128)(2,1)S(1)}, u32[]{:S(2)}, u32[]{:S(2)}) collective-permute-start(bf16[48,1280]{1,0:T(8,128)(2,1)S(1)} %get-tuple-element.204), channel_id=1, source_target_pairs={{0,16},{4,20},{8,24},{12,28},{16,0},{20,4},{24,8},{28,12},{1,17},{... | collective-permute-start | bytes 368648 | tf_op jit(solution)/shard_map/ppermute | solution.py:203
  671.7 19.5 %collective-permute-start.54 = (bf16[48,1280]{1,0:T(8,128)(2,1)S(1)}, bf16[48,1280]{1,0:T(8,128)(2,1)S(1)}, u32[]{:S(2)}, u32[]{:S(2)}) collective-permute-start(bf16[48,1280]{1,0:T(8,128)(2,1)S(1)} %get-tuple-element.205), channel_id=1, source_target_pairs={{0,24},{4,28},{8,0},{12,4},{16,8},{20,12},{24,16},{28,20},{1,25},{... | collective-permute-start | bytes 368648 | tf_op jit(solution)/shard_map/ppermute | solution.py:203
  (95 other events, 1022.6 us)
Sparse Core Ops, SparseCore 0:
  9.6 72.8 all-gather.6
  84.0 113.6 all-gather.4
  238.4 45.1 all-gather.8
  320.3 38.7 all-gather.10

commit v6 on v5

--- a/solution.py
+++ b/solution.py
@@ -193,7 +193,7 @@
     dz = width // planes
     ds = width // seq_count
     share = rows // mlp_count
-    chunks = 2 if share % 32 == 0 else 1
+    chunks = 2 if share % 32 == 0 and planes > 3 else 1
     sub = share // chunks
     crows = mlp_count * sub
     piece_len = rows // PIECES_DEV
@@ -245,33 +245,50 @@
     half = max(1, planes // 2)
     orders = [list(range(bits)), [(b + bits // 2) % bits for b in range(bits)]]
 
-    def mlp_scatter(x):
-        out = []
-        for part, order in zip((x[:half], x[half:]), orders):
-            slots = {j: part[:, j] for j in range(mlp_count)}
-            for b in order:
-                bit = 1 << b
-                sent = [j for j in sorted(slots) if j & bit]
-                got = partner(jnp.stack([slots[j].astype(BF16) for j in sent], axis=0), bit)
-                slots = {
-                    j ^ bit: slots[j ^ bit].astype(F32) + got[i].astype(F32)
-                    for i, j in enumerate(sent)
-                }
-            out.append(slots[0])
-        return jnp.concatenate(out, axis=0)
-
-    def mlp_gather(x):
-        out = []
-        for part, order in zip((x[:half], x[half:]), orders):
-            slots = {0: part}
-            for b in reversed(order):
-                bit = 1 << b
-                have = sorted(slots)
-                got = partner(jnp.stack([slots[j] for j in have], axis=0), bit)
-                for i, j in enumerate(have):
-                    slots[j | bit] = got[i]
-            out.append(jnp.stack([slots[j] for j in range(mlp_count)], axis=1))
-        return out
+    def sum_begin(x):
+        return [{j: part[:, j] for j in range(mlp_count)} for part in (x[:half], x[half:])]
+
+    def sum_sent(states, n):
+        return [[j for j in sorted(v) if j & (1 << o[n])] for v, o in zip(states, orders)]
+
+    def sum_launch(states, n):
+        sends = [
+            jnp.stack([v[j].astype(BF16) for j in w], axis=0) for v, w in zip(states, sum_sent(states, n))
+        ]
+        sends = lax.optimization_barrier(sends)
+        return [partner(send, 1 << o[n]) for send, o in zip(sends, orders)]
+
+    def sum_land(states, n, gots):
+        return [
+            {j ^ (1 << o[n]): v[j ^ (1 << o[n])].astype(F32) + got[i].astype(F32) for i, j in enumerate(w)}
+            for v, w, o, got in zip(states, sum_sent(states, n), orders, gots)
+        ]
+
+    def sum_stage(states, n):
+        return sum_land(states, n, sum_launch(states, n))
+
+    def sum_end(states):
+        return jnp.concatenate([v[0] for v in states], axis=0)
+
+    def spread_begin(x):
+        return [{0: x[:half]}, {0: x[half:]}]
+
+    def spread_launch(states, n):
+        sends = [jnp.stack([v[j] for j in sorted(v)], axis=0) for v in states]
+        sends = lax.optimization_barrier(sends)
+        return [partner(send, 1 << o[bits - 1 - n]) for send, o in zip(sends, orders)]
+
+    def spread_land(states, n, gots):
+        return [
+            v | {j | (1 << o[bits - 1 - n]): got[i] for i, j in enumerate(sorted(v))}
+            for v, o, got in zip(states, orders, gots)
+        ]
+
+    def spread_stage(states, n):
+        return spread_land(states, n, spread_launch(states, n))
+
+    def spread_end(states):
+        return [jnp.stack([v[j] for j in range(mlp_count)], axis=1) for v in states]
 
     lines = [[z * CORES + e for z in range(planes)] for e in range(CORES)]
 
@@ -285,13 +302,6 @@
     for k in range(1, planes // 2 + 1):
         order += [k] if 2 * k == planes else [k, planes - k]
     order.append(0)
-    own_share = lax.dynamic_slice_in_dim(layer_input, mlp_rank * share, share, 0)
-    lane_parts = []
-    for k in order:
-        part = lax.dynamic_slice_in_dim(own_share, (plane + k) % planes * dz, dz, 1)
-        if k:
-            part = move(part, [(i, (i + k) % planes) for i in range(planes)])
-        lane_parts.append(part)
 
     kv_cols = max(HD, KVH * HD // mlp_count)
     kv_first = mlp_rank * KVH // mlp_count * HD
@@ -340,10 +350,11 @@
     out_wide = jnp.concatenate([out_weight, sibling(out_weight)], axis=1)
     down_wide = jnp.concatenate([down_weight, sibling(down_weight)], axis=1)
 
-    lane_input = swap_halves(jnp.stack(lane_parts, axis=0)).reshape(planes, chunks, sub, dz)
+    own_share = lax.dynamic_slice_in_dim(layer_input, mlp_rank * share, share, 0)
+    lane_sends = [lax.dynamic_slice_in_dim(own_share, (plane + k) % planes * dz, dz, 1) for k in order]
     gain_lane = swap_halves(lax.dynamic_slice_in_dim(feedforward_gain, plane * dz, dz, 0)).astype(F32)
-    both, glu_weight, out_wide, down_wide, lane_input = lax.optimization_barrier(
-        (both, glu_weight, out_wide, down_wide, lane_input)
+    both, glu_weight, out_wide, down_wide, lane_sends = lax.optimization_barrier(
+        (both, glu_weight, out_wide, down_wide, lane_sends)
     )
 
     row_ids = seq_rank * rows + jnp.arange(rows, dtype=jnp.int32)
@@ -376,8 +387,14 @@
         pages.append(lax.dynamic_slice(kv_rows, (source * piece_len, offset), (piece_len, cache_width)))
     kv_cache = jnp.concatenate(pages, axis=0)
 
+    lane_sends, q_weight = after(lane_sends, q_weight)
+    lane_parts = [
+        move(v, [(i, (i + k) % planes) for i in range(planes)]) if k else v
+        for k, v in zip(order, lane_sends)
+    ]
     query = product(both, q_weight, F32)
-    query_sib = sibling(query[rows:])
+    query_sib, lane_parts = after(sibling(query[rows:]), lane_parts)
+    lane_input = swap_halves(jnp.stack(lane_parts, axis=0)).reshape(planes, chunks, sub, dz)
     mixed = attend(
         query, query_sib, query_bias.astype(F32)[None, :], cosine, sine, kv_rows, doc_first, stream, piece_stream, kv_heads
     )
@@ -394,7 +411,7 @@
 
     collected = [line_collect(v) for v in chunked]
 
-    def attn_sum(h):
+    def attn_terms(h):
         heads = jnp.concatenate(
             [
                 lax.dynamic_slice_in_dim(collected[h], (plane - k) % planes * crows, crows, 0)
@@ -402,15 +419,16 @@
             ],
             axis=0,
         )
-        attn = product(heads, out_wide, BF16)
-        attn = mlp_scatter(attn.reshape(planes, mlp_count, sub, dz))
-        return lane_input[:, h].astype(F32) + attn
-
-    def spread(residual):
+        return sum_begin(product(heads, out_wide, BF16).reshape(planes, mlp_count, sub, dz))
+
+    def attn_end(h, states):
+        return lane_input[:, h].astype(F32) + sum_end(states)
+
+    def lane_terms(residual):
         square = residual * residual
         square = sum(square[..., i : i + HD] for i in range(0, dz, HD))
         lane = jnp.concatenate([(residual * gain_lane).astype(BF16), square.astype(BF16)], axis=-1)
-        return mlp_gather(lane)
+        return spread_begin(lane)
 
     def contract_half(lane):
         part = product(lane.reshape(-1, dz + HD), glu_weight, BF16).reshape(-1, crows, 2 * units + HD)
@@ -442,56 +460,81 @@
         }
         return jnp.stack([found[k] for k in range(planes)])
 
-    def project_down(state):
+    def down_terms(state):
         slots = gather_slots(state)
         hidden = jnp.concatenate([slots[k] for k in order], axis=0)
-        down = product(hidden, down_wide, BF16)
-        return mlp_scatter(down.reshape(planes, mlp_count, sub, dz))
+        return sum_begin(product(hidden, down_wide, BF16).reshape(planes, mlp_count, sub, dz))
 
     steps = planes - 1
-    residuals = [attn_sum(0)]
-    lanes = spread(residuals[0])
+    states = attn_terms(0)
+    for n in range(bits):
+        states = sum_stage(states, n)
+    residuals = [attn_end(0, states)]
+    states = lane_terms(residuals[0])
+    for n in range(bits):
+        states = spread_stage(states, n)
+    lanes = lax.optimization_barrier(spread_end(states))
     first = contract_half(lanes[0])
     carried, last = scatter_step(dict(zip(order, first)), None, 1, lanes[1])
     parts = dict(zip(order, first + contract_half(last)))
-    queued = None
-    for t in range(1, steps + 1):
-        if t > 1:
-            carried, queued = scatter_step(parts, carried, t, queued)
-        if chunks > 1:
-            if t == 1:
-                collected[1], carried = after(collected[1], carried)
-            if t == min(2, steps):
-                residuals.append(attn_sum(1))
-                queued, carried = after(residuals[1], carried)
-            if t == steps:
-                queued = contract(spread(queued))
+    following = None
+    if chunks > 1:
+        collected[1], parts[0] = after(collected[1], parts[0])
+        states = attn_terms(1)
+        gots = sum_launch(states, 0)
+    for t in range(2, steps + 1):
+        if chunks > 1 and t == 2:
+            carried, gots = scatter_step(parts, carried, t, gots)
+            states = sum_land(states, 0, gots)
+            for n in range(1, bits):
+                states = sum_stage(states, n)
+            residuals.append(attn_end(1, states))
+            states = lane_terms(residuals[1])
+            gots = spread_launch(states, 0)
+        elif chunks > 1 and t == 3:
+            carried, gots = scatter_step(parts, carried, t, gots)
+            states = spread_land(states, 0, gots)
+            for n in range(1, bits):
+                states = spread_stage(states, n)
+            following = contract(spread_end(states))
+        else:
+            carried, _ = scatter_step(parts, carried, t)
     finals = []
-    for h in range(chunks):
-        following = queued if h + 1 < chunks else None
-        ahead = None
-        if following is not None:
-            ahead, carried = scatter_step(following, None, 1, carried)
+    if following is not None:
+        ahead, carried = scatter_step(following, None, 1, carried)
         hidden = activate(parts, carried)
         state = ([hidden], [hidden])
-        if following is None:
-            for t in range(1, steps + 1):
-                gather_step(state, t)
-            finals.append(deliver(h, project_down(state)))
-            continue
         gather_step(state, 1)
         gather_step(state, 2)
         for t in range(2, steps + 1):
-            ahead, (state[0][-1], state[1][-1]) = after(ahead, (state[0][-1], state[1][-1]))
             ahead, (state[0][-1], state[1][-1]) = scatter_step(
                 following, ahead, t, (state[0][-1], state[1][-1])
             )
             if t < steps:
                 gather_step(state, t + 1)
-        down = project_down(state)
-        down, carried = after(down, ahead)
-        parts = following
-        finals.append(deliver(h, down))
+        states = down_terms(state)
+        gots = sum_launch(states, 0)
+        hidden = activate(following, ahead)
+        state = ([hidden], [hidden])
+        for t in range(1, steps + 1):
+            gather_step(state, t)
+            if t <= bits:
+                (state[0][-1], state[1][-1]), gots = after((state[0][-1], state[1][-1]), gots)
+                states = sum_land(states, t - 1, gots)
+                if t < bits:
+                    gots = sum_launch(states, t)
+        for n in range(steps, bits):
+            states = sum_stage(states, n)
+        finals.append(deliver(0, sum_end(states)))
+    else:
+        hidden = activate(parts, carried)
+        state = ([hidden], [hidden])
+        for t in range(1, steps + 1):
+            gather_step(state, t)
+    states = down_terms(state)
+    for n in range(bits):
+        states = sum_stage(states, n)
+    finals.append(deliver(chunks - 1, sum_end(states)))
     final = swap_halves(jnp.concatenate(finals, axis=1))
     final = lax.dynamic_slice_in_dim(
         jnp.concatenate([final, final], axis=0), (planes - plane) % planes, planes, 0

time: 712 us -> 709 us (level)
  waiting for transfers between devices: 374 us -> 360 us
  starting transfers between devices: 112 us -> 120 us
    ppermute x39, waiting for transfers between devices: 268 us -> 250 us  [move(): lax.ppermute(x, 'seq', [(a * CORES + e, b * CORES + e) for a, b in pairs...]
    ppermute x24, starting transfers between devices: 28.9 us -> 36.4 us  [partner(): return lax.ppermute(x, 'mlp', [(a, a ^ bit) for a in range(mlp_count)])]
    unnamed x101 -> x103, local copies, waits for them, and re-layouts: 15.5 us -> 12.6 us
  transfers between devices with their start and end apart: 74 -> 74, of which waited for: 41 -> 41; matrix products, arithmetic and copies ran while one was open for 12% -> 14% of each run, Pallas kernels for 7% -> 8%
where the time goes in v6:
time: 709 us; the launch traced here: 697 us
  waiting for transfers between devices  360 us (51%)
  starting transfers between devices  120 us (17%)
  Pallas kernels  76.5 us (11%)
  other arithmetic  70.8 us (10%)
  local copies, waits for them, and re-layouts  53.2 us (8%)
  between operations  17.2 us (2%)
    ppermute x39, waiting for transfers between devices, move(): lax.ppermute(x, 'seq', [(a * CORES + e, b * CORES + e) for a, b in pairs...  250 us
    ppermute x39, starting transfers between devices, move(): lax.ppermute(x, 'seq', [(a * CORES + e, b * CORES + e) for a, b in pairs...  81.1 us
    pallas_call x10, Pallas kernels, product(): pl.pallas_call(product_kernel, grid=(cols // tile,), in_specs=[pl.BlockSp...  65.8 us
    ppermute x24, waiting for transfers between devices, partner(): return lax.ppermute(x, 'mlp', [(a, a ^ bit) for a in range(mlp_count)])  65.7 us
    all_gather x4, waiting for transfers between devices, line_collect(): return lax.all_gather(x, 'seq', axis=0, tiled=True, axis_index_groups=lines)  42.5 us
    ppermute x24, starting transfers between devices, partner(): return lax.ppermute(x, 'mlp', [(a, a ^ bit) for a in range(mlp_count)])  36.4 us
  transfers between devices with their start and end apart: 74, of which 41 were waited for; matrix products, arithmetic and copies ran while one was open for 14% of the time, Pallas kernels for 8%

profile of v6, /device:TPU:0, one launch (start us, length us, event | category | flops | bytes accessed | tf_op | source)
XLA Modules:
  0.0 697.2 jit_solution(3047390758890664795)
XLA Ops:
  21.5 7.1 %concatenate.133 = bf16[640,3456]{1,0:T(8,128)(2,1)} concatenate(bf16[640,1664]{1,0:T(8,128)(2,1)S(1)} %slice-done.3, bf16[640,1664]{1,0:T(8,128)(2,1)} %slice.599, bf16[640,64]{1,0:T(8,128)(2,1)S(1)} %slice-done.4, bf16[640,64]{1,0:T(8,128)(2,1)S(1)} %slice-done.5), dimensions={1} | concatenate | bytes 8847360 | tf_op jit(solution)/shard_map/concatenate | solution.py:338
  64.2 7.3 %pad_maximum_fusion.w_ref = bf16[1408,3584]{1,0:T(8,128)(2,1)} fusion(bf16[128,3584]{1,0:T(8,128)(2,1)S(1)} %pad_convert_fusion, bf16[1280,3584]{1,0:T(8,128)(2,1)S(1)} %fusion.2), kind=kLoop, calls=%fused_computation.3 | loop fusion | flops 20185088 | bytes 20185088 | tf_op jit(solution)/shard_map/concatenate | solution.py:343
  86.3 5.6 collective-permute-start.9
  91.9 27.0 %collective-permute-done.10 = bf16[384,512]{1,0:T(8,128)(2,1)S(1)} collective-permute-done((bf16[384,512]{1,0:T(8,128)(2,1)}, bf16[384,512]{1,0:T(8,128)(2,1)S(1)}, u32[]{:S(2)}, u32[]{:S(2)}) %collective-permute-start.10) | collective-permute-done | bytes 393248 | tf_op jit(solution)/shard_map/ppermute | solution.py:203
  120.9 25.7 %collective-permute-done.11 = bf16[384,512]{1,0:T(8,128)(2,1)S(1)} collective-permute-done((bf16[384,512]{1,0:T(8,128)(2,1)S(1)}, bf16[384,512]{1,0:T(8,128)(2,1)S(1)}, u32[]{:S(2)}, u32[]{:S(2)}) %collective-permute-start.11) | collective-permute-done | bytes 393248 | tf_op jit(solution)/shard_map/ppermute | solution.py:203
  150.6 38.2 %collective-permute-done.12 = bf16[384,512]{1,0:T(8,128)(2,1)S(1)} collective-permute-done((bf16[384,512]{1,0:T(8,128)(2,1)S(1)}, bf16[384,512]{1,0:T(8,128)(2,1)S(1)}, u32[]{:S(2)}, u32[]{:S(2)}) %collective-permute-start.12) | collective-permute-done | bytes 393248 | tf_op jit(solution)/shard_map/ppermute | solution.py:203
  193.1 7.5 %shard_map.167.own_ref = f32[768,1024]{1,0:T(8,128)S(1)} custom-call(bf16[768,2560]{1,0:T(8,128)(2,1)} %pad_maximum_fusion.2.x_ref, bf16[2560,1024]{1,0:T(8,128)(2,1)} %all-gather.5.cloned.1.call-done.w_ref), custom_call_target="tpu_custom_call" | custom-call | tf_op jit(solution)/shard_map/pallas_call | solution.py:141
  223.8 7.2 %collective-permute-done.7 = bf16[96,1280]{1,0:T(8,128)(2,1)S(1)} collective-permute-done((bf16[96,1280]{1,0:T(8,128)(2,1)}, bf16[96,1280]{1,0:T(8,128)(2,1)S(1)}, u32[]{:S(2)}, u32[]{:S(2)}) %collective-permute-start.7) | collective-permute-done | bytes 245792 | tf_op jit(solution)/shard_map/ppermute | solution.py:203
  231.7 8.0 %shard_map.170 = bf16[384,1024]{1,0:T(8,128)(2,1)S(1)} custom-call(s32[2]{0:T(128)S(1)} %convert_reduce_fusion.1.count, s32[2,16]{1,0:T(2,128)S(1)} %select_reduce_fusion.1.active, s32[16]{0:T(128)S(1)} %select_reduce_fusion.2.piece_stream, f32[768,1024]{1,0:T(8,128)S(1)} %copy-done.3, f32[384,1024]{1,0:T(8,128)} %collective-permute-done.4.sib_ref, ...), custom_call_target="tpu_custom_call" | custom-call | tf_op jit(solution)/shard_map/pallas_call | solution.py:109
  241.6 42.5 %all-gather.9.cloned.1.call-done = bf16[768,1024]{1,0:T(8,128)(2,1)} async-done(((bf16[192,1024]{1,0:T(8,128)(2,1)}), bf16[768,1024]{1,0:T(8,128)(2,1)}) %all-gather.9.cloned.1.call-update) | async-done | bytes 1572880 | tf_op jit(solution)/shard_map/all_gather | solution.py:296
  292.6 9.6 %collective-permute-done.16 = bf16[2,2,48,1280]{3,2,1,0:T(8,128)(2,1)S(1)} collective-permute-done((bf16[2,2,48,1280]{3,2,1,0:T(8,128)(2,1)S(1)}, bf16[2,2,48,1280]{3,2,1,0:T(8,128)(2,1)S(1)}, u32[]{:S(2)}, u32[]{:S(2)}) %collective-permute-start.16) | collective-permute-done | bytes 491552 | tf_op jit(solution)/shard_map/ppermute | solution.py:213
  324.1 8.1 %collective-permute-done.22 = bf16[2,2,48,1408]{3,2,1,0:T(8,128)(2,1)} collective-permute-done((bf16[2,2,48,1408]{3,2,1,0:T(8,128)(2,1)S(1)}, bf16[2,2,48,1408]{3,2,1,0:T(8,128)(2,1)}, u32[]{:S(2)}, u32[]{:S(2)}) %collective-permute-start.22) | collective-permute-done | bytes 540704 | tf_op jit(solution)/shard_map/ppermute | solution.py:213
  333.8 8.7 %shard_map.172 = bf16[384,3584]{1,0:T(8,128)(2,1)S(1)} custom-call(bf16[384,1408]{1,0:T(8,128)(2,1)S(1)} %bitcast.345, bf16[1408,3584]{1,0:T(8,128)(2,1)} %pad_maximum_fusion.w_ref), custom_call_target="tpu_custom_call" | custom-call | tf_op jit(solution)/shard_map/pallas_call | solution.py:141
  346.1 8.7 %shard_map.173 = bf16[384,3584]{1,0:T(8,128)(2,1)S(1)} custom-call(bf16[384,1408]{1,0:T(8,128)(2,1)S(1)} %bitcast.346, bf16[1408,3584]{1,0:T(8,128)(2,1)} %pad_maximum_fusion.w_ref), custom_call_target="tpu_custom_call" | custom-call | tf_op jit(solution)/shard_map/pallas_call | solution.py:141
  368.6 15.7 %collective-permute-done.24 = bf16[192,3584]{1,0:T(8,128)(2,1)} collective-permute-done((bf16[192,3584]{1,0:T(8,128)(2,1)}, bf16[192,3584]{1,0:T(8,128)(2,1)}, u32[]{:S(2)}, u32[]{:S(2)}) %collective-permute-start.24) | collective-permute-done | bytes 1376288 | tf_op jit(solution)/shard_map/ppermute | solution.py:203
  389.2 6.1 collective-permute-start.30
  406.1 16.8 %collective-permute-done.30 = bf16[192,3584]{1,0:T(8,128)(2,1)S(1)} collective-permute-done((bf16[192,3584]{1,0:T(8,128)(2,1)S(1)}, bf16[192,3584]{1,0:T(8,128)(2,1)S(1)}, u32[]{:S(2)}, u32[]{:S(2)}) %collective-permute-start.30) | collective-permute-done | bytes 1376288 | tf_op jit(solution)/shard_map/ppermute | solution.py:203
  427.8 5.5 collective-permute-start.36
  437.7 8.7 %shard_map.175 = bf16[384,3584]{1,0:T(8,128)(2,1)S(1)} custom-call(bf16[384,1408]{1,0:T(8,128)(2,1)S(1)} %bitcast.347, bf16[1408,3584]{1,0:T(8,128)(2,1)} %pad_maximum_fusion.w_ref), custom_call_target="tpu_custom_call" | custom-call | tf_op jit(solution)/shard_map/pallas_call | solution.py:141
  446.8 12.8 %collective-permute-done.36 = bf16[192,3584]{1,0:T(8,128)(2,1)S(1)} collective-permute-done((bf16[192,3584]{1,0:T(8,128)(2,1)}, bf16[192,3584]{1,0:T(8,128)(2,1)S(1)}, u32[]{:S(2)}, u32[]{:S(2)}) %collective-permute-start.36) | collective-permute-done | bytes 1376288 | tf_op jit(solution)/shard_map/ppermute | solution.py:203
  472.8 8.7 %shard_map.176 = bf16[384,3584]{1,0:T(8,128)(2,1)S(1)} custom-call(bf16[384,1408]{1,0:T(8,128)(2,1)S(1)} %bitcast.344, bf16[1408,3584]{1,0:T(8,128)(2,1)} %pad_maximum_fusion.w_ref), custom_call_target="tpu_custom_call" | custom-call | tf_op jit(solution)/shard_map/pallas_call | solution.py:141
  481.5 27.6 %collective-permute-done.38 = bf16[192,1728]{1,0:T(8,128)(2,1)S(1)} collective-permute-done((bf16[192,1728]{1,0:T(8,128)(2,1)S(1)}, bf16[192,1728]{1,0:T(8,128)(2,1)S(1)}, u32[]{:S(2)}, u32[]{:S(2)}) %collective-permute-start.38) | collective-permute-done | bytes 663584 | tf_op jit(solution)/shard_map/ppermute | solution.py:203
  511.7 13.2 %collective-permute-done.43 = bf16[192,1728]{1,0:T(8,128)(2,1)S(1)} collective-permute-done((bf16[192,1728]{1,0:T(8,128)(2,1)}, bf16[192,1728]{1,0:T(8,128)(2,1)S(1)}, u32[]{:S(2)}, u32[]{:S(2)}) %collective-permute-start.43) | collective-permute-done | bytes 663584 | tf_op jit(solution)/shard_map/ppermute | solution.py:203
  531.8 19.8 %collective-permute-done.44 = bf16[192,3584]{1,0:T(8,128)(2,1)S(1)} collective-permute-done((bf16[192,3584]{1,0:T(8,128)(2,1)S(1)}, bf16[192,3584]{1,0:T(8,128)(2,1)S(1)}, u32[]{:S(2)}, u32[]{:S(2)}) %collective-permute-start.44) | collective-permute-done | bytes 1376288 | tf_op jit(solution)/shard_map/ppermute | solution.py:203
  553.6 10.7 %collective-permute-start.48 = (bf16[192,3584]{1,0:T(8,128)(2,1)S(1)}, bf16[192,3584]{1,0:T(8,128)(2,1)}, u32[]{:S(2)}, u32[]{:S(2)}) collective-permute-start(bf16[192,3584]{1,0:T(8,128)(2,1)S(1)} %add_convert_fusion.1), channel_id=1, source_target_pairs={{0,8},{4,12},{8,16},{12,20},{16,24},{20,28},{1,9},{5,13},{9,17},{1... | collective-permute-start | bytes 4128776 | tf_op jit(solution)/shard_map/ppermute | solution.py:203
  568.3 6.2 shard_map.177
  574.8 6.5 collective-permute-done.49
  618.7 11.8 %collective-permute-done.55 = bf16[192,1728]{1,0:T(8,128)(2,1)} collective-permute-done((bf16[192,1728]{1,0:T(8,128)(2,1)S(1)}, bf16[192,1728]{1,0:T(8,128)(2,1)}, u32[]{:S(2)}, u32[]{:S(2)}) %collective-permute-start.55) | collective-permute-done | bytes 663584 | tf_op jit(solution)/shard_map/ppermute | solution.py:203
  637.5 7.7 %collective-permute-done.61 = bf16[192,1728]{1,0:T(8,128)(2,1)} collective-permute-done((bf16[192,1728]{1,0:T(8,128)(2,1)}, bf16[192,1728]{1,0:T(8,128)(2,1)}, u32[]{:S(2)}, u32[]{:S(2)}) %collective-permute-start.61) | collective-permute-done | bytes 663584 | tf_op jit(solution)/shard_map/ppermute | solution.py:203
  649.0 6.2 shard_map.178
  658.7 8.7 %collective-permute-done.63 = bf16[2,2,48,1280]{3,2,1,0:T(8,128)(2,1)S(1)} collective-permute-done((bf16[2,2,48,1280]{3,2,1,0:T(8,128)(2,1)S(1)}, bf16[2,2,48,1280]{3,2,1,0:T(8,128)(2,1)S(1)}, u32[]{:S(2)}, u32[]{:S(2)}) %collective-permute-start.63) | collective-permute-done | bytes 491552 | tf_op jit(solution)/shard_map/ppermute | solution.py:213
  667.9 5.9 collective-permute-done.66
  (417 shorter events, 270.0 us)
Async XLA Ops:
  7.2 64.3 %all-gather.7.cloned.1.call-start = ((), (), s32[]{:S(2)}) async-start(), calls=%async_computation.1 | async-start | bytes 3276800 | tf_op jit(solution)/shard_map/all_gather | solution.py:296
  9.3 183.8 %all-gather.5.cloned.1.call-start = ((), (), s32[]{:S(2)}) async-start(), calls=%async_computation | async-start | bytes 6553600 | tf_op jit(solution)/shard_map/all_gather | solution.py:296
  28.6 30.8 %collective-permute-start.1 = (bf16[640,3456]{1,0:T(8,128)(2,1)}, bf16[640,3456]{1,0:T(8,128)(2,1)}, u32[]{:S(2)}, u32[]{:S(2)}) collective-permute-start(bf16[640,3456]{1,0:T(8,128)(2,1)} %concatenate.133), channel_id=1, source_target_pairs={{0,4},{4,0},{8,12},{12,8},{16,20},{20,16},{24,28},{28,24},{1,5},{5... | collective-permute-start | bytes 13271048 | tf_op jit(solution)/shard_map/ppermute | solution.py:208
  41.1 243.0 %all-gather.9.cloned.1.call-start = ((), (), s32[]{:S(2)}) async-start(), calls=%async_computation.2 | async-start | bytes 1966080 | tf_op jit(solution)/shard_map/all_gather | solution.py:296
  85.0 33.9 %collective-permute-start.10 = (bf16[384,512]{1,0:T(8,128)(2,1)}, bf16[384,512]{1,0:T(8,128)(2,1)S(1)}, u32[]{:S(2)}, u32[]{:S(2)}) collective-permute-start(bf16[384,512]{1,0:T(8,128)(2,1)} %shard_map.169), channel_id=1, source_target_pairs={{8,0},{12,4},{16,8},{20,12},{24,16},{28,20},{9,1},{13,5},{17,9},{2... | collective-permute-start | bytes 1179656 | tf_op jit(solution)/shard_map/ppermute | solution.py:203
  86.3 33.9 %collective-permute-start.9 = (bf16[384,512]{1,0:T(8,128)(2,1)}, bf16[384,512]{1,0:T(8,128)(2,1)S(1)}, u32[]{:S(2)}, u32[]{:S(2)}) collective-permute-start(bf16[384,512]{1,0:T(8,128)(2,1)} %shard_map.169), channel_id=1, source_target_pairs={{0,8},{4,12},{8,16},{12,20},{16,24},{20,28},{1,9},{5,13},{9,17},{1... | collective-permute-start | bytes 1179656 | tf_op jit(solution)/shard_map/ppermute | solution.py:203
  118.9 27.7 %collective-permute-start.11 = (bf16[384,512]{1,0:T(8,128)(2,1)S(1)}, bf16[384,512]{1,0:T(8,128)(2,1)S(1)}, u32[]{:S(2)}, u32[]{:S(2)}) collective-permute-start(bf16[384,512]{1,0:T(8,128)(2,1)S(1)} %collective-permute-done.10), channel_id=1, source_target_pairs={{8,0},{12,4},{16,8},{20,12},{9,1},{13,5},{17,9},{21,13},{10,2},{14... | collective-permute-start | bytes 1179656 | tf_op jit(solution)/shard_map/ppermute | solution.py:203
  120.2 29.6 %collective-permute-start.13 = (bf16[384,512]{1,0:T(8,128)(2,1)S(1)}, bf16[384,512]{1,0:T(8,128)(2,1)S(1)}, u32[]{:S(2)}, u32[]{:S(2)}) collective-permute-start(bf16[384,512]{1,0:T(8,128)(2,1)S(1)} %collective-permute-done.9), channel_id=1, source_target_pairs={{8,16},{12,20},{16,24},{20,28},{9,17},{13,21},{17,25},{21,29},{10,... | collective-permute-start | bytes 1179656 | tf_op jit(solution)/shard_map/ppermute | solution.py:203
  146.6 42.3 %collective-permute-start.12 = (bf16[384,512]{1,0:T(8,128)(2,1)S(1)}, bf16[384,512]{1,0:T(8,128)(2,1)S(1)}, u32[]{:S(2)}, u32[]{:S(2)}) collective-permute-start(bf16[384,512]{1,0:T(8,128)(2,1)S(1)} %collective-permute-done.11), channel_id=1, source_target_pairs={{8,0},{12,4},{9,1},{13,5},{10,2},{14,6},{11,3},{15,7}} | collective-permute-start | bytes 1179656 | tf_op jit(solution)/shard_map/ppermute | solution.py:203
  149.8 40.8 %collective-permute-start.14 = (bf16[384,512]{1,0:T(8,128)(2,1)S(1)}, bf16[384,512]{1,0:T(8,128)(2,1)S(1)}, u32[]{:S(2)}, u32[]{:S(2)}) collective-permute-start(bf16[384,512]{1,0:T(8,128)(2,1)S(1)} %collective-permute-done.13), channel_id=1, source_target_pairs={{16,24},{20,28},{17,25},{21,29},{18,26},{22,30},{19,27},{23,31}} | collective-permute-start | bytes 1179656 | tf_op jit(solution)/shard_map/ppermute | solution.py:203
  203.7 27.3 %collective-permute-start.4 = (f32[384,1024]{1,0:T(8,128)}, f32[384,1024]{1,0:T(8,128)}, u32[]{:S(2)}, u32[]{:S(2)}) collective-permute-start(f32[384,1024]{1,0:T(8,128)} %slice.602), channel_id=1, source_target_pairs={{0,4},{4,0},{8,12},{12,8},{16,20},{20,16},{24,28},{28,24},{1,5},{5... | collective-permute-start | bytes 4718600 | tf_op jit(solution)/shard_map/ppermute | solution.py:208
  241.3 116.7 %all-gather.11.cloned.1.call-start = ((), (), s32[]{:S(2)}) async-start(), calls=%async_computation.3 | async-start | bytes 1966080 | tf_op jit(solution)/shard_map/all_gather | solution.py:296
  344.3 24.4 %collective-permute-start.25 = (bf16[192,3584]{1,0:T(8,128)(2,1)}, bf16[192,3584]{1,0:T(8,128)(2,1)}, u32[]{:S(2)}, u32[]{:S(2)}) collective-permute-start(bf16[192,3584]{1,0:T(8,128)(2,1)} %get-tuple-element.124), channel_id=1, source_target_pairs={{24,16},{28,20},{25,17},{29,21},{26,18},{30,22},{27,19},{31,23}} | collective-permute-start | bytes 4128776 | tf_op jit(solution)/shard_map/ppermute | solution.py:203
  354.8 29.5 %collective-permute-start.24 = (bf16[192,3584]{1,0:T(8,128)(2,1)}, bf16[192,3584]{1,0:T(8,128)(2,1)}, u32[]{:S(2)}, u32[]{:S(2)}) collective-permute-start(bf16[192,3584]{1,0:T(8,128)(2,1)} %get-tuple-element.123), channel_id=1, source_target_pairs={{0,8},{4,12},{1,9},{5,13},{2,10},{6,14},{3,11},{7,15}} | collective-permute-start | bytes 4128776 | tf_op jit(solution)/shard_map/ppermute | solution.py:203
  364.8 21.9 %collective-permute-start.26 = (bf16[2,2,48,1280]{3,2,1,0:T(8,128)(2,1)S(1)}, bf16[2,2,48,1280]{3,2,1,0:T(8,128)(2,1)S(1)}, u32[]{:S(2)}, u32[]{:S(2)}) collective-permute-start(bf16[2,2,48,1280]{3,2,1,0:T(8,128)(2,1)S(1)} %pad_maximum_fusion.24), channel_id=1, source_target_pairs={{0,1},{1,0},{2,3},{3,2},{4,5},{5,4},{6,7},{7,6},{8,9},{9,8},{10,11... | collective-permute-start | bytes 1474568 | tf_op jit(solution)/shard_map/ppermute | solution.py:213
  366.0 20.6 %collective-permute-start.27 = (bf16[2,2,48,1280]{3,2,1,0:T(8,128)(2,1)S(1)}, bf16[2,2,48,1280]{3,2,1,0:T(8,128)(2,1)S(1)}, u32[]{:S(2)}, u32[]{:S(2)}) collective-permute-start(bf16[2,2,48,1280]{3,2,1,0:T(8,128)(2,1)S(1)} %pad_maximum_fusion.25), channel_id=1, source_target_pairs={{0,2},{1,3},{2,0},{3,1},{4,6},{5,7},{6,4},{7,5},{8,10},{9,11},{10,... | collective-permute-start | bytes 1474568 | tf_op jit(solution)/shard_map/ppermute | solution.py:213
  389.2 33.7 %collective-permute-start.30 = (bf16[192,3584]{1,0:T(8,128)(2,1)S(1)}, bf16[192,3584]{1,0:T(8,128)(2,1)S(1)}, u32[]{:S(2)}, u32[]{:S(2)}) collective-permute-start(bf16[192,3584]{1,0:T(8,128)(2,1)S(1)} %get-tuple-element.131), channel_id=1, source_target_pairs={{0,8},{4,12},{8,16},{12,20},{1,9},{5,13},{9,17},{13,21},{2,10},{6,... | collective-permute-start | bytes 4128776 | tf_op jit(solution)/shard_map/ppermute | solution.py:203
  402.6 22.2 %collective-permute-start.32 = (bf16[1,2,48,1408]{3,2,1,0:T(8,128)(2,1)S(1)}, bf16[1,2,48,1408]{3,2,1,0:T(8,128)(2,1)S(1)}, u32[]{:S(2)}, u32[]{:S(2)}) collective-permute-start(bf16[1,2,48,1408]{3,2,1,0:T(8,128)(2,1)S(1)} %get-tuple-element.133), channel_id=1, source_target_pairs={{0,2},{1,3},{2,0},{3,1},{4,6},{5,7},{6,4},{7,5},{8,10},{9,11},{10,... | collective-permute-start | bytes 811016 | tf_op jit(solution)/shard_map/ppermute | solution.py:213
  404.4 20.4 %collective-permute-start.33 = (bf16[1,2,48,1408]{3,2,1,0:T(8,128)(2,1)S(1)}, bf16[1,2,48,1408]{3,2,1,0:T(8,128)(2,1)S(1)}, u32[]{:S(2)}, u32[]{:S(2)}) collective-permute-start(bf16[1,2,48,1408]{3,2,1,0:T(8,128)(2,1)S(1)} %get-tuple-element.134), channel_id=1, source_target_pairs={{0,1},{1,0},{2,3},{3,2},{4,5},{5,4},{6,7},{7,6},{8,9},{9,8},{10,11... | collective-permute-start | bytes 811016 | tf_op jit(solution)/shard_map/ppermute | solution.py:213
  427.8 31.7 %collective-permute-start.36 = (bf16[192,3584]{1,0:T(8,128)(2,1)}, bf16[192,3584]{1,0:T(8,128)(2,1)S(1)}, u32[]{:S(2)}, u32[]{:S(2)}) collective-permute-start(bf16[192,3584]{1,0:T(8,128)(2,1)} %get-tuple-element.140), channel_id=1, source_target_pairs={{0,8},{4,12},{8,16},{12,20},{16,24},{20,28},{1,9},{5,13},{9,17},{1... | collective-permute-start | bytes 4128776 | tf_op jit(solution)/shard_map/ppermute | solution.py:203
  433.3 30.8 %collective-permute-start.37 = (bf16[192,3584]{1,0:T(8,128)(2,1)S(1)}, bf16[192,3584]{1,0:T(8,128)(2,1)S(1)}, u32[]{:S(2)}, u32[]{:S(2)}) collective-permute-start(bf16[192,3584]{1,0:T(8,128)(2,1)S(1)} %get-tuple-element.141), channel_id=1, source_target_pairs={{8,0},{12,4},{16,8},{20,12},{24,16},{28,20},{9,1},{13,5},{17,9},{2... | collective-permute-start | bytes 4128776 | tf_op jit(solution)/shard_map/ppermute | solution.py:203
  465.2 46.0 %collective-permute-start.40 = (bf16[192,3584]{1,0:T(8,128)(2,1)S(1)}, bf16[192,3584]{1,0:T(8,128)(2,1)S(1)}, u32[]{:S(2)}, u32[]{:S(2)}) collective-permute-start(bf16[192,3584]{1,0:T(8,128)(2,1)S(1)} %get-tuple-element.146), channel_id=1, source_target_pairs={{24,16},{28,20},{25,17},{29,21},{26,18},{30,22},{27,19},{31,23}} | collective-permute-start | bytes 4128776 | tf_op jit(solution)/shard_map/ppermute | solution.py:203
  465.9 45.2 %collective-permute-start.39 = (bf16[192,3584]{1,0:T(8,128)(2,1)S(1)}, bf16[192,3584]{1,0:T(8,128)(2,1)S(1)}, u32[]{:S(2)}, u32[]{:S(2)}) collective-permute-start(bf16[192,3584]{1,0:T(8,128)(2,1)S(1)} %get-tuple-element.145), channel_id=1, source_target_pairs={{0,8},{4,12},{1,9},{5,13},{2,10},{6,14},{3,11},{7,15}} | collective-permute-start | bytes 4128776 | tf_op jit(solution)/shard_map/ppermute | solution.py:203
  470.1 39.0 %collective-permute-start.38 = (bf16[192,1728]{1,0:T(8,128)(2,1)S(1)}, bf16[192,1728]{1,0:T(8,128)(2,1)S(1)}, u32[]{:S(2)}, u32[]{:S(2)}) collective-permute-start(bf16[192,1728]{1,0:T(8,128)(2,1)S(1)} %pad_maximum_fusion.15), channel_id=1, source_target_pairs={{0,8},{4,12},{8,16},{12,20},{16,24},{20,28},{1,9},{5,13},{9,17},{1... | collective-permute-start | bytes 1990664 | tf_op jit(solution)/shard_map/ppermute | solution.py:203
  471.4 38.4 %collective-permute-start.42 = (bf16[192,1728]{1,0:T(8,128)(2,1)S(1)}, bf16[192,1728]{1,0:T(8,128)(2,1)}, u32[]{:S(2)}, u32[]{:S(2)}) collective-permute-start(bf16[192,1728]{1,0:T(8,128)(2,1)S(1)} %pad_maximum_fusion.15), channel_id=1, source_target_pairs={{8,0},{12,4},{16,8},{20,12},{24,16},{28,20},{9,1},{13,5},{17,9},{2... | collective-permute-start | bytes 1990664 | tf_op jit(solution)/shard_map/ppermute | solution.py:203
  525.0 26.6 %collective-permute-start.44 = (bf16[192,3584]{1,0:T(8,128)(2,1)S(1)}, bf16[192,3584]{1,0:T(8,128)(2,1)S(1)}, u32[]{:S(2)}, u32[]{:S(2)}) collective-permute-start(bf16[192,3584]{1,0:T(8,128)(2,1)S(1)} %get-tuple-element.147), channel_id=1, source_target_pairs={{0,8},{4,12},{8,16},{12,20},{1,9},{5,13},{9,17},{13,21},{2,10},{6,... | collective-permute-start | bytes 4128776 | tf_op jit(solution)/shard_map/ppermute | solution.py:203
  528.8 23.2 %collective-permute-start.45 = (bf16[192,3584]{1,0:T(8,128)(2,1)S(1)}, bf16[192,3584]{1,0:T(8,128)(2,1)S(1)}, u32[]{:S(2)}, u32[]{:S(2)}) collective-permute-start(bf16[192,3584]{1,0:T(8,128)(2,1)S(1)} %get-tuple-element.148), channel_id=1, source_target_pairs={{16,8},{20,12},{24,16},{28,20},{17,9},{21,13},{25,17},{29,21},{18,... | collective-permute-start | bytes 4128776 | tf_op jit(solution)/shard_map/ppermute | solution.py:203
  529.6 22.7 %collective-permute-start.46 = (bf16[192,1728]{1,0:T(8,128)(2,1)S(1)}, bf16[192,1728]{1,0:T(8,128)(2,1)S(1)}, u32[]{:S(2)}, u32[]{:S(2)}) collective-permute-start(bf16[192,1728]{1,0:T(8,128)(2,1)S(1)} %collective-permute-done.41), channel_id=1, source_target_pairs={{16,24},{20,28},{17,25},{21,29},{18,26},{22,30},{19,27},{23,31}} | collective-permute-start | bytes 1990664 | tf_op jit(solution)/shard_map/ppermute | solution.py:203
  530.5 21.9 %collective-permute-start.47 = (bf16[192,1728]{1,0:T(8,128)(2,1)S(1)}, bf16[192,1728]{1,0:T(8,128)(2,1)S(1)}, u32[]{:S(2)}, u32[]{:S(2)}) collective-permute-start(bf16[192,1728]{1,0:T(8,128)(2,1)S(1)} %collective-permute-done.43), channel_id=1, source_target_pairs={{8,0},{12,4},{9,1},{13,5},{10,2},{14,6},{11,3},{15,7}} | collective-permute-start | bytes 1990664 | tf_op jit(solution)/shard_map/ppermute | solution.py:203
  552.3 28.9 %collective-permute-start.49 = (bf16[192,3584]{1,0:T(8,128)(2,1)S(1)}, bf16[192,3584]{1,0:T(8,128)(2,1)S(1)}, u32[]{:S(2)}, u32[]{:S(2)}) collective-permute-start(bf16[192,3584]{1,0:T(8,128)(2,1)S(1)} %add_convert_fusion), channel_id=1, source_target_pairs={{8,0},{12,4},{16,8},{20,12},{24,16},{28,20},{9,1},{13,5},{17,9},{2... | collective-permute-start | bytes 4128776 | tf_op jit(solution)/shard_map/ppermute | solution.py:203
  553.6 28.9 %collective-permute-start.48 = (bf16[192,3584]{1,0:T(8,128)(2,1)S(1)}, bf16[192,3584]{1,0:T(8,128)(2,1)}, u32[]{:S(2)}, u32[]{:S(2)}) collective-permute-start(bf16[192,3584]{1,0:T(8,128)(2,1)S(1)} %add_convert_fusion.1), channel_id=1, source_target_pairs={{0,8},{4,12},{8,16},{12,20},{16,24},{20,28},{1,9},{5,13},{9,17},{1... | collective-permute-start | bytes 4128776 | tf_op jit(solution)/shard_map/ppermute | solution.py:203
  607.8 22.7 %collective-permute-start.55 = (bf16[192,1728]{1,0:T(8,128)(2,1)S(1)}, bf16[192,1728]{1,0:T(8,128)(2,1)}, u32[]{:S(2)}, u32[]{:S(2)}) collective-permute-start(bf16[192,1728]{1,0:T(8,128)(2,1)S(1)} %collective-permute-done.51), channel_id=1, source_target_pairs={{8,0},{12,4},{16,8},{20,12},{9,1},{13,5},{17,9},{21,13},{10,2},{14... | collective-permute-start | bytes 1990664 | tf_op jit(solution)/shard_map/ppermute | solution.py:203
  (97 other events, 1093.2 us)
Sparse Core Ops, SparseCore 0:
  10.1 57.4 all-gather.6
  69.2 118.4 all-gather.4
  241.4 42.6 all-gather.8
  323.3 33.8 all-gather.10

commit v7 on v6

--- a/solution.py
+++ b/solution.py
@@ -134,16 +134,17 @@
     o_ref[...] = jnp.dot(x_ref[...], w_ref[...], preferred_element_type=F32).astype(o_ref.dtype)
 
 
-def product(x, w, out_type):
+def product(x, w, out_type, first=0, cols=None):
     rows, inner = x.shape
-    cols = w.shape[1]
-    tile = next((t for t in (512, 384, 256) if cols % t == 0), cols)
+    cols = w.shape[1] if cols is None else cols
+    tile = next((t for t in (512, 384, 256) if cols % t == 0 and first % t == 0), cols)
+    skip = first // tile
     return pl.pallas_call(
         product_kernel,
         grid=(cols // tile,),
         in_specs=[
             pl.BlockSpec((rows, inner), lambda n: (0, 0)),
-            pl.BlockSpec((inner, tile), lambda n: (0, n)),
+            pl.BlockSpec((inner, tile), lambda n: (0, n + skip if skip else n)),
         ],
         out_specs=pl.BlockSpec((rows, tile), lambda n: (0, n)),
         out_shape=jax.ShapeDtypeStruct((rows, cols), out_type),
@@ -227,12 +228,6 @@
         ups, downs = state
         return [ups[0]] + [ups[k] + downs[planes - k] for k in range(1, planes)]
 
-    def line_gather(x):
-        state = ([x], [x])
-        for t in range(1, planes):
-            gather_step(state, t)
-        return gather_slots(state)
-
     def scatter_step(parts, carried, t, held=()):
         send_up, send_down = parts[t], parts[planes - t]
         if carried is not None:
@@ -309,6 +304,7 @@
         [
             lax.dynamic_slice_in_dim(key_weight, kv_first, kv_cols, 1),
             lax.dynamic_slice_in_dim(value_weight, kv_first, kv_cols, 1),
+            query_weight,
         ],
         axis=1,
     )
@@ -321,8 +317,7 @@
     kv_weight, (gate_weight, up_weight, out_weight, down_weight, layer_input) = after(
         kv_weight, (gate_weight, up_weight, out_weight, down_weight, layer_input)
     )
-    kv_weight = line_collect(kv_weight)
-    q_weight = line_collect(query_weight)
+    qkv_weight = line_collect(kv_weight)
 
     x = layer_input.astype(F32)
     mean_sq = jnp.mean(x * x, axis=-1, keepdims=True)
@@ -365,11 +360,21 @@
     cosine, sine = rope_tables(stream - doc_first, HD)
 
     kv_heads = kv_cols // HD
-    kv = product(both, kv_weight, F32)
+    lane_sends, qkv_weight = after(lane_sends, qkv_weight)
+    lane_parts = [
+        move(v, [(i, (i + k) % planes) for i in range(planes)]) if k else v
+        for k, v in zip(order, lane_sends)
+    ]
+    kv = product(both, qkv_weight, F32, 0, 2 * kv_cols)
     joined = pl.pallas_call(
         join_kernel, out_shape=jax.ShapeDtypeStruct((rows, 2 * kv_cols), BF16)
     )(kv, sibling(kv[rows:]), kv_bias[None, :], cosine, sine)
-    core_rows = jnp.concatenate(line_gather(joined), axis=0)
+    state = ([joined], [joined])
+    for t in range(1, planes):
+        if t == planes - 1:
+            (state[0][-1], state[1][-1]), lane_parts = after((state[0][-1], state[1][-1]), lane_parts)
+        gather_step(state, t)
+    core_rows = jnp.concatenate(gather_slots(state), axis=0)
     kv_rows = jnp.concatenate([core_rows, sibling(core_rows)], axis=0)
     offsets = (plane - jnp.arange(planes, dtype=jnp.int32)) % planes
     slots = jnp.concatenate([offsets * CORES + core, offsets * CORES + 1 - core])
@@ -387,13 +392,8 @@
         pages.append(lax.dynamic_slice(kv_rows, (source * piece_len, offset), (piece_len, cache_width)))
     kv_cache = jnp.concatenate(pages, axis=0)
 
-    lane_sends, q_weight = after(lane_sends, q_weight)
-    lane_parts = [
-        move(v, [(i, (i + k) % planes) for i in range(planes)]) if k else v
-        for k, v in zip(order, lane_sends)
-    ]
-    query = product(both, q_weight, F32)
-    query_sib, lane_parts = after(sibling(query[rows:]), lane_parts)
+    query = product(both, qkv_weight, F32, 2 * kv_cols, query_weight.shape[1])
+    query_sib = sibling(query[rows:])
     lane_input = swap_halves(jnp.stack(lane_parts, axis=0)).reshape(planes, chunks, sub, dz)
     mixed = attend(
         query, query_sib, query_bias.astype(F32)[None, :], cosine, sine, kv_rows, doc_first, stream, piece_stream, kv_heads

time: 709 us -> 730 us (1.030)
  waiting for transfers between devices: 360 us -> 373 us
  Pallas kernels: 76.5 us -> 86.6 us
    all_gather x4 -> x3, waiting for transfers between devices: 42.5 us -> 117 us  [line_collect(): return lax.all_gather(x, 'seq', axis=0, tiled=True, axis_index_groups=lines)]
    ppermute x39, waiting for transfers between devices: 250 us -> 189 us  [move(): lax.ppermute(x, 'seq', [(a * CORES + e, b * CORES + e) for a, b in pairs...]
    pallas_call x1, Pallas kernels: 8.02 us -> 18.8 us  [attend(): pl.pallas_call(attend_kernel, grid_spec=pltpu.PrefetchScalarGridSpec(num_...]
  transfers between devices with their start and end apart: 74 -> 73, of which waited for: 41 -> 42; matrix products, arithmetic and copies ran while one was open for 14% -> 13% of each run, Pallas kernels for 8% -> 7%
where the time goes in v7:
time: 730 us; the launch traced here: 721 us
  waiting for transfers between devices  373 us (51%)
  starting transfers between devices  117 us (16%)
  Pallas kernels  86.6 us (12%)
  other arithmetic  73.3 us (10%)
  local copies, waits for them, and re-layouts  53.5 us (7%)
  between operations  17.3 us (2%)
    ppermute x39, waiting for transfers between devices, move(): lax.ppermute(x, 'seq', [(a * CORES + e, b * CORES + e) for a, b in pairs...  189 us
    all_gather x3, waiting for transfers between devices, line_collect(): return lax.all_gather(x, 'seq', axis=0, tiled=True, axis_index_groups=lines)  117 us
    ppermute x39, starting transfers between devices, move(): lax.ppermute(x, 'seq', [(a * CORES + e, b * CORES + e) for a, b in pairs...  78.9 us
    ppermute x24, waiting for transfers between devices, partner(): return lax.ppermute(x, 'mlp', [(a, a ^ bit) for a in range(mlp_count)])  65.6 us
    pallas_call x10, Pallas kernels, product(): pl.pallas_call(product_kernel, grid=(cols // tile,), in_specs=[pl.BlockSp...  65.1 us
    ppermute x24, starting transfers between devices, partner(): return lax.ppermute(x, 'mlp', [(a, a ^ bit) for a in range(mlp_count)])  36.2 us
    pallas_call x1, Pallas kernels, attend(): pl.pallas_call(attend_kernel, grid_spec=pltpu.PrefetchScalarGridSpec(num_...  18.8 us
  transfers between devices with their start and end apart: 73, of which 42 were waited for; matrix products, arithmetic and copies ran while one was open for 13% of the time, Pallas kernels for 7%

profile of v7, /device:TPU:0, one launch (start us, length us, event | category | flops | bytes accessed | tf_op | source)
XLA Modules:
  0.0 720.8 jit_solution(5528455953274185646)
XLA Ops:
  22.5 7.1 concatenate.133
  65.2 7.3 %pad_maximum_fusion.w_ref = bf16[1408,3584]{1,0:T(8,128)(2,1)} fusion(bf16[128,3584]{1,0:T(8,128)(2,1)S(1)} %pad_convert_fusion, bf16[1280,3584]{1,0:T(8,128)(2,1)S(1)} %fusion.2), kind=kLoop, calls=%fused_computation.3 | loop fusion | flops 20185088 | bytes 20185088 | tf_op jit(solution)/shard_map/concatenate | solution.py:338
  72.5 81.6 %all-gather.4.cloned.1.call-done.w_ref = bf16[2560,1536]{1,0:T(8,128)(2,1)} async-done(((bf16[640,1536]{1,0:T(8,128)(2,1)}), bf16[2560,1536]{1,0:T(8,128)(2,1)}) %all-gather.4.cloned.1.call-update) | async-done | bytes 7864336 | tf_op jit(solution)/shard_map/all_gather | solution.py:291
  170.0 7.9 %collective-permute-done.5 = bf16[384,512]{1,0:T(8,128)(2,1)S(1)} collective-permute-done((bf16[384,512]{1,0:T(8,128)(2,1)}, bf16[384,512]{1,0:T(8,128)(2,1)S(1)}, u32[]{:S(2)}, u32[]{:S(2)}) %collective-permute-start.5) | collective-permute-done | bytes 393248 | tf_op jit(solution)/shard_map/ppermute | solution.py:204
  194.2 10.5 %collective-permute-done.10 = bf16[96,1280]{1,0:T(8,128)(2,1)S(1)} collective-permute-done((bf16[96,1280]{1,0:T(8,128)(2,1)}, bf16[96,1280]{1,0:T(8,128)(2,1)S(1)}, u32[]{:S(2)}, u32[]{:S(2)}) %collective-permute-start.10) | collective-permute-done | bytes 245792 | tf_op jit(solution)/shard_map/ppermute | solution.py:204
  204.7 11.6 %collective-permute-done.11 = bf16[96,1280]{1,0:T(8,128)(2,1)} collective-permute-done((bf16[96,1280]{1,0:T(8,128)(2,1)}, bf16[96,1280]{1,0:T(8,128)(2,1)}, u32[]{:S(2)}, u32[]{:S(2)}) %collective-permute-start.11) | collective-permute-done | bytes 245792 | tf_op jit(solution)/shard_map/ppermute | solution.py:204
  220.3 8.4 %collective-permute-done.13 = bf16[384,512]{1,0:T(8,128)(2,1)S(1)} collective-permute-done((bf16[384,512]{1,0:T(8,128)(2,1)S(1)}, bf16[384,512]{1,0:T(8,128)(2,1)S(1)}, u32[]{:S(2)}, u32[]{:S(2)}) %collective-permute-start.13) | collective-permute-done | bytes 393248 | tf_op jit(solution)/shard_map/ppermute | solution.py:204
  232.9 7.5 %shard_map.169.own_ref = f32[768,1024]{1,0:T(8,128)S(1)} custom-call(bf16[768,2560]{1,0:T(8,128)(2,1)} %pad_maximum_fusion.2.x_ref, bf16[2560,1536]{1,0:T(8,128)(2,1)} %all-gather.4.cloned.1.call-done.w_ref), custom_call_target="tpu_custom_call" | custom-call | tf_op jit(solution)/shard_map/pallas_call | solution.py:142
  250.5 18.8 %shard_map.170 = bf16[384,1024]{1,0:T(8,128)(2,1)S(1)} custom-call(s32[2]{0:T(128)S(1)} %convert_reduce_fusion.1.count, s32[2,16]{1,0:T(2,128)S(1)} %select_reduce_fusion.1.active, s32[16]{0:T(128)S(1)} %select_reduce_fusion.2.piece_stream, f32[768,1024]{1,0:T(8,128)S(1)} %copy-done.4, f32[384,1024]{1,0:T(8,128)} %collective-permute-done.12.sib_ref, ...), custom_call_target="tpu_custom_call" | custom-call | tf_op jit(solution)/shard_map/pallas_call | solution.py:109
  271.3 35.1 %all-gather.6.cloned.1.call-done = bf16[768,1024]{1,0:T(8,128)(2,1)} async-done(((bf16[192,1024]{1,0:T(8,128)(2,1)}), bf16[768,1024]{1,0:T(8,128)(2,1)}) %all-gather.6.cloned.1.call-update) | async-done | bytes 1572880 | tf_op jit(solution)/shard_map/all_gather | solution.py:291
  315.7 8.7 %collective-permute-done.16 = bf16[2,2,48,1280]{3,2,1,0:T(8,128)(2,1)S(1)} collective-permute-done((bf16[2,2,48,1280]{3,2,1,0:T(8,128)(2,1)S(1)}, bf16[2,2,48,1280]{3,2,1,0:T(8,128)(2,1)S(1)}, u32[]{:S(2)}, u32[]{:S(2)}) %collective-permute-start.16) | collective-permute-done | bytes 491552 | tf_op jit(solution)/shard_map/ppermute | solution.py:214
  348.1 8.0 %collective-permute-done.22 = bf16[2,2,48,1408]{3,2,1,0:T(8,128)(2,1)} collective-permute-done((bf16[2,2,48,1408]{3,2,1,0:T(8,128)(2,1)S(1)}, bf16[2,2,48,1408]{3,2,1,0:T(8,128)(2,1)}, u32[]{:S(2)}, u32[]{:S(2)}) %collective-permute-start.22) | collective-permute-done | bytes 540704 | tf_op jit(solution)/shard_map/ppermute | solution.py:214
  357.7 8.7 %shard_map.172 = bf16[384,3584]{1,0:T(8,128)(2,1)S(1)} custom-call(bf16[384,1408]{1,0:T(8,128)(2,1)S(1)} %bitcast.345, bf16[1408,3584]{1,0:T(8,128)(2,1)} %pad_maximum_fusion.w_ref), custom_call_target="tpu_custom_call" | custom-call | tf_op jit(solution)/shard_map/pallas_call | solution.py:142
  370.0 8.7 %shard_map.173 = bf16[384,3584]{1,0:T(8,128)(2,1)S(1)} custom-call(bf16[384,1408]{1,0:T(8,128)(2,1)S(1)} %bitcast.346, bf16[1408,3584]{1,0:T(8,128)(2,1)} %pad_maximum_fusion.w_ref), custom_call_target="tpu_custom_call" | custom-call | tf_op jit(solution)/shard_map/pallas_call | solution.py:142
  392.4 15.8 %collective-permute-done.24 = bf16[192,3584]{1,0:T(8,128)(2,1)} collective-permute-done((bf16[192,3584]{1,0:T(8,128)(2,1)}, bf16[192,3584]{1,0:T(8,128)(2,1)}, u32[]{:S(2)}, u32[]{:S(2)}) %collective-permute-start.24) | collective-permute-done | bytes 1376288 | tf_op jit(solution)/shard_map/ppermute | solution.py:204
  413.1 6.0 collective-permute-start.30
  429.9 16.8 %collective-permute-done.30 = bf16[192,3584]{1,0:T(8,128)(2,1)S(1)} collective-permute-done((bf16[192,3584]{1,0:T(8,128)(2,1)S(1)}, bf16[192,3584]{1,0:T(8,128)(2,1)S(1)}, u32[]{:S(2)}, u32[]{:S(2)}) %collective-permute-start.30) | collective-permute-done | bytes 1376288 | tf_op jit(solution)/shard_map/ppermute | solution.py:204
  451.6 5.5 collective-permute-start.36
  461.4 8.7 %shard_map.175 = bf16[384,3584]{1,0:T(8,128)(2,1)S(1)} custom-call(bf16[384,1408]{1,0:T(8,128)(2,1)S(1)} %bitcast.347, bf16[1408,3584]{1,0:T(8,128)(2,1)} %pad_maximum_fusion.w_ref), custom_call_target="tpu_custom_call" | custom-call | tf_op jit(solution)/shard_map/pallas_call | solution.py:142
  470.5 12.8 %collective-permute-done.36 = bf16[192,3584]{1,0:T(8,128)(2,1)S(1)} collective-permute-done((bf16[192,3584]{1,0:T(8,128)(2,1)}, bf16[192,3584]{1,0:T(8,128)(2,1)S(1)}, u32[]{:S(2)}, u32[]{:S(2)}) %collective-permute-start.36) | collective-permute-done | bytes 1376288 | tf_op jit(solution)/shard_map/ppermute | solution.py:204
  496.6 8.7 %shard_map.176 = bf16[384,3584]{1,0:T(8,128)(2,1)S(1)} custom-call(bf16[384,1408]{1,0:T(8,128)(2,1)S(1)} %bitcast.344, bf16[1408,3584]{1,0:T(8,128)(2,1)} %pad_maximum_fusion.w_ref), custom_call_target="tpu_custom_call" | custom-call | tf_op jit(solution)/shard_map/pallas_call | solution.py:142
  505.3 27.6 %collective-permute-done.38 = bf16[192,1728]{1,0:T(8,128)(2,1)S(1)} collective-permute-done((bf16[192,1728]{1,0:T(8,128)(2,1)S(1)}, bf16[192,1728]{1,0:T(8,128)(2,1)S(1)}, u32[]{:S(2)}, u32[]{:S(2)}) %collective-permute-start.38) | collective-permute-done | bytes 663584 | tf_op jit(solution)/shard_map/ppermute | solution.py:204
  535.5 13.3 %collective-permute-done.43 = bf16[192,1728]{1,0:T(8,128)(2,1)S(1)} collective-permute-done((bf16[192,1728]{1,0:T(8,128)(2,1)}, bf16[192,1728]{1,0:T(8,128)(2,1)S(1)}, u32[]{:S(2)}, u32[]{:S(2)}) %collective-permute-start.43) | collective-permute-done | bytes 663584 | tf_op jit(solution)/shard_map/ppermute | solution.py:204
  555.5 19.8 %collective-permute-done.44 = bf16[192,3584]{1,0:T(8,128)(2,1)S(1)} collective-permute-done((bf16[192,3584]{1,0:T(8,128)(2,1)S(1)}, bf16[192,3584]{1,0:T(8,128)(2,1)S(1)}, u32[]{:S(2)}, u32[]{:S(2)}) %collective-permute-start.44) | collective-permute-done | bytes 1376288 | tf_op jit(solution)/shard_map/ppermute | solution.py:204
  577.4 10.7 %collective-permute-start.48 = (bf16[192,3584]{1,0:T(8,128)(2,1)S(1)}, bf16[192,3584]{1,0:T(8,128)(2,1)}, u32[]{:S(2)}, u32[]{:S(2)}) collective-permute-start(bf16[192,3584]{1,0:T(8,128)(2,1)S(1)} %add_convert_fusion.1), channel_id=1, source_target_pairs={{0,8},{4,12},{8,16},{12,20},{16,24},{20,28},{1,9},{5,13},{9,17},{1... | collective-permute-start | bytes 4128776 | tf_op jit(solution)/shard_map/ppermute | solution.py:204
  592.1 6.2 shard_map.177
  598.6 6.5 collective-permute-done.49
  642.5 11.7 %collective-permute-done.55 = bf16[192,1728]{1,0:T(8,128)(2,1)} collective-permute-done((bf16[192,1728]{1,0:T(8,128)(2,1)S(1)}, bf16[192,1728]{1,0:T(8,128)(2,1)}, u32[]{:S(2)}, u32[]{:S(2)}) %collective-permute-start.55) | collective-permute-done | bytes 663584 | tf_op jit(solution)/shard_map/ppermute | solution.py:204
  661.2 7.6 %collective-permute-done.61 = bf16[192,1728]{1,0:T(8,128)(2,1)} collective-permute-done((bf16[192,1728]{1,0:T(8,128)(2,1)}, bf16[192,1728]{1,0:T(8,128)(2,1)}, u32[]{:S(2)}, u32[]{:S(2)}) %collective-permute-start.61) | collective-permute-done | bytes 663584 | tf_op jit(solution)/shard_map/ppermute | solution.py:204
  672.6 6.2 shard_map.178
  682.3 8.7 %collective-permute-done.63 = bf16[2,2,48,1280]{3,2,1,0:T(8,128)(2,1)S(1)} collective-permute-done((bf16[2,2,48,1280]{3,2,1,0:T(8,128)(2,1)S(1)}, bf16[2,2,48,1280]{3,2,1,0:T(8,128)(2,1)S(1)}, u32[]{:S(2)}, u32[]{:S(2)}) %collective-permute-start.63) | collective-permute-done | bytes 491552 | tf_op jit(solution)/shard_map/ppermute | solution.py:214
  691.6 5.9 collective-permute-done.66
  (412 shorter events, 275.1 us)
Async XLA Ops:
  7.2 146.9 %all-gather.4.cloned.1.call-start = ((), (), s32[]{:S(2)}) async-start(), calls=%async_computation | async-start | bytes 9830400 | tf_op jit(solution)/shard_map/all_gather | solution.py:291
  10.1 296.2 %all-gather.6.cloned.1.call-start = ((), (), s32[]{:S(2)}) async-start(), calls=%async_computation.1 | async-start | bytes 1966080 | tf_op jit(solution)/shard_map/all_gather | solution.py:291
  29.6 30.8 %collective-permute-start.1 = (bf16[640,3456]{1,0:T(8,128)(2,1)}, bf16[640,3456]{1,0:T(8,128)(2,1)}, u32[]{:S(2)}, u32[]{:S(2)}) collective-permute-start(bf16[640,3456]{1,0:T(8,128)(2,1)} %concatenate.133), channel_id=1, source_target_pairs={{0,4},{4,0},{8,12},{12,8},{16,20},{20,16},{24,28},{28,24},{1,5},{5... | collective-permute-start | bytes 13271048 | tf_op jit(solution)/shard_map/ppermute | solution.py:209
  177.9 38.4 %collective-permute-start.6 = (bf16[384,512]{1,0:T(8,128)(2,1)S(1)}, bf16[384,512]{1,0:T(8,128)(2,1)S(1)}, u32[]{:S(2)}, u32[]{:S(2)}) collective-permute-start(bf16[384,512]{1,0:T(8,128)(2,1)S(1)} %collective-permute-done.5), channel_id=1, source_target_pairs={{8,16},{12,20},{16,24},{20,28},{9,17},{13,21},{17,25},{21,29},{10,... | collective-permute-start | bytes 1179656 | tf_op jit(solution)/shard_map/ppermute | solution.py:204
  181.9 34.4 %collective-permute-start.8 = (bf16[384,512]{1,0:T(8,128)(2,1)S(1)}, bf16[384,512]{1,0:T(8,128)(2,1)S(1)}, u32[]{:S(2)}, u32[]{:S(2)}) collective-permute-start(bf16[384,512]{1,0:T(8,128)(2,1)S(1)} %collective-permute-done.7), channel_id=1, source_target_pairs={{8,0},{12,4},{16,8},{20,12},{9,1},{13,5},{17,9},{21,13},{10,2},{14... | collective-permute-start | bytes 1179656 | tf_op jit(solution)/shard_map/ppermute | solution.py:204
  185.9 18.8 %collective-permute-start.10 = (bf16[96,1280]{1,0:T(8,128)(2,1)}, bf16[96,1280]{1,0:T(8,128)(2,1)S(1)}, u32[]{:S(2)}, u32[]{:S(2)}) collective-permute-start(bf16[96,1280]{1,0:T(8,128)(2,1)} %get-tuple-element.101), channel_id=1, source_target_pairs={{0,24},{4,28},{8,0},{12,4},{16,8},{20,12},{24,16},{28,20},{1,25},{... | collective-permute-start | bytes 737288 | tf_op jit(solution)/shard_map/ppermute | solution.py:204
  187.1 29.2 %collective-permute-start.11 = (bf16[96,1280]{1,0:T(8,128)(2,1)}, bf16[96,1280]{1,0:T(8,128)(2,1)}, u32[]{:S(2)}, u32[]{:S(2)}) collective-permute-start(bf16[96,1280]{1,0:T(8,128)(2,1)} %get-tuple-element.102), channel_id=1, source_target_pairs={{0,16},{4,20},{8,24},{12,28},{16,0},{20,4},{24,8},{28,12},{1,17},{... | collective-permute-start | bytes 737288 | tf_op jit(solution)/shard_map/ppermute | solution.py:204
  232.6 15.1 %collective-permute-start.15 = (bf16[1536,512]{1,0:T(8,128)(2,1)}, bf16[1536,512]{1,0:T(8,128)(2,1)}, u32[]{:S(2)}, u32[]{:S(2)}) collective-permute-start(bf16[1536,512]{1,0:T(8,128)(2,1)} %pad_maximum_fusion.7), channel_id=1, source_target_pairs={{0,4},{4,0},{8,12},{12,8},{16,20},{20,16},{24,28},{28,24},{1,5},{5... | collective-permute-start | bytes 4718600 | tf_op jit(solution)/shard_map/ppermute | solution.py:209
  270.9 111.1 %all-gather.8.cloned.1.call-start = ((), (), s32[]{:S(2)}) async-start(), calls=%async_computation.2 | async-start | bytes 1966080 | tf_op jit(solution)/shard_map/all_gather | solution.py:291
  368.2 24.2 %collective-permute-start.25 = (bf16[192,3584]{1,0:T(8,128)(2,1)}, bf16[192,3584]{1,0:T(8,128)(2,1)}, u32[]{:S(2)}, u32[]{:S(2)}) collective-permute-start(bf16[192,3584]{1,0:T(8,128)(2,1)} %get-tuple-element.126), channel_id=1, source_target_pairs={{24,16},{28,20},{25,17},{29,21},{26,18},{30,22},{27,19},{31,23}} | collective-permute-start | bytes 4128776 | tf_op jit(solution)/shard_map/ppermute | solution.py:204
  378.7 29.5 %collective-permute-start.24 = (bf16[192,3584]{1,0:T(8,128)(2,1)}, bf16[192,3584]{1,0:T(8,128)(2,1)}, u32[]{:S(2)}, u32[]{:S(2)}) collective-permute-start(bf16[192,3584]{1,0:T(8,128)(2,1)} %get-tuple-element.125), channel_id=1, source_target_pairs={{0,8},{4,12},{1,9},{5,13},{2,10},{6,14},{3,11},{7,15}} | collective-permute-start | bytes 4128776 | tf_op jit(solution)/shard_map/ppermute | solution.py:204
  388.7 21.8 %collective-permute-start.26 = (bf16[2,2,48,1280]{3,2,1,0:T(8,128)(2,1)S(1)}, bf16[2,2,48,1280]{3,2,1,0:T(8,128)(2,1)S(1)}, u32[]{:S(2)}, u32[]{:S(2)}) collective-permute-start(bf16[2,2,48,1280]{3,2,1,0:T(8,128)(2,1)S(1)} %pad_maximum_fusion.24), channel_id=1, source_target_pairs={{0,1},{1,0},{2,3},{3,2},{4,5},{5,4},{6,7},{7,6},{8,9},{9,8},{10,11... | collective-permute-start | bytes 1474568 | tf_op jit(solution)/shard_map/ppermute | solution.py:214
  389.9 20.7 %collective-permute-start.27 = (bf16[2,2,48,1280]{3,2,1,0:T(8,128)(2,1)S(1)}, bf16[2,2,48,1280]{3,2,1,0:T(8,128)(2,1)S(1)}, u32[]{:S(2)}, u32[]{:S(2)}) collective-permute-start(bf16[2,2,48,1280]{3,2,1,0:T(8,128)(2,1)S(1)} %pad_maximum_fusion.25), channel_id=1, source_target_pairs={{0,2},{1,3},{2,0},{3,1},{4,6},{5,7},{6,4},{7,5},{8,10},{9,11},{10,... | collective-permute-start | bytes 1474568 | tf_op jit(solution)/shard_map/ppermute | solution.py:214
  412.4 17.5 %collective-permute-start.31 = (bf16[192,3584]{1,0:T(8,128)(2,1)S(1)}, bf16[192,3584]{1,0:T(8,128)(2,1)S(1)}, u32[]{:S(2)}, u32[]{:S(2)}) collective-permute-start(bf16[192,3584]{1,0:T(8,128)(2,1)S(1)} %get-tuple-element.134), channel_id=1, source_target_pairs={{16,8},{20,12},{24,16},{28,20},{17,9},{21,13},{25,17},{29,21},{18,... | collective-permute-start | bytes 4128776 | tf_op jit(solution)/shard_map/ppermute | solution.py:204
  413.1 33.6 %collective-permute-start.30 = (bf16[192,3584]{1,0:T(8,128)(2,1)S(1)}, bf16[192,3584]{1,0:T(8,128)(2,1)S(1)}, u32[]{:S(2)}, u32[]{:S(2)}) collective-permute-start(bf16[192,3584]{1,0:T(8,128)(2,1)S(1)} %get-tuple-element.133), channel_id=1, source_target_pairs={{0,8},{4,12},{8,16},{12,20},{1,9},{5,13},{9,17},{13,21},{2,10},{6,... | collective-permute-start | bytes 4128776 | tf_op jit(solution)/shard_map/ppermute | solution.py:204
  426.4 22.2 %collective-permute-start.32 = (bf16[1,2,48,1408]{3,2,1,0:T(8,128)(2,1)S(1)}, bf16[1,2,48,1408]{3,2,1,0:T(8,128)(2,1)S(1)}, u32[]{:S(2)}, u32[]{:S(2)}) collective-permute-start(bf16[1,2,48,1408]{3,2,1,0:T(8,128)(2,1)S(1)} %get-tuple-element.135), channel_id=1, source_target_pairs={{0,2},{1,3},{2,0},{3,1},{4,6},{5,7},{6,4},{7,5},{8,10},{9,11},{10,... | collective-permute-start | bytes 811016 | tf_op jit(solution)/shard_map/ppermute | solution.py:214
  428.2 20.3 %collective-permute-start.33 = (bf16[1,2,48,1408]{3,2,1,0:T(8,128)(2,1)S(1)}, bf16[1,2,48,1408]{3,2,1,0:T(8,128)(2,1)S(1)}, u32[]{:S(2)}, u32[]{:S(2)}) collective-permute-start(bf16[1,2,48,1408]{3,2,1,0:T(8,128)(2,1)S(1)} %get-tuple-element.136), channel_id=1, source_target_pairs={{0,1},{1,0},{2,3},{3,2},{4,5},{5,4},{6,7},{7,6},{8,9},{9,8},{10,11... | collective-permute-start | bytes 811016 | tf_op jit(solution)/shard_map/ppermute | solution.py:214
  451.6 31.7 %collective-permute-start.36 = (bf16[192,3584]{1,0:T(8,128)(2,1)}, bf16[192,3584]{1,0:T(8,128)(2,1)S(1)}, u32[]{:S(2)}, u32[]{:S(2)}) collective-permute-start(bf16[192,3584]{1,0:T(8,128)(2,1)} %get-tuple-element.142), channel_id=1, source_target_pairs={{0,8},{4,12},{8,16},{12,20},{16,24},{20,28},{1,9},{5,13},{9,17},{1... | collective-permute-start | bytes 4128776 | tf_op jit(solution)/shard_map/ppermute | solution.py:204
  457.1 30.8 %collective-permute-start.37 = (bf16[192,3584]{1,0:T(8,128)(2,1)S(1)}, bf16[192,3584]{1,0:T(8,128)(2,1)S(1)}, u32[]{:S(2)}, u32[]{:S(2)}) collective-permute-start(bf16[192,3584]{1,0:T(8,128)(2,1)S(1)} %get-tuple-element.143), channel_id=1, source_target_pairs={{8,0},{12,4},{16,8},{20,12},{24,16},{28,20},{9,1},{13,5},{17,9},{2... | collective-permute-start | bytes 4128776 | tf_op jit(solution)/shard_map/ppermute | solution.py:204
  488.9 46.0 %collective-permute-start.40 = (bf16[192,3584]{1,0:T(8,128)(2,1)S(1)}, bf16[192,3584]{1,0:T(8,128)(2,1)S(1)}, u32[]{:S(2)}, u32[]{:S(2)}) collective-permute-start(bf16[192,3584]{1,0:T(8,128)(2,1)S(1)} %get-tuple-element.148), channel_id=1, source_target_pairs={{24,16},{28,20},{25,17},{29,21},{26,18},{30,22},{27,19},{31,23}} | collective-permute-start | bytes 4128776 | tf_op jit(solution)/shard_map/ppermute | solution.py:204
  489.7 45.2 %collective-permute-start.39 = (bf16[192,3584]{1,0:T(8,128)(2,1)S(1)}, bf16[192,3584]{1,0:T(8,128)(2,1)S(1)}, u32[]{:S(2)}, u32[]{:S(2)}) collective-permute-start(bf16[192,3584]{1,0:T(8,128)(2,1)S(1)} %get-tuple-element.147), channel_id=1, source_target_pairs={{0,8},{4,12},{1,9},{5,13},{2,10},{6,14},{3,11},{7,15}} | collective-permute-start | bytes 4128776 | tf_op jit(solution)/shard_map/ppermute | solution.py:204
  493.8 39.0 %collective-permute-start.38 = (bf16[192,1728]{1,0:T(8,128)(2,1)S(1)}, bf16[192,1728]{1,0:T(8,128)(2,1)S(1)}, u32[]{:S(2)}, u32[]{:S(2)}) collective-permute-start(bf16[192,1728]{1,0:T(8,128)(2,1)S(1)} %pad_maximum_fusion.16), channel_id=1, source_target_pairs={{0,8},{4,12},{8,16},{12,20},{16,24},{20,28},{1,9},{5,13},{9,17},{1... | collective-permute-start | bytes 1990664 | tf_op jit(solution)/shard_map/ppermute | solution.py:204
  495.2 38.4 %collective-permute-start.42 = (bf16[192,1728]{1,0:T(8,128)(2,1)S(1)}, bf16[192,1728]{1,0:T(8,128)(2,1)}, u32[]{:S(2)}, u32[]{:S(2)}) collective-permute-start(bf16[192,1728]{1,0:T(8,128)(2,1)S(1)} %pad_maximum_fusion.16), channel_id=1, source_target_pairs={{8,0},{12,4},{16,8},{20,12},{24,16},{28,20},{9,1},{13,5},{17,9},{2... | collective-permute-start | bytes 1990664 | tf_op jit(solution)/shard_map/ppermute | solution.py:204
  548.7 26.6 %collective-permute-start.44 = (bf16[192,3584]{1,0:T(8,128)(2,1)S(1)}, bf16[192,3584]{1,0:T(8,128)(2,1)S(1)}, u32[]{:S(2)}, u32[]{:S(2)}) collective-permute-start(bf16[192,3584]{1,0:T(8,128)(2,1)S(1)} %get-tuple-element.149), channel_id=1, source_target_pairs={{0,8},{4,12},{8,16},{12,20},{1,9},{5,13},{9,17},{13,21},{2,10},{6,... | collective-permute-start | bytes 4128776 | tf_op jit(solution)/shard_map/ppermute | solution.py:204
  552.6 23.2 %collective-permute-start.45 = (bf16[192,3584]{1,0:T(8,128)(2,1)S(1)}, bf16[192,3584]{1,0:T(8,128)(2,1)S(1)}, u32[]{:S(2)}, u32[]{:S(2)}) collective-permute-start(bf16[192,3584]{1,0:T(8,128)(2,1)S(1)} %get-tuple-element.150), channel_id=1, source_target_pairs={{16,8},{20,12},{24,16},{28,20},{17,9},{21,13},{25,17},{29,21},{18,... | collective-permute-start | bytes 4128776 | tf_op jit(solution)/shard_map/ppermute | solution.py:204
  553.3 22.8 %collective-permute-start.46 = (bf16[192,1728]{1,0:T(8,128)(2,1)S(1)}, bf16[192,1728]{1,0:T(8,128)(2,1)S(1)}, u32[]{:S(2)}, u32[]{:S(2)}) collective-permute-start(bf16[192,1728]{1,0:T(8,128)(2,1)S(1)} %collective-permute-done.41), channel_id=1, source_target_pairs={{16,24},{20,28},{17,25},{21,29},{18,26},{22,30},{19,27},{23,31}} | collective-permute-start | bytes 1990664 | tf_op jit(solution)/shard_map/ppermute | solution.py:204
  554.2 21.9 %collective-permute-start.47 = (bf16[192,1728]{1,0:T(8,128)(2,1)S(1)}, bf16[192,1728]{1,0:T(8,128)(2,1)S(1)}, u32[]{:S(2)}, u32[]{:S(2)}) collective-permute-start(bf16[192,1728]{1,0:T(8,128)(2,1)S(1)} %collective-permute-done.43), channel_id=1, source_target_pairs={{8,0},{12,4},{9,1},{13,5},{10,2},{14,6},{11,3},{15,7}} | collective-permute-start | bytes 1990664 | tf_op jit(solution)/shard_map/ppermute | solution.py:204
  576.1 28.9 %collective-permute-start.49 = (bf16[192,3584]{1,0:T(8,128)(2,1)S(1)}, bf16[192,3584]{1,0:T(8,128)(2,1)S(1)}, u32[]{:S(2)}, u32[]{:S(2)}) collective-permute-start(bf16[192,3584]{1,0:T(8,128)(2,1)S(1)} %add_convert_fusion), channel_id=1, source_target_pairs={{8,0},{12,4},{16,8},{20,12},{24,16},{28,20},{9,1},{13,5},{17,9},{2... | collective-permute-start | bytes 4128776 | tf_op jit(solution)/shard_map/ppermute | solution.py:204
  577.4 28.9 %collective-permute-start.48 = (bf16[192,3584]{1,0:T(8,128)(2,1)S(1)}, bf16[192,3584]{1,0:T(8,128)(2,1)}, u32[]{:S(2)}, u32[]{:S(2)}) collective-permute-start(bf16[192,3584]{1,0:T(8,128)(2,1)S(1)} %add_convert_fusion.1), channel_id=1, source_target_pairs={{0,8},{4,12},{8,16},{12,20},{16,24},{20,28},{1,9},{5,13},{9,17},{1... | collective-permute-start | bytes 4128776 | tf_op jit(solution)/shard_map/ppermute | solution.py:204
  609.2 19.9 %collective-permute-start.50 = (bf16[192,1728]{1,0:T(8,128)(2,1)S(1)}, bf16[192,1728]{1,0:T(8,128)(2,1)S(1)}, u32[]{:S(2)}, u32[]{:S(2)}) collective-permute-start(bf16[192,1728]{1,0:T(8,128)(2,1)S(1)} %pad_maximum_fusion.17), channel_id=1, source_target_pairs={{0,8},{4,12},{8,16},{12,20},{16,24},{20,28},{1,9},{5,13},{9,17},{1... | collective-permute-start | bytes 1990664 | tf_op jit(solution)/shard_map/ppermute | solution.py:204
  614.3 15.5 %collective-permute-start.51 = (bf16[192,1728]{1,0:T(8,128)(2,1)S(1)}, bf16[192,1728]{1,0:T(8,128)(2,1)S(1)}, u32[]{:S(2)}, u32[]{:S(2)}) collective-permute-start(bf16[192,1728]{1,0:T(8,128)(2,1)S(1)} %pad_maximum_fusion.17), channel_id=1, source_target_pairs={{8,0},{12,4},{16,8},{20,12},{24,16},{28,20},{9,1},{13,5},{17,9},{2... | collective-permute-start | bytes 1990664 | tf_op jit(solution)/shard_map/ppermute | solution.py:204
  631.6 22.6 %collective-permute-start.55 = (bf16[192,1728]{1,0:T(8,128)(2,1)S(1)}, bf16[192,1728]{1,0:T(8,128)(2,1)}, u32[]{:S(2)}, u32[]{:S(2)}) collective-permute-start(bf16[192,1728]{1,0:T(8,128)(2,1)S(1)} %collective-permute-done.51), channel_id=1, source_target_pairs={{8,0},{12,4},{16,8},{20,12},{9,1},{13,5},{17,9},{21,13},{10,2},{14... | collective-permute-start | bytes 1990664 | tf_op jit(solution)/shard_map/ppermute | solution.py:204
  (95 other events, 997.7 us)
Sparse Core Ops, SparseCore 0:
  10.3 143.7 all-gather.3
  271.1 35.2 all-gather.5
  347.3 33.7 all-gather.7

commit v8 on v6

--- a/solution.py
+++ b/solution.py
@@ -318,11 +318,25 @@
             lax.dynamic_slice_in_dim(value_bias, kv_first, kv_cols, 0),
         ]
     ).astype(F32)
-    kv_weight, (gate_weight, up_weight, out_weight, down_weight, layer_input) = after(
-        kv_weight, (gate_weight, up_weight, out_weight, down_weight, layer_input)
-    )
-    kv_weight = line_collect(kv_weight)
     q_weight = line_collect(query_weight)
+    kv_state = ([kv_weight], [kv_weight])
+    gather_step(kv_state, 1)
+    if planes > 3:
+        ends, (gate_weight, up_weight) = after(
+            (kv_state[0][-1], kv_state[1][-1]), (gate_weight, up_weight)
+        )
+        kv_state[0][-1], kv_state[1][-1] = ends
+    for t in range(2, planes):
+        gather_step(kv_state, t)
+        if t == 2 and planes > 3:
+            ends, (out_weight, down_weight) = after(
+                (kv_state[0][-1], kv_state[1][-1]), (out_weight, down_weight)
+            )
+            kv_state[0][-1], kv_state[1][-1] = ends
+    kv_slots = jnp.stack(gather_slots(kv_state), axis=0)
+    kv_weight = jnp.concatenate(
+        [lax.dynamic_index_in_dim(kv_slots, (plane - z) % planes, 0, False) for z in range(planes)], axis=0
+    )
 
     x = layer_input.astype(F32)
     mean_sq = jnp.mean(x * x, axis=-1, keepdims=True)
@@ -401,7 +415,7 @@
     chunked = [
         jnp.concatenate(
             [
-                lax.dynamic_slice_in_dim(mixed, (mlp_rank ^ j) * share + h * sub, sub, 0)
+                lax.dynamic_slice_in_dim(mixed, ((mlp_rank ^ j) if h == 0 else j) * share + h * sub, sub, 0)
                 for j in range(mlp_count)
             ],
             axis=0,
@@ -411,24 +425,28 @@
 
     collected = [line_collect(v) for v in chunked]
 
-    def attn_terms(h):
-        heads = jnp.concatenate(
+    def heads_of(h):
+        return jnp.concatenate(
             [
                 lax.dynamic_slice_in_dim(collected[h], (plane - k) % planes * crows, crows, 0)
                 for k in order
             ],
             axis=0,
         )
-        return sum_begin(product(heads, out_wide, BF16).reshape(planes, mlp_count, sub, dz))
-
-    def attn_end(h, states):
-        return lane_input[:, h].astype(F32) + sum_end(states)
-
-    def lane_terms(residual):
+
+    def attn_terms(h):
+        return sum_begin(product(heads_of(h), out_wide, BF16).reshape(planes, mlp_count, sub, dz))
+
+    def share_first(x):
+        return jnp.swapaxes(x.reshape(planes, mlp_count, sub, -1), 0, 1).reshape(x.shape)
+
+    def attn_end(h, summed):
+        return lane_input[:, h].astype(F32) + summed
+
+    def lane_of(residual):
         square = residual * residual
         square = sum(square[..., i : i + HD] for i in range(0, dz, HD))
-        lane = jnp.concatenate([(residual * gain_lane).astype(BF16), square.astype(BF16)], axis=-1)
-        return spread_begin(lane)
+        return jnp.concatenate([(residual * gain_lane).astype(BF16), square.astype(BF16)], axis=-1)
 
     def contract_half(lane):
         part = product(lane.reshape(-1, dz + HD), glu_weight, BF16).reshape(-1, crows, 2 * units + HD)
@@ -469,8 +487,8 @@
     states = attn_terms(0)
     for n in range(bits):
         states = sum_stage(states, n)
-    residuals = [attn_end(0, states)]
-    states = lane_terms(residuals[0])
+    residuals = [attn_end(0, sum_end(states))]
+    states = spread_begin(lane_of(residuals[0]))
     for n in range(bits):
         states = spread_stage(states, n)
     lanes = lax.optimization_barrier(spread_end(states))
@@ -480,25 +498,19 @@
     following = None
     if chunks > 1:
         collected[1], parts[0] = after(collected[1], parts[0])
-        states = attn_terms(1)
-        gots = sum_launch(states, 0)
+        terms = product(share_first(heads_of(1)), out_wide, BF16)
+        _, carried = after(terms, carried)
+        terms = lax.psum_scatter(terms, "mlp", scatter_dimension=0, tiled=True)
     for t in range(2, steps + 1):
+        carried, _ = scatter_step(parts, carried, t)
         if chunks > 1 and t == 2:
-            carried, gots = scatter_step(parts, carried, t, gots)
-            states = sum_land(states, 0, gots)
-            for n in range(1, bits):
-                states = sum_stage(states, n)
-            residuals.append(attn_end(1, states))
-            states = lane_terms(residuals[1])
-            gots = spread_launch(states, 0)
-        elif chunks > 1 and t == 3:
-            carried, gots = scatter_step(parts, carried, t, gots)
-            states = spread_land(states, 0, gots)
-            for n in range(1, bits):
-                states = spread_stage(states, n)
-            following = contract(spread_end(states))
-        else:
-            carried, _ = scatter_step(parts, carried, t)
+            terms, _ = after(terms, carried)
+            residuals.append(attn_end(1, terms.astype(F32).reshape(planes, sub, dz)))
+            lane = lane_of(residuals[1]).reshape(planes * sub, dz + HD)
+            lane = lax.all_gather(lane, "mlp", axis=0, tiled=True)
+            lane = lane.reshape(mlp_count, planes, sub, dz + HD)
+    if chunks > 1:
+        following = contract([jnp.swapaxes(v, 0, 1) for v in (lane[:, :half], lane[:, half:])])
     finals = []
     if following is not None:
         ahead, carried = scatter_step(following, None, 1, carried)
@@ -515,6 +527,13 @@
         states = down_terms(state)
         gots = sum_launch(states, 0)
         hidden = activate(following, ahead)
+        hidden = jnp.concatenate(
+            [
+                lax.dynamic_slice_in_dim(hidden, (mlp_rank ^ j) * sub, sub, 0)
+                for j in range(mlp_count)
+            ],
+            axis=0,
+        )
         state = ([hidden], [hidden])
         for t in range(1, steps + 1):
             gather_step(state, t)

time: 709 us -> 777 us (1.096)
  waiting for transfers between devices: 360 us -> 433 us
  starting transfers between devices: 120 us -> 106 us
    ppermute x39 -> x45, waiting for transfers between devices: 250 us -> 303 us  [move(): lax.ppermute(x, 'seq', [(a * CORES + e, b * CORES + e) for a, b in pairs...]
    all_gather x0 -> x1, waiting for transfers between devices: none -> 25.4 us  [shards(): lane = lax.all_gather(lane, 'mlp', axis=0, tiled=True)]
    ppermute x24 -> x16, starting transfers between devices: 36.4 us -> 18.4 us  [partner(): return lax.ppermute(x, 'mlp', [(a, a ^ bit) for a in range(mlp_count)])]
    ppermute x24 -> x16, waiting for transfers between devices: 65.7 us -> 59.6 us  [partner(): return lax.ppermute(x, 'mlp', [(a, a ^ bit) for a in range(mlp_count)])]
    unnamed x103 -> x126, local copies, waits for them, and re-layouts: 12.6 us -> 18.5 us
    ppermute x39 -> x45, starting transfers between devices: 81.1 us -> 85.9 us  [move(): lax.ppermute(x, 'seq', [(a * CORES + e, b * CORES + e) for a, b in pairs...]
    all_gather x4 -> x3, waiting for transfers between devices: 42.5 us -> 43.6 us  [line_collect(): return lax.all_gather(x, 'seq', axis=0, tiled=True, axis_index_groups=lines)]
  transfers between devices with their start and end apart: 74 -> 73, of which waited for: 41 -> 42; matrix products, arithmetic and copies ran while one was open for 14% -> 12% of each run, Pallas kernels for 8% -> 7%
where the time goes in v8:
time: 777 us; the launch traced here: 769 us
  waiting for transfers between devices  433 us (56%)
  starting transfers between devices  106 us (14%)
  Pallas kernels  79.4 us (10%)
  other arithmetic  74.6 us (10%)
  local copies, waits for them, and re-layouts  59.2 us (8%)
  between operations  17.4 us (2%)
    ppermute x45, waiting for transfers between devices, move(): lax.ppermute(x, 'seq', [(a * CORES + e, b * CORES + e) for a, b in pairs...  303 us
    ppermute x45, starting transfers between devices, move(): lax.ppermute(x, 'seq', [(a * CORES + e, b * CORES + e) for a, b in pairs...  85.9 us
    pallas_call x10, Pallas kernels, product(): pl.pallas_call(product_kernel, grid=(cols // tile,), in_specs=[pl.BlockSp...  65.5 us
    ppermute x16, waiting for transfers between devices, partner(): return lax.ppermute(x, 'mlp', [(a, a ^ bit) for a in range(mlp_count)])  59.6 us
    all_gather x3, waiting for transfers between devices, line_collect(): return lax.all_gather(x, 'seq', axis=0, tiled=True, axis_index_groups=lines)  43.6 us
    all_gather x1, waiting for transfers between devices, shards(): lane = lax.all_gather(lane, 'mlp', axis=0, tiled=True)  25.4 us
    unnamed x126, local copies, waits for them, and re-layouts  18.5 us
    ppermute x16, starting transfers between devices, partner(): return lax.ppermute(x, 'mlp', [(a, a ^ bit) for a in range(mlp_count)])  18.4 us
  transfers between devices with their start and end apart: 73, of which 42 were waited for; matrix products, arithmetic and copies ran while one was open for 12% of the time, Pallas kernels for 7%

profile of v8, /device:TPU:0, one launch (start us, length us, event | category | flops | bytes accessed | tf_op | source)
XLA Modules:
  0.0 769.0 jit_solution(10171895924571333013)
XLA Ops:
  9.3 5.8 collective-permute-start.1
  45.4 7.0 concatenate.137
  55.4 42.4 %collective-permute-done.5 = bf16[640,512]{1,0:T(8,128)(2,1)S(1)} collective-permute-done((bf16[640,512]{1,0:T(8,128)(2,1)}, bf16[640,512]{1,0:T(8,128)(2,1)S(1)}, u32[]{:S(2)}, u32[]{:S(2)}) %collective-permute-start.5) | collective-permute-done | bytes 655392 | tf_op jit(solution)/shard_map/ppermute | solution.py:203
  106.3 44.0 %collective-permute-done.12 = bf16[640,512]{1,0:T(8,128)(2,1)S(1)} collective-permute-done((bf16[640,512]{1,0:T(8,128)(2,1)S(1)}, bf16[640,512]{1,0:T(8,128)(2,1)S(1)}, u32[]{:S(2)}, u32[]{:S(2)}) %collective-permute-start.12) | collective-permute-done | bytes 655392 | tf_op jit(solution)/shard_map/ppermute | solution.py:203
  167.0 7.3 pad_maximum_fusion.w_ref
  191.7 7.4 collective-permute-done.16
  201.1 10.2 %collective-permute-done.17 = bf16[384,512]{1,0:T(8,128)(2,1)S(1)} collective-permute-done((bf16[384,512]{1,0:T(8,128)(2,1)S(1)}, bf16[384,512]{1,0:T(8,128)(2,1)S(1)}, u32[]{:S(2)}, u32[]{:S(2)}) %collective-permute-start.17) | collective-permute-done | bytes 393248 | tf_op jit(solution)/shard_map/ppermute | solution.py:203
  215.3 7.3 collective-permute-done.18
  226.8 7.5 shard_map.167.own_ref
  252.1 13.5 %collective-permute-done.11 = bf16[96,1280]{1,0:T(8,128)(2,1)S(1)} collective-permute-done((bf16[96,1280]{1,0:T(8,128)(2,1)}, bf16[96,1280]{1,0:T(8,128)(2,1)S(1)}, u32[]{:S(2)}, u32[]{:S(2)}) %collective-permute-start.11) | collective-permute-done | bytes 245792 | tf_op jit(solution)/shard_map/ppermute | solution.py:203
  266.3 11.2 %shard_map.170 = bf16[384,1024]{1,0:T(8,128)(2,1)S(1)} custom-call(s32[2]{0:T(128)S(1)} %convert_reduce_fusion.1.count, s32[2,16]{1,0:T(2,128)S(1)} %select_reduce_fusion.1.active, s32[16]{0:T(128)S(1)} %select_reduce_fusion.2.piece_stream, f32[768,1024]{1,0:T(8,128)S(1)} %copy-done.3, f32[384,1024]{1,0:T(8,128)} %collective-permute-done.8.sib_ref, ...), custom_call_target="tpu_custom_call" | custom-call | tf_op jit(solution)/shard_map/pallas_call | solution.py:109
  279.6 39.2 %all-gather.7.cloned.1.call-done = bf16[768,1024]{1,0:T(8,128)(2,1)} async-done(((bf16[192,1024]{1,0:T(8,128)(2,1)}), bf16[768,1024]{1,0:T(8,128)(2,1)}) %all-gather.7.cloned.1.call-update) | async-done | bytes 1572880 | tf_op jit(solution)/shard_map/all_gather | solution.py:296
  327.2 9.6 %collective-permute-done.23 = bf16[2,2,48,1280]{3,2,1,0:T(8,128)(2,1)S(1)} collective-permute-done((bf16[2,2,48,1280]{3,2,1,0:T(8,128)(2,1)S(1)}, bf16[2,2,48,1280]{3,2,1,0:T(8,128)(2,1)S(1)}, u32[]{:S(2)}, u32[]{:S(2)}) %collective-permute-start.23) | collective-permute-done | bytes 491552 | tf_op jit(solution)/shard_map/ppermute | solution.py:213
  358.6 8.0 %collective-permute-done.29 = bf16[2,2,48,1408]{3,2,1,0:T(8,128)(2,1)S(1)} collective-permute-done((bf16[2,2,48,1408]{3,2,1,0:T(8,128)(2,1)S(1)}, bf16[2,2,48,1408]{3,2,1,0:T(8,128)(2,1)S(1)}, u32[]{:S(2)}, u32[]{:S(2)}) %collective-permute-start.29) | collective-permute-done | bytes 540704 | tf_op jit(solution)/shard_map/ppermute | solution.py:213
  367.4 8.7 %shard_map.172 = bf16[384,3584]{1,0:T(8,128)(2,1)S(1)} custom-call(bf16[384,1408]{1,0:T(8,128)(2,1)S(1)} %bitcast.296, bf16[1408,3584]{1,0:T(8,128)(2,1)} %pad_maximum_fusion.w_ref), custom_call_target="tpu_custom_call" | custom-call | tf_op jit(solution)/shard_map/pallas_call | solution.py:141
  378.0 8.7 %shard_map.173 = bf16[384,3584]{1,0:T(8,128)(2,1)S(1)} custom-call(bf16[384,1408]{1,0:T(8,128)(2,1)S(1)} %bitcast.297, bf16[1408,3584]{1,0:T(8,128)(2,1)} %pad_maximum_fusion.w_ref), custom_call_target="tpu_custom_call" | custom-call | tf_op jit(solution)/shard_map/pallas_call | solution.py:141
  403.8 28.7 %collective-permute-done.30 = bf16[192,3584]{1,0:T(8,128)(2,1)S(1)} collective-permute-done((bf16[192,3584]{1,0:T(8,128)(2,1)}, bf16[192,3584]{1,0:T(8,128)(2,1)S(1)}, u32[]{:S(2)}, u32[]{:S(2)}) %collective-permute-start.30) | collective-permute-done | bytes 1376288 | tf_op jit(solution)/shard_map/ppermute | solution.py:203
  440.6 26.5 %collective-permute-done.32 = bf16[192,3584]{1,0:T(8,128)(2,1)S(1)} collective-permute-done((bf16[192,3584]{1,0:T(8,128)(2,1)S(1)}, bf16[192,3584]{1,0:T(8,128)(2,1)S(1)}, u32[]{:S(2)}, u32[]{:S(2)}) %collective-permute-start.32) | collective-permute-done | bytes 1376288 | tf_op jit(solution)/shard_map/ppermute | solution.py:203
  474.4 8.6 %collective-permute-start.34 = (bf16[192,3584]{1,0:T(8,128)(2,1)}, bf16[192,3584]{1,0:T(8,128)(2,1)}, u32[]{:S(2)}, u32[]{:S(2)}) collective-permute-start(bf16[192,3584]{1,0:T(8,128)(2,1)} %get-tuple-element.126), channel_id=1, source_target_pairs={{0,8},{4,12},{8,16},{12,20},{16,24},{20,28},{1,9},{5,13},{9,17},{1... | collective-permute-start | bytes 4128776 | tf_op jit(solution)/shard_map/ppermute | solution.py:203
  484.3 25.4 %all-gather.11.cloned.1.call-done = bf16[768,1408]{1,0:T(8,128)(2,1)} async-done(((bf16[192,1408]{1,0:T(8,128)(2,1)}), bf16[768,1408]{1,0:T(8,128)(2,1)}) %all-gather.11.cloned.1.call-update) | async-done | bytes 2162704 | tf_op jit(solution)/shard_map/all_gather | solution.py:510
  511.5 8.7 %shard_map.175 = bf16[384,3584]{1,0:T(8,128)(2,1)S(1)} custom-call(bf16[384,1408]{1,0:T(8,128)(2,1)S(1)} %bitcast.298, bf16[1408,3584]{1,0:T(8,128)(2,1)} %pad_maximum_fusion.w_ref), custom_call_target="tpu_custom_call" | custom-call | tf_op jit(solution)/shard_map/pallas_call | solution.py:141
  532.3 8.7 %shard_map.176 = bf16[384,3584]{1,0:T(8,128)(2,1)S(1)} custom-call(bf16[384,1408]{1,0:T(8,128)(2,1)S(1)} %bitcast.295, bf16[1408,3584]{1,0:T(8,128)(2,1)} %pad_maximum_fusion.w_ref), custom_call_target="tpu_custom_call" | custom-call | tf_op jit(solution)/shard_map/pallas_call | solution.py:141
  541.0 31.4 %collective-permute-done.36 = bf16[192,1728]{1,0:T(8,128)(2,1)S(1)} collective-permute-done((bf16[192,1728]{1,0:T(8,128)(2,1)S(1)}, bf16[192,1728]{1,0:T(8,128)(2,1)S(1)}, u32[]{:S(2)}, u32[]{:S(2)}) %collective-permute-start.36) | collective-permute-done | bytes 663584 | tf_op jit(solution)/shard_map/ppermute | solution.py:203
  576.9 15.9 %collective-permute-done.41 = bf16[192,1728]{1,0:T(8,128)(2,1)S(1)} collective-permute-done((bf16[192,1728]{1,0:T(8,128)(2,1)S(1)}, bf16[192,1728]{1,0:T(8,128)(2,1)S(1)}, u32[]{:S(2)}, u32[]{:S(2)}) %collective-permute-start.41) | collective-permute-done | bytes 663584 | tf_op jit(solution)/shard_map/ppermute | solution.py:203
  605.1 21.4 %collective-permute-done.42 = bf16[192,3584]{1,0:T(8,128)(2,1)} collective-permute-done((bf16[192,3584]{1,0:T(8,128)(2,1)}, bf16[192,3584]{1,0:T(8,128)(2,1)}, u32[]{:S(2)}, u32[]{:S(2)}) %collective-permute-start.42) | collective-permute-done | bytes 1376288 | tf_op jit(solution)/shard_map/ppermute | solution.py:203
  637.5 6.2 shard_map.177
  644.0 15.9 %collective-permute-done.46 = bf16[192,3584]{1,0:T(8,128)(2,1)S(1)} collective-permute-done((bf16[192,3584]{1,0:T(8,128)(2,1)S(1)}, bf16[192,3584]{1,0:T(8,128)(2,1)S(1)}, u32[]{:S(2)}, u32[]{:S(2)}) %collective-permute-start.46) | collective-permute-done | bytes 1376288 | tf_op jit(solution)/shard_map/ppermute | solution.py:203
  672.5 6.8 collective-permute-done.50
  694.3 6.4 collective-permute-done.53
  704.8 9.5 %collective-permute-done.59 = bf16[192,1728]{1,0:T(8,128)(2,1)} collective-permute-done((bf16[192,1728]{1,0:T(8,128)(2,1)}, bf16[192,1728]{1,0:T(8,128)(2,1)}, u32[]{:S(2)}, u32[]{:S(2)}) %collective-permute-start.59) | collective-permute-done | bytes 663584 | tf_op jit(solution)/shard_map/ppermute | solution.py:203
  718.6 6.2 shard_map.178
  727.5 9.3 %collective-permute-done.62 = bf16[2,2,48,1280]{3,2,1,0:T(8,128)(2,1)S(1)} collective-permute-done((bf16[2,2,48,1280]{3,2,1,0:T(8,128)(2,1)S(1)}, bf16[2,2,48,1280]{3,2,1,0:T(8,128)(2,1)S(1)}, u32[]{:S(2)}, u32[]{:S(2)}) %collective-permute-start.62) | collective-permute-done | bytes 491552 | tf_op jit(solution)/shard_map/ppermute | solution.py:213
  (433 shorter events, 278.1 us)
Async XLA Ops:
  7.2 219.6 %all-gather.5.cloned.1.call-start = ((), (), s32[]{:S(2)}) async-start(), calls=%async_computation.1 | async-start | bytes 6553600 | tf_op jit(solution)/shard_map/all_gather | solution.py:296
  9.3 18.9 %collective-permute-start.1 = (bf16[640,512]{1,0:T(8,128)(2,1)S(1)}, bf16[640,512]{1,0:T(8,128)(2,1)}, u32[]{:S(2)}, u32[]{:S(2)}) collective-permute-start(bf16[640,512]{1,0:T(8,128)(2,1)S(1)} %get-tuple-element.249), channel_id=1, source_target_pairs={{0,8},{4,12},{8,16},{12,20},{16,24},{20,28},{1,9},{5,13},{9,17},{1... | collective-permute-start | bytes 1966088 | tf_op jit(solution)/shard_map/ppermute | solution.py:203
  23.6 128.6 %collective-permute-start = (bf16[384,2560]{1,0:T(8,128)(2,1)}, bf16[384,2560]{1,0:T(8,128)(2,1)}, u32[]{:S(2)}, u32[]{:S(2)}) collective-permute-start(bf16[384,2560]{1,0:T(8,128)(2,1)} %get-tuple-element.173), channel_id=1, source_target_pairs={{0,4},{4,0},{8,12},{12,8},{16,20},{20,16},{24,28},{28,24},{1,5},{5... | collective-permute-start | bytes 5898248 | tf_op jit(solution)/shard_map/ppermute | solution.py:208
  23.7 295.1 %all-gather.7.cloned.1.call-start = ((), (), s32[]{:S(2)}) async-start(), calls=%async_computation.2 | async-start | bytes 1966080 | tf_op jit(solution)/shard_map/all_gather | solution.py:296
  52.4 109.9 %collective-permute-start.3 = (bf16[640,3456]{1,0:T(8,128)(2,1)}, bf16[640,3456]{1,0:T(8,128)(2,1)}, u32[]{:S(2)}, u32[]{:S(2)}) collective-permute-start(bf16[640,3456]{1,0:T(8,128)(2,1)} %concatenate.137), channel_id=1, source_target_pairs={{0,4},{4,0},{8,12},{12,8},{16,20},{20,16},{24,28},{28,24},{1,5},{5... | collective-permute-start | bytes 13271048 | tf_op jit(solution)/shard_map/ppermute | solution.py:208
  53.4 44.4 %collective-permute-start.5 = (bf16[640,512]{1,0:T(8,128)(2,1)}, bf16[640,512]{1,0:T(8,128)(2,1)S(1)}, u32[]{:S(2)}, u32[]{:S(2)}) collective-permute-start(bf16[640,512]{1,0:T(8,128)(2,1)} %collective-permute-done.2), channel_id=1, source_target_pairs={{8,0},{12,4},{16,8},{20,12},{9,1},{13,5},{17,9},{21,13},{10,2},{14... | collective-permute-start | bytes 1966088 | tf_op jit(solution)/shard_map/ppermute | solution.py:203
  102.2 48.1 %collective-permute-start.12 = (bf16[640,512]{1,0:T(8,128)(2,1)S(1)}, bf16[640,512]{1,0:T(8,128)(2,1)S(1)}, u32[]{:S(2)}, u32[]{:S(2)}) collective-permute-start(bf16[640,512]{1,0:T(8,128)(2,1)S(1)} %collective-permute-done.5), channel_id=1, source_target_pairs={{8,0},{12,4},{9,1},{13,5},{10,2},{14,6},{11,3},{15,7}} | collective-permute-start | bytes 1966088 | tf_op jit(solution)/shard_map/ppermute | solution.py:203
  104.2 53.4 %collective-permute-start.7 = (bf16[1728,640]{1,0:T(8,128)(2,1)}, bf16[1728,640]{1,0:T(8,128)(2,1)S(1)}, u32[]{:S(2)}, u32[]{:S(2)}) collective-permute-start(bf16[1728,640]{1,0:T(8,128)(2,1)} %param.25), channel_id=1, source_target_pairs={{0,4},{4,0},{8,12},{12,8},{16,20},{20,16},{24,28},{28,24},{1,5},{5... | collective-permute-start | bytes 6635528 | tf_op jit(solution)/shard_map/ppermute | solution.py:208
  104.4 52.9 %collective-permute-start.6 = (bf16[1024,640]{1,0:T(8,128)(2,1)S(1)}, bf16[1024,640]{1,0:T(8,128)(2,1)S(1)}, u32[]{:S(2)}, u32[]{:S(2)}) collective-permute-start(bf16[1024,640]{1,0:T(8,128)(2,1)S(1)} %copy-done.28), channel_id=1, source_target_pairs={{0,4},{4,0},{8,12},{12,8},{16,20},{20,16},{24,28},{28,24},{1,5},{5... | collective-permute-start | bytes 3932168 | tf_op jit(solution)/shard_map/ppermute | solution.py:208
  226.4 19.6 %collective-permute-start.21 = (bf16[1536,512]{1,0:T(8,128)(2,1)}, bf16[1536,512]{1,0:T(8,128)(2,1)}, u32[]{:S(2)}, u32[]{:S(2)}) collective-permute-start(bf16[1536,512]{1,0:T(8,128)(2,1)} %pad_maximum_fusion.8), channel_id=1, source_target_pairs={{0,4},{4,0},{8,12},{12,8},{16,20},{20,16},{24,28},{28,24},{1,5},{5... | collective-permute-start | bytes 4718600 | tf_op jit(solution)/shard_map/ppermute | solution.py:208
  237.4 28.2 %collective-permute-start.8 = (f32[384,1024]{1,0:T(8,128)}, f32[384,1024]{1,0:T(8,128)}, u32[]{:S(2)}, u32[]{:S(2)}) collective-permute-start(f32[384,1024]{1,0:T(8,128)} %slice.522), channel_id=1, source_target_pairs={{0,4},{4,0},{8,12},{12,8},{16,20},{20,16},{24,28},{28,24},{1,5},{5... | collective-permute-start | bytes 4718600 | tf_op jit(solution)/shard_map/ppermute | solution.py:208
  245.4 20.2 %collective-permute-start.11 = (bf16[96,1280]{1,0:T(8,128)(2,1)}, bf16[96,1280]{1,0:T(8,128)(2,1)S(1)}, u32[]{:S(2)}, u32[]{:S(2)}) collective-permute-start(bf16[96,1280]{1,0:T(8,128)(2,1)} %get-tuple-element.94), channel_id=1, source_target_pairs={{0,16},{4,20},{8,24},{12,28},{16,0},{20,4},{24,8},{28,12},{1,17},{... | collective-permute-start | bytes 737288 | tf_op jit(solution)/shard_map/ppermute | solution.py:203
  245.4 20.2 %collective-permute-start.9 = (bf16[96,1280]{1,0:T(8,128)(2,1)}, bf16[96,1280]{1,0:T(8,128)(2,1)S(1)}, u32[]{:S(2)}, u32[]{:S(2)}) collective-permute-start(bf16[96,1280]{1,0:T(8,128)(2,1)} %get-tuple-element.92), channel_id=1, source_target_pairs={{0,8},{4,12},{8,16},{12,20},{16,24},{20,28},{24,0},{28,4},{1,9},{5... | collective-permute-start | bytes 737288 | tf_op jit(solution)/shard_map/ppermute | solution.py:203
  279.1 113.6 %all-gather.9.cloned.1.call-start = ((), (), s32[]{:S(2)}) async-start(), calls=%async_computation.3 | async-start | bytes 1966080 | tf_op jit(solution)/shard_map/all_gather | solution.py:296
  357.6 110.5 %reduce-scatter.2.cloned.1.call-start = ((), (), s32[]{:S(2)}) async-start(), calls=%async_computation.4 | async-start | bytes 2457600 | tf_op jit(solution)/shard_map/reduce_scatter | solution.py:503
  400.5 109.2 %all-gather.11.cloned.1.call-start = ((), (), s32[]{:S(2)}) async-start(), calls=%async_computation.5 | async-start | bytes 2703360 | tf_op jit(solution)/shard_map/all_gather | solution.py:510
  400.6 31.9 %collective-permute-start.30 = (bf16[192,3584]{1,0:T(8,128)(2,1)}, bf16[192,3584]{1,0:T(8,128)(2,1)S(1)}, u32[]{:S(2)}, u32[]{:S(2)}) collective-permute-start(bf16[192,3584]{1,0:T(8,128)(2,1)} %get-tuple-element.118), channel_id=1, source_target_pairs={{0,8},{4,12},{1,9},{5,13},{2,10},{6,14},{3,11},{7,15}} | collective-permute-start | bytes 4128776 | tf_op jit(solution)/shard_map/ppermute | solution.py:203
  403.1 29.4 %collective-permute-start.31 = (bf16[192,3584]{1,0:T(8,128)(2,1)}, bf16[192,3584]{1,0:T(8,128)(2,1)S(1)}, u32[]{:S(2)}, u32[]{:S(2)}) collective-permute-start(bf16[192,3584]{1,0:T(8,128)(2,1)} %get-tuple-element.119), channel_id=1, source_target_pairs={{24,16},{28,20},{25,17},{29,21},{26,18},{30,22},{27,19},{31,23}} | collective-permute-start | bytes 4128776 | tf_op jit(solution)/shard_map/ppermute | solution.py:203
  434.4 32.7 %collective-permute-start.32 = (bf16[192,3584]{1,0:T(8,128)(2,1)S(1)}, bf16[192,3584]{1,0:T(8,128)(2,1)S(1)}, u32[]{:S(2)}, u32[]{:S(2)}) collective-permute-start(bf16[192,3584]{1,0:T(8,128)(2,1)S(1)} %get-tuple-element.122), channel_id=1, source_target_pairs={{0,8},{4,12},{8,16},{12,20},{1,9},{5,13},{9,17},{13,21},{2,10},{6,... | collective-permute-start | bytes 4128776 | tf_op jit(solution)/shard_map/ppermute | solution.py:203
  438.7 29.4 %collective-permute-start.33 = (bf16[192,3584]{1,0:T(8,128)(2,1)S(1)}, bf16[192,3584]{1,0:T(8,128)(2,1)}, u32[]{:S(2)}, u32[]{:S(2)}) collective-permute-start(bf16[192,3584]{1,0:T(8,128)(2,1)S(1)} %get-tuple-element.123), channel_id=1, source_target_pairs={{16,8},{20,12},{24,16},{28,20},{17,9},{21,13},{25,17},{29,21},{18,... | collective-permute-start | bytes 4128776 | tf_op jit(solution)/shard_map/ppermute | solution.py:203
  474.4 46.1 %collective-permute-start.34 = (bf16[192,3584]{1,0:T(8,128)(2,1)}, bf16[192,3584]{1,0:T(8,128)(2,1)}, u32[]{:S(2)}, u32[]{:S(2)}) collective-permute-start(bf16[192,3584]{1,0:T(8,128)(2,1)} %get-tuple-element.126), channel_id=1, source_target_pairs={{0,8},{4,12},{8,16},{12,20},{16,24},{20,28},{1,9},{5,13},{9,17},{1... | collective-permute-start | bytes 4128776 | tf_op jit(solution)/shard_map/ppermute | solution.py:203
  483.0 37.4 %collective-permute-start.35 = (bf16[192,3584]{1,0:T(8,128)(2,1)}, bf16[192,3584]{1,0:T(8,128)(2,1)}, u32[]{:S(2)}, u32[]{:S(2)}) collective-permute-start(bf16[192,3584]{1,0:T(8,128)(2,1)} %get-tuple-element.127), channel_id=1, source_target_pairs={{8,0},{12,4},{16,8},{20,12},{24,16},{28,20},{9,1},{13,5},{17,9},{2... | collective-permute-start | bytes 4128776 | tf_op jit(solution)/shard_map/ppermute | solution.py:203
  524.9 49.8 %collective-permute-start.37 = (bf16[192,3584]{1,0:T(8,128)(2,1)S(1)}, bf16[192,3584]{1,0:T(8,128)(2,1)S(1)}, u32[]{:S(2)}, u32[]{:S(2)}) collective-permute-start(bf16[192,3584]{1,0:T(8,128)(2,1)S(1)} %get-tuple-element.131), channel_id=1, source_target_pairs={{0,8},{4,12},{1,9},{5,13},{2,10},{6,14},{3,11},{7,15}} | collective-permute-start | bytes 4128776 | tf_op jit(solution)/shard_map/ppermute | solution.py:203
  528.4 46.4 %collective-permute-start.38 = (bf16[192,3584]{1,0:T(8,128)(2,1)S(1)}, bf16[192,3584]{1,0:T(8,128)(2,1)S(1)}, u32[]{:S(2)}, u32[]{:S(2)}) collective-permute-start(bf16[192,3584]{1,0:T(8,128)(2,1)S(1)} %get-tuple-element.132), channel_id=1, source_target_pairs={{24,16},{28,20},{25,17},{29,21},{26,18},{30,22},{27,19},{31,23}} | collective-permute-start | bytes 4128776 | tf_op jit(solution)/shard_map/ppermute | solution.py:203
  529.6 42.9 %collective-permute-start.36 = (bf16[192,1728]{1,0:T(8,128)(2,1)S(1)}, bf16[192,1728]{1,0:T(8,128)(2,1)S(1)}, u32[]{:S(2)}, u32[]{:S(2)}) collective-permute-start(bf16[192,1728]{1,0:T(8,128)(2,1)S(1)} %pad_maximum_fusion.15), channel_id=1, source_target_pairs={{0,8},{4,12},{8,16},{12,20},{16,24},{20,28},{1,9},{5,13},{9,17},{1... | collective-permute-start | bytes 1990664 | tf_op jit(solution)/shard_map/ppermute | solution.py:203
  530.9 42.3 %collective-permute-start.40 = (bf16[192,1728]{1,0:T(8,128)(2,1)S(1)}, bf16[192,1728]{1,0:T(8,128)(2,1)S(1)}, u32[]{:S(2)}, u32[]{:S(2)}) collective-permute-start(bf16[192,1728]{1,0:T(8,128)(2,1)S(1)} %pad_maximum_fusion.15), channel_id=1, source_target_pairs={{8,0},{12,4},{16,8},{20,12},{24,16},{28,20},{9,1},{13,5},{17,9},{2... | collective-permute-start | bytes 1990664 | tf_op jit(solution)/shard_map/ppermute | solution.py:203
  573.2 19.6 %collective-permute-start.41 = (bf16[192,1728]{1,0:T(8,128)(2,1)S(1)}, bf16[192,1728]{1,0:T(8,128)(2,1)S(1)}, u32[]{:S(2)}, u32[]{:S(2)}) collective-permute-start(bf16[192,1728]{1,0:T(8,128)(2,1)S(1)} %collective-permute-done.40), channel_id=1, source_target_pairs={{8,0},{12,4},{16,8},{20,12},{9,1},{13,5},{17,9},{21,13},{10,2},{14... | collective-permute-start | bytes 1990664 | tf_op jit(solution)/shard_map/ppermute | solution.py:203
  595.4 31.1 %collective-permute-start.42 = (bf16[192,3584]{1,0:T(8,128)(2,1)}, bf16[192,3584]{1,0:T(8,128)(2,1)}, u32[]{:S(2)}, u32[]{:S(2)}) collective-permute-start(bf16[192,3584]{1,0:T(8,128)(2,1)} %get-tuple-element.133), channel_id=1, source_target_pairs={{0,8},{4,12},{8,16},{12,20},{1,9},{5,13},{9,17},{13,21},{2,10},{6,... | collective-permute-start | bytes 4128776 | tf_op jit(solution)/shard_map/ppermute | solution.py:203
  599.7 28.5 %collective-permute-start.44 = (bf16[192,1728]{1,0:T(8,128)(2,1)}, bf16[192,1728]{1,0:T(8,128)(2,1)S(1)}, u32[]{:S(2)}, u32[]{:S(2)}) collective-permute-start(bf16[192,1728]{1,0:T(8,128)(2,1)} %copy-done.38), channel_id=1, source_target_pairs={{16,24},{20,28},{17,25},{21,29},{18,26},{22,30},{19,27},{23,31}} | collective-permute-start | bytes 1990664 | tf_op jit(solution)/shard_map/ppermute | solution.py:203
  600.5 27.7 %collective-permute-start.45 = (bf16[192,1728]{1,0:T(8,128)(2,1)}, bf16[192,1728]{1,0:T(8,128)(2,1)S(1)}, u32[]{:S(2)}, u32[]{:S(2)}) collective-permute-start(bf16[192,1728]{1,0:T(8,128)(2,1)} %copy-done.39), channel_id=1, source_target_pairs={{8,0},{12,4},{9,1},{13,5},{10,2},{14,6},{11,3},{15,7}} | collective-permute-start | bytes 1990664 | tf_op jit(solution)/shard_map/ppermute | solution.py:203
  628.2 31.7 %collective-permute-start.46 = (bf16[192,3584]{1,0:T(8,128)(2,1)S(1)}, bf16[192,3584]{1,0:T(8,128)(2,1)S(1)}, u32[]{:S(2)}, u32[]{:S(2)}) collective-permute-start(bf16[192,3584]{1,0:T(8,128)(2,1)S(1)} %add_convert_fusion.1), channel_id=1, source_target_pairs={{0,8},{4,12},{8,16},{12,20},{16,24},{20,28},{1,9},{5,13},{9,17},{1... | collective-permute-start | bytes 4128776 | tf_op jit(solution)/shard_map/ppermute | solution.py:203
  633.3 30.8 %collective-permute-start.47 = (bf16[192,3584]{1,0:T(8,128)(2,1)S(1)}, bf16[192,3584]{1,0:T(8,128)(2,1)S(1)}, u32[]{:S(2)}, u32[]{:S(2)}) collective-permute-start(bf16[192,3584]{1,0:T(8,128)(2,1)S(1)} %add_convert_fusion), channel_id=1, source_target_pairs={{8,0},{12,4},{16,8},{20,12},{24,16},{28,20},{9,1},{13,5},{17,9},{2... | collective-permute-start | bytes 4128776 | tf_op jit(solution)/shard_map/ppermute | solution.py:203
  (106 other events, 1214.4 us)
Sparse Core Ops, SparseCore 0:
  23.8 114.3 all-gather.4
  279.2 39.5 all-gather.6
  357.8 34.8 all-gather.8
  400.7 32.9 reduce-scatter.1
  470.6 39.0 all-gather.10

commit v9 on v6

--- a/solution.py
+++ b/solution.py
@@ -11,6 +11,7 @@
 HD = 128
 PIECES_DEV = 2
 CORES = 2
+CHUNKS = 3
 
 rope_base = 1000000.0
 norm_eps = 1e-06
@@ -193,7 +194,7 @@
     dz = width // planes
     ds = width // seq_count
     share = rows // mlp_count
-    chunks = 2 if share % 32 == 0 and planes > 3 else 1
+    chunks = CHUNKS if share % (16 * CHUNKS) == 0 and planes > 3 else 1
     sub = share // chunks
     crows = mlp_count * sub
     piece_len = rows // PIECES_DEV
@@ -393,11 +394,12 @@
         for k, v in zip(order, lane_sends)
     ]
     query = product(both, q_weight, F32)
-    query_sib, lane_parts = after(sibling(query[rows:]), lane_parts)
-    lane_input = swap_halves(jnp.stack(lane_parts, axis=0)).reshape(planes, chunks, sub, dz)
+    query_sib = sibling(query[rows:])
     mixed = attend(
         query, query_sib, query_bias.astype(F32)[None, :], cosine, sine, kv_rows, doc_first, stream, piece_stream, kv_heads
     )
+    mixed, lane_parts = after(mixed, lane_parts)
+    lane_input = swap_halves(jnp.stack(lane_parts, axis=0)).reshape(planes, chunks, sub, dz)
     chunked = [
         jnp.concatenate(
             [
@@ -477,64 +479,82 @@
     first = contract_half(lanes[0])
     carried, last = scatter_step(dict(zip(order, first)), None, 1, lanes[1])
     parts = dict(zip(order, first + contract_half(last)))
-    following = None
+    finals = [None] * chunks
+    before, summing, following = None, None, None
+    for h in range(chunks):
+        flight = {}
+        for t in range(1, steps + 1):
+            if t > 1:
+                if before is not None:
+                    flight["state"] = (state[0][-1], state[1][-1])
+                carried, flight = scatter_step(parts, carried, t, flight)
+                if before is not None:
+                    state[0][-1], state[1][-1] = flight.pop("state")
+            if summing is not None:
+                who, n, terms, gots = summing
+                gots = flight.pop("down", gots)
+                terms = sum_land(terms, n, gots)
+                if n + 1 < bits:
+                    flight["down"] = sum_launch(terms, n + 1)
+                    summing = (who, n + 1, terms, None)
+                else:
+                    finals[who] = deliver(who, sum_end(terms))
+                    summing = None
+            if before is not None:
+                if t == 1:
+                    hidden = activate(*before)
+                    state = ([hidden], [hidden])
+                    gather_step(state, 1)
+                    gather_step(state, 2)
+                elif t < steps:
+                    gather_step(state, t + 1)
+                else:
+                    terms = down_terms(state)
+                    summing = (h - 1, 0, terms, sum_launch(terms, 0))
+            if h + 1 < chunks:
+                if t == 1:
+                    collected[h + 1], parts[0] = after(collected[h + 1], parts[0])
+                    states = attn_terms(h + 1)
+                    flight["lead"] = sum_launch(states, 0)
+                elif t == 2:
+                    states = sum_land(states, 0, flight.pop("lead"))
+                    for n in range(1, bits):
+                        states = sum_stage(states, n)
+                    residuals.append(attn_end(h + 1, states))
+                    states = lane_terms(residuals[h + 1])
+                    flight["lead"] = spread_launch(states, 0)
+                elif t == 3:
+                    states = spread_land(states, 0, flight.pop("lead"))
+                    for n in range(1, bits):
+                        states = spread_stage(states, n)
+                    following = contract(spread_end(states))
+        before = (parts, carried)
+        if h + 1 < chunks:
+            gots = summing[3] if summing is not None else ()
+            carried, (behind, gots) = scatter_step(following, None, 1, (carried, gots))
+            if summing is not None:
+                summing = summing[:3] + (gots,)
+            before = (parts, behind)
+            parts = following
+    hidden = activate(*before)
+    state = ([hidden], [hidden])
+    for t in range(1, steps + 1):
+        gather_step(state, t)
+        if summing is not None:
+            who, n, terms, gots = summing
+            (state[0][-1], state[1][-1]), gots = after((state[0][-1], state[1][-1]), gots)
+            terms = sum_land(terms, n, gots)
+            if n + 1 < bits:
+                summing = (who, n + 1, terms, sum_launch(terms, n + 1))
+            else:
+                finals[who] = deliver(who, sum_end(terms))
+                summing = None
     if chunks > 1:
-        collected[1], parts[0] = after(collected[1], parts[0])
-        states = attn_terms(1)
-        gots = sum_launch(states, 0)
-    for t in range(2, steps + 1):
-        if chunks > 1 and t == 2:
-            carried, gots = scatter_step(parts, carried, t, gots)
-            states = sum_land(states, 0, gots)
-            for n in range(1, bits):
-                states = sum_stage(states, n)
-            residuals.append(attn_end(1, states))
-            states = lane_terms(residuals[1])
-            gots = spread_launch(states, 0)
-        elif chunks > 1 and t == 3:
-            carried, gots = scatter_step(parts, carried, t, gots)
-            states = spread_land(states, 0, gots)
-            for n in range(1, bits):
-                states = spread_stage(states, n)
-            following = contract(spread_end(states))
-        else:
-            carried, _ = scatter_step(parts, carried, t)
-    finals = []
-    if following is not None:
-        ahead, carried = scatter_step(following, None, 1, carried)
-        hidden = activate(parts, carried)
-        state = ([hidden], [hidden])
-        gather_step(state, 1)
-        gather_step(state, 2)
-        for t in range(2, steps + 1):
-            ahead, (state[0][-1], state[1][-1]) = scatter_step(
-                following, ahead, t, (state[0][-1], state[1][-1])
-            )
-            if t < steps:
-                gather_step(state, t + 1)
-        states = down_terms(state)
-        gots = sum_launch(states, 0)
-        hidden = activate(following, ahead)
-        state = ([hidden], [hidden])
-        for t in range(1, steps + 1):
-            gather_step(state, t)
-            if t <= bits:
-                (state[0][-1], state[1][-1]), gots = after((state[0][-1], state[1][-1]), gots)
-                states = sum_land(states, t - 1, gots)
-                if t < bits:
-                    gots = sum_launch(states, t)
-        for n in range(steps, bits):
-            states = sum_stage(states, n)
-        finals.append(deliver(0, sum_end(states)))
-    else:
-        hidden = activate(parts, carried)
-        state = ([hidden], [hidden])
-        for t in range(1, steps + 1):
-            gather_step(state, t)
+        (state[0][-1], state[1][-1]), finals[:-1] = after((state[0][-1], state[1][-1]), finals[:-1])
     states = down_terms(state)
     for n in range(bits):
         states = sum_stage(states, n)
-    finals.append(deliver(chunks - 1, sum_end(states)))
+    finals[chunks - 1] = deliver(chunks - 1, sum_end(states))
     final = swap_halves(jnp.concatenate(finals, axis=1))
     final = lax.dynamic_slice_in_dim(
         jnp.concatenate([final, final], axis=0), (planes - plane) % planes, planes, 0

time: 709 us -> 719 us (1.014)
  waiting for transfers between devices: 360 us -> 294 us
  starting transfers between devices: 120 us -> 173 us
  Pallas kernels: 76.5 us -> 100 us
    ppermute x39 -> x54, waiting for transfers between devices: 250 us -> 204 us  [move(): lax.ppermute(x, 'seq', [(a * CORES + e, b * CORES + e) for a, b in pairs...]
    ppermute x39 -> x54, starting transfers between devices: 81.1 us -> 123 us  [move(): lax.ppermute(x, 'seq', [(a * CORES + e, b * CORES + e) for a, b in pairs...]
    pallas_call x10 -> x14, Pallas kernels: 65.8 us -> 83.2 us  [product(): pl.pallas_call(product_kernel, grid=(cols // tile,), in_specs=[pl.BlockSp...]
    ppermute x24 -> x36, waiting for transfers between devices: 65.7 us -> 50.1 us  [partner(): return lax.ppermute(x, 'mlp', [(a, a ^ bit) for a in range(mlp_count)])]
    ppermute x24 -> x36, starting transfers between devices: 36.4 us -> 47.4 us  [partner(): return lax.ppermute(x, 'mlp', [(a, a ^ bit) for a in range(mlp_count)])]
    all_gather x4 -> x5, waiting for transfers between devices: 42.5 us -> 37.8 us  [line_collect(): return lax.all_gather(x, 'seq', axis=0, tiled=True, axis_index_groups=lines)]
  transfers between devices with their start and end apart: 74 -> 102, of which waited for: 41 -> 50; matrix products, arithmetic and copies ran while one was open for 14% -> 14% of each run, Pallas kernels for 8% -> 13%
where the time goes in v9:
time: 719 us; the launch traced here: 707 us
  waiting for transfers between devices  294 us (41%)
  starting transfers between devices  173 us (24%)
  Pallas kernels  100 us (14%)
  other arithmetic  69.1 us (10%)
  local copies, waits for them, and re-layouts  53.9 us (7%)
  between operations  17.9 us (2%)
    ppermute x54, waiting for transfers between devices, move(): lax.ppermute(x, 'seq', [(a * CORES + e, b * CORES + e) for a, b in pairs...  204 us
    ppermute x54, starting transfers between devices, move(): lax.ppermute(x, 'seq', [(a * CORES + e, b * CORES + e) for a, b in pairs...  123 us
    pallas_call x14, Pallas kernels, product(): pl.pallas_call(product_kernel, grid=(cols // tile,), in_specs=[pl.BlockSp...  83.2 us
    ppermute x36, waiting for transfers between devices, partner(): return lax.ppermute(x, 'mlp', [(a, a ^ bit) for a in range(mlp_count)])  50.1 us
    ppermute x36, starting transfers between devices, partner(): return lax.ppermute(x, 'mlp', [(a, a ^ bit) for a in range(mlp_count)])  47.4 us
    all_gather x5, waiting for transfers between devices, line_collect(): return lax.all_gather(x, 'seq', axis=0, tiled=True, axis_index_groups=lines)  37.8 us
    pallas_call x1, Pallas kernels, attend(): pl.pallas_call(attend_kernel, grid_spec=pltpu.PrefetchScalarGridSpec(num_...  14.5 us
  transfers between devices with their start and end apart: 102, of which 50 were waited for; matrix products, arithmetic and copies ran while one was open for 14% of the time, Pallas kernels for 13%

profile of v9, /device:TPU:0, one launch (start us, length us, event | category | flops | bytes accessed | tf_op | source)
XLA Modules:
  0.0 707.5 jit_solution(15131920961589402258)
XLA Ops:
  21.6 7.1 concatenate.156
  63.3 7.5 %pad_maximum_fusion.w_ref = bf16[1408,3584]{1,0:T(8,128)(2,1)} fusion(bf16[128,3584]{1,0:T(8,128)(2,1)S(1)} %pad_convert_fusion, bf16[1280,3584]{1,0:T(8,128)(2,1)S(1)} %fusion.2), kind=kLoop, calls=%fused_computation.3 | loop fusion | flops 20185088 | bytes 20185088 | tf_op jit(solution)/shard_map/concatenate | solution.py:344
  85.4 5.7 collective-permute-start.6
  91.1 26.9 %collective-permute-done.7 = bf16[384,512]{1,0:T(8,128)(2,1)S(1)} collective-permute-done((bf16[384,512]{1,0:T(8,128)(2,1)}, bf16[384,512]{1,0:T(8,128)(2,1)S(1)}, u32[]{:S(2)}, u32[]{:S(2)}) %collective-permute-start.7) | collective-permute-done | bytes 393248 | tf_op jit(solution)/shard_map/ppermute | solution.py:204
  120.0 24.8 %collective-permute-done.8 = bf16[384,512]{1,0:T(8,128)(2,1)S(1)} collective-permute-done((bf16[384,512]{1,0:T(8,128)(2,1)S(1)}, bf16[384,512]{1,0:T(8,128)(2,1)S(1)}, u32[]{:S(2)}, u32[]{:S(2)}) %collective-permute-start.8) | collective-permute-done | bytes 393248 | tf_op jit(solution)/shard_map/ppermute | solution.py:204
  148.8 40.0 %collective-permute-done.9 = bf16[384,512]{1,0:T(8,128)(2,1)S(1)} collective-permute-done((bf16[384,512]{1,0:T(8,128)(2,1)S(1)}, bf16[384,512]{1,0:T(8,128)(2,1)S(1)}, u32[]{:S(2)}, u32[]{:S(2)}) %collective-permute-start.9) | collective-permute-done | bytes 393248 | tf_op jit(solution)/shard_map/ppermute | solution.py:204
  193.1 7.5 %shard_map.167.own_ref = f32[768,1024]{1,0:T(8,128)S(1)} custom-call(bf16[768,2560]{1,0:T(8,128)(2,1)} %pad_maximum_fusion.2.x_ref, bf16[2560,1024]{1,0:T(8,128)(2,1)} %all-gather.6.cloned.1.call-done.w_ref), custom_call_target="tpu_custom_call" | custom-call | tf_op jit(solution)/shard_map/pallas_call | solution.py:142
  214.4 14.5 %shard_map.170 = bf16[384,1024]{1,0:T(8,128)(2,1)S(1)} custom-call(s32[2]{0:T(128)S(1)} %convert_reduce_fusion.1.count, s32[2,16]{1,0:T(2,128)S(1)} %select_reduce_fusion.1.active, s32[16]{0:T(128)S(1)} %select_reduce_fusion.2.piece_stream, f32[768,1024]{1,0:T(8,128)S(1)} %copy-done.1, f32[384,1024]{1,0:T(8,128)} %collective-permute-done.4.sib_ref, ...), custom_call_target="tpu_custom_call" | custom-call | tf_op jit(solution)/shard_map/pallas_call | solution.py:110
  232.8 26.4 %all-gather.14.cloned.1.call-done = bf16[512,1024]{1,0:T(8,128)(2,1)} async-done(((bf16[128,1024]{1,0:T(8,128)(2,1)}), bf16[512,1024]{1,0:T(8,128)(2,1)}) %all-gather.14.cloned.1.call-update) | async-done | bytes 1048592 | tf_op jit(solution)/shard_map/all_gather | solution.py:297
  266.6 6.1 collective-permute-done.16
  299.3 7.9 %shard_map.172 = bf16[256,3584]{1,0:T(8,128)(2,1)S(1)} custom-call(bf16[256,1408]{1,0:T(8,128)(2,1)S(1)} %bitcast.501, bf16[1408,3584]{1,0:T(8,128)(2,1)} %pad_maximum_fusion.w_ref), custom_call_target="tpu_custom_call" | custom-call | tf_op jit(solution)/shard_map/pallas_call | solution.py:142
  310.1 7.9 %shard_map.173 = bf16[256,3584]{1,0:T(8,128)(2,1)S(1)} custom-call(bf16[256,1408]{1,0:T(8,128)(2,1)S(1)} %bitcast.502, bf16[1408,3584]{1,0:T(8,128)(2,1)} %pad_maximum_fusion.w_ref), custom_call_target="tpu_custom_call" | custom-call | tf_op jit(solution)/shard_map/pallas_call | solution.py:142
  327.8 7.7 %collective-permute-done.24 = bf16[128,3584]{1,0:T(8,128)(2,1)} collective-permute-done((bf16[128,3584]{1,0:T(8,128)(2,1)S(1)}, bf16[128,3584]{1,0:T(8,128)(2,1)}, u32[]{:S(2)}, u32[]{:S(2)}) %collective-permute-start.24) | collective-permute-done | bytes 917536 | tf_op jit(solution)/shard_map/ppermute | solution.py:204
  354.6 7.9 %collective-permute-done.30 = bf16[128,3584]{1,0:T(8,128)(2,1)S(1)} collective-permute-done((bf16[128,3584]{1,0:T(8,128)(2,1)S(1)}, bf16[128,3584]{1,0:T(8,128)(2,1)S(1)}, u32[]{:S(2)}, u32[]{:S(2)}) %collective-permute-start.30) | collective-permute-done | bytes 917536 | tf_op jit(solution)/shard_map/ppermute | solution.py:204
  369.1 5.6 collective-permute-start.36
  377.5 7.9 %shard_map.175 = bf16[256,3584]{1,0:T(8,128)(2,1)S(1)} custom-call(bf16[256,1408]{1,0:T(8,128)(2,1)S(1)} %bitcast.503, bf16[1408,3584]{1,0:T(8,128)(2,1)} %pad_maximum_fusion.w_ref), custom_call_target="tpu_custom_call" | custom-call | tf_op jit(solution)/shard_map/pallas_call | solution.py:142
  386.9 7.9 %shard_map.176 = bf16[256,3584]{1,0:T(8,128)(2,1)S(1)} custom-call(bf16[256,1408]{1,0:T(8,128)(2,1)S(1)} %bitcast.504, bf16[1408,3584]{1,0:T(8,128)(2,1)} %pad_maximum_fusion.w_ref), custom_call_target="tpu_custom_call" | custom-call | tf_op jit(solution)/shard_map/pallas_call | solution.py:142
  396.1 11.4 %all-gather.10.cloned.1.call-done = bf16[512,1024]{1,0:T(8,128)(2,1)} async-done(((bf16[128,1024]{1,0:T(8,128)(2,1)}), bf16[512,1024]{1,0:T(8,128)(2,1)}) %all-gather.10.cloned.1.call-update) | async-done | bytes 1048592 | tf_op jit(solution)/shard_map/all_gather | solution.py:297
  413.3 5.8 collective-permute-start.38
  425.7 23.0 %collective-permute-done.42 = bf16[128,1728]{1,0:T(8,128)(2,1)S(1)} collective-permute-done((bf16[128,1728]{1,0:T(8,128)(2,1)S(1)}, bf16[128,1728]{1,0:T(8,128)(2,1)S(1)}, u32[]{:S(2)}, u32[]{:S(2)}) %collective-permute-start.42) | collective-permute-done | bytes 442400 | tf_op jit(solution)/shard_map/ppermute | solution.py:204
  457.5 8.0 %collective-permute-done.45 = bf16[128,1728]{1,0:T(8,128)(2,1)S(1)} collective-permute-done((bf16[128,1728]{1,0:T(8,128)(2,1)S(1)}, bf16[128,1728]{1,0:T(8,128)(2,1)S(1)}, u32[]{:S(2)}, u32[]{:S(2)}) %collective-permute-start.45) | collective-permute-done | bytes 442400 | tf_op jit(solution)/shard_map/ppermute | solution.py:204
  481.8 9.2 %collective-permute-done.48 = bf16[128,3584]{1,0:T(8,128)(2,1)S(1)} collective-permute-done((bf16[128,3584]{1,0:T(8,128)(2,1)S(1)}, bf16[128,3584]{1,0:T(8,128)(2,1)S(1)}, u32[]{:S(2)}, u32[]{:S(2)}) %collective-permute-start.48) | collective-permute-done | bytes 917536 | tf_op jit(solution)/shard_map/ppermute | solution.py:204
  506.2 5.5 shard_map.180
  513.1 7.9 %shard_map.178 = bf16[256,3584]{1,0:T(8,128)(2,1)S(1)} custom-call(bf16[256,1408]{1,0:T(8,128)(2,1)S(1)} %bitcast.505, bf16[1408,3584]{1,0:T(8,128)(2,1)} %pad_maximum_fusion.w_ref), custom_call_target="tpu_custom_call" | custom-call | tf_op jit(solution)/shard_map/pallas_call | solution.py:142
  521.3 7.9 %shard_map.179 = bf16[256,3584]{1,0:T(8,128)(2,1)S(1)} custom-call(bf16[256,1408]{1,0:T(8,128)(2,1)S(1)} %bitcast.500, bf16[1408,3584]{1,0:T(8,128)(2,1)} %pad_maximum_fusion.w_ref), custom_call_target="tpu_custom_call" | custom-call | tf_op jit(solution)/shard_map/pallas_call | solution.py:142
  549.4 10.3 %collective-permute-done.60 = bf16[128,3584]{1,0:T(8,128)(2,1)S(1)} collective-permute-done((bf16[128,3584]{1,0:T(8,128)(2,1)S(1)}, bf16[128,3584]{1,0:T(8,128)(2,1)S(1)}, u32[]{:S(2)}, u32[]{:S(2)}) %collective-permute-start.60) | collective-permute-done | bytes 917536 | tf_op jit(solution)/shard_map/ppermute | solution.py:204
  560.9 12.0 %collective-permute-start.68 = (bf16[128,3584]{1,0:T(8,128)(2,1)S(1)}, bf16[128,3584]{1,0:T(8,128)(2,1)S(1)}, u32[]{:S(2)}, u32[]{:S(2)}) collective-permute-start(bf16[128,3584]{1,0:T(8,128)(2,1)S(1)} %get-tuple-element.222), channel_id=1, source_target_pairs={{0,8},{4,12},{8,16},{12,20},{1,9},{5,13},{9,17},{13,21},{2,10},{6,... | collective-permute-start | bytes 2752520 | tf_op jit(solution)/shard_map/ppermute | solution.py:204
  576.1 8.9 %collective-permute-done.68 = bf16[128,3584]{1,0:T(8,128)(2,1)S(1)} collective-permute-done((bf16[128,3584]{1,0:T(8,128)(2,1)S(1)}, bf16[128,3584]{1,0:T(8,128)(2,1)S(1)}, u32[]{:S(2)}, u32[]{:S(2)}) %collective-permute-start.68) | collective-permute-done | bytes 917536 | tf_op jit(solution)/shard_map/ppermute | solution.py:204
  586.7 15.7 %collective-permute-start.72 = (bf16[128,3584]{1,0:T(8,128)(2,1)S(1)}, bf16[128,3584]{1,0:T(8,128)(2,1)S(1)}, u32[]{:S(2)}, u32[]{:S(2)}) collective-permute-start(bf16[128,3584]{1,0:T(8,128)(2,1)S(1)} %add_convert_fusion.1), channel_id=1, source_target_pairs={{0,8},{4,12},{8,16},{12,20},{16,24},{20,28},{1,9},{5,13},{9,17},{1... | collective-permute-start | bytes 2752520 | tf_op jit(solution)/shard_map/ppermute | solution.py:204
  602.8 5.5 shard_map.181
  643.7 5.5 collective-permute-done.79
  667.8 5.5 shard_map.182
  (535 shorter events, 328.4 us)
Async XLA Ops:
  7.2 63.6 %all-gather.8.cloned.1.call-start = ((), (), s32[]{:S(2)}) async-start(), calls=%async_computation.1 | async-start | bytes 3276800 | tf_op jit(solution)/shard_map/all_gather | solution.py:297
  9.3 183.8 %all-gather.6.cloned.1.call-start = ((), (), s32[]{:S(2)}) async-start(), calls=%async_computation | async-start | bytes 6553600 | tf_op jit(solution)/shard_map/all_gather | solution.py:297
  28.6 30.0 %collective-permute-start.1 = (bf16[640,3456]{1,0:T(8,128)(2,1)}, bf16[640,3456]{1,0:T(8,128)(2,1)}, u32[]{:S(2)}, u32[]{:S(2)}) collective-permute-start(bf16[640,3456]{1,0:T(8,128)(2,1)} %concatenate.156), channel_id=1, source_target_pairs={{0,4},{4,0},{8,12},{12,8},{16,20},{20,16},{24,28},{28,24},{1,5},{5... | collective-permute-start | bytes 13271048 | tf_op jit(solution)/shard_map/ppermute | solution.py:209
  41.0 218.2 %all-gather.14.cloned.1.call-start = ((), (), s32[]{:S(2)}) async-start(), calls=%async_computation.4 | async-start | bytes 1310720 | tf_op jit(solution)/shard_map/all_gather | solution.py:297
  84.1 33.9 %collective-permute-start.7 = (bf16[384,512]{1,0:T(8,128)(2,1)}, bf16[384,512]{1,0:T(8,128)(2,1)S(1)}, u32[]{:S(2)}, u32[]{:S(2)}) collective-permute-start(bf16[384,512]{1,0:T(8,128)(2,1)} %shard_map.169), channel_id=1, source_target_pairs={{8,0},{12,4},{16,8},{20,12},{24,16},{28,20},{9,1},{13,5},{17,9},{2... | collective-permute-start | bytes 1179656 | tf_op jit(solution)/shard_map/ppermute | solution.py:204
  85.4 33.9 %collective-permute-start.6 = (bf16[384,512]{1,0:T(8,128)(2,1)}, bf16[384,512]{1,0:T(8,128)(2,1)S(1)}, u32[]{:S(2)}, u32[]{:S(2)}) collective-permute-start(bf16[384,512]{1,0:T(8,128)(2,1)} %shard_map.169), channel_id=1, source_target_pairs={{0,8},{4,12},{8,16},{12,20},{16,24},{20,28},{1,9},{5,13},{9,17},{1... | collective-permute-start | bytes 1179656 | tf_op jit(solution)/shard_map/ppermute | solution.py:204
  118.0 26.8 %collective-permute-start.8 = (bf16[384,512]{1,0:T(8,128)(2,1)S(1)}, bf16[384,512]{1,0:T(8,128)(2,1)S(1)}, u32[]{:S(2)}, u32[]{:S(2)}) collective-permute-start(bf16[384,512]{1,0:T(8,128)(2,1)S(1)} %collective-permute-done.7), channel_id=1, source_target_pairs={{8,0},{12,4},{16,8},{20,12},{9,1},{13,5},{17,9},{21,13},{10,2},{14... | collective-permute-start | bytes 1179656 | tf_op jit(solution)/shard_map/ppermute | solution.py:204
  119.3 28.7 %collective-permute-start.10 = (bf16[384,512]{1,0:T(8,128)(2,1)S(1)}, bf16[384,512]{1,0:T(8,128)(2,1)S(1)}, u32[]{:S(2)}, u32[]{:S(2)}) collective-permute-start(bf16[384,512]{1,0:T(8,128)(2,1)S(1)} %collective-permute-done.6), channel_id=1, source_target_pairs={{8,16},{12,20},{16,24},{20,28},{9,17},{13,21},{17,25},{21,29},{10,... | collective-permute-start | bytes 1179656 | tf_op jit(solution)/shard_map/ppermute | solution.py:204
  144.8 44.1 %collective-permute-start.9 = (bf16[384,512]{1,0:T(8,128)(2,1)S(1)}, bf16[384,512]{1,0:T(8,128)(2,1)S(1)}, u32[]{:S(2)}, u32[]{:S(2)}) collective-permute-start(bf16[384,512]{1,0:T(8,128)(2,1)S(1)} %collective-permute-done.8), channel_id=1, source_target_pairs={{8,0},{12,4},{9,1},{13,5},{10,2},{14,6},{11,3},{15,7}} | collective-permute-start | bytes 1179656 | tf_op jit(solution)/shard_map/ppermute | solution.py:204
  148.0 42.6 %collective-permute-start.11 = (bf16[384,512]{1,0:T(8,128)(2,1)S(1)}, bf16[384,512]{1,0:T(8,128)(2,1)S(1)}, u32[]{:S(2)}, u32[]{:S(2)}) collective-permute-start(bf16[384,512]{1,0:T(8,128)(2,1)S(1)} %collective-permute-done.10), channel_id=1, source_target_pairs={{16,24},{20,28},{17,25},{21,29},{18,26},{22,30},{19,27},{23,31}} | collective-permute-start | bytes 1179656 | tf_op jit(solution)/shard_map/ppermute | solution.py:204
  207.8 21.1 %collective-permute-start.13 = (bf16[96,1280]{1,0:T(8,128)(2,1)}, bf16[96,1280]{1,0:T(8,128)(2,1)S(1)}, u32[]{:S(2)}, u32[]{:S(2)}) collective-permute-start(bf16[96,1280]{1,0:T(8,128)(2,1)} %get-tuple-element.139), channel_id=1, source_target_pairs={{0,8},{4,12},{8,16},{12,20},{16,24},{20,28},{24,0},{28,4},{1,9},{5... | collective-permute-start | bytes 737288 | tf_op jit(solution)/shard_map/ppermute | solution.py:204
  207.8 21.1 %collective-permute-start.14 = (bf16[96,1280]{1,0:T(8,128)(2,1)}, bf16[96,1280]{1,0:T(8,128)(2,1)S(1)}, u32[]{:S(2)}, u32[]{:S(2)}) collective-permute-start(bf16[96,1280]{1,0:T(8,128)(2,1)} %get-tuple-element.140), channel_id=1, source_target_pairs={{0,24},{4,28},{8,0},{12,4},{16,8},{20,12},{24,16},{28,20},{1,25},{... | collective-permute-start | bytes 737288 | tf_op jit(solution)/shard_map/ppermute | solution.py:204
  232.5 89.8 %all-gather.12.cloned.1.call-start = ((), (), s32[]{:S(2)}) async-start(), calls=%async_computation.3 | async-start | bytes 1310720 | tf_op jit(solution)/shard_map/all_gather | solution.py:297
  291.3 116.3 %all-gather.10.cloned.1.call-start = ((), (), s32[]{:S(2)}) async-start(), calls=%async_computation.2 | async-start | bytes 1310720 | tf_op jit(solution)/shard_map/all_gather | solution.py:297
  339.7 22.9 %collective-permute-start.30 = (bf16[128,3584]{1,0:T(8,128)(2,1)S(1)}, bf16[128,3584]{1,0:T(8,128)(2,1)S(1)}, u32[]{:S(2)}, u32[]{:S(2)}) collective-permute-start(bf16[128,3584]{1,0:T(8,128)(2,1)S(1)} %get-tuple-element.170), channel_id=1, source_target_pairs={{0,8},{4,12},{8,16},{12,20},{1,9},{5,13},{9,17},{13,21},{2,10},{6,... | collective-permute-start | bytes 2752520 | tf_op jit(solution)/shard_map/ppermute | solution.py:204
  369.1 42.4 %collective-permute-start.36 = (bf16[128,3584]{1,0:T(8,128)(2,1)}, bf16[128,3584]{1,0:T(8,128)(2,1)}, u32[]{:S(2)}, u32[]{:S(2)}) collective-permute-start(bf16[128,3584]{1,0:T(8,128)(2,1)} %get-tuple-element.181), channel_id=1, source_target_pairs={{0,8},{4,12},{8,16},{12,20},{16,24},{20,28},{1,9},{5,13},{9,17},{1... | collective-permute-start | bytes 2752520 | tf_op jit(solution)/shard_map/ppermute | solution.py:204
  374.7 37.4 %collective-permute-start.37 = (bf16[128,3584]{1,0:T(8,128)(2,1)}, bf16[128,3584]{1,0:T(8,128)(2,1)}, u32[]{:S(2)}, u32[]{:S(2)}) collective-permute-start(bf16[128,3584]{1,0:T(8,128)(2,1)} %get-tuple-element.182), channel_id=1, source_target_pairs={{8,0},{12,4},{16,8},{20,12},{24,16},{28,20},{9,1},{13,5},{17,9},{2... | collective-permute-start | bytes 2752520 | tf_op jit(solution)/shard_map/ppermute | solution.py:204
  412.6 38.3 %collective-permute-start.39 = (bf16[128,3584]{1,0:T(8,128)(2,1)S(1)}, bf16[128,3584]{1,0:T(8,128)(2,1)S(1)}, u32[]{:S(2)}, u32[]{:S(2)}) collective-permute-start(bf16[128,3584]{1,0:T(8,128)(2,1)S(1)} %copy-done.34), channel_id=1, source_target_pairs={{24,16},{28,20},{25,17},{29,21},{26,18},{30,22},{27,19},{31,23}} | collective-permute-start | bytes 2752520 | tf_op jit(solution)/shard_map/ppermute | solution.py:204
  413.3 38.9 %collective-permute-start.38 = (bf16[128,3584]{1,0:T(8,128)(2,1)S(1)}, bf16[128,3584]{1,0:T(8,128)(2,1)S(1)}, u32[]{:S(2)}, u32[]{:S(2)}) collective-permute-start(bf16[128,3584]{1,0:T(8,128)(2,1)S(1)} %get-tuple-element.183), channel_id=1, source_target_pairs={{0,8},{4,12},{1,9},{5,13},{2,10},{6,14},{3,11},{7,15}} | collective-permute-start | bytes 2752520 | tf_op jit(solution)/shard_map/ppermute | solution.py:204
  421.6 27.1 %collective-permute-start.42 = (bf16[128,1728]{1,0:T(8,128)(2,1)S(1)}, bf16[128,1728]{1,0:T(8,128)(2,1)S(1)}, u32[]{:S(2)}, u32[]{:S(2)}) collective-permute-start(bf16[128,1728]{1,0:T(8,128)(2,1)S(1)} %pad_maximum_fusion.19), channel_id=1, source_target_pairs={{0,8},{4,12},{8,16},{12,20},{16,24},{20,28},{1,9},{5,13},{9,17},{1... | collective-permute-start | bytes 1327112 | tf_op jit(solution)/shard_map/ppermute | solution.py:204
  423.1 27.1 %collective-permute-start.44 = (bf16[128,1728]{1,0:T(8,128)(2,1)S(1)}, bf16[128,1728]{1,0:T(8,128)(2,1)S(1)}, u32[]{:S(2)}, u32[]{:S(2)}) collective-permute-start(bf16[128,1728]{1,0:T(8,128)(2,1)S(1)} %pad_maximum_fusion.19), channel_id=1, source_target_pairs={{8,0},{12,4},{16,8},{20,12},{24,16},{28,20},{9,1},{13,5},{17,9},{2... | collective-permute-start | bytes 1327112 | tf_op jit(solution)/shard_map/ppermute | solution.py:204
  424.5 28.1 %collective-permute-start.40 = (bf16[2,2,32,1280]{3,2,1,0:T(8,128)(2,1)S(1)}, bf16[2,2,32,1280]{3,2,1,0:T(8,128)(2,1)S(1)}, u32[]{:S(2)}, u32[]{:S(2)}) collective-permute-start(bf16[2,2,32,1280]{3,2,1,0:T(8,128)(2,1)S(1)} %pad_maximum_fusion.33), channel_id=1, source_target_pairs={{0,1},{1,0},{2,3},{3,2},{4,5},{5,4},{6,7},{7,6},{8,9},{9,8},{10,11... | collective-permute-start | bytes 983048 | tf_op jit(solution)/shard_map/ppermute | solution.py:214
  466.8 30.2 %collective-permute-start.52 = (bf16[128,1728]{1,0:T(8,128)(2,1)S(1)}, bf16[128,1728]{1,0:T(8,128)(2,1)S(1)}, u32[]{:S(2)}, u32[]{:S(2)}) collective-permute-start(bf16[128,1728]{1,0:T(8,128)(2,1)S(1)} %collective-permute-done.43), channel_id=1, source_target_pairs={{16,24},{20,28},{17,25},{21,29},{18,26},{22,30},{19,27},{23,31}} | collective-permute-start | bytes 1327112 | tf_op jit(solution)/shard_map/ppermute | solution.py:204
  467.5 29.5 %collective-permute-start.53 = (bf16[128,1728]{1,0:T(8,128)(2,1)S(1)}, bf16[128,1728]{1,0:T(8,128)(2,1)S(1)}, u32[]{:S(2)}, u32[]{:S(2)}) collective-permute-start(bf16[128,1728]{1,0:T(8,128)(2,1)S(1)} %collective-permute-done.45), channel_id=1, source_target_pairs={{8,0},{12,4},{9,1},{13,5},{10,2},{14,6},{11,3},{15,7}} | collective-permute-start | bytes 1327112 | tf_op jit(solution)/shard_map/ppermute | solution.py:204
  468.9 22.1 %collective-permute-start.48 = (bf16[128,3584]{1,0:T(8,128)(2,1)S(1)}, bf16[128,3584]{1,0:T(8,128)(2,1)S(1)}, u32[]{:S(2)}, u32[]{:S(2)}) collective-permute-start(bf16[128,3584]{1,0:T(8,128)(2,1)S(1)} %get-tuple-element.194), channel_id=1, source_target_pairs={{0,8},{4,12},{8,16},{12,20},{1,9},{5,13},{9,17},{13,21},{2,10},{6,... | collective-permute-start | bytes 2752520 | tf_op jit(solution)/shard_map/ppermute | solution.py:204
  497.1 24.0 %collective-permute-start.54 = (bf16[2,2,32,1408]{3,2,1,0:T(8,128)(2,1)S(1)}, bf16[2,2,32,1408]{3,2,1,0:T(8,128)(2,1)S(1)}, u32[]{:S(2)}, u32[]{:S(2)}) collective-permute-start(bf16[2,2,32,1408]{3,2,1,0:T(8,128)(2,1)S(1)} %pad_maximum_fusion.28), channel_id=1, source_target_pairs={{0,2},{1,3},{2,0},{3,1},{4,6},{5,7},{6,4},{7,5},{8,10},{9,11},{10,... | collective-permute-start | bytes 1081352 | tf_op jit(solution)/shard_map/ppermute | solution.py:214
  500.4 29.0 %collective-permute-start.56 = (bf16[128,3584]{1,0:T(8,128)(2,1)S(1)}, bf16[128,3584]{1,0:T(8,128)(2,1)S(1)}, u32[]{:S(2)}, u32[]{:S(2)}) collective-permute-start(bf16[128,3584]{1,0:T(8,128)(2,1)S(1)} %add_convert_fusion.3), channel_id=1, source_target_pairs={{0,8},{4,12},{8,16},{12,20},{16,24},{20,28},{1,9},{5,13},{9,17},{1... | collective-permute-start | bytes 2752520 | tf_op jit(solution)/shard_map/ppermute | solution.py:204
  504.5 24.9 %collective-permute-start.57 = (bf16[128,3584]{1,0:T(8,128)(2,1)S(1)}, bf16[128,3584]{1,0:T(8,128)(2,1)S(1)}, u32[]{:S(2)}, u32[]{:S(2)}) collective-permute-start(bf16[128,3584]{1,0:T(8,128)(2,1)S(1)} %add_convert_fusion.2), channel_id=1, source_target_pairs={{8,0},{12,4},{16,8},{20,12},{24,16},{28,20},{9,1},{13,5},{17,9},{2... | collective-permute-start | bytes 2752520 | tf_op jit(solution)/shard_map/ppermute | solution.py:204
  537.0 22.7 %collective-permute-start.60 = (bf16[128,3584]{1,0:T(8,128)(2,1)S(1)}, bf16[128,3584]{1,0:T(8,128)(2,1)S(1)}, u32[]{:S(2)}, u32[]{:S(2)}) collective-permute-start(bf16[128,3584]{1,0:T(8,128)(2,1)S(1)} %get-tuple-element.213), channel_id=1, source_target_pairs={{0,8},{4,12},{1,9},{5,13},{2,10},{6,14},{3,11},{7,15}} | collective-permute-start | bytes 2752520 | tf_op jit(solution)/shard_map/ppermute | solution.py:204
  560.9 24.0 %collective-permute-start.68 = (bf16[128,3584]{1,0:T(8,128)(2,1)S(1)}, bf16[128,3584]{1,0:T(8,128)(2,1)S(1)}, u32[]{:S(2)}, u32[]{:S(2)}) collective-permute-start(bf16[128,3584]{1,0:T(8,128)(2,1)S(1)} %get-tuple-element.222), channel_id=1, source_target_pairs={{0,8},{4,12},{8,16},{12,20},{1,9},{5,13},{9,17},{13,21},{2,10},{6,... | collective-permute-start | bytes 2752520 | tf_op jit(solution)/shard_map/ppermute | solution.py:204
  585.4 27.4 %collective-permute-start.73 = (bf16[128,3584]{1,0:T(8,128)(2,1)S(1)}, bf16[128,3584]{1,0:T(8,128)(2,1)S(1)}, u32[]{:S(2)}, u32[]{:S(2)}) collective-permute-start(bf16[128,3584]{1,0:T(8,128)(2,1)S(1)} %add_convert_fusion), channel_id=1, source_target_pairs={{8,0},{12,4},{16,8},{20,12},{24,16},{28,20},{9,1},{13,5},{17,9},{2... | collective-permute-start | bytes 2752520 | tf_op jit(solution)/shard_map/ppermute | solution.py:204
  586.7 31.5 %collective-permute-start.72 = (bf16[128,3584]{1,0:T(8,128)(2,1)S(1)}, bf16[128,3584]{1,0:T(8,128)(2,1)S(1)}, u32[]{:S(2)}, u32[]{:S(2)}) collective-permute-start(bf16[128,3584]{1,0:T(8,128)(2,1)S(1)} %add_convert_fusion.1), channel_id=1, source_target_pairs={{0,8},{4,12},{8,16},{12,20},{16,24},{20,28},{1,9},{5,13},{9,17},{1... | collective-permute-start | bytes 2752520 | tf_op jit(solution)/shard_map/ppermute | solution.py:204
  (128 other events, 1146.7 us)
Sparse Core Ops, SparseCore 0:
  10.1 57.4 all-gather.7
  69.2 118.5 all-gather.5
  232.6 26.5 all-gather.13
  291.4 27.1 all-gather.11
  368.1 39.4 all-gather.9

commit v10 on v9

--- a/solution.py
+++ b/solution.py
@@ -11,7 +11,7 @@
 HD = 128
 PIECES_DEV = 2
 CORES = 2
-CHUNKS = 3
+CHUNKS = 2
 
 rope_base = 1000000.0
 norm_eps = 1e-06

time: 719 us -> 694 us (0.965)
  starting transfers between devices: 173 us -> 124 us
  waiting for transfers between devices: 294 us -> 340 us
  Pallas kernels: 100 us -> 77 us
    ppermute x54 -> x39, starting transfers between devices: 123 us -> 81.5 us  [move(): lax.ppermute(x, 'seq', [(a * CORES + e, b * CORES + e) for a, b in pairs...]
    ppermute x54 -> x39, waiting for transfers between devices: 204 us -> 243 us  [move(): lax.ppermute(x, 'seq', [(a * CORES + e, b * CORES + e) for a, b in pairs...]
    pallas_call x14 -> x10, Pallas kernels: 83.2 us -> 65.8 us  [product(): pl.pallas_call(product_kernel, grid=(cols // tile,), in_specs=[pl.BlockSp...]
    ppermute x36 -> x24, waiting for transfers between devices: 50.1 us -> 60.1 us  [partner(): return lax.ppermute(x, 'mlp', [(a, a ^ bit) for a in range(mlp_count)])]
    ppermute x36 -> x24, starting transfers between devices: 47.4 us -> 40.6 us  [partner(): return lax.ppermute(x, 'mlp', [(a, a ^ bit) for a in range(mlp_count)])]
    all_gather x5 -> x4, waiting for transfers between devices: 37.8 us -> 35.5 us  [line_collect(): return lax.all_gather(x, 'seq', axis=0, tiled=True, axis_index_groups=lines)]
  transfers between devices with their start and end apart: 102 -> 74, of which waited for: 50 -> 42; matrix products, arithmetic and copies ran while one was open for 14% -> 14% of each run, Pallas kernels for 13% -> 10%
where the time goes in v10:
time: 694 us; the launch traced here: 683 us
  waiting for transfers between devices  340 us (49%)
  starting transfers between devices  124 us (18%)
  Pallas kernels  77 us (11%)
  other arithmetic  72.6 us (10%)
  local copies, waits for them, and re-layouts  52 us (7%)
  between operations  17.2 us (2%)
    ppermute x39, waiting for transfers between devices, move(): lax.ppermute(x, 'seq', [(a * CORES + e, b * CORES + e) for a, b in pairs...  243 us
    ppermute x39, starting transfers between devices, move(): lax.ppermute(x, 'seq', [(a * CORES + e, b * CORES + e) for a, b in pairs...  81.5 us
    pallas_call x10, Pallas kernels, product(): pl.pallas_call(product_kernel, grid=(cols // tile,), in_specs=[pl.BlockSp...  65.8 us
    ppermute x24, waiting for transfers between devices, partner(): return lax.ppermute(x, 'mlp', [(a, a ^ bit) for a in range(mlp_count)])  60.1 us
    ppermute x24, starting transfers between devices, partner(): return lax.ppermute(x, 'mlp', [(a, a ^ bit) for a in range(mlp_count)])  40.6 us
    all_gather x4, waiting for transfers between devices, line_collect(): return lax.all_gather(x, 'seq', axis=0, tiled=True, axis_index_groups=lines)  35.5 us
  transfers between devices with their start and end apart: 74, of which 42 were waited for; matrix products, arithmetic and copies ran while one was open for 14% of the time, Pallas kernels for 10%

profile of v10, /device:TPU:0, one launch (start us, length us, event | category | flops | bytes accessed | tf_op | source)
XLA Modules:
  0.0 683.2 jit_solution(17595524786832681008)
XLA Ops:
  21.5 7.1 %concatenate.134 = bf16[640,3456]{1,0:T(8,128)(2,1)} concatenate(bf16[640,1664]{1,0:T(8,128)(2,1)S(1)} %slice-done.3, bf16[640,1664]{1,0:T(8,128)(2,1)} %slice.599, bf16[640,64]{1,0:T(8,128)(2,1)S(1)} %slice-done.4, bf16[640,64]{1,0:T(8,128)(2,1)S(1)} %slice-done.5), dimensions={1} | concatenate | bytes 8847360 | tf_op jit(solution)/shard_map/concatenate | solution.py:339
  64.1 7.3 %pad_maximum_fusion.w_ref = bf16[1408,3584]{1,0:T(8,128)(2,1)} fusion(bf16[128,3584]{1,0:T(8,128)(2,1)S(1)} %pad_convert_fusion, bf16[1280,3584]{1,0:T(8,128)(2,1)S(1)} %fusion.2), kind=kLoop, calls=%fused_computation.3 | loop fusion | flops 20185088 | bytes 20185088 | tf_op jit(solution)/shard_map/concatenate | solution.py:344
  86.3 5.7 collective-permute-start.6
  92.0 27.0 %collective-permute-done.7 = bf16[384,512]{1,0:T(8,128)(2,1)S(1)} collective-permute-done((bf16[384,512]{1,0:T(8,128)(2,1)}, bf16[384,512]{1,0:T(8,128)(2,1)S(1)}, u32[]{:S(2)}, u32[]{:S(2)}) %collective-permute-start.7) | collective-permute-done | bytes 393248 | tf_op jit(solution)/shard_map/ppermute | solution.py:204
  121.0 25.7 %collective-permute-done.8 = bf16[384,512]{1,0:T(8,128)(2,1)S(1)} collective-permute-done((bf16[384,512]{1,0:T(8,128)(2,1)S(1)}, bf16[384,512]{1,0:T(8,128)(2,1)S(1)}, u32[]{:S(2)}, u32[]{:S(2)}) %collective-permute-start.8) | collective-permute-done | bytes 393248 | tf_op jit(solution)/shard_map/ppermute | solution.py:204
  150.8 38.0 %collective-permute-done.9 = bf16[384,512]{1,0:T(8,128)(2,1)S(1)} collective-permute-done((bf16[384,512]{1,0:T(8,128)(2,1)S(1)}, bf16[384,512]{1,0:T(8,128)(2,1)S(1)}, u32[]{:S(2)}, u32[]{:S(2)}) %collective-permute-start.9) | collective-permute-done | bytes 393248 | tf_op jit(solution)/shard_map/ppermute | solution.py:204
  193.1 7.5 %shard_map.167.own_ref = f32[768,1024]{1,0:T(8,128)S(1)} custom-call(bf16[768,2560]{1,0:T(8,128)(2,1)} %pad_maximum_fusion.2.x_ref, bf16[2560,1024]{1,0:T(8,128)(2,1)} %all-gather.5.cloned.1.call-done.w_ref), custom_call_target="tpu_custom_call" | custom-call | tf_op jit(solution)/shard_map/pallas_call | solution.py:142
  214.4 8.6 %shard_map.170 = bf16[384,1024]{1,0:T(8,128)(2,1)S(1)} custom-call(s32[2]{0:T(128)S(1)} %convert_reduce_fusion.1.count, s32[2,16]{1,0:T(2,128)S(1)} %select_reduce_fusion.1.active, s32[16]{0:T(128)S(1)} %select_reduce_fusion.2.piece_stream, f32[768,1024]{1,0:T(8,128)S(1)} %copy-done.3, f32[384,1024]{1,0:T(8,128)} %collective-permute-done.4.sib_ref, ...), custom_call_target="tpu_custom_call" | custom-call | tf_op jit(solution)/shard_map/pallas_call | solution.py:110
  223.8 7.1 %collective-permute-done.15 = bf16[96,1280]{1,0:T(8,128)(2,1)S(1)} collective-permute-done((bf16[96,1280]{1,0:T(8,128)(2,1)}, bf16[96,1280]{1,0:T(8,128)(2,1)S(1)}, u32[]{:S(2)}, u32[]{:S(2)}) %collective-permute-start.15) | collective-permute-done | bytes 245792 | tf_op jit(solution)/shard_map/ppermute | solution.py:204
  232.9 35.5 %all-gather.11.cloned.1.call-done = bf16[768,1024]{1,0:T(8,128)(2,1)} async-done(((bf16[192,1024]{1,0:T(8,128)(2,1)}), bf16[768,1024]{1,0:T(8,128)(2,1)}) %all-gather.11.cloned.1.call-update) | async-done | bytes 1572880 | tf_op jit(solution)/shard_map/all_gather | solution.py:297
  276.9 9.6 %collective-permute-done.16 = bf16[2,2,48,1280]{3,2,1,0:T(8,128)(2,1)S(1)} collective-permute-done((bf16[2,2,48,1280]{3,2,1,0:T(8,128)(2,1)S(1)}, bf16[2,2,48,1280]{3,2,1,0:T(8,128)(2,1)S(1)}, u32[]{:S(2)}, u32[]{:S(2)}) %collective-permute-start.16) | collective-permute-done | bytes 491552 | tf_op jit(solution)/shard_map/ppermute | solution.py:214
  308.2 8.1 %collective-permute-done.22 = bf16[2,2,48,1408]{3,2,1,0:T(8,128)(2,1)} collective-permute-done((bf16[2,2,48,1408]{3,2,1,0:T(8,128)(2,1)S(1)}, bf16[2,2,48,1408]{3,2,1,0:T(8,128)(2,1)}, u32[]{:S(2)}, u32[]{:S(2)}) %collective-permute-start.22) | collective-permute-done | bytes 540704 | tf_op jit(solution)/shard_map/ppermute | solution.py:214
  317.9 8.7 %shard_map.172 = bf16[384,3584]{1,0:T(8,128)(2,1)S(1)} custom-call(bf16[384,1408]{1,0:T(8,128)(2,1)S(1)} %bitcast.345, bf16[1408,3584]{1,0:T(8,128)(2,1)} %pad_maximum_fusion.w_ref), custom_call_target="tpu_custom_call" | custom-call | tf_op jit(solution)/shard_map/pallas_call | solution.py:142
  330.2 8.7 %shard_map.173 = bf16[384,3584]{1,0:T(8,128)(2,1)S(1)} custom-call(bf16[384,1408]{1,0:T(8,128)(2,1)S(1)} %bitcast.346, bf16[1408,3584]{1,0:T(8,128)(2,1)} %pad_maximum_fusion.w_ref), custom_call_target="tpu_custom_call" | custom-call | tf_op jit(solution)/shard_map/pallas_call | solution.py:142
  352.7 15.6 %collective-permute-done.24 = bf16[192,3584]{1,0:T(8,128)(2,1)} collective-permute-done((bf16[192,3584]{1,0:T(8,128)(2,1)}, bf16[192,3584]{1,0:T(8,128)(2,1)}, u32[]{:S(2)}, u32[]{:S(2)}) %collective-permute-start.24) | collective-permute-done | bytes 1376288 | tf_op jit(solution)/shard_map/ppermute | solution.py:204
  373.3 6.1 collective-permute-start.30
  390.2 16.8 %collective-permute-done.30 = bf16[192,3584]{1,0:T(8,128)(2,1)S(1)} collective-permute-done((bf16[192,3584]{1,0:T(8,128)(2,1)S(1)}, bf16[192,3584]{1,0:T(8,128)(2,1)S(1)}, u32[]{:S(2)}, u32[]{:S(2)}) %collective-permute-start.30) | collective-permute-done | bytes 1376288 | tf_op jit(solution)/shard_map/ppermute | solution.py:204
  411.9 5.5 collective-permute-start.36
  421.8 8.7 %shard_map.175 = bf16[384,3584]{1,0:T(8,128)(2,1)S(1)} custom-call(bf16[384,1408]{1,0:T(8,128)(2,1)S(1)} %bitcast.347, bf16[1408,3584]{1,0:T(8,128)(2,1)} %pad_maximum_fusion.w_ref), custom_call_target="tpu_custom_call" | custom-call | tf_op jit(solution)/shard_map/pallas_call | solution.py:142
  430.8 12.8 %collective-permute-done.36 = bf16[192,3584]{1,0:T(8,128)(2,1)S(1)} collective-permute-done((bf16[192,3584]{1,0:T(8,128)(2,1)}, bf16[192,3584]{1,0:T(8,128)(2,1)S(1)}, u32[]{:S(2)}, u32[]{:S(2)}) %collective-permute-start.36) | collective-permute-done | bytes 1376288 | tf_op jit(solution)/shard_map/ppermute | solution.py:204
  457.8 8.7 %shard_map.176 = bf16[384,3584]{1,0:T(8,128)(2,1)S(1)} custom-call(bf16[384,1408]{1,0:T(8,128)(2,1)S(1)} %bitcast.344, bf16[1408,3584]{1,0:T(8,128)(2,1)} %pad_maximum_fusion.w_ref), custom_call_target="tpu_custom_call" | custom-call | tf_op jit(solution)/shard_map/pallas_call | solution.py:142
  466.5 25.6 %collective-permute-done.40 = bf16[192,1728]{1,0:T(8,128)(2,1)} collective-permute-done((bf16[192,1728]{1,0:T(8,128)(2,1)S(1)}, bf16[192,1728]{1,0:T(8,128)(2,1)}, u32[]{:S(2)}, u32[]{:S(2)}) %collective-permute-start.40) | collective-permute-done | bytes 663584 | tf_op jit(solution)/shard_map/ppermute | solution.py:204
  494.7 13.3 %collective-permute-done.43 = bf16[192,1728]{1,0:T(8,128)(2,1)S(1)} collective-permute-done((bf16[192,1728]{1,0:T(8,128)(2,1)}, bf16[192,1728]{1,0:T(8,128)(2,1)S(1)}, u32[]{:S(2)}, u32[]{:S(2)}) %collective-permute-start.43) | collective-permute-done | bytes 663584 | tf_op jit(solution)/shard_map/ppermute | solution.py:204
  514.9 19.8 %collective-permute-done.44 = bf16[192,3584]{1,0:T(8,128)(2,1)S(1)} collective-permute-done((bf16[192,3584]{1,0:T(8,128)(2,1)S(1)}, bf16[192,3584]{1,0:T(8,128)(2,1)S(1)}, u32[]{:S(2)}, u32[]{:S(2)}) %collective-permute-start.44) | collective-permute-done | bytes 1376288 | tf_op jit(solution)/shard_map/ppermute | solution.py:204
  536.9 10.5 %collective-permute-start.48 = (bf16[192,3584]{1,0:T(8,128)(2,1)S(1)}, bf16[192,3584]{1,0:T(8,128)(2,1)}, u32[]{:S(2)}, u32[]{:S(2)}) collective-permute-start(bf16[192,3584]{1,0:T(8,128)(2,1)S(1)} %add_convert_fusion.1), channel_id=1, source_target_pairs={{0,8},{4,12},{8,16},{12,20},{16,24},{20,28},{1,9},{5,13},{9,17},{1... | collective-permute-start | bytes 4128776 | tf_op jit(solution)/shard_map/ppermute | solution.py:204
  552.5 6.2 shard_map.177
  559.0 5.6 collective-permute-done.49
  568.9 5.1 collective-permute-start.50
  579.2 5.6 collective-permute-done.52
  602.4 14.0 %collective-permute-done.55 = bf16[192,1728]{1,0:T(8,128)(2,1)S(1)} collective-permute-done((bf16[192,1728]{1,0:T(8,128)(2,1)S(1)}, bf16[192,1728]{1,0:T(8,128)(2,1)S(1)}, u32[]{:S(2)}, u32[]{:S(2)}) %collective-permute-start.55) | collective-permute-done | bytes 663584 | tf_op jit(solution)/shard_map/ppermute | solution.py:204
  628.2 5.6 collective-permute-done.60
  636.8 6.2 shard_map.178
  (405 shorter events, 269.3 us)
Async XLA Ops:
  7.2 64.3 %all-gather.7.cloned.1.call-start = ((), (), s32[]{:S(2)}) async-start(), calls=%async_computation.1 | async-start | bytes 3276800 | tf_op jit(solution)/shard_map/all_gather | solution.py:297
  9.3 183.8 %all-gather.5.cloned.1.call-start = ((), (), s32[]{:S(2)}) async-start(), calls=%async_computation | async-start | bytes 6553600 | tf_op jit(solution)/shard_map/all_gather | solution.py:297
  28.6 30.8 %collective-permute-start.1 = (bf16[640,3456]{1,0:T(8,128)(2,1)}, bf16[640,3456]{1,0:T(8,128)(2,1)}, u32[]{:S(2)}, u32[]{:S(2)}) collective-permute-start(bf16[640,3456]{1,0:T(8,128)(2,1)} %concatenate.134), channel_id=1, source_target_pairs={{0,4},{4,0},{8,12},{12,8},{16,20},{20,16},{24,28},{28,24},{1,5},{5... | collective-permute-start | bytes 13271048 | tf_op jit(solution)/shard_map/ppermute | solution.py:209
  41.0 227.4 %all-gather.11.cloned.1.call-start = ((), (), s32[]{:S(2)}) async-start(), calls=%async_computation.3 | async-start | bytes 1966080 | tf_op jit(solution)/shard_map/all_gather | solution.py:297
  85.0 34.0 %collective-permute-start.7 = (bf16[384,512]{1,0:T(8,128)(2,1)}, bf16[384,512]{1,0:T(8,128)(2,1)S(1)}, u32[]{:S(2)}, u32[]{:S(2)}) collective-permute-start(bf16[384,512]{1,0:T(8,128)(2,1)} %shard_map.169), channel_id=1, source_target_pairs={{8,0},{12,4},{16,8},{20,12},{24,16},{28,20},{9,1},{13,5},{17,9},{2... | collective-permute-start | bytes 1179656 | tf_op jit(solution)/shard_map/ppermute | solution.py:204
  86.3 34.0 %collective-permute-start.6 = (bf16[384,512]{1,0:T(8,128)(2,1)}, bf16[384,512]{1,0:T(8,128)(2,1)S(1)}, u32[]{:S(2)}, u32[]{:S(2)}) collective-permute-start(bf16[384,512]{1,0:T(8,128)(2,1)} %shard_map.169), channel_id=1, source_target_pairs={{0,8},{4,12},{8,16},{12,20},{16,24},{20,28},{1,9},{5,13},{9,17},{1... | collective-permute-start | bytes 1179656 | tf_op jit(solution)/shard_map/ppermute | solution.py:204
  119.0 27.7 %collective-permute-start.8 = (bf16[384,512]{1,0:T(8,128)(2,1)S(1)}, bf16[384,512]{1,0:T(8,128)(2,1)S(1)}, u32[]{:S(2)}, u32[]{:S(2)}) collective-permute-start(bf16[384,512]{1,0:T(8,128)(2,1)S(1)} %collective-permute-done.7), channel_id=1, source_target_pairs={{8,0},{12,4},{16,8},{20,12},{9,1},{13,5},{17,9},{21,13},{10,2},{14... | collective-permute-start | bytes 1179656 | tf_op jit(solution)/shard_map/ppermute | solution.py:204
  120.3 29.5 %collective-permute-start.10 = (bf16[384,512]{1,0:T(8,128)(2,1)S(1)}, bf16[384,512]{1,0:T(8,128)(2,1)S(1)}, u32[]{:S(2)}, u32[]{:S(2)}) collective-permute-start(bf16[384,512]{1,0:T(8,128)(2,1)S(1)} %collective-permute-done.6), channel_id=1, source_target_pairs={{8,16},{12,20},{16,24},{20,28},{9,17},{13,21},{17,25},{21,29},{10,... | collective-permute-start | bytes 1179656 | tf_op jit(solution)/shard_map/ppermute | solution.py:204
  146.7 42.2 %collective-permute-start.9 = (bf16[384,512]{1,0:T(8,128)(2,1)S(1)}, bf16[384,512]{1,0:T(8,128)(2,1)S(1)}, u32[]{:S(2)}, u32[]{:S(2)}) collective-permute-start(bf16[384,512]{1,0:T(8,128)(2,1)S(1)} %collective-permute-done.8), channel_id=1, source_target_pairs={{8,0},{12,4},{9,1},{13,5},{10,2},{14,6},{11,3},{15,7}} | collective-permute-start | bytes 1179656 | tf_op jit(solution)/shard_map/ppermute | solution.py:204
  149.8 40.7 %collective-permute-start.11 = (bf16[384,512]{1,0:T(8,128)(2,1)S(1)}, bf16[384,512]{1,0:T(8,128)(2,1)S(1)}, u32[]{:S(2)}, u32[]{:S(2)}) collective-permute-start(bf16[384,512]{1,0:T(8,128)(2,1)S(1)} %collective-permute-done.10), channel_id=1, source_target_pairs={{16,24},{20,28},{17,25},{21,29},{18,26},{22,30},{19,27},{23,31}} | collective-permute-start | bytes 1179656 | tf_op jit(solution)/shard_map/ppermute | solution.py:204
  232.6 109.5 %all-gather.9.cloned.1.call-start = ((), (), s32[]{:S(2)}) async-start(), calls=%async_computation.2 | async-start | bytes 1966080 | tf_op jit(solution)/shard_map/all_gather | solution.py:297
  328.3 24.4 %collective-permute-start.25 = (bf16[192,3584]{1,0:T(8,128)(2,1)}, bf16[192,3584]{1,0:T(8,128)(2,1)}, u32[]{:S(2)}, u32[]{:S(2)}) collective-permute-start(bf16[192,3584]{1,0:T(8,128)(2,1)} %get-tuple-element.126), channel_id=1, source_target_pairs={{24,16},{28,20},{25,17},{29,21},{26,18},{30,22},{27,19},{31,23}} | collective-permute-start | bytes 4128776 | tf_op jit(solution)/shard_map/ppermute | solution.py:204
  338.9 29.5 %collective-permute-start.24 = (bf16[192,3584]{1,0:T(8,128)(2,1)}, bf16[192,3584]{1,0:T(8,128)(2,1)}, u32[]{:S(2)}, u32[]{:S(2)}) collective-permute-start(bf16[192,3584]{1,0:T(8,128)(2,1)} %get-tuple-element.125), channel_id=1, source_target_pairs={{0,8},{4,12},{1,9},{5,13},{2,10},{6,14},{3,11},{7,15}} | collective-permute-start | bytes 4128776 | tf_op jit(solution)/shard_map/ppermute | solution.py:204
  348.8 21.9 %collective-permute-start.26 = (bf16[2,2,48,1280]{3,2,1,0:T(8,128)(2,1)S(1)}, bf16[2,2,48,1280]{3,2,1,0:T(8,128)(2,1)S(1)}, u32[]{:S(2)}, u32[]{:S(2)}) collective-permute-start(bf16[2,2,48,1280]{3,2,1,0:T(8,128)(2,1)S(1)} %pad_maximum_fusion.24), channel_id=1, source_target_pairs={{0,1},{1,0},{2,3},{3,2},{4,5},{5,4},{6,7},{7,6},{8,9},{9,8},{10,11... | collective-permute-start | bytes 1474568 | tf_op jit(solution)/shard_map/ppermute | solution.py:214
  350.1 20.6 %collective-permute-start.27 = (bf16[2,2,48,1280]{3,2,1,0:T(8,128)(2,1)S(1)}, bf16[2,2,48,1280]{3,2,1,0:T(8,128)(2,1)S(1)}, u32[]{:S(2)}, u32[]{:S(2)}) collective-permute-start(bf16[2,2,48,1280]{3,2,1,0:T(8,128)(2,1)S(1)} %pad_maximum_fusion.25), channel_id=1, source_target_pairs={{0,2},{1,3},{2,0},{3,1},{4,6},{5,7},{6,4},{7,5},{8,10},{9,11},{10,... | collective-permute-start | bytes 1474568 | tf_op jit(solution)/shard_map/ppermute | solution.py:214
  373.3 33.7 %collective-permute-start.30 = (bf16[192,3584]{1,0:T(8,128)(2,1)S(1)}, bf16[192,3584]{1,0:T(8,128)(2,1)S(1)}, u32[]{:S(2)}, u32[]{:S(2)}) collective-permute-start(bf16[192,3584]{1,0:T(8,128)(2,1)S(1)} %get-tuple-element.133), channel_id=1, source_target_pairs={{0,8},{4,12},{8,16},{12,20},{1,9},{5,13},{9,17},{13,21},{2,10},{6,... | collective-permute-start | bytes 4128776 | tf_op jit(solution)/shard_map/ppermute | solution.py:204
  386.6 22.2 %collective-permute-start.32 = (bf16[1,2,48,1408]{3,2,1,0:T(8,128)(2,1)S(1)}, bf16[1,2,48,1408]{3,2,1,0:T(8,128)(2,1)S(1)}, u32[]{:S(2)}, u32[]{:S(2)}) collective-permute-start(bf16[1,2,48,1408]{3,2,1,0:T(8,128)(2,1)S(1)} %get-tuple-element.135), channel_id=1, source_target_pairs={{0,2},{1,3},{2,0},{3,1},{4,6},{5,7},{6,4},{7,5},{8,10},{9,11},{10,... | collective-permute-start | bytes 811016 | tf_op jit(solution)/shard_map/ppermute | solution.py:214
  388.4 20.5 %collective-permute-start.33 = (bf16[1,2,48,1408]{3,2,1,0:T(8,128)(2,1)S(1)}, bf16[1,2,48,1408]{3,2,1,0:T(8,128)(2,1)S(1)}, u32[]{:S(2)}, u32[]{:S(2)}) collective-permute-start(bf16[1,2,48,1408]{3,2,1,0:T(8,128)(2,1)S(1)} %get-tuple-element.136), channel_id=1, source_target_pairs={{0,1},{1,0},{2,3},{3,2},{4,5},{5,4},{6,7},{7,6},{8,9},{9,8},{10,11... | collective-permute-start | bytes 811016 | tf_op jit(solution)/shard_map/ppermute | solution.py:214
  411.9 31.7 %collective-permute-start.36 = (bf16[192,3584]{1,0:T(8,128)(2,1)}, bf16[192,3584]{1,0:T(8,128)(2,1)S(1)}, u32[]{:S(2)}, u32[]{:S(2)}) collective-permute-start(bf16[192,3584]{1,0:T(8,128)(2,1)} %get-tuple-element.143), channel_id=1, source_target_pairs={{0,8},{4,12},{8,16},{12,20},{16,24},{20,28},{1,9},{5,13},{9,17},{1... | collective-permute-start | bytes 4128776 | tf_op jit(solution)/shard_map/ppermute | solution.py:204
  417.4 30.8 %collective-permute-start.37 = (bf16[192,3584]{1,0:T(8,128)(2,1)S(1)}, bf16[192,3584]{1,0:T(8,128)(2,1)S(1)}, u32[]{:S(2)}, u32[]{:S(2)}) collective-permute-start(bf16[192,3584]{1,0:T(8,128)(2,1)S(1)} %get-tuple-element.144), channel_id=1, source_target_pairs={{8,0},{12,4},{16,8},{20,12},{24,16},{28,20},{9,1},{13,5},{17,9},{2... | collective-permute-start | bytes 4128776 | tf_op jit(solution)/shard_map/ppermute | solution.py:204
  448.2 46.0 %collective-permute-start.39 = (bf16[192,3584]{1,0:T(8,128)(2,1)S(1)}, bf16[192,3584]{1,0:T(8,128)(2,1)S(1)}, u32[]{:S(2)}, u32[]{:S(2)}) collective-permute-start(bf16[192,3584]{1,0:T(8,128)(2,1)S(1)} %get-tuple-element.146), channel_id=1, source_target_pairs={{24,16},{28,20},{25,17},{29,21},{26,18},{30,22},{27,19},{31,23}} | collective-permute-start | bytes 4128776 | tf_op jit(solution)/shard_map/ppermute | solution.py:204
  448.9 45.2 %collective-permute-start.38 = (bf16[192,3584]{1,0:T(8,128)(2,1)S(1)}, bf16[192,3584]{1,0:T(8,128)(2,1)S(1)}, u32[]{:S(2)}, u32[]{:S(2)}) collective-permute-start(bf16[192,3584]{1,0:T(8,128)(2,1)S(1)} %get-tuple-element.145), channel_id=1, source_target_pairs={{0,8},{4,12},{1,9},{5,13},{2,10},{6,14},{3,11},{7,15}} | collective-permute-start | bytes 4128776 | tf_op jit(solution)/shard_map/ppermute | solution.py:204
  454.2 38.0 %collective-permute-start.40 = (bf16[192,1728]{1,0:T(8,128)(2,1)S(1)}, bf16[192,1728]{1,0:T(8,128)(2,1)}, u32[]{:S(2)}, u32[]{:S(2)}) collective-permute-start(bf16[192,1728]{1,0:T(8,128)(2,1)S(1)} %pad_maximum_fusion.15), channel_id=1, source_target_pairs={{0,8},{4,12},{8,16},{12,20},{16,24},{20,28},{1,9},{5,13},{9,17},{1... | collective-permute-start | bytes 1990664 | tf_op jit(solution)/shard_map/ppermute | solution.py:204
  456.4 36.4 %collective-permute-start.42 = (bf16[192,1728]{1,0:T(8,128)(2,1)S(1)}, bf16[192,1728]{1,0:T(8,128)(2,1)}, u32[]{:S(2)}, u32[]{:S(2)}) collective-permute-start(bf16[192,1728]{1,0:T(8,128)(2,1)S(1)} %pad_maximum_fusion.15), channel_id=1, source_target_pairs={{8,0},{12,4},{16,8},{20,12},{24,16},{28,20},{9,1},{13,5},{17,9},{2... | collective-permute-start | bytes 1990664 | tf_op jit(solution)/shard_map/ppermute | solution.py:204
  508.1 26.6 %collective-permute-start.44 = (bf16[192,3584]{1,0:T(8,128)(2,1)S(1)}, bf16[192,3584]{1,0:T(8,128)(2,1)S(1)}, u32[]{:S(2)}, u32[]{:S(2)}) collective-permute-start(bf16[192,3584]{1,0:T(8,128)(2,1)S(1)} %get-tuple-element.150), channel_id=1, source_target_pairs={{0,8},{4,12},{8,16},{12,20},{1,9},{5,13},{9,17},{13,21},{2,10},{6,... | collective-permute-start | bytes 4128776 | tf_op jit(solution)/shard_map/ppermute | solution.py:204
  511.9 23.2 %collective-permute-start.45 = (bf16[192,3584]{1,0:T(8,128)(2,1)S(1)}, bf16[192,3584]{1,0:T(8,128)(2,1)S(1)}, u32[]{:S(2)}, u32[]{:S(2)}) collective-permute-start(bf16[192,3584]{1,0:T(8,128)(2,1)S(1)} %get-tuple-element.151), channel_id=1, source_target_pairs={{16,8},{20,12},{24,16},{28,20},{17,9},{21,13},{25,17},{29,21},{18,... | collective-permute-start | bytes 4128776 | tf_op jit(solution)/shard_map/ppermute | solution.py:204
  512.7 22.9 %collective-permute-start.46 = (bf16[192,1728]{1,0:T(8,128)(2,1)S(1)}, bf16[192,1728]{1,0:T(8,128)(2,1)S(1)}, u32[]{:S(2)}, u32[]{:S(2)}) collective-permute-start(bf16[192,1728]{1,0:T(8,128)(2,1)S(1)} %collective-permute-done.41), channel_id=1, source_target_pairs={{16,24},{20,28},{17,25},{21,29},{18,26},{22,30},{19,27},{23,31}} | collective-permute-start | bytes 1990664 | tf_op jit(solution)/shard_map/ppermute | solution.py:204
  513.4 22.2 %collective-permute-start.47 = (bf16[192,1728]{1,0:T(8,128)(2,1)S(1)}, bf16[192,1728]{1,0:T(8,128)(2,1)S(1)}, u32[]{:S(2)}, u32[]{:S(2)}) collective-permute-start(bf16[192,1728]{1,0:T(8,128)(2,1)S(1)} %collective-permute-done.43), channel_id=1, source_target_pairs={{8,0},{12,4},{9,1},{13,5},{10,2},{14,6},{11,3},{15,7}} | collective-permute-start | bytes 1990664 | tf_op jit(solution)/shard_map/ppermute | solution.py:204
  535.6 29.1 %collective-permute-start.49 = (bf16[192,3584]{1,0:T(8,128)(2,1)S(1)}, bf16[192,3584]{1,0:T(8,128)(2,1)}, u32[]{:S(2)}, u32[]{:S(2)}) collective-permute-start(bf16[192,3584]{1,0:T(8,128)(2,1)S(1)} %add_convert_fusion), channel_id=1, source_target_pairs={{8,0},{12,4},{16,8},{20,12},{24,16},{28,20},{9,1},{13,5},{17,9},{2... | collective-permute-start | bytes 4128776 | tf_op jit(solution)/shard_map/ppermute | solution.py:204
  536.9 28.8 %collective-permute-start.48 = (bf16[192,3584]{1,0:T(8,128)(2,1)S(1)}, bf16[192,3584]{1,0:T(8,128)(2,1)}, u32[]{:S(2)}, u32[]{:S(2)}) collective-permute-start(bf16[192,3584]{1,0:T(8,128)(2,1)S(1)} %add_convert_fusion.1), channel_id=1, source_target_pairs={{0,8},{4,12},{8,16},{12,20},{16,24},{20,28},{1,9},{5,13},{9,17},{1... | collective-permute-start | bytes 4128776 | tf_op jit(solution)/shard_map/ppermute | solution.py:204
  568.9 19.7 %collective-permute-start.50 = (bf16[192,1728]{1,0:T(8,128)(2,1)S(1)}, bf16[192,1728]{1,0:T(8,128)(2,1)S(1)}, u32[]{:S(2)}, u32[]{:S(2)}) collective-permute-start(bf16[192,1728]{1,0:T(8,128)(2,1)S(1)} %pad_maximum_fusion.16), channel_id=1, source_target_pairs={{0,8},{4,12},{8,16},{12,20},{16,24},{20,28},{1,9},{5,13},{9,17},{1... | collective-permute-start | bytes 1990664 | tf_op jit(solution)/shard_map/ppermute | solution.py:204
  591.6 24.8 %collective-permute-start.55 = (bf16[192,1728]{1,0:T(8,128)(2,1)S(1)}, bf16[192,1728]{1,0:T(8,128)(2,1)S(1)}, u32[]{:S(2)}, u32[]{:S(2)}) collective-permute-start(bf16[192,1728]{1,0:T(8,128)(2,1)S(1)} %collective-permute-done.51), channel_id=1, source_target_pairs={{8,0},{12,4},{16,8},{20,12},{9,1},{13,5},{17,9},{21,13},{10,2},{14... | collective-permute-start | bytes 1990664 | tf_op jit(solution)/shard_map/ppermute | solution.py:204
  (90 other events, 1068.2 us)
Sparse Core Ops, SparseCore 0:
  10.1 57.4 all-gather.6
  69.2 118.5 all-gather.4
  232.7 35.6 all-gather.10
  307.4 33.8 all-gather.8

commit v11 on v10

--- a/solution.py
+++ b/solution.py
@@ -432,14 +432,10 @@
         lane = jnp.concatenate([(residual * gain_lane).astype(BF16), square.astype(BF16)], axis=-1)
         return spread_begin(lane)
 
-    def contract_half(lane):
-        part = product(lane.reshape(-1, dz + HD), glu_weight, BF16).reshape(-1, crows, 2 * units + HD)
-        return [part[i] for i in range(part.shape[0])]
-
     def contract(lanes):
-        first = contract_half(lanes[0])
-        last, first[0] = after(lanes[1], first[0])
-        return dict(zip(order, first + contract_half(last)))
+        lane = jnp.concatenate(lanes, axis=0).reshape(planes * crows, dz + HD)
+        part = product(lane, glu_weight, BF16).reshape(planes, crows, 2 * units + HD)
+        return {k: part[i] for i, k in enumerate(order)}
 
     def activate(part, carried):
         act = part[0].astype(F32) + carried[0].astype(F32) + carried[1].astype(F32)
@@ -475,10 +471,8 @@
     states = lane_terms(residuals[0])
     for n in range(bits):
         states = spread_stage(states, n)
-    lanes = lax.optimization_barrier(spread_end(states))
-    first = contract_half(lanes[0])
-    carried, last = scatter_step(dict(zip(order, first)), None, 1, lanes[1])
-    parts = dict(zip(order, first + contract_half(last)))
+    parts = contract(spread_end(states))
+    carried, _ = scatter_step(parts, None, 1)
     finals = [None] * chunks
     before, summing, following = None, None, None
     for h in range(chunks):
@@ -502,9 +496,6 @@
                     summing = None
             if before is not None:
                 if t == 1:
-                    hidden = activate(*before)
-                    state = ([hidden], [hidden])
-                    gather_step(state, 1)
                     gather_step(state, 2)
                 elif t < steps:
                     gather_step(state, t + 1)
@@ -530,12 +521,14 @@
                     following = contract(spread_end(states))
         before = (parts, carried)
         if h + 1 < chunks:
+            hidden = activate(*before)
+            state = ([hidden], [hidden])
+            gather_step(state, 1)
             gots = summing[3] if summing is not None else ()
-            carried, (behind, gots) = scatter_step(following, None, 1, (carried, gots))
+            (state[0][-1], state[1][-1]), (parts, gots) = after((state[0][-1], state[1][-1]), (following, gots))
             if summing is not None:
                 summing = summing[:3] + (gots,)
-            before = (parts, behind)
-            parts = following
+            carried, _ = scatter_step(parts, None, 1)
     hidden = activate(*before)
     state = ([hidden], [hidden])
     for t in range(1, steps + 1):

time: 694 us -> 682 us (0.983)
  starting transfers between devices: 124 us -> 113 us
    ppermute x24, starting transfers between devices: 40.6 us -> 25.9 us  [partner(): return lax.ppermute(x, 'mlp', [(a, a ^ bit) for a in range(mlp_count)])]
    pallas_call x10 -> x8, Pallas kernels: 65.8 us -> 56.4 us  [product(): pl.pallas_call(product_kernel, grid=(cols // tile,), in_specs=[pl.BlockSp...]
  transfers between devices with their start and end apart: 74 -> 74, of which waited for: 42 -> 42; matrix products, arithmetic and copies ran while one was open for 14% -> 15% of each run, Pallas kernels for 10% -> 9%
where the time goes in v11:
time: 682 us; the launch traced here: 673 us
  waiting for transfers between devices  346 us (51%)
  starting transfers between devices  113 us (17%)
  Pallas kernels  72.5 us (11%)
  other arithmetic  70.6 us (10%)
  local copies, waits for them, and re-layouts  54.5 us (8%)
  between operations  17.2 us (3%)
    ppermute x39, waiting for transfers between devices, move(): lax.ppermute(x, 'seq', [(a * CORES + e, b * CORES + e) for a, b in pairs...  238 us
    ppermute x39, starting transfers between devices, move(): lax.ppermute(x, 'seq', [(a * CORES + e, b * CORES + e) for a, b in pairs...  84.5 us
    ppermute x24, waiting for transfers between devices, partner(): return lax.ppermute(x, 'mlp', [(a, a ^ bit) for a in range(mlp_count)])  66.5 us
    pallas_call x8, Pallas kernels, product(): pl.pallas_call(product_kernel, grid=(cols // tile,), in_specs=[pl.BlockSp...  56.4 us
    all_gather x4, waiting for transfers between devices, line_collect(): return lax.all_gather(x, 'seq', axis=0, tiled=True, axis_index_groups=lines)  39.9 us
    ppermute x24, starting transfers between devices, partner(): return lax.ppermute(x, 'mlp', [(a, a ^ bit) for a in range(mlp_count)])  25.9 us
  transfers between devices with their start and end apart: 74, of which 42 were waited for; matrix products, arithmetic and copies ran while one was open for 15% of the time, Pallas kernels for 9%

profile of v11, /device:TPU:0, one launch (start us, length us, event | category | flops | bytes accessed | tf_op | source)
XLA Modules:
  0.0 673.1 jit_solution(6609765477721528932)
XLA Ops:
  21.4 7.1 %concatenate.140 = bf16[640,3456]{1,0:T(8,128)(2,1)} concatenate(bf16[640,1664]{1,0:T(8,128)(2,1)S(1)} %slice-done.6, bf16[640,1664]{1,0:T(8,128)(2,1)} %slice.599, bf16[640,64]{1,0:T(8,128)(2,1)S(1)} %slice-done.7, bf16[640,64]{1,0:T(8,128)(2,1)S(1)} %slice-done.8), dimensions={1} | concatenate | bytes 8847360 | tf_op jit(solution)/shard_map/concatenate | solution.py:339
  63.3 7.3 %pad_maximum_fusion.w_ref = bf16[1408,3584]{1,0:T(8,128)(2,1)} fusion(bf16[128,3584]{1,0:T(8,128)(2,1)S(1)} %pad_convert_fusion, bf16[1280,3584]{1,0:T(8,128)(2,1)S(1)} %fusion.2), kind=kLoop, calls=%fused_computation.3 | loop fusion | flops 20185088 | bytes 20185088 | tf_op jit(solution)/shard_map/concatenate | solution.py:344
  85.2 5.9 collective-permute-start.6
  91.1 26.9 %collective-permute-done.7 = bf16[384,512]{1,0:T(8,128)(2,1)S(1)} collective-permute-done((bf16[384,512]{1,0:T(8,128)(2,1)}, bf16[384,512]{1,0:T(8,128)(2,1)S(1)}, u32[]{:S(2)}, u32[]{:S(2)}) %collective-permute-start.7) | collective-permute-done | bytes 393248 | tf_op jit(solution)/shard_map/ppermute | solution.py:204
  120.0 24.8 %collective-permute-done.8 = bf16[384,512]{1,0:T(8,128)(2,1)S(1)} collective-permute-done((bf16[384,512]{1,0:T(8,128)(2,1)S(1)}, bf16[384,512]{1,0:T(8,128)(2,1)S(1)}, u32[]{:S(2)}, u32[]{:S(2)}) %collective-permute-start.8) | collective-permute-done | bytes 393248 | tf_op jit(solution)/shard_map/ppermute | solution.py:204
  148.9 40.0 %collective-permute-done.9 = bf16[384,512]{1,0:T(8,128)(2,1)S(1)} collective-permute-done((bf16[384,512]{1,0:T(8,128)(2,1)S(1)}, bf16[384,512]{1,0:T(8,128)(2,1)S(1)}, u32[]{:S(2)}, u32[]{:S(2)}) %collective-permute-start.9) | collective-permute-done | bytes 393248 | tf_op jit(solution)/shard_map/ppermute | solution.py:204
  193.0 7.5 %shard_map.167.own_ref = f32[768,1024]{1,0:T(8,128)S(1)} custom-call(bf16[768,2560]{1,0:T(8,128)(2,1)} %pad_maximum_fusion.2.x_ref, bf16[2560,1024]{1,0:T(8,128)(2,1)} %all-gather.5.cloned.1.call-done.w_ref), custom_call_target="tpu_custom_call" | custom-call | tf_op jit(solution)/shard_map/pallas_call | solution.py:142
  214.4 13.4 %shard_map.170 = bf16[384,1024]{1,0:T(8,128)(2,1)S(1)} custom-call(s32[2]{0:T(128)S(1)} %convert_reduce_fusion.1.count, s32[2,16]{1,0:T(2,128)S(1)} %select_reduce_fusion.1.active, s32[16]{0:T(128)S(1)} %select_reduce_fusion.2.piece_stream, f32[768,1024]{1,0:T(8,128)S(1)} %copy-done.1, f32[384,1024]{1,0:T(8,128)} %collective-permute-done.4.sib_ref, ...), custom_call_target="tpu_custom_call" | custom-call | tf_op jit(solution)/shard_map/pallas_call | solution.py:110
  232.8 37.7 %all-gather.11.cloned.1.call-done = bf16[768,1024]{1,0:T(8,128)(2,1)} async-done(((bf16[192,1024]{1,0:T(8,128)(2,1)}), bf16[768,1024]{1,0:T(8,128)(2,1)}) %all-gather.11.cloned.1.call-update) | async-done | bytes 1572880 | tf_op jit(solution)/shard_map/all_gather | solution.py:297
  279.0 9.6 %collective-permute-done.16 = bf16[2,2,48,1280]{3,2,1,0:T(8,128)(2,1)S(1)} collective-permute-done((bf16[2,2,48,1280]{3,2,1,0:T(8,128)(2,1)S(1)}, bf16[2,2,48,1280]{3,2,1,0:T(8,128)(2,1)S(1)}, u32[]{:S(2)}, u32[]{:S(2)}) %collective-permute-start.16) | collective-permute-done | bytes 491552 | tf_op jit(solution)/shard_map/ppermute | solution.py:214
  311.8 7.9 %collective-permute-done.23 = bf16[2,2,48,1408]{3,2,1,0:T(8,128)(2,1)} collective-permute-done((bf16[2,2,48,1408]{3,2,1,0:T(8,128)(2,1)}, bf16[2,2,48,1408]{3,2,1,0:T(8,128)(2,1)}, u32[]{:S(2)}, u32[]{:S(2)}) %collective-permute-start.23) | collective-permute-done | bytes 540704 | tf_op jit(solution)/shard_map/ppermute | solution.py:214
  322.6 12.8 %shard_map.172 = bf16[768,3584]{1,0:T(8,128)(2,1)} custom-call(bf16[768,1408]{1,0:T(8,128)(2,1)S(1)} %bitcast.343, bf16[1408,3584]{1,0:T(8,128)(2,1)} %pad_maximum_fusion.w_ref), custom_call_target="tpu_custom_call" | custom-call | tf_op jit(solution)/shard_map/pallas_call | solution.py:142
  356.3 17.1 %collective-permute-done.24 = bf16[192,3584]{1,0:T(8,128)(2,1)} collective-permute-done((bf16[192,3584]{1,0:T(8,128)(2,1)}, bf16[192,3584]{1,0:T(8,128)(2,1)}, u32[]{:S(2)}, u32[]{:S(2)}) %collective-permute-start.24) | collective-permute-done | bytes 1376288 | tf_op jit(solution)/shard_map/ppermute | solution.py:204
  378.3 5.2 collective-permute-start.28
  385.1 5.1 collective-permute-done.30
  392.6 18.1 %collective-permute-done.28 = bf16[192,3584]{1,0:T(8,128)(2,1)S(1)} collective-permute-done((bf16[192,3584]{1,0:T(8,128)(2,1)S(1)}, bf16[192,3584]{1,0:T(8,128)(2,1)S(1)}, u32[]{:S(2)}, u32[]{:S(2)}) %collective-permute-start.28) | collective-permute-done | bytes 1376288 | tf_op jit(solution)/shard_map/ppermute | solution.py:204
  415.0 5.8 collective-permute-start.34
  424.6 12.9 %shard_map.174 = bf16[768,3584]{1,0:T(8,128)(2,1)} custom-call(bf16[768,1408]{1,0:T(8,128)(2,1)S(1)} %bitcast.342, bf16[1408,3584]{1,0:T(8,128)(2,1)} %pad_maximum_fusion.w_ref), custom_call_target="tpu_custom_call" | custom-call | tf_op jit(solution)/shard_map/pallas_call | solution.py:142
  437.5 8.2 %collective-permute-done.35 = bf16[192,3584]{1,0:T(8,128)(2,1)S(1)} collective-permute-done((bf16[192,3584]{1,0:T(8,128)(2,1)S(1)}, bf16[192,3584]{1,0:T(8,128)(2,1)S(1)}, u32[]{:S(2)}, u32[]{:S(2)}) %collective-permute-start.35) | collective-permute-done | bytes 1376288 | tf_op jit(solution)/shard_map/ppermute | solution.py:204
  454.7 8.8 %collective-permute-done.36 = bf16[192,1728]{1,0:T(8,128)(2,1)S(1)} collective-permute-done((bf16[192,1728]{1,0:T(8,128)(2,1)S(1)}, bf16[192,1728]{1,0:T(8,128)(2,1)S(1)}, u32[]{:S(2)}, u32[]{:S(2)}) %collective-permute-start.36) | collective-permute-done | bytes 663584 | tf_op jit(solution)/shard_map/ppermute | solution.py:204
  474.9 23.3 %collective-permute-done.40 = bf16[192,3584]{1,0:T(8,128)(2,1)S(1)} collective-permute-done((bf16[192,3584]{1,0:T(8,128)(2,1)S(1)}, bf16[192,3584]{1,0:T(8,128)(2,1)S(1)}, u32[]{:S(2)}, u32[]{:S(2)}) %collective-permute-start.40) | collective-permute-done | bytes 1376288 | tf_op jit(solution)/shard_map/ppermute | solution.py:204
  506.1 20.2 %collective-permute-done.44 = bf16[192,3584]{1,0:T(8,128)(2,1)S(1)} collective-permute-done((bf16[192,3584]{1,0:T(8,128)(2,1)S(1)}, bf16[192,3584]{1,0:T(8,128)(2,1)S(1)}, u32[]{:S(2)}, u32[]{:S(2)}) %collective-permute-start.44) | collective-permute-done | bytes 1376288 | tf_op jit(solution)/shard_map/ppermute | solution.py:204
  528.6 10.8 %collective-permute-start.48 = (bf16[192,3584]{1,0:T(8,128)(2,1)S(1)}, bf16[192,3584]{1,0:T(8,128)(2,1)}, u32[]{:S(2)}, u32[]{:S(2)}) collective-permute-start(bf16[192,3584]{1,0:T(8,128)(2,1)S(1)} %add_convert_fusion.1), channel_id=1, source_target_pairs={{0,8},{4,12},{8,16},{12,20},{16,24},{20,28},{1,9},{5,13},{9,17},{1... | collective-permute-start | bytes 4128776 | tf_op jit(solution)/shard_map/ppermute | solution.py:204
  542.2 6.2 shard_map.175
  548.8 6.6 collective-permute-done.49
  559.6 5.4 collective-permute-start.50
  567.9 10.0 %collective-permute-done.52 = bf16[2,2,48,1280]{3,2,1,0:T(8,128)(2,1)S(1)} collective-permute-done((bf16[2,2,48,1280]{3,2,1,0:T(8,128)(2,1)S(1)}, bf16[2,2,48,1280]{3,2,1,0:T(8,128)(2,1)S(1)}, u32[]{:S(2)}, u32[]{:S(2)}) %collective-permute-start.52) | collective-permute-done | bytes 491552 | tf_op jit(solution)/shard_map/ppermute | solution.py:214
  586.4 5.3 collective-permute-done.56
  591.8 16.1 %collective-permute-done.55 = bf16[192,1728]{1,0:T(8,128)(2,1)S(1)} collective-permute-done((bf16[192,1728]{1,0:T(8,128)(2,1)S(1)}, bf16[192,1728]{1,0:T(8,128)(2,1)S(1)}, u32[]{:S(2)}, u32[]{:S(2)}) %collective-permute-start.55) | collective-permute-done | bytes 663584 | tf_op jit(solution)/shard_map/ppermute | solution.py:204
  619.7 5.6 collective-permute-done.60
  628.3 6.2 shard_map.176
  635.1 8.7 %collective-permute-done.63 = bf16[2,2,48,1280]{3,2,1,0:T(8,128)(2,1)S(1)} collective-permute-done((bf16[2,2,48,1280]{3,2,1,0:T(8,128)(2,1)S(1)}, bf16[2,2,48,1280]{3,2,1,0:T(8,128)(2,1)S(1)}, u32[]{:S(2)}, u32[]{:S(2)}) %collective-permute-start.63) | collective-permute-done | bytes 491552 | tf_op jit(solution)/shard_map/ppermute | solution.py:214
  (401 shorter events, 249.1 us)
Async XLA Ops:
  7.2 63.5 %all-gather.7.cloned.1.call-start = ((), (), s32[]{:S(2)}) async-start(), calls=%async_computation.1 | async-start | bytes 3276800 | tf_op jit(solution)/shard_map/all_gather | solution.py:297
  9.3 183.8 %all-gather.5.cloned.1.call-start = ((), (), s32[]{:S(2)}) async-start(), calls=%async_computation | async-start | bytes 6553600 | tf_op jit(solution)/shard_map/all_gather | solution.py:297
  28.5 30.0 %collective-permute-start.1 = (bf16[640,3456]{1,0:T(8,128)(2,1)}, bf16[640,3456]{1,0:T(8,128)(2,1)}, u32[]{:S(2)}, u32[]{:S(2)}) collective-permute-start(bf16[640,3456]{1,0:T(8,128)(2,1)} %concatenate.140), channel_id=1, source_target_pairs={{0,4},{4,0},{8,12},{12,8},{16,20},{20,16},{24,28},{28,24},{1,5},{5... | collective-permute-start | bytes 13271048 | tf_op jit(solution)/shard_map/ppermute | solution.py:209
  40.9 229.6 %all-gather.11.cloned.1.call-start = ((), (), s32[]{:S(2)}) async-start(), calls=%async_computation.3 | async-start | bytes 1966080 | tf_op jit(solution)/shard_map/all_gather | solution.py:297
  83.9 34.1 %collective-permute-start.7 = (bf16[384,512]{1,0:T(8,128)(2,1)}, bf16[384,512]{1,0:T(8,128)(2,1)S(1)}, u32[]{:S(2)}, u32[]{:S(2)}) collective-permute-start(bf16[384,512]{1,0:T(8,128)(2,1)} %shard_map.169), channel_id=1, source_target_pairs={{8,0},{12,4},{16,8},{20,12},{24,16},{28,20},{9,1},{13,5},{17,9},{2... | collective-permute-start | bytes 1179656 | tf_op jit(solution)/shard_map/ppermute | solution.py:204
  85.2 34.1 %collective-permute-start.6 = (bf16[384,512]{1,0:T(8,128)(2,1)}, bf16[384,512]{1,0:T(8,128)(2,1)S(1)}, u32[]{:S(2)}, u32[]{:S(2)}) collective-permute-start(bf16[384,512]{1,0:T(8,128)(2,1)} %shard_map.169), channel_id=1, source_target_pairs={{0,8},{4,12},{8,16},{12,20},{16,24},{20,28},{1,9},{5,13},{9,17},{1... | collective-permute-start | bytes 1179656 | tf_op jit(solution)/shard_map/ppermute | solution.py:204
  118.0 26.8 %collective-permute-start.8 = (bf16[384,512]{1,0:T(8,128)(2,1)S(1)}, bf16[384,512]{1,0:T(8,128)(2,1)S(1)}, u32[]{:S(2)}, u32[]{:S(2)}) collective-permute-start(bf16[384,512]{1,0:T(8,128)(2,1)S(1)} %collective-permute-done.7), channel_id=1, source_target_pairs={{8,0},{12,4},{16,8},{20,12},{9,1},{13,5},{17,9},{21,13},{10,2},{14... | collective-permute-start | bytes 1179656 | tf_op jit(solution)/shard_map/ppermute | solution.py:204
  119.3 28.7 %collective-permute-start.10 = (bf16[384,512]{1,0:T(8,128)(2,1)S(1)}, bf16[384,512]{1,0:T(8,128)(2,1)S(1)}, u32[]{:S(2)}, u32[]{:S(2)}) collective-permute-start(bf16[384,512]{1,0:T(8,128)(2,1)S(1)} %collective-permute-done.6), channel_id=1, source_target_pairs={{8,16},{12,20},{16,24},{20,28},{9,17},{13,21},{17,25},{21,29},{10,... | collective-permute-start | bytes 1179656 | tf_op jit(solution)/shard_map/ppermute | solution.py:204
  144.8 44.1 %collective-permute-start.9 = (bf16[384,512]{1,0:T(8,128)(2,1)S(1)}, bf16[384,512]{1,0:T(8,128)(2,1)S(1)}, u32[]{:S(2)}, u32[]{:S(2)}) collective-permute-start(bf16[384,512]{1,0:T(8,128)(2,1)S(1)} %collective-permute-done.8), channel_id=1, source_target_pairs={{8,0},{12,4},{9,1},{13,5},{10,2},{14,6},{11,3},{15,7}} | collective-permute-start | bytes 1179656 | tf_op jit(solution)/shard_map/ppermute | solution.py:204
  147.9 42.6 %collective-permute-start.11 = (bf16[384,512]{1,0:T(8,128)(2,1)S(1)}, bf16[384,512]{1,0:T(8,128)(2,1)S(1)}, u32[]{:S(2)}, u32[]{:S(2)}) collective-permute-start(bf16[384,512]{1,0:T(8,128)(2,1)S(1)} %collective-permute-done.10), channel_id=1, source_target_pairs={{16,24},{20,28},{17,25},{21,29},{18,26},{22,30},{19,27},{23,31}} | collective-permute-start | bytes 1179656 | tf_op jit(solution)/shard_map/ppermute | solution.py:204
  207.7 20.1 %collective-permute-start.13 = (bf16[96,1280]{1,0:T(8,128)(2,1)}, bf16[96,1280]{1,0:T(8,128)(2,1)S(1)}, u32[]{:S(2)}, u32[]{:S(2)}) collective-permute-start(bf16[96,1280]{1,0:T(8,128)(2,1)} %get-tuple-element.101), channel_id=1, source_target_pairs={{0,8},{4,12},{8,16},{12,20},{16,24},{20,28},{24,0},{28,4},{1,9},{5... | collective-permute-start | bytes 737288 | tf_op jit(solution)/shard_map/ppermute | solution.py:204
  207.8 20.1 %collective-permute-start.14 = (bf16[96,1280]{1,0:T(8,128)(2,1)}, bf16[96,1280]{1,0:T(8,128)(2,1)S(1)}, u32[]{:S(2)}, u32[]{:S(2)}) collective-permute-start(bf16[96,1280]{1,0:T(8,128)(2,1)} %get-tuple-element.102), channel_id=1, source_target_pairs={{0,24},{4,28},{8,0},{12,4},{16,8},{20,12},{24,16},{28,20},{1,25},{... | collective-permute-start | bytes 737288 | tf_op jit(solution)/shard_map/ppermute | solution.py:204
  211.6 19.3 %collective-permute-start.15 = (bf16[96,1280]{1,0:T(8,128)(2,1)}, bf16[96,1280]{1,0:T(8,128)(2,1)S(1)}, u32[]{:S(2)}, u32[]{:S(2)}) collective-permute-start(bf16[96,1280]{1,0:T(8,128)(2,1)} %get-tuple-element.103), channel_id=1, source_target_pairs={{0,16},{4,20},{8,24},{12,28},{16,0},{20,4},{24,8},{28,12},{1,17},{... | collective-permute-start | bytes 737288 | tf_op jit(solution)/shard_map/ppermute | solution.py:204
  232.5 114.2 %all-gather.9.cloned.1.call-start = ((), (), s32[]{:S(2)}) async-start(), calls=%async_computation.2 | async-start | bytes 1966080 | tf_op jit(solution)/shard_map/all_gather | solution.py:297
  341.4 31.9 %collective-permute-start.24 = (bf16[192,3584]{1,0:T(8,128)(2,1)}, bf16[192,3584]{1,0:T(8,128)(2,1)}, u32[]{:S(2)}, u32[]{:S(2)}) collective-permute-start(bf16[192,3584]{1,0:T(8,128)(2,1)} %get-tuple-element.121), channel_id=1, source_target_pairs={{0,8},{4,12},{1,9},{5,13},{2,10},{6,14},{3,11},{7,15}} | collective-permute-start | bytes 4128776 | tf_op jit(solution)/shard_map/ppermute | solution.py:204
  351.8 23.8 %collective-permute-start.26 = (bf16[2,2,48,1280]{3,2,1,0:T(8,128)(2,1)S(1)}, bf16[2,2,48,1280]{3,2,1,0:T(8,128)(2,1)S(1)}, u32[]{:S(2)}, u32[]{:S(2)}) collective-permute-start(bf16[2,2,48,1280]{3,2,1,0:T(8,128)(2,1)S(1)} %pad_maximum_fusion.20), channel_id=1, source_target_pairs={{0,1},{1,0},{2,3},{3,2},{4,5},{5,4},{6,7},{7,6},{8,9},{9,8},{10,11... | collective-permute-start | bytes 1474568 | tf_op jit(solution)/shard_map/ppermute | solution.py:214
  354.8 20.9 %collective-permute-start.27 = (bf16[2,2,48,1280]{3,2,1,0:T(8,128)(2,1)S(1)}, bf16[2,2,48,1280]{3,2,1,0:T(8,128)(2,1)S(1)}, u32[]{:S(2)}, u32[]{:S(2)}) collective-permute-start(bf16[2,2,48,1280]{3,2,1,0:T(8,128)(2,1)S(1)} %pad_maximum_fusion.21), channel_id=1, source_target_pairs={{0,2},{1,3},{2,0},{3,1},{4,6},{5,7},{6,4},{7,5},{8,10},{9,11},{10,... | collective-permute-start | bytes 1474568 | tf_op jit(solution)/shard_map/ppermute | solution.py:214
  378.3 32.4 %collective-permute-start.28 = (bf16[192,3584]{1,0:T(8,128)(2,1)S(1)}, bf16[192,3584]{1,0:T(8,128)(2,1)S(1)}, u32[]{:S(2)}, u32[]{:S(2)}) collective-permute-start(bf16[192,3584]{1,0:T(8,128)(2,1)S(1)} %get-tuple-element.126), channel_id=1, source_target_pairs={{0,8},{4,12},{8,16},{12,20},{1,9},{5,13},{9,17},{13,21},{2,10},{6,... | collective-permute-start | bytes 4128776 | tf_op jit(solution)/shard_map/ppermute | solution.py:204
  390.6 20.7 %collective-permute-start.32 = (bf16[1,2,48,1408]{3,2,1,0:T(8,128)(2,1)S(1)}, bf16[1,2,48,1408]{3,2,1,0:T(8,128)(2,1)S(1)}, u32[]{:S(2)}, u32[]{:S(2)}) collective-permute-start(bf16[1,2,48,1408]{3,2,1,0:T(8,128)(2,1)S(1)} %get-tuple-element.132), channel_id=1, source_target_pairs={{0,2},{1,3},{2,0},{3,1},{4,6},{5,7},{6,4},{7,5},{8,10},{9,11},{10,... | collective-permute-start | bytes 811016 | tf_op jit(solution)/shard_map/ppermute | solution.py:214
  413.7 32.1 %collective-permute-start.35 = (bf16[192,3584]{1,0:T(8,128)(2,1)S(1)}, bf16[192,3584]{1,0:T(8,128)(2,1)S(1)}, u32[]{:S(2)}, u32[]{:S(2)}) collective-permute-start(bf16[192,3584]{1,0:T(8,128)(2,1)S(1)} %get-tuple-element.135), channel_id=1, source_target_pairs={{8,0},{12,4},{16,8},{20,12},{24,16},{28,20},{9,1},{13,5},{17,9},{2... | collective-permute-start | bytes 4128776 | tf_op jit(solution)/shard_map/ppermute | solution.py:204
  415.0 31.9 %collective-permute-start.34 = (bf16[192,3584]{1,0:T(8,128)(2,1)S(1)}, bf16[192,3584]{1,0:T(8,128)(2,1)S(1)}, u32[]{:S(2)}, u32[]{:S(2)}) collective-permute-start(bf16[192,3584]{1,0:T(8,128)(2,1)S(1)} %get-tuple-element.134), channel_id=1, source_target_pairs={{0,8},{4,12},{8,16},{12,20},{16,24},{20,28},{1,9},{5,13},{9,17},{1... | collective-permute-start | bytes 4128776 | tf_op jit(solution)/shard_map/ppermute | solution.py:204
  469.1 29.0 %collective-permute-start.40 = (bf16[192,3584]{1,0:T(8,128)(2,1)S(1)}, bf16[192,3584]{1,0:T(8,128)(2,1)S(1)}, u32[]{:S(2)}, u32[]{:S(2)}) collective-permute-start(bf16[192,3584]{1,0:T(8,128)(2,1)S(1)} %get-tuple-element.144), channel_id=1, source_target_pairs={{0,8},{4,12},{1,9},{5,13},{2,10},{6,14},{3,11},{7,15}} | collective-permute-start | bytes 4128776 | tf_op jit(solution)/shard_map/ppermute | solution.py:204
  472.9 25.8 %collective-permute-start.42 = (bf16[192,1728]{1,0:T(8,128)(2,1)S(1)}, bf16[192,1728]{1,0:T(8,128)(2,1)S(1)}, u32[]{:S(2)}, u32[]{:S(2)}) collective-permute-start(bf16[192,1728]{1,0:T(8,128)(2,1)S(1)} %collective-permute-done.36), channel_id=1, source_target_pairs={{8,16},{12,20},{16,24},{20,28},{9,17},{13,21},{17,25},{21,29},{10,... | collective-permute-start | bytes 1990664 | tf_op jit(solution)/shard_map/ppermute | solution.py:204
  473.6 25.1 %collective-permute-start.43 = (bf16[192,1728]{1,0:T(8,128)(2,1)S(1)}, bf16[192,1728]{1,0:T(8,128)(2,1)S(1)}, u32[]{:S(2)}, u32[]{:S(2)}) collective-permute-start(bf16[192,1728]{1,0:T(8,128)(2,1)S(1)} %collective-permute-done.37), channel_id=1, source_target_pairs={{8,0},{12,4},{16,8},{20,12},{9,1},{13,5},{17,9},{21,13},{10,2},{14... | collective-permute-start | bytes 1990664 | tf_op jit(solution)/shard_map/ppermute | solution.py:204
  498.7 27.6 %collective-permute-start.44 = (bf16[192,3584]{1,0:T(8,128)(2,1)S(1)}, bf16[192,3584]{1,0:T(8,128)(2,1)S(1)}, u32[]{:S(2)}, u32[]{:S(2)}) collective-permute-start(bf16[192,3584]{1,0:T(8,128)(2,1)S(1)} %get-tuple-element.148), channel_id=1, source_target_pairs={{0,8},{4,12},{8,16},{12,20},{1,9},{5,13},{9,17},{13,21},{2,10},{6,... | collective-permute-start | bytes 4128776 | tf_op jit(solution)/shard_map/ppermute | solution.py:204
  503.2 23.6 %collective-permute-start.45 = (bf16[192,3584]{1,0:T(8,128)(2,1)S(1)}, bf16[192,3584]{1,0:T(8,128)(2,1)S(1)}, u32[]{:S(2)}, u32[]{:S(2)}) collective-permute-start(bf16[192,3584]{1,0:T(8,128)(2,1)S(1)} %get-tuple-element.149), channel_id=1, source_target_pairs={{16,8},{20,12},{24,16},{28,20},{17,9},{21,13},{25,17},{29,21},{18,... | collective-permute-start | bytes 4128776 | tf_op jit(solution)/shard_map/ppermute | solution.py:204
  504.0 23.3 %collective-permute-start.46 = (bf16[192,1728]{1,0:T(8,128)(2,1)S(1)}, bf16[192,1728]{1,0:T(8,128)(2,1)S(1)}, u32[]{:S(2)}, u32[]{:S(2)}) collective-permute-start(bf16[192,1728]{1,0:T(8,128)(2,1)S(1)} %collective-permute-done.42), channel_id=1, source_target_pairs={{16,24},{20,28},{17,25},{21,29},{18,26},{22,30},{19,27},{23,31}} | collective-permute-start | bytes 1990664 | tf_op jit(solution)/shard_map/ppermute | solution.py:204
  504.7 22.6 %collective-permute-start.47 = (bf16[192,1728]{1,0:T(8,128)(2,1)S(1)}, bf16[192,1728]{1,0:T(8,128)(2,1)S(1)}, u32[]{:S(2)}, u32[]{:S(2)}) collective-permute-start(bf16[192,1728]{1,0:T(8,128)(2,1)S(1)} %collective-permute-done.43), channel_id=1, source_target_pairs={{8,0},{12,4},{9,1},{13,5},{10,2},{14,6},{11,3},{15,7}} | collective-permute-start | bytes 1990664 | tf_op jit(solution)/shard_map/ppermute | solution.py:204
  527.3 28.1 %collective-permute-start.49 = (bf16[192,3584]{1,0:T(8,128)(2,1)S(1)}, bf16[192,3584]{1,0:T(8,128)(2,1)S(1)}, u32[]{:S(2)}, u32[]{:S(2)}) collective-permute-start(bf16[192,3584]{1,0:T(8,128)(2,1)S(1)} %add_convert_fusion), channel_id=1, source_target_pairs={{8,0},{12,4},{16,8},{20,12},{24,16},{28,20},{9,1},{13,5},{17,9},{2... | collective-permute-start | bytes 4128776 | tf_op jit(solution)/shard_map/ppermute | solution.py:204
  528.6 28.2 %collective-permute-start.48 = (bf16[192,3584]{1,0:T(8,128)(2,1)S(1)}, bf16[192,3584]{1,0:T(8,128)(2,1)}, u32[]{:S(2)}, u32[]{:S(2)}) collective-permute-start(bf16[192,3584]{1,0:T(8,128)(2,1)S(1)} %add_convert_fusion.1), channel_id=1, source_target_pairs={{0,8},{4,12},{8,16},{12,20},{16,24},{20,28},{1,9},{5,13},{9,17},{1... | collective-permute-start | bytes 4128776 | tf_op jit(solution)/shard_map/ppermute | solution.py:204
  559.6 19.3 %collective-permute-start.50 = (bf16[192,1728]{1,0:T(8,128)(2,1)S(1)}, bf16[192,1728]{1,0:T(8,128)(2,1)S(1)}, u32[]{:S(2)}, u32[]{:S(2)}) collective-permute-start(bf16[192,1728]{1,0:T(8,128)(2,1)S(1)} %pad_maximum_fusion.12), channel_id=1, source_target_pairs={{0,8},{4,12},{8,16},{12,20},{16,24},{20,28},{1,9},{5,13},{9,17},{1... | collective-permute-start | bytes 1990664 | tf_op jit(solution)/shard_map/ppermute | solution.py:204
  584.0 23.9 %collective-permute-start.55 = (bf16[192,1728]{1,0:T(8,128)(2,1)S(1)}, bf16[192,1728]{1,0:T(8,128)(2,1)S(1)}, u32[]{:S(2)}, u32[]{:S(2)}) collective-permute-start(bf16[192,1728]{1,0:T(8,128)(2,1)S(1)} %collective-permute-done.51), channel_id=1, source_target_pairs={{8,0},{12,4},{16,8},{20,12},{9,1},{13,5},{17,9},{21,13},{10,2},{14... | collective-permute-start | bytes 1990664 | tf_op jit(solution)/shard_map/ppermute | solution.py:204
  (90 other events, 840.7 us)
Sparse Core Ops, SparseCore 0:
  10.1 57.4 all-gather.6
  69.2 118.5 all-gather.4
  232.6 37.8 all-gather.10
  311.8 34.8 all-gather.8

commit v12 on v11

--- a/solution.py
+++ b/solution.py
@@ -131,11 +131,14 @@
     )(count, active, piece_stream, query, query_sib, bias, cosine, sine, kv_rows, kv_rows, lo_wide, hi_wide)
 
 
-def product_kernel(x_ref, w_ref, o_ref):
-    o_ref[...] = jnp.dot(x_ref[...], w_ref[...], preferred_element_type=F32).astype(o_ref.dtype)
-
-
-def product(x, w, out_type):
+def product_kernel(x_ref, w_ref, *o_refs):
+    found = jnp.dot(x_ref[...], w_ref[...], preferred_element_type=F32)
+    rows = o_refs[0].shape[0]
+    for i, o_ref in enumerate(o_refs):
+        o_ref[...] = found[i * rows : (i + 1) * rows].astype(o_ref.dtype)
+
+
+def product(x, w, out_type, pieces=1):
     rows, inner = x.shape
     cols = w.shape[1]
     tile = next((t for t in (512, 384, 256) if cols % t == 0), cols)
@@ -146,8 +149,8 @@
             pl.BlockSpec((rows, inner), lambda n: (0, 0)),
             pl.BlockSpec((inner, tile), lambda n: (0, n)),
         ],
-        out_specs=pl.BlockSpec((rows, tile), lambda n: (0, n)),
-        out_shape=jax.ShapeDtypeStruct((rows, cols), out_type),
+        out_specs=[pl.BlockSpec((rows // pieces, tile), lambda n: (0, n))] * pieces,
+        out_shape=[jax.ShapeDtypeStruct((rows // pieces, cols), out_type)] * pieces,
         cost_estimate=pl.CostEstimate(flops=0, transcendentals=0, bytes_accessed=0),
         compiler_params=pltpu.CompilerParams(vmem_limit_bytes=48 * 2**20),
     )(x, w)
@@ -366,10 +369,10 @@
     cosine, sine = rope_tables(stream - doc_first, HD)
 
     kv_heads = kv_cols // HD
-    kv = product(both, kv_weight, F32)
+    kv, kv_theirs = product(both, kv_weight, F32, 2)
     joined = pl.pallas_call(
         join_kernel, out_shape=jax.ShapeDtypeStruct((rows, 2 * kv_cols), BF16)
-    )(kv, sibling(kv[rows:]), kv_bias[None, :], cosine, sine)
+    )(kv, sibling(kv_theirs), kv_bias[None, :], cosine, sine)
     core_rows = jnp.concatenate(line_gather(joined), axis=0)
     kv_rows = jnp.concatenate([core_rows, sibling(core_rows)], axis=0)
     offsets = (plane - jnp.arange(planes, dtype=jnp.int32)) % planes
@@ -393,8 +396,8 @@
         move(v, [(i, (i + k) % planes) for i in range(planes)]) if k else v
         for k, v in zip(order, lane_sends)
     ]
-    query = product(both, q_weight, F32)
-    query_sib = sibling(query[rows:])
+    query, query_theirs = product(both, q_weight, F32, 2)
+    query_sib = sibling(query_theirs)
     mixed = attend(
         query, query_sib, query_bias.astype(F32)[None, :], cosine, sine, kv_rows, doc_first, stream, piece_stream, kv_heads
     )
@@ -421,7 +424,7 @@
             ],
             axis=0,
         )
-        return sum_begin(product(heads, out_wide, BF16).reshape(planes, mlp_count, sub, dz))
+        return sum_begin(product(heads, out_wide, BF16)[0].reshape(planes, mlp_count, sub, dz))
 
     def attn_end(h, states):
         return lane_input[:, h].astype(F32) + sum_end(states)
@@ -434,8 +437,7 @@
 
     def contract(lanes):
         lane = jnp.concatenate(lanes, axis=0).reshape(planes * crows, dz + HD)
-        part = product(lane, glu_weight, BF16).reshape(planes, crows, 2 * units + HD)
-        return {k: part[i] for i, k in enumerate(order)}
+        return dict(zip(order, product(lane, glu_weight, BF16, planes)))
 
     def activate(part, carried):
         act = part[0].astype(F32) + carried[0].astype(F32) + carried[1].astype(F32)
@@ -461,7 +463,7 @@
     def down_terms(state):
         slots = gather_slots(state)
         hidden = jnp.concatenate([slots[k] for k in order], axis=0)
-        return sum_begin(product(hidden, down_wide, BF16).reshape(planes, mlp_count, sub, dz))
+        return sum_begin(product(hidden, down_wide, BF16)[0].reshape(planes, mlp_count, sub, dz))
 
     steps = planes - 1
     states = attn_terms(0)

time: 682 us -> 665 us (0.975)
  waiting for transfers between devices: 346 us -> 337 us
    ppermute x39, waiting for transfers between devices: 238 us -> 230 us  [move(): lax.ppermute(x, 'seq', [(a * CORES + e, b * CORES + e) for a, b in pairs...]
  transfers between devices with their start and end apart: 74 -> 74, of which waited for: 42 -> 40; matrix products, arithmetic and copies ran while one was open for 15% -> 15% of each run, Pallas kernels for 9% -> 9%
where the time goes in v12:
time: 665 us; the launch traced here: 657 us
  waiting for transfers between devices  337 us (51%)
  starting transfers between devices  109 us (16%)
  other arithmetic  74.3 us (11%)
  Pallas kernels  69.9 us (11%)
  local copies, waits for them, and re-layouts  49.2 us (7%)
  between operations  17 us (3%)
    ppermute x39, waiting for transfers between devices, move(): lax.ppermute(x, 'seq', [(a * CORES + e, b * CORES + e) for a, b in pairs...  230 us
    ppermute x39, starting transfers between devices, move(): lax.ppermute(x, 'seq', [(a * CORES + e, b * CORES + e) for a, b in pairs...  79.2 us
    ppermute x24, waiting for transfers between devices, partner(): return lax.ppermute(x, 'mlp', [(a, a ^ bit) for a in range(mlp_count)])  67.2 us
    pallas_call x8, Pallas kernels, product(): pl.pallas_call(product_kernel, grid=(cols // tile,), in_specs=[pl.BlockSp...  56.1 us
    all_gather x4, waiting for transfers between devices, line_collect(): return lax.all_gather(x, 'seq', axis=0, tiled=True, axis_index_groups=lines)  38.5 us
    ppermute x24, starting transfers between devices, partner(): return lax.ppermute(x, 'mlp', [(a, a ^ bit) for a in range(mlp_count)])  27.8 us
  transfers between devices with their start and end apart: 74, of which 40 were waited for; matrix products, arithmetic and copies ran while one was open for 15% of the time, Pallas kernels for 9%

profile of v12, /device:TPU:0, one launch (start us, length us, event | category | flops | bytes accessed | tf_op | source)
XLA Modules:
  0.0 656.5 jit_solution(10592335148532856839)
XLA Ops:
  21.5 7.0 %concatenate.140 = bf16[640,3456]{1,0:T(8,128)(2,1)} concatenate(bf16[640,1664]{1,0:T(8,128)(2,1)S(1)} %slice-done.2, bf16[640,1664]{1,0:T(8,128)(2,1)} %slice.551, bf16[640,64]{1,0:T(8,128)(2,1)S(1)} %slice-done.3, bf16[640,64]{1,0:T(8,128)(2,1)S(1)} %slice-done.4), dimensions={1} | concatenate | bytes 8847360 | tf_op jit(solution)/shard_map/concatenate | solution.py:342
  53.7 4.7 pad_maximum_fusion.1.w_ref
  63.2 7.3 %pad_maximum_fusion.w_ref = bf16[1408,3584]{1,0:T(8,128)(2,1)} fusion(bf16[128,3584]{1,0:T(8,128)(2,1)S(1)} %pad_convert_fusion, bf16[1280,3584]{1,0:T(8,128)(2,1)S(1)} %fusion.2), kind=kLoop, calls=%fused_computation.3 | loop fusion | flops 20185088 | bytes 20185088 | tf_op jit(solution)/shard_map/concatenate | solution.py:347
  84.4 5.9 collective-permute-start.6
  90.4 24.2 %collective-permute-done.7 = bf16[384,512]{1,0:T(8,128)(2,1)S(1)} collective-permute-done((bf16[384,512]{1,0:T(8,128)(2,1)}, bf16[384,512]{1,0:T(8,128)(2,1)S(1)}, u32[]{:S(2)}, u32[]{:S(2)}) %collective-permute-start.7) | collective-permute-done | bytes 393248 | tf_op jit(solution)/shard_map/ppermute | solution.py:207
  116.6 25.3 %collective-permute-done.8 = bf16[384,512]{1,0:T(8,128)(2,1)S(1)} collective-permute-done((bf16[384,512]{1,0:T(8,128)(2,1)S(1)}, bf16[384,512]{1,0:T(8,128)(2,1)S(1)}, u32[]{:S(2)}, u32[]{:S(2)}) %collective-permute-start.8) | collective-permute-done | bytes 393248 | tf_op jit(solution)/shard_map/ppermute | solution.py:207
  146.1 42.8 %collective-permute-done.9 = bf16[384,512]{1,0:T(8,128)(2,1)S(1)} collective-permute-done((bf16[384,512]{1,0:T(8,128)(2,1)S(1)}, bf16[384,512]{1,0:T(8,128)(2,1)S(1)}, u32[]{:S(2)}, u32[]{:S(2)}) %collective-permute-start.9) | collective-permute-done | bytes 393248 | tf_op jit(solution)/shard_map/ppermute | solution.py:207
  193.1 8.3 %shard_map.167 = (f32[384,1024]{1,0:T(8,128)S(1)}, f32[384,1024]{1,0:T(8,128)}) custom-call(bf16[768,2560]{1,0:T(8,128)(2,1)} %pad_maximum_fusion.2.x_ref, bf16[2560,1024]{1,0:T(8,128)(2,1)} %all-gather.5.cloned.1.call-done.w_ref), custom_call_target="tpu_custom_call" | custom-call | tf_op jit(solution)/shard_map/pallas_call | solution.py:145
  213.2 11.3 %shard_map.170 = bf16[384,1024]{1,0:T(8,128)(2,1)S(1)} custom-call(s32[2]{0:T(128)S(1)} %convert_reduce_fusion.1.count, s32[2,16]{1,0:T(2,128)S(1)} %select_reduce_fusion.1.active, s32[16]{0:T(128)S(1)} %select_reduce_fusion.2.piece_stream, f32[384,1024]{1,0:T(8,128)S(1)} %copy-done.4, f32[384,1024]{1,0:T(8,128)} %collective-permute-done.4.sib_ref, ...), custom_call_target="tpu_custom_call" | custom-call | tf_op jit(solution)/shard_map/pallas_call | solution.py:110
  224.6 5.3 collective-permute-done.15
  231.8 38.5 %all-gather.11.cloned.1.call-done = bf16[768,1024]{1,0:T(8,128)(2,1)} async-done(((bf16[192,1024]{1,0:T(8,128)(2,1)}), bf16[768,1024]{1,0:T(8,128)(2,1)}) %all-gather.11.cloned.1.call-update) | async-done | bytes 1572880 | tf_op jit(solution)/shard_map/all_gather | solution.py:300
  278.7 9.6 %collective-permute-done.16 = bf16[2,2,48,1280]{3,2,1,0:T(8,128)(2,1)S(1)} collective-permute-done((bf16[2,2,48,1280]{3,2,1,0:T(8,128)(2,1)S(1)}, bf16[2,2,48,1280]{3,2,1,0:T(8,128)(2,1)S(1)}, u32[]{:S(2)}, u32[]{:S(2)}) %collective-permute-start.16) | collective-permute-done | bytes 491552 | tf_op jit(solution)/shard_map/ppermute | solution.py:217
  310.2 8.8 %collective-permute-done.23 = bf16[2,2,48,1408]{3,2,1,0:T(8,128)(2,1)S(1)} collective-permute-done((bf16[2,2,48,1408]{3,2,1,0:T(8,128)(2,1)S(1)}, bf16[2,2,48,1408]{3,2,1,0:T(8,128)(2,1)S(1)}, u32[]{:S(2)}, u32[]{:S(2)}) %collective-permute-start.23) | collective-permute-done | bytes 540704 | tf_op jit(solution)/shard_map/ppermute | solution.py:217
  322.8 12.6 %shard_map.172 = (bf16[192,3584]{1,0:T(8,128)(2,1)}, bf16[192,3584]{1,0:T(8,128)(2,1)}, bf16[192,3584]{1,0:T(8,128)(2,1)S(1)}, bf16[192,3584]{1,0:T(8,128)(2,1)S(1)}) custom-call(bf16[768,1408]{1,0:T(8,128)(2,1)} %bitcast.346, bf16[1408,3584]{1,0:T(8,128)(2,1)} %pad_maximum_fusion.w_ref), custom_call_target="tpu_custom_call" | custom-call | tf_op jit(solution)/shard_map/pallas_call | solution.py:145
  349.3 17.4 %collective-permute-done.24 = bf16[192,3584]{1,0:T(8,128)(2,1)} collective-permute-done((bf16[192,3584]{1,0:T(8,128)(2,1)}, bf16[192,3584]{1,0:T(8,128)(2,1)}, u32[]{:S(2)}, u32[]{:S(2)}) %collective-permute-start.24) | collective-permute-done | bytes 1376288 | tf_op jit(solution)/shard_map/ppermute | solution.py:207
  375.9 6.7 %collective-permute-done.30 = bf16[1,2,48,1280]{3,2,1,0:T(8,128)(2,1)S(1)} collective-permute-done((bf16[1,2,48,1280]{3,2,1,0:T(8,128)(2,1)S(1)}, bf16[1,2,48,1280]{3,2,1,0:T(8,128)(2,1)S(1)}, u32[]{:S(2)}, u32[]{:S(2)}) %collective-permute-start.30) | collective-permute-done | bytes 245792 | tf_op jit(solution)/shard_map/ppermute | solution.py:217
  385.6 12.1 %collective-permute-done.28 = bf16[192,3584]{1,0:T(8,128)(2,1)S(1)} collective-permute-done((bf16[192,3584]{1,0:T(8,128)(2,1)S(1)}, bf16[192,3584]{1,0:T(8,128)(2,1)S(1)}, u32[]{:S(2)}, u32[]{:S(2)}) %collective-permute-start.28) | collective-permute-done | bytes 1376288 | tf_op jit(solution)/shard_map/ppermute | solution.py:207
  402.7 6.4 collective-permute-start.34
  411.7 6.9 %collective-permute-done.39 = bf16[2,2,48,1408]{3,2,1,0:T(8,128)(2,1)S(1)} collective-permute-done((bf16[2,2,48,1408]{3,2,1,0:T(8,128)(2,1)S(1)}, bf16[2,2,48,1408]{3,2,1,0:T(8,128)(2,1)S(1)}, u32[]{:S(2)}, u32[]{:S(2)}) %collective-permute-start.39) | collective-permute-done | bytes 540704 | tf_op jit(solution)/shard_map/ppermute | solution.py:217
  418.6 11.3 %collective-permute-done.35 = bf16[192,3584]{1,0:T(8,128)(2,1)S(1)} collective-permute-done((bf16[192,3584]{1,0:T(8,128)(2,1)S(1)}, bf16[192,3584]{1,0:T(8,128)(2,1)S(1)}, u32[]{:S(2)}, u32[]{:S(2)}) %collective-permute-start.35) | collective-permute-done | bytes 1376288 | tf_op jit(solution)/shard_map/ppermute | solution.py:207
  442.7 12.1 %shard_map.174 = (bf16[192,3584]{1,0:T(8,128)(2,1)S(1)}, bf16[192,3584]{1,0:T(8,128)(2,1)S(1)}, bf16[192,3584]{1,0:T(8,128)(2,1)S(1)}, bf16[192,3584]{1,0:T(8,128)(2,1)S(1)}) custom-call(bf16[768,1408]{1,0:T(8,128)(2,1)} %bitcast.345, bf16[1408,3584]{1,0:T(8,128)(2,1)} %pad_maximum_fusion.w_ref), custom_call_target="tpu_custom_call" | custom-call | tf_op jit(solution)/shard_map/pallas_call | solution.py:145
  462.3 23.3 %collective-permute-done.40 = bf16[192,3584]{1,0:T(8,128)(2,1)S(1)} collective-permute-done((bf16[192,3584]{1,0:T(8,128)(2,1)S(1)}, bf16[192,3584]{1,0:T(8,128)(2,1)S(1)}, u32[]{:S(2)}, u32[]{:S(2)}) %collective-permute-start.40) | collective-permute-done | bytes 1376288 | tf_op jit(solution)/shard_map/ppermute | solution.py:207
  493.5 20.3 %collective-permute-done.44 = bf16[192,3584]{1,0:T(8,128)(2,1)S(1)} collective-permute-done((bf16[192,3584]{1,0:T(8,128)(2,1)S(1)}, bf16[192,3584]{1,0:T(8,128)(2,1)S(1)}, u32[]{:S(2)}, u32[]{:S(2)}) %collective-permute-start.44) | collective-permute-done | bytes 1376288 | tf_op jit(solution)/shard_map/ppermute | solution.py:207
  515.8 5.2 collective-permute-start.48
  525.0 6.2 shard_map.175
  535.3 9.6 %collective-permute-done.48 = bf16[192,3584]{1,0:T(8,128)(2,1)S(1)} collective-permute-done((bf16[192,3584]{1,0:T(8,128)(2,1)S(1)}, bf16[192,3584]{1,0:T(8,128)(2,1)S(1)}, u32[]{:S(2)}, u32[]{:S(2)}) %collective-permute-start.48) | collective-permute-done | bytes 1376288 | tf_op jit(solution)/shard_map/ppermute | solution.py:207
  555.0 6.4 collective-permute-done.52
  562.0 7.0 %collective-permute-done.51 = bf16[192,1728]{1,0:T(8,128)(2,1)S(1)} collective-permute-done((bf16[192,1728]{1,0:T(8,128)(2,1)S(1)}, bf16[192,1728]{1,0:T(8,128)(2,1)S(1)}, u32[]{:S(2)}, u32[]{:S(2)}) %collective-permute-start.51) | collective-permute-done | bytes 663584 | tf_op jit(solution)/shard_map/ppermute | solution.py:207
  579.4 11.5 %collective-permute-done.55 = bf16[192,1728]{1,0:T(8,128)(2,1)S(1)} collective-permute-done((bf16[192,1728]{1,0:T(8,128)(2,1)S(1)}, bf16[192,1728]{1,0:T(8,128)(2,1)S(1)}, u32[]{:S(2)}, u32[]{:S(2)}) %collective-permute-start.55) | collective-permute-done | bytes 663584 | tf_op jit(solution)/shard_map/ppermute | solution.py:207
  603.0 5.4 collective-permute-done.60
  611.4 6.2 shard_map.176
  620.1 6.8 %collective-permute-done.63 = bf16[2,2,48,1280]{3,2,1,0:T(8,128)(2,1)S(1)} collective-permute-done((bf16[2,2,48,1280]{3,2,1,0:T(8,128)(2,1)S(1)}, bf16[2,2,48,1280]{3,2,1,0:T(8,128)(2,1)S(1)}, u32[]{:S(2)}, u32[]{:S(2)}) %collective-permute-start.63) | collective-permute-done | bytes 491552 | tf_op jit(solution)/shard_map/ppermute | solution.py:217
  (390 shorter events, 247.1 us)
Async XLA Ops:
  7.2 63.4 %all-gather.7.cloned.1.call-start = ((), (), s32[]{:S(2)}) async-start(), calls=%async_computation.1 | async-start | bytes 3276800 | tf_op jit(solution)/shard_map/all_gather | solution.py:300
  9.3 183.8 %all-gather.5.cloned.1.call-start = ((), (), s32[]{:S(2)}) async-start(), calls=%async_computation | async-start | bytes 6553600 | tf_op jit(solution)/shard_map/all_gather | solution.py:300
  28.5 30.0 %collective-permute-start.1 = (bf16[640,3456]{1,0:T(8,128)(2,1)}, bf16[640,3456]{1,0:T(8,128)(2,1)}, u32[]{:S(2)}, u32[]{:S(2)}) collective-permute-start(bf16[640,3456]{1,0:T(8,128)(2,1)} %concatenate.140), channel_id=1, source_target_pairs={{0,4},{4,0},{8,12},{12,8},{16,20},{20,16},{24,28},{28,24},{1,5},{5... | collective-permute-start | bytes 13271048 | tf_op jit(solution)/shard_map/ppermute | solution.py:212
  40.9 229.4 %all-gather.11.cloned.1.call-start = ((), (), s32[]{:S(2)}) async-start(), calls=%async_computation.3 | async-start | bytes 1966080 | tf_op jit(solution)/shard_map/all_gather | solution.py:300
  83.1 31.5 %collective-permute-start.7 = (bf16[384,512]{1,0:T(8,128)(2,1)}, bf16[384,512]{1,0:T(8,128)(2,1)S(1)}, u32[]{:S(2)}, u32[]{:S(2)}) collective-permute-start(bf16[384,512]{1,0:T(8,128)(2,1)} %shard_map.169), channel_id=1, source_target_pairs={{8,0},{12,4},{16,8},{20,12},{24,16},{28,20},{9,1},{13,5},{17,9},{2... | collective-permute-start | bytes 1179656 | tf_op jit(solution)/shard_map/ppermute | solution.py:207
  84.4 31.5 %collective-permute-start.6 = (bf16[384,512]{1,0:T(8,128)(2,1)}, bf16[384,512]{1,0:T(8,128)(2,1)S(1)}, u32[]{:S(2)}, u32[]{:S(2)}) collective-permute-start(bf16[384,512]{1,0:T(8,128)(2,1)} %shard_map.169), channel_id=1, source_target_pairs={{0,8},{4,12},{8,16},{12,20},{16,24},{20,28},{1,9},{5,13},{9,17},{1... | collective-permute-start | bytes 1179656 | tf_op jit(solution)/shard_map/ppermute | solution.py:207
  114.6 27.3 %collective-permute-start.8 = (bf16[384,512]{1,0:T(8,128)(2,1)S(1)}, bf16[384,512]{1,0:T(8,128)(2,1)S(1)}, u32[]{:S(2)}, u32[]{:S(2)}) collective-permute-start(bf16[384,512]{1,0:T(8,128)(2,1)S(1)} %collective-permute-done.7), channel_id=1, source_target_pairs={{8,0},{12,4},{16,8},{20,12},{9,1},{13,5},{17,9},{21,13},{10,2},{14... | collective-permute-start | bytes 1179656 | tf_op jit(solution)/shard_map/ppermute | solution.py:207
  115.9 29.2 %collective-permute-start.10 = (bf16[384,512]{1,0:T(8,128)(2,1)S(1)}, bf16[384,512]{1,0:T(8,128)(2,1)S(1)}, u32[]{:S(2)}, u32[]{:S(2)}) collective-permute-start(bf16[384,512]{1,0:T(8,128)(2,1)S(1)} %collective-permute-done.6), channel_id=1, source_target_pairs={{8,16},{12,20},{16,24},{20,28},{9,17},{13,21},{17,25},{21,29},{10,... | collective-permute-start | bytes 1179656 | tf_op jit(solution)/shard_map/ppermute | solution.py:207
  141.9 47.0 %collective-permute-start.9 = (bf16[384,512]{1,0:T(8,128)(2,1)S(1)}, bf16[384,512]{1,0:T(8,128)(2,1)S(1)}, u32[]{:S(2)}, u32[]{:S(2)}) collective-permute-start(bf16[384,512]{1,0:T(8,128)(2,1)S(1)} %collective-permute-done.8), channel_id=1, source_target_pairs={{8,0},{12,4},{9,1},{13,5},{10,2},{14,6},{11,3},{15,7}} | collective-permute-start | bytes 1179656 | tf_op jit(solution)/shard_map/ppermute | solution.py:207
  145.1 45.5 %collective-permute-start.11 = (bf16[384,512]{1,0:T(8,128)(2,1)S(1)}, bf16[384,512]{1,0:T(8,128)(2,1)S(1)}, u32[]{:S(2)}, u32[]{:S(2)}) collective-permute-start(bf16[384,512]{1,0:T(8,128)(2,1)S(1)} %collective-permute-done.10), channel_id=1, source_target_pairs={{16,24},{20,28},{17,25},{21,29},{18,26},{22,30},{19,27},{23,31}} | collective-permute-start | bytes 1179656 | tf_op jit(solution)/shard_map/ppermute | solution.py:207
  210.6 19.3 %collective-permute-start.15 = (bf16[96,1280]{1,0:T(8,128)(2,1)}, bf16[96,1280]{1,0:T(8,128)(2,1)S(1)}, u32[]{:S(2)}, u32[]{:S(2)}) collective-permute-start(bf16[96,1280]{1,0:T(8,128)(2,1)} %get-tuple-element.119), channel_id=1, source_target_pairs={{0,16},{4,20},{8,24},{12,28},{16,0},{20,4},{24,8},{28,12},{1,17},{... | collective-permute-start | bytes 737288 | tf_op jit(solution)/shard_map/ppermute | solution.py:207
  231.5 111.1 %all-gather.9.cloned.1.call-start = ((), (), s32[]{:S(2)}) async-start(), calls=%async_computation.2 | async-start | bytes 1966080 | tf_op jit(solution)/shard_map/all_gather | solution.py:300
  339.5 27.2 %collective-permute-start.24 = (bf16[192,3584]{1,0:T(8,128)(2,1)}, bf16[192,3584]{1,0:T(8,128)(2,1)}, u32[]{:S(2)}, u32[]{:S(2)}) collective-permute-start(bf16[192,3584]{1,0:T(8,128)(2,1)} %get-tuple-element.141), channel_id=1, source_target_pairs={{0,8},{4,12},{1,9},{5,13},{2,10},{6,14},{3,11},{7,15}} | collective-permute-start | bytes 4128776 | tf_op jit(solution)/shard_map/ppermute | solution.py:207
  347.7 21.3 %collective-permute-start.26 = (bf16[2,2,48,1280]{3,2,1,0:T(8,128)(2,1)S(1)}, bf16[2,2,48,1280]{3,2,1,0:T(8,128)(2,1)S(1)}, u32[]{:S(2)}, u32[]{:S(2)}) collective-permute-start(bf16[2,2,48,1280]{3,2,1,0:T(8,128)(2,1)S(1)} %pad_maximum_fusion.20), channel_id=1, source_target_pairs={{0,1},{1,0},{2,3},{3,2},{4,5},{5,4},{6,7},{7,6},{8,9},{9,8},{10,11... | collective-permute-start | bytes 1474568 | tf_op jit(solution)/shard_map/ppermute | solution.py:217
  348.4 20.6 %collective-permute-start.27 = (bf16[2,2,48,1280]{3,2,1,0:T(8,128)(2,1)S(1)}, bf16[2,2,48,1280]{3,2,1,0:T(8,128)(2,1)S(1)}, u32[]{:S(2)}, u32[]{:S(2)}) collective-permute-start(bf16[2,2,48,1280]{3,2,1,0:T(8,128)(2,1)S(1)} %pad_maximum_fusion.21), channel_id=1, source_target_pairs={{0,2},{1,3},{2,0},{3,1},{4,6},{5,7},{6,4},{7,5},{8,10},{9,11},{10,... | collective-permute-start | bytes 1474568 | tf_op jit(solution)/shard_map/ppermute | solution.py:217
  369.6 28.1 %collective-permute-start.28 = (bf16[192,3584]{1,0:T(8,128)(2,1)S(1)}, bf16[192,3584]{1,0:T(8,128)(2,1)S(1)}, u32[]{:S(2)}, u32[]{:S(2)}) collective-permute-start(bf16[192,3584]{1,0:T(8,128)(2,1)S(1)} %get-tuple-element.146), channel_id=1, source_target_pairs={{0,8},{4,12},{8,16},{12,20},{1,9},{5,13},{9,17},{13,21},{2,10},{6,... | collective-permute-start | bytes 4128776 | tf_op jit(solution)/shard_map/ppermute | solution.py:207
  374.1 25.3 %collective-permute-start.29 = (bf16[192,3584]{1,0:T(8,128)(2,1)S(1)}, bf16[192,3584]{1,0:T(8,128)(2,1)S(1)}, u32[]{:S(2)}, u32[]{:S(2)}) collective-permute-start(bf16[192,3584]{1,0:T(8,128)(2,1)S(1)} %get-tuple-element.147), channel_id=1, source_target_pairs={{16,8},{20,12},{24,16},{28,20},{17,9},{21,13},{25,17},{29,21},{18,... | collective-permute-start | bytes 4128776 | tf_op jit(solution)/shard_map/ppermute | solution.py:207
  401.0 28.9 %collective-permute-start.35 = (bf16[192,3584]{1,0:T(8,128)(2,1)S(1)}, bf16[192,3584]{1,0:T(8,128)(2,1)S(1)}, u32[]{:S(2)}, u32[]{:S(2)}) collective-permute-start(bf16[192,3584]{1,0:T(8,128)(2,1)S(1)} %add_convert_fusion.2), channel_id=1, source_target_pairs={{8,0},{12,4},{16,8},{20,12},{24,16},{28,20},{9,1},{13,5},{17,9},{2... | collective-permute-start | bytes 4128776 | tf_op jit(solution)/shard_map/ppermute | solution.py:207
  402.7 30.8 %collective-permute-start.34 = (bf16[192,3584]{1,0:T(8,128)(2,1)S(1)}, bf16[192,3584]{1,0:T(8,128)(2,1)S(1)}, u32[]{:S(2)}, u32[]{:S(2)}) collective-permute-start(bf16[192,3584]{1,0:T(8,128)(2,1)S(1)} %add_convert_fusion.3), channel_id=1, source_target_pairs={{0,8},{4,12},{8,16},{12,20},{16,24},{20,28},{1,9},{5,13},{9,17},{1... | collective-permute-start | bytes 4128776 | tf_op jit(solution)/shard_map/ppermute | solution.py:207
  410.8 29.8 %collective-permute-start.38 = (bf16[2,2,48,1408]{3,2,1,0:T(8,128)(2,1)S(1)}, bf16[2,2,48,1408]{3,2,1,0:T(8,128)(2,1)S(1)}, u32[]{:S(2)}, u32[]{:S(2)}) collective-permute-start(bf16[2,2,48,1408]{3,2,1,0:T(8,128)(2,1)S(1)} %pad_maximum_fusion.16), channel_id=1, source_target_pairs={{0,1},{1,0},{2,3},{3,2},{4,5},{5,4},{6,7},{7,6},{8,9},{9,8},{10,11... | collective-permute-start | bytes 1622024 | tf_op jit(solution)/shard_map/ppermute | solution.py:217
  434.9 19.9 %collective-permute-start.36 = (bf16[192,1728]{1,0:T(8,128)(2,1)S(1)}, bf16[192,1728]{1,0:T(8,128)(2,1)S(1)}, u32[]{:S(2)}, u32[]{:S(2)}) collective-permute-start(bf16[192,1728]{1,0:T(8,128)(2,1)S(1)} %pad_maximum_fusion.11), channel_id=1, source_target_pairs={{0,8},{4,12},{8,16},{12,20},{16,24},{20,28},{1,9},{5,13},{9,17},{1... | collective-permute-start | bytes 1990664 | tf_op jit(solution)/shard_map/ppermute | solution.py:207
  455.6 29.9 %collective-permute-start.40 = (bf16[192,3584]{1,0:T(8,128)(2,1)S(1)}, bf16[192,3584]{1,0:T(8,128)(2,1)S(1)}, u32[]{:S(2)}, u32[]{:S(2)}) collective-permute-start(bf16[192,3584]{1,0:T(8,128)(2,1)S(1)} %get-tuple-element.168), channel_id=1, source_target_pairs={{0,8},{4,12},{1,9},{5,13},{2,10},{6,14},{3,11},{7,15}} | collective-permute-start | bytes 4128776 | tf_op jit(solution)/shard_map/ppermute | solution.py:207
  460.3 25.8 %collective-permute-start.42 = (bf16[192,1728]{1,0:T(8,128)(2,1)S(1)}, bf16[192,1728]{1,0:T(8,128)(2,1)S(1)}, u32[]{:S(2)}, u32[]{:S(2)}) collective-permute-start(bf16[192,1728]{1,0:T(8,128)(2,1)S(1)} %collective-permute-done.36), channel_id=1, source_target_pairs={{8,16},{12,20},{16,24},{20,28},{9,17},{13,21},{17,25},{21,29},{10,... | collective-permute-start | bytes 1990664 | tf_op jit(solution)/shard_map/ppermute | solution.py:207
  461.0 25.1 %collective-permute-start.43 = (bf16[192,1728]{1,0:T(8,128)(2,1)}, bf16[192,1728]{1,0:T(8,128)(2,1)S(1)}, u32[]{:S(2)}, u32[]{:S(2)}) collective-permute-start(bf16[192,1728]{1,0:T(8,128)(2,1)} %collective-permute-done.37), channel_id=1, source_target_pairs={{8,0},{12,4},{16,8},{20,12},{9,1},{13,5},{17,9},{21,13},{10,2},{14... | collective-permute-start | bytes 1990664 | tf_op jit(solution)/shard_map/ppermute | solution.py:207
  486.1 27.7 %collective-permute-start.44 = (bf16[192,3584]{1,0:T(8,128)(2,1)S(1)}, bf16[192,3584]{1,0:T(8,128)(2,1)S(1)}, u32[]{:S(2)}, u32[]{:S(2)}) collective-permute-start(bf16[192,3584]{1,0:T(8,128)(2,1)S(1)} %get-tuple-element.172), channel_id=1, source_target_pairs={{0,8},{4,12},{8,16},{12,20},{1,9},{5,13},{9,17},{13,21},{2,10},{6,... | collective-permute-start | bytes 4128776 | tf_op jit(solution)/shard_map/ppermute | solution.py:207
  490.6 23.6 %collective-permute-start.45 = (bf16[192,3584]{1,0:T(8,128)(2,1)S(1)}, bf16[192,3584]{1,0:T(8,128)(2,1)S(1)}, u32[]{:S(2)}, u32[]{:S(2)}) collective-permute-start(bf16[192,3584]{1,0:T(8,128)(2,1)S(1)} %get-tuple-element.173), channel_id=1, source_target_pairs={{16,8},{20,12},{24,16},{28,20},{17,9},{21,13},{25,17},{29,21},{18,... | collective-permute-start | bytes 4128776 | tf_op jit(solution)/shard_map/ppermute | solution.py:207
  491.4 23.2 %collective-permute-start.46 = (bf16[192,1728]{1,0:T(8,128)(2,1)S(1)}, bf16[192,1728]{1,0:T(8,128)(2,1)S(1)}, u32[]{:S(2)}, u32[]{:S(2)}) collective-permute-start(bf16[192,1728]{1,0:T(8,128)(2,1)S(1)} %collective-permute-done.42), channel_id=1, source_target_pairs={{16,24},{20,28},{17,25},{21,29},{18,26},{22,30},{19,27},{23,31}} | collective-permute-start | bytes 1990664 | tf_op jit(solution)/shard_map/ppermute | solution.py:207
  492.1 22.5 %collective-permute-start.47 = (bf16[192,1728]{1,0:T(8,128)(2,1)S(1)}, bf16[192,1728]{1,0:T(8,128)(2,1)S(1)}, u32[]{:S(2)}, u32[]{:S(2)}) collective-permute-start(bf16[192,1728]{1,0:T(8,128)(2,1)S(1)} %collective-permute-done.43), channel_id=1, source_target_pairs={{8,0},{12,4},{9,1},{13,5},{10,2},{14,6},{11,3},{15,7}} | collective-permute-start | bytes 1990664 | tf_op jit(solution)/shard_map/ppermute | solution.py:207
  514.5 20.7 %collective-permute-start.49 = (bf16[192,3584]{1,0:T(8,128)(2,1)S(1)}, bf16[192,3584]{1,0:T(8,128)(2,1)S(1)}, u32[]{:S(2)}, u32[]{:S(2)}) collective-permute-start(bf16[192,3584]{1,0:T(8,128)(2,1)S(1)} %add_convert_fusion), channel_id=1, source_target_pairs={{8,0},{12,4},{16,8},{20,12},{24,16},{28,20},{9,1},{13,5},{17,9},{2... | collective-permute-start | bytes 4128776 | tf_op jit(solution)/shard_map/ppermute | solution.py:207
  515.8 29.0 %collective-permute-start.48 = (bf16[192,3584]{1,0:T(8,128)(2,1)S(1)}, bf16[192,3584]{1,0:T(8,128)(2,1)S(1)}, u32[]{:S(2)}, u32[]{:S(2)}) collective-permute-start(bf16[192,3584]{1,0:T(8,128)(2,1)S(1)} %add_convert_fusion.1), channel_id=1, source_target_pairs={{0,8},{4,12},{8,16},{12,20},{16,24},{20,28},{1,9},{5,13},{9,17},{1... | collective-permute-start | bytes 4128776 | tf_op jit(solution)/shard_map/ppermute | solution.py:207
  550.8 18.2 %collective-permute-start.51 = (bf16[192,1728]{1,0:T(8,128)(2,1)S(1)}, bf16[192,1728]{1,0:T(8,128)(2,1)S(1)}, u32[]{:S(2)}, u32[]{:S(2)}) collective-permute-start(bf16[192,1728]{1,0:T(8,128)(2,1)S(1)} %pad_maximum_fusion.12), channel_id=1, source_target_pairs={{8,0},{12,4},{16,8},{20,12},{24,16},{28,20},{9,1},{13,5},{17,9},{2... | collective-permute-start | bytes 1990664 | tf_op jit(solution)/shard_map/ppermute | solution.py:207
  569.7 21.2 %collective-permute-start.55 = (bf16[192,1728]{1,0:T(8,128)(2,1)S(1)}, bf16[192,1728]{1,0:T(8,128)(2,1)S(1)}, u32[]{:S(2)}, u32[]{:S(2)}) collective-permute-start(bf16[192,1728]{1,0:T(8,128)(2,1)S(1)} %collective-permute-done.51), channel_id=1, source_target_pairs={{8,0},{12,4},{16,8},{20,12},{9,1},{13,5},{17,9},{21,13},{10,2},{14... | collective-permute-start | bytes 1990664 | tf_op jit(solution)/shard_map/ppermute | solution.py:207
  (87 other events, 806.5 us)
Sparse Core Ops, SparseCore 0:
  10.1 57.4 all-gather.6
  69.2 118.5 all-gather.4
  231.6 38.6 all-gather.10
  302.1 35.4 all-gather.8
